TPU v7x, 32 devices: a whole 2x2x4 slice. The times are simulated.
32 devices in a mesh: dp: 16 (over z, y, core), tensor: 2 (over x).
Axes of the slice: x: 2, y: 2, z: 4, core: 2. Of those that a mesh axis runs over, the one named last changes fastest.
Arguments:
- hidden_in: bfloat16 [1024, 16, 1024], P('tensor', 'dp'), may hold values from -12 to 12
- query_w: bfloat16 [1024, 1024], P(None, 'tensor'), may hold values from -0.125 to 0.125
- key_w: bfloat16 [1024, 1024], P(None, 'tensor'), may hold values from -0.1875 to 0.1875
- value_w: bfloat16 [1024, 1024], P(None, 'tensor'), may hold values from -0.1875 to 0.1875
- query_b: bfloat16 [1024], P('tensor'), may hold values from -3 to 3
- value_b: bfloat16 [1024], P('tensor'), may hold values from -3 to 3
- out_w: bfloat16 [1024, 1024], P('tensor'), may hold values from -1.5 to 1.5
- out_b: bfloat16 [1024], replicated, may hold values from -3 to 3
- gain_attn: bfloat16 [1024], replicated, may hold values from 0.5 to 1.5
- shift_attn: bfloat16 [1024], replicated, may hold values from -3 to 3
- up_w: bfloat16 [1024, 4096], P(None, 'tensor'), may hold values from -0.1875 to 0.1875
- up_b: bfloat16 [4096], P('tensor'), may hold values from -3 to 3
- down_w: bfloat16 [4096, 1024], P('tensor'), may hold values from -0.125 to 0.125
- down_b: bfloat16 [1024], replicated, may hold values from -3 to 3
- gain_ffn: bfloat16 [1024], replicated, may hold values from 0.5 to 1.5
- shift_ffn: bfloat16 [1024], replicated, may hold values from -3 to 3
- random_blocks: int32 [16, 14, 3], P('tensor'), may hold values from 1 to 14, as said below
- cotangent: bfloat16 [1024, 16, 1024], P('tensor', 'dp'), may hold values from -6 to 6
Outputs:
- layer_out: bfloat16 [1024, 16, 1024], P('tensor', 'dp')
- grad_input: bfloat16 [1024, 16, 1024], P('tensor', 'dp')
- grad_query_w: float32 [1024, 1024], P(None, 'tensor')
- grad_key_w: float32 [1024, 1024], P(None, 'tensor')
- grad_value_w: float32 [1024, 1024], P(None, 'tensor')
- grad_query_b: float32 [1024], P('tensor')
- grad_value_b: float32 [1024], P('tensor')
- grad_out_w: float32 [1024, 1024], P('tensor')
- grad_out_b: float32 [1024], replicated
- grad_gain_attn: float32 [1024], replicated
- grad_shift_attn: float32 [1024], replicated
- grad_up_w: float32 [1024, 4096], P(None, 'tensor')
- grad_up_b: float32 [4096], P('tensor')
- grad_down_w: float32 [4096, 1024], P('tensor')
- grad_down_b: float32 [1024], replicated
- grad_gain_ffn: float32 [1024], replicated
- grad_shift_ffn: float32 [1024], replicated
- rms_stats: float32 [3], replicated
Inputs may be any that keep to these rules, and one draw needn't show every extreme that they name: `random_blocks`: entry [h, i, :] names 3 different key blocks for head h and query block i + 1, none of them 0, 15, i, i + 1 or i + 2.
All inputs are finite; a program needn't handle non-finite values.
Results may differ from a plain program's by a relative error of at most 0.025.
Values may be sent and summed in bfloat16 or wider, within the bound.
No kernel may reach another device: no remote copies, remote signals or barrier semaphores. Data moves between devices by JAX's collectives and lax.ppermute only.
A program may use at most 256 MiB of HBM per device.

v0:
```python
import math

import jax
import jax.numpy as jnp
from jax import lax
from jax.sharding import PartitionSpec as P

HD = 64
BLOCK = 64


NEG = -1e30
EPS = 1e-12
GELU_C = math.sqrt(2.0 / math.pi)


def layer_norm(rows, gain, shift):
    centre = rows - jnp.mean(rows, -1, keepdims=True)
    inverse = lax.rsqrt(jnp.mean(centre * centre, -1, keepdims=True) + EPS)
    normed = centre * inverse
    return (gain * normed + shift, normed, inverse)


def norm_back(grad, normed, inverse, gain):
    scaled = grad * gain
    dresid = inverse * (
        scaled
        - jnp.mean(scaled, -1, keepdims=True)
        - normed * jnp.mean(scaled * normed, -1, keepdims=True)
    )
    return (dresid, jnp.sum(grad * normed, (0, 1)), jnp.sum(grad, (0, 1)))


def gelu_parts(values):
    tanh_val = jnp.tanh(GELU_C * (values + 0.044715 * values * values * values))
    output = 0.5 * values * (1.0 + tanh_val)
    gelu_slope = 0.5 * (1.0 + tanh_val) + 0.5 * values * (1.0 - tanh_val * tanh_val) * GELU_C * (
        1.0 + 3.0 * 0.044715 * values * values
    )
    return (output, gelu_slope)


def key_table(random_ids):
    middle = random_ids.shape[-2]
    blocks = middle + 2
    query_ids = jnp.arange(middle, dtype=jnp.int32) + 1
    fixed_ids = jnp.stack(
        [
            query_ids - 1,
            query_ids,
            query_ids + 1,
            jnp.zeros_like(query_ids),
            jnp.full_like(query_ids, blocks - 1),
        ],
        -1,
    )
    fixed_ids = jnp.broadcast_to(fixed_ids, random_ids.shape[:-1] + (5,))
    tile_ids = jnp.concatenate([fixed_ids, random_ids], -1)
    tile_keep = jnp.concatenate(
        [
            jnp.ones((middle, 3), bool),
            (query_ids != 1)[:, None],
            (query_ids != blocks - 2)[:, None],
            jnp.ones((middle, random_ids.shape[-1]), bool),
        ],
        -1,
    )
    return (tile_ids, tile_keep)


def to_blocks(rows, head_dim):
    length, seqs_here, channels = rows.shape
    return rows.reshape(
        length // BLOCK, BLOCK, seqs_here, channels // head_dim, head_dim
    ).transpose(2, 3, 0, 1, 4)


def from_blocks(blocks):
    seqs_here, heads_here, count_blocks, block_len, head_dim = blocks.shape
    return blocks.transpose(2, 3, 0, 1, 4).reshape(
        count_blocks * block_len, seqs_here, heads_here * head_dim
    )


def gather_tiles(blocks, tile_ids):
    picked = jax.vmap(lambda one_head, head_ids: one_head[:, head_ids], in_axes=(1, 0), out_axes=1)(
        blocks, tile_ids
    )
    return picked.reshape(picked.shape[0], picked.shape[1], picked.shape[2], -1, picked.shape[-1])


def middle_scores(query_blocks, key_tiles, tile_keep):
    score_scale = query_blocks.shape[-1] ** (-0.5)
    scores = (
        jnp.einsum(
            "shmqd,shmkd->shmqk",
            query_blocks[:, :, 1:-1],
            key_tiles,
            preferred_element_type=jnp.float32,
        )
        * score_scale
    )
    key_mask = jnp.repeat(tile_keep, BLOCK, axis=-1)
    return jnp.where(key_mask[:, None, :], scores, NEG)


def end_rows(blocks):
    return jnp.concatenate([blocks[:, :, :1], blocks[:, :, -1:]], 2)


def flat_keys(blocks):
    return blocks.reshape(blocks.shape[0], blocks.shape[1], -1, blocks.shape[-1])


def end_scores_of(query_blocks, key_blocks):
    score_scale = query_blocks.shape[-1] ** (-0.5)
    return (
        jnp.einsum(
            "shgqd,shkd->shgqk",
            end_rows(query_blocks),
            flat_keys(key_blocks),
            preferred_element_type=jnp.float32,
        )
        * score_scale
    )


def log_total_of(scores):
    row_top = jnp.max(scores, -1, keepdims=True)
    return row_top + jnp.log(jnp.sum(jnp.exp(scores - row_top), -1, keepdims=True))


def attend(query_blocks, key_blocks, value_blocks, tile_ids, tile_keep):
    key_tiles = gather_tiles(key_blocks, tile_ids)
    value_tiles = gather_tiles(value_blocks, tile_ids)
    mid_scores = middle_scores(query_blocks, key_tiles, tile_keep)
    mid_total = log_total_of(mid_scores)
    mid_probs = jnp.exp(mid_scores - mid_total).astype(jnp.bfloat16)
    mid_out = jnp.einsum(
        "shmqk,shmkd->shmqd", mid_probs, value_tiles, preferred_element_type=jnp.float32
    )
    end_scores = end_scores_of(query_blocks, key_blocks)
    end_total = log_total_of(end_scores)
    end_probs = jnp.exp(end_scores - end_total).astype(jnp.bfloat16)
    end_out = jnp.einsum(
        "shgqk,shkd->shgqd", end_probs, flat_keys(value_blocks), preferred_element_type=jnp.float32
    )
    joined = jnp.concatenate([end_out[:, :, :1], mid_out, end_out[:, :, 1:]], 2)
    return (joined, mid_total, end_total)


def attend_back(
    query_blocks, key_blocks, value_blocks, dout_blocks, tile_ids, tile_keep, mid_total, end_total
):
    seqs_here, heads_here, count_blocks, block_len, head_dim = query_blocks.shape
    score_scale = head_dim ** (-0.5)
    key_tiles = gather_tiles(key_blocks, tile_ids)
    value_tiles = gather_tiles(value_blocks, tile_ids)
    mid_probs = jnp.exp(middle_scores(query_blocks, key_tiles, tile_keep) - mid_total)
    mid_low = mid_probs.astype(jnp.bfloat16)
    dout_mid = dout_blocks[:, :, 1:-1]
    dprobs = jnp.einsum(
        "shmqd,shmkd->shmqk", dout_mid, value_tiles, preferred_element_type=jnp.float32
    )
    row_dot = jnp.sum(mid_probs * dprobs, -1, keepdims=True)
    dscores = (mid_probs * (dprobs - row_dot)).astype(jnp.bfloat16)
    dq_mid = (
        jnp.einsum("shmqk,shmkd->shmqd", dscores, key_tiles, preferred_element_type=jnp.float32)
        * score_scale
    )
    dk_tiles = (
        jnp.einsum(
            "shmqk,shmqd->shmkd",
            dscores,
            query_blocks[:, :, 1:-1],
            preferred_element_type=jnp.float32,
        )
        * score_scale
    )
    dv_tiles = jnp.einsum(
        "shmqk,shmqd->shmkd", mid_low, dout_mid, preferred_element_type=jnp.float32
    )
    onehot = (tile_ids[..., None] == jnp.arange(count_blocks, dtype=jnp.int32)).astype(jnp.float32)
    tile_shape = (seqs_here, heads_here, count_blocks - 2, tile_ids.shape[-1], block_len, head_dim)
    dkeys = jnp.einsum("hmjn,shmjbd->shnbd", onehot, dk_tiles.reshape(tile_shape))
    dvalues = jnp.einsum("hmjn,shmjbd->shnbd", onehot, dv_tiles.reshape(tile_shape))
    end_probs = jnp.exp(end_scores_of(query_blocks, key_blocks) - end_total)
    end_low = end_probs.astype(jnp.bfloat16)
    dout_end = end_rows(dout_blocks)
    dprobs_end = jnp.einsum(
        "shgqd,shkd->shgqk", dout_end, flat_keys(value_blocks), preferred_element_type=jnp.float32
    )
    row_dot_end = jnp.sum(end_probs * dprobs_end, -1, keepdims=True)
    dscores_end = (end_probs * (dprobs_end - row_dot_end)).astype(jnp.bfloat16)
    dq_end = (
        jnp.einsum(
            "shgqk,shkd->shgqd",
            dscores_end,
            flat_keys(key_blocks),
            preferred_element_type=jnp.float32,
        )
        * score_scale
    )
    dk_end = (
        jnp.einsum(
            "shgqk,shgqd->shkd",
            dscores_end,
            end_rows(query_blocks),
            preferred_element_type=jnp.float32,
        )
        * score_scale
    )
    dv_end = jnp.einsum("shgqk,shgqd->shkd", end_low, dout_end, preferred_element_type=jnp.float32)
    dkeys = dkeys + dk_end.reshape(dkeys.shape)
    dvalues = dvalues + dv_end.reshape(dvalues.shape)
    dqueries = jnp.concatenate([dq_end[:, :, :1], dq_mid, dq_end[:, :, 1:]], 2)
    return (dqueries, dkeys, dvalues)


def local(
    hidden_in,
    query_w,
    key_w,
    value_w,
    query_b,
    value_b,
    out_w,
    out_b,
    gain_attn,
    shift_attn,
    up_w,
    up_b,
    down_w,
    down_b,
    gain_ffn,
    shift_ffn,
    random_blocks,
    cotangent,
):
    local_rows, seqs_here, width = hidden_in.shape
    seq_rows = lax.all_gather(hidden_in, "tensor", axis=0, tiled=True)
    length = seq_rows.shape[0]
    flat_rows = seq_rows.reshape(-1, width)
    channels = query_w.shape[1]
    queries = (jnp.dot(flat_rows, query_w, preferred_element_type=jnp.float32) + query_b).astype(
        jnp.bfloat16
    )
    key_rows = jnp.dot(flat_rows, key_w, preferred_element_type=jnp.float32).astype(jnp.bfloat16)
    value_rows = (jnp.dot(flat_rows, value_w, preferred_element_type=jnp.float32) + value_b).astype(
        jnp.bfloat16
    )
    query_blocks = to_blocks(queries.reshape(length, seqs_here, channels), HD)
    key_blocks = to_blocks(key_rows.reshape(length, seqs_here, channels), HD)
    value_blocks = to_blocks(value_rows.reshape(length, seqs_here, channels), HD)
    tile_ids, tile_keep = key_table(random_blocks)
    context_blocks, mid_total, end_total = attend(
        query_blocks, key_blocks, value_blocks, tile_ids, tile_keep
    )
    context = from_blocks(context_blocks).astype(jnp.bfloat16)
    piece = context.reshape(-1, channels)
    attn_out = lax.psum_scatter(
        jnp.dot(piece, out_w, preferred_element_type=jnp.float32).reshape(
            lax.axis_size("tensor") * local_rows, seqs_here, width
        ),
        "tensor",
        scatter_dimension=0,
        tiled=True,
    )
    resid = hidden_in.astype(jnp.float32) + attn_out + out_b
    hidden, normed_one, inverse_one = layer_norm(resid, gain_attn, shift_attn)
    hidden_low = hidden.astype(jnp.bfloat16)
    ffn_rows = lax.all_gather(hidden_low, "tensor", axis=0, tiled=True)
    ffn_flat = ffn_rows.reshape(-1, width)
    up_rows = jnp.dot(ffn_flat, up_w, preferred_element_type=jnp.float32) + up_b
    act_rows, gelu_slope = gelu_parts(up_rows)
    act_low = act_rows.astype(jnp.bfloat16)
    act_seq = act_low.reshape(length, seqs_here, -1)
    piece = act_seq.reshape(-1, act_seq.shape[-1])
    mlp_out = lax.psum_scatter(
        jnp.dot(piece, down_w, preferred_element_type=jnp.float32)
        .reshape(local_rows * lax.axis_size("tensor"), seqs_here, width)
        .astype(jnp.bfloat16),
        "tensor",
        scatter_dimension=0,
        tiled=True,
    ).astype(jnp.float32)
    resid2 = hidden + mlp_out + down_b
    layer_out, normed_two, inverse_two = layer_norm(resid2, gain_ffn, shift_ffn)
    square_sums = (jnp.sum(resid * resid), jnp.sum(attn_out * attn_out), jnp.sum(mlp_out * mlp_out))
    dresid2, grad_gain_ffn, grad_shift_ffn = norm_back(
        cotangent.astype(jnp.float32), normed_two, inverse_two, gain_ffn
    )
    grad_down_b = jnp.sum(dresid2, (0, 1))
    dmlp = dresid2.astype(jnp.bfloat16)
    dmlp_rows = lax.all_gather(dmlp, "tensor", axis=0, tiled=True)
    dmlp_flat = dmlp_rows.reshape(-1, width)
    dact = jnp.einsum("rd,fd->rf", dmlp_flat, down_w, preferred_element_type=jnp.float32)
    dup = (dact * gelu_slope).astype(jnp.bfloat16)
    grad_down_w = jnp.einsum("rf,rd->fd", act_low, dmlp_flat, preferred_element_type=jnp.float32)
    grad_up_w = jnp.einsum("rd,rf->df", ffn_flat, dup, preferred_element_type=jnp.float32)
    grad_up_b = jnp.sum(dup.astype(jnp.float32), 0)
    dup_seq = dup.reshape(length, seqs_here, -1)
    piece = dup_seq.reshape(-1, dup_seq.shape[-1])
    dhidden_part = lax.psum_scatter(
        jnp.einsum("rf,df->rd", piece, up_w, preferred_element_type=jnp.float32)
        .reshape(local_rows * lax.axis_size("tensor"), seqs_here, width)
        .astype(jnp.bfloat16),
        "tensor",
        scatter_dimension=0,
        tiled=True,
    ).astype(jnp.float32)
    dhidden = dhidden_part + dresid2
    dresid, grad_gain_attn, grad_shift_attn = norm_back(dhidden, normed_one, inverse_one, gain_attn)
    grad_out_b = jnp.sum(dresid, (0, 1))
    dattn = dresid.astype(jnp.bfloat16)
    dattn_rows = lax.all_gather(dattn, "tensor", axis=0, tiled=True)
    dattn_flat = dattn_rows.reshape(-1, width)
    grad_out_w = jnp.einsum(
        "rc,rd->cd", context.reshape(-1, channels), dattn_flat, preferred_element_type=jnp.float32
    )
    dcontext = jnp.einsum(
        "rd,cd->rc", dattn_flat, out_w, preferred_element_type=jnp.float32
    ).astype(jnp.bfloat16)
    dout_blocks = to_blocks(dcontext.reshape(length, seqs_here, channels), HD)
    dq_blocks, dk_blocks, dv_blocks = attend_back(
        query_blocks,
        key_blocks,
        value_blocks,
        dout_blocks,
        tile_ids,
        tile_keep,
        mid_total,
        end_total,
    )
    dqueries = from_blocks(dq_blocks).astype(jnp.bfloat16)
    dkeys = from_blocks(dk_blocks).astype(jnp.bfloat16)
    dvalues = from_blocks(dv_blocks).astype(jnp.bfloat16)
    grad_query_w = jnp.einsum(
        "rd,rc->dc", flat_rows, dqueries.reshape(-1, channels), preferred_element_type=jnp.float32
    )
    grad_key_w = jnp.einsum(
        "rd,rc->dc", flat_rows, dkeys.reshape(-1, channels), preferred_element_type=jnp.float32
    )
    grad_value_w = jnp.einsum(
        "rd,rc->dc", flat_rows, dvalues.reshape(-1, channels), preferred_element_type=jnp.float32
    )
    grad_query_b = jnp.sum(dqueries.astype(jnp.float32), (0, 1))
    grad_value_b = jnp.sum(dvalues.astype(jnp.float32), (0, 1))
    q_piece = dqueries.reshape(-1, channels)
    k_piece = dkeys.reshape(-1, channels)
    v_piece = dvalues.reshape(-1, channels)
    summed = jnp.einsum("rc,dc->rd", q_piece, query_w, preferred_element_type=jnp.float32)
    summed = summed + jnp.einsum("rc,dc->rd", k_piece, key_w, preferred_element_type=jnp.float32)
    summed = summed + jnp.einsum("rc,dc->rd", v_piece, value_w, preferred_element_type=jnp.float32)
    dinput_part = lax.psum_scatter(
        summed.reshape(local_rows * lax.axis_size("tensor"), seqs_here, width).astype(jnp.bfloat16),
        "tensor",
        scatter_dimension=0,
        tiled=True,
    ).astype(jnp.float32)
    grad_input = (dinput_part + dresid).astype(jnp.bfloat16)
    (
        grad_query_w,
        grad_key_w,
        grad_value_w,
        grad_out_w,
        grad_up_w,
        grad_down_w,
        grad_query_b,
        grad_value_b,
        grad_up_b,
    ) = (
        lax.psum(grad_query_w.astype(jnp.bfloat16), "dp").astype(jnp.float32),
        lax.psum(grad_key_w.astype(jnp.bfloat16), "dp").astype(jnp.float32),
        lax.psum(grad_value_w.astype(jnp.bfloat16), "dp").astype(jnp.float32),
        lax.psum(grad_out_w.astype(jnp.bfloat16), "dp").astype(jnp.float32),
        lax.psum(grad_up_w.astype(jnp.bfloat16), "dp").astype(jnp.float32),
        lax.psum(grad_down_w.astype(jnp.bfloat16), "dp").astype(jnp.float32),
        lax.psum(grad_query_b.astype(jnp.bfloat16), "dp").astype(jnp.float32),
        lax.psum(grad_value_b.astype(jnp.bfloat16), "dp").astype(jnp.float32),
        lax.psum(grad_up_b.astype(jnp.bfloat16), "dp").astype(jnp.float32),
    )
    (
        grad_out_b,
        grad_gain_attn,
        grad_shift_attn,
        grad_down_b,
        grad_gain_ffn,
        grad_shift_ffn,
        sum_resid,
        sum_attn,
        sum_mlp,
    ) = lax.psum(
        (
            grad_out_b,
            grad_gain_attn,
            grad_shift_attn,
            grad_down_b,
            grad_gain_ffn,
            grad_shift_ffn,
            square_sums[0],
            square_sums[1],
            square_sums[2],
        ),
        ("dp", "tensor"),
    )
    entries = float(hidden_in.size * lax.axis_size("dp") * lax.axis_size("tensor"))
    rms_stats = jnp.sqrt(jnp.stack([sum_resid, sum_attn, sum_mlp]) / entries)
    return (
        layer_out.astype(jnp.bfloat16),
        grad_input,
        grad_query_w,
        grad_key_w,
        grad_value_w,
        grad_query_b,
        grad_value_b,
        grad_out_w,
        grad_out_b,
        grad_gain_attn,
        grad_shift_attn,
        grad_up_w,
        grad_up_b,
        grad_down_w,
        grad_down_b,
        grad_gain_ffn,
        grad_shift_ffn,
        rms_stats,
    )


def solution(mesh):
    return jax.shard_map(
        local,
        mesh=mesh,
        in_specs=(
            P("tensor", "dp", None),
            P(None, "tensor"),
            P(None, "tensor"),
            P(None, "tensor"),
            P("tensor"),
            P("tensor"),
            P("tensor", None),
            P(),
            P(),
            P(),
            P(None, "tensor"),
            P("tensor"),
            P("tensor", None),
            P(),
            P(),
            P(),
            P("tensor", None, None),
            P("tensor", "dp", None),
        ),
        out_specs=(
            P("tensor", "dp", None),
            P("tensor", "dp", None),
            P(None, "tensor"),
            P(None, "tensor"),
            P(None, "tensor"),
            P("tensor"),
            P("tensor"),
            P("tensor", None),
            P(),
            P(),
            P(),
            P(None, "tensor"),
            P("tensor"),
            P("tensor", None),
            P(),
            P(),
            P(),
            P(),
        ),
        check_vma=False,
    )
```

profile of v0, /device:TPU:0, one launch (start us, length us, event | category | flops | bytes accessed | tf_op | source)
XLA Modules:
  0.0 935.9 jit_solution(5058792545610152636)
XLA Ops:
  10.8 34.6 %all-gather.5.cloned.1.call-done = bf16[1024,1,1024]{2,0,1:T(8,128)(2,1)} async-done(((bf16[512,1,1024]{2,0,1:T(8,128)(2,1)}), bf16[1024,1,1024]{2,0,1:T(8,128)(2,1)}) %all-gather.5.cloned.1.call-update) | async-done | bytes 2097168 | tf_op jit(solution)/shard_map/all_gather | solution.py:241
  45.4 3.1 add_convert_fusion.3
  52.8 3.3 copy.85
  56.1 4.1 add_convert_fusion.4
  60.1 3.9 reshape_reshape.12
  69.9 3.9 reshape_reshape.13
  73.8 3.5 copy.117
  77.3 3.3 copy.84
  85.3 11.6 %gather_fusion.1 = bf16[896,64,64]{2,1,0:T(8,128)(2,1)} fusion(bf16[8,16,64,64]{3,2,1,0:T(8,128)(2,1)S(1)} %bitcast.250, s32[896]{0:T(1024)S(1)} %reshape.478), kind=kCustom, calls=%fused_computation.1 | custom fusion | bytes 14687232 | tf_op jit(solution)/shard_map/vmap()/gather | solution.py:86
  96.9 15.7 %gather_fusion = bf16[896,64,64]{2,1,0:T(8,128)(2,1)} fusion(bf16[8,16,64,64]{3,2,1,0:T(8,128)(2,1)} %bitcast.251, s32[896]{0:T(1024)S(1)} %reshape.478), kind=kCustom, calls=%fused_computation | custom fusion | bytes 14687232 | tf_op jit(solution)/shard_map/vmap()/gather | solution.py:86
  112.6 11.7 %fusion = (f32[8,14,64]{2,1,0:T(8,128)S(1)}, f32[8,14,64,512]{3,2,1,0:T(8,128)}) fusion(pred[14,512]{1,0:T(8,128)(4,1)S(1)} %broadcast_in_dim_reshape.4, bf16[8,14,512,64]{3,2,1,0:T(8,128)(2,1)} %bitcast.246, bf16[1,8,16,64,64]{4,3,2,1,0:T(8,128)(2,1)S(1)} %bitcast.256), kind=kOutput, calls=%fused_computation.9 | convolution fusion | flops 480764928 | bytes 23891968 | tf_op jit(solution)/shard_map/shmqd,shmkd->shmqk/dot_general | solution.py:95
  124.4 7.4 exponential_reduce_fusion
  131.8 13.5 %convolution_bitcast_fusion.3 = bf16[1,8,14,64,64]{4,3,2,1,0:T(8,128)(2,1)S(1)} fusion(bf16[8,14,512,64]{3,2,1,0:T(8,128)(2,1)} %bitcast.252, f32[8,14,64,512]{3,2,1,0:T(8,128)} %get-tuple-element.108, f32[8,14,64]{2,1,0:T(8,128)S(1)} %log_add_fusion, pred[14,512]{1,0:T(8,128)(4,1)S(1)} %broadcast_in_dim_reshape.4), kind=kOutput, calls=%fused_computation.99 | convolution fusion | flops 484442112 | bytes 22973440 | tf_op jit(solution)/shard_map/shmqk,shmkd->shmqd/dot_general | solution.py:139
  149.7 4.5 convolution_bitcast_fusion.2
  154.9 53.8 %reduce-scatter.5.cloned.1.call-done = f32[512,1,1024]{2,0,1:T(8,128)} async-done(((f32[1024,1,1024]{2,0,1:T(8,128)}), f32[512,1,1024]{2,0,1:T(8,128)}) %reduce-scatter.5.cloned.1.call-update) | async-done | bytes 2097168 | tf_op jit(solution)/shard_map/reduce_scatter | solution.py:261
  208.6 3.2 fusion.118
  213.7 33.2 %all-gather.7.cloned.1.call-done = bf16[1024,1,1024]{2,0,1:T(8,128)(2,1)} async-done(((bf16[512,1,1024]{2,0,1:T(8,128)(2,1)}), bf16[1024,1,1024]{2,0,1:T(8,128)(2,1)}) %all-gather.7.cloned.1.call-update) | async-done | bytes 2097168 | tf_op jit(solution)/shard_map/all_gather | solution.py:272
  246.9 7.5 fusion.32
  254.4 3.4 copy-done.51
  257.8 6.6 convert_bitcast_fusion.1
  264.6 31.9 %reduce-scatter.7.cloned.1.call-done = bf16[512,1,1024]{2,0,1:T(8,128)(2,1)} async-done(((bf16[1024,1,1024]{2,0,1:T(8,128)(2,1)}), bf16[512,1,1024]{2,0,1:T(8,128)(2,1)}) %reduce-scatter.7.cloned.1.call-update) | async-done | bytes 1048592 | tf_op jit(solution)/shard_map/reduce_scatter | solution.py:279
  296.4 3.0 fusion.116
  301.4 2.9 fusion.114
  304.3 33.2 %all-gather.9.cloned.1.call-done = bf16[1024,1,1024]{2,0,1:T(8,128)(2,1)} async-done(((bf16[512,1,1024]{2,0,1:T(8,128)(2,1)}), bf16[1024,1,1024]{2,0,1:T(8,128)(2,1)}) %all-gather.9.cloned.1.call-update) | async-done | bytes 2097168 | tf_op jit(solution)/shard_map/all_gather | solution.py:295
  337.5 13.5 %fusion.123 = (bf16[2048]{0:T(1024)(128)(2,1)}, bf16[1024,2048]{1,0:T(8,128)(2,1)S(1)}) fusion(f32[1024,2048]{1,0:T(8,128)} %copy-done.51, f32[2048]{0:T(1024)S(1)} %convert_element_type.248, bf16[2048,1024]{1,0:T(8,128)(2,1)} %param.30, bf16[1024,1,1024]{2,0,1:T(8,128)(2,1)} %all-gather.9.cloned.1.call-done), kind=kOutput, calls=%fused_computation.174 | convolution fusion | flops 4339005440 | bytes 18886656 | tf_op jit(solution)/shard_map/rd,fd->rf/dot_general | solution.py:297
  353.0 5.7 convert_bitcast_fusion
  358.8 31.9 %reduce-scatter.9.cloned.1.call-done = bf16[512,1,1024]{2,0,1:T(8,128)(2,1)} async-done(((bf16[1024,1,1024]{2,0,1:T(8,128)(2,1)}), bf16[512,1,1024]{2,0,1:T(8,128)(2,1)}) %reduce-scatter.9.cloned.1.call-update) | async-done | bytes 1048592 | tf_op jit(solution)/shard_map/reduce_scatter | solution.py:304
  390.7 4.0 multiply_reduce_fusion.5
  398.8 32.5 %all-gather.11.cloned.1.call-done = bf16[1024,1,1024]{2,0,1:T(8,128)(2,1)} async-done(((bf16[512,1,1024]{2,0,1:T(8,128)(2,1)}), bf16[1024,1,1024]{2,0,1:T(8,128)(2,1)}) %all-gather.11.cloned.1.call-update) | async-done | bytes 2097168 | tf_op jit(solution)/shard_map/all_gather | solution.py:316
  431.3 3.8 fusion.67
  435.1 3.0 reshape_reshape.15
  440.0 18.3 %multiply_reduce_fusion = (f32[8,14,64]{2,1,0:T(8,128)S(1)}, f32[8,14,64,512]{3,2,1,0:T(8,128)}) fusion(f32[8,14,64,512]{3,2,1,0:T(8,128)} %get-tuple-element.108, f32[8,14,64]{2,1,0:T(8,128)S(1)} %log_add_fusion, pred[14,512]{1,0:T(8,128)(4,1)S(1)} %broadcast_in_dim_reshape.4, bf16[8,14,512,64]{3,2,1,0:T(8,128)(2,1)} %bitcast.253, ...), kind=kOutput, calls=%fused_computation.3 | convolution fusion | flops 488104960 | bytes 38637568 | tf_op jit(solution)/shard_map/shmqd,shmkd->shmqk/dot_general | solution.py:162
  458.2 9.8 %fusion.49 = bf16[8,14,512,64]{2,3,1,0:T(8,128)(2,1)} fusion(bf16[1,8,16,64,64]{4,3,2,1,0:T(8,128)(2,1)} %bitcast.260, f32[8,14,64,512]{3,2,1,0:T(8,128)} %get-tuple-element.108, f32[8,14,64]{2,1,0:T(8,128)S(1)} %log_add_fusion, pred[14,512]{1,0:T(8,128)(4,1)S(1)} %broadcast_in_dim_reshape.4), kind=kOutput, calls=%fused_computation.109 | convolution fusion | flops 484442112 | bytes 23890944 | tf_op jit(solution)/shard_map/shmqk,shmqd->shmkd/dot_general | solution.py:180
  468.0 15.3 %multiply_convert_fusion = bf16[8,14,64,512]{3,2,1,0:T(8,128)(2,1)} fusion(f32[8,14,64,512]{3,2,1,0:T(8,128)} %get-tuple-element.112, f32[8,14,64,512]{3,2,1,0:T(8,128)} %get-tuple-element.108, f32[8,14,64]{2,1,0:T(8,128)S(1)} %get-tuple-element.111, f32[8,14,64]{2,1,0:T(8,128)S(1)} %log_add_fusion, pred[14,512]{1,0:T(8,128)(4,1)S(1)} %broadcast_in_dim_reshape.4), kind=kLoop, calls=%fused_computation.2 | loop fusion | flops 22020096 | bytes 36764672 | tf_op jit(solution)/shard_map/convert_element_type | solution.py:166
  483.3 7.2 multiply_bitcast_fusion
  490.6 8.6 convolution_multiply_fusion
  500.3 5.1 convolution_bitcast_fusion.4
  509.7 4.5 reshape.475
  514.2 6.1 copy.79
  522.6 3.1 copy.68
  525.7 3.2 convert_element_type.268
  528.9 2.7 reshape.473
  531.6 6.1 copy.74
  537.7 3.4 fusion.124
  541.1 18.9 %reshape.472 = bf16[8,14,8,64,64]{3,2,4,1,0:T(8,128)(2,1)} reshape(bf16[8,14,512,64]{2,3,1,0:T(8,128)(2,1)} %convolution_multiply_fusion) | data formatting | bytes 14680064 | tf_op jit(solution)/shard_map/reshape.102
  559.9 8.5 convolution_bitcast_fusion.1
  568.4 6.0 copy.89
  574.5 4.0 fusion.21
  581.1 4.9 fusion.125
  586.0 18.9 %reshape.474 = bf16[8,14,8,64,64]{3,2,4,1,0:T(8,128)(2,1)} reshape(bf16[8,14,512,64]{2,3,1,0:T(8,128)(2,1)} %fusion.49) | data formatting | bytes 14680064 | tf_op jit(solution)/shard_map/reshape.111
  604.8 8.4 convolution_bitcast_fusion
  613.2 6.0 copy.94
  619.2 4.0 fusion.110
  625.9 6.5 fusion.47
  632.5 8.7 convolution_convert_fusion.1
  641.2 12.0 %convolution_convert_fusion = bf16[2048,1024]{1,0:T(8,128)(2,1)} fusion(bf16[1024,1,1024]{2,0,1:T(8,128)(2,1)S(1)} %copy-done.47, f32[1024,2048]{1,0:T(8,128)} %copy-done.51, f32[2048]{0:T(1024)S(1)} %convert_element_type.248), kind=kOutput, calls=%fused_computation.31 | convolution fusion | flops 4318035968 | bytes 14688256 | tf_op jit(solution)/shard_map/rf,rd->fd/dot_general | solution.py:299
  663.0 41.6 %all-reduce = (f32[1024]{0:T(1024)}, f32[1024]{0:T(1024)}, f32[1024]{0:T(1024)}, f32[1024]{0:T(1024)}, f32[1024]{0:T(1024)}, /*index=5*/f32[1024]{0:T(1024)}, f32[1]{0:T(128)}, f32[1]{0:T(128)}, f32[1]{0:T(128)}) all-reduce(f32[1024]{0:T(1024)S(1)} %get-tuple-element.82, ...), channel_id=1, replica_groups=mesh['dp'=16,'tensor'=2] {'dp','tensor'}, use_global_device_ids=true, to_apply=%region_27.28 | all-reduce | flops 6147 | bytes 49176 | tf_op jit(solution)/shard_map/psum | solution.py:393
  707.3 35.5 %all-reduce.1 = (bf16[512]{0:T(512)(128)(2,1)S(1)}, bf16[512]{0:T(512)(128)(2,1)S(1)}, bf16[2048]{0:T(1024)(128)(2,1)S(1)}) all-reduce(bf16[512]{0:T(512)(128)(2,1)S(1)} %reduce_sum.242, bf16[512]{0:T(512)(128)(2,1)S(1)} %reduce_sum.244, bf16[2048]{0:T(1024)(128)(2,1)S(1)} %copy-done.37), channel_id=1, replica_groups=mesh['dp'=16,'tensor'=2] {'dp'}, use_global_device_ids=true, to_apply=%region_22.23 | all-reduce | flops 3072 | bytes 12288 | tf_op jit(solution)/shard_map/psum | solution.py:379
  744.6 2.6 add_convert_fusion.1
  747.1 162.1 %all-reduce.5.cloned.1.call-done = (bf16[1024,512]{0,1:T(8,128)(2,1)}, bf16[1024,512]{0,1:T(8,128)(2,1)}, bf16[1024,512]{0,1:T(8,128)(2,1)}, bf16[512,1024]{1,0:...) async-done(((bf16[1024,512]{0,1:T(8,128)(2,1)}, bf16[1024,512]{0,1:T(8,128)(2,1)}, bf16[1024,512]{0,1:T(8,128)(2,1)}, bf16[512,1024]{1,0:T(8,128)(2,1)}, ...) | async-done | bytes 12582928 | tf_op jit(solution)/shard_map/psum | solution.py:373
  909.2 2.7 copy.81
  911.9 2.6 copy.82
  917.7 6.8 convert_element_type.293
  924.5 4.4 convert_element_type.296
  (212 shorter events, 65.4 us)
Async XLA Ops:
  7.2 142.5 %copy-start = (bf16[512,1024]{1,0:T(8,128)(2,1)S(1)}, bf16[512,1024]{1,0:T(8,128)(2,1)}, u32[]{:S(2)}) copy-start(bf16[512,1024]{1,0:T(8,128)(2,1)} %param.24) | copy-start | bytes 3145732
  7.2 38.2 %all-gather.5.cloned.1.call-start = ((), (), s32[]{:S(2)}) async-start(), calls=%async_computation.4 | async-start | bytes 3145728 | tf_op jit(solution)/shard_map/all_gather | solution.py:241
  7.9 200.7 %reduce-scatter.5.cloned.1.call-start = ((), (), s32[]{:S(2)}) async-start(), calls=%async_computation.5 | async-start | bytes 6291456 | tf_op jit(solution)/shard_map/reduce_scatter | solution.py:261
  64.0 3.6 copy-start.9
  64.0 3.6 copy-start.49
  66.3 1.3 copy-start.4
  67.7 12.9 %copy-start.24 = (bf16[1,8,1,64,64]{4,3,2,1,0:T(8,128)(2,1)}, bf16[1,8,1,64,64]{4,3,2,1,0:T(8,128)(2,1)S(1)}, u32[]{:S(2)}) copy-start(bf16[1,8,1,64,64]{4,3,2,1,0:T(8,128)(2,1)S(1)} %get-tuple-element.98) | copy-start | bytes 196612
  67.7 12.9 %copy-start.26 = (bf16[1,8,1,64,64]{4,3,2,1,0:T(8,128)(2,1)}, bf16[1,8,1,64,64]{4,3,2,1,0:T(8,128)(2,1)S(1)}, u32[]{:S(2)}) copy-start(bf16[1,8,1,64,64]{4,3,2,1,0:T(8,128)(2,1)S(1)} %get-tuple-element.99) | copy-start | bytes 196612
  80.6 3.1 copy-start.13
  82.7 1.9 copy-start.2
  83.6 13.3 %copy-start.31 = (f32[2,8,64]{2,1,0:T(8,128)}, f32[2,8,64]{2,1,0:T(8,128)S(1)}, u32[]{:S(2)}) copy-start(f32[2,8,64]{2,1,0:T(8,128)S(1)} %log_add_fusion.1) | copy-start | bytes 12292
  96.9 15.7 %copy-start.5 = (bf16[16,64,1,8,64]{4,1,0,3,2:T(8,128)(2,1)S(1)}, bf16[16,64,1,8,64]{4,1,0,3,2:T(8,128)(2,1)}, u32[]{:S(2)}) copy-start(bf16[16,64,1,8,64]{4,1,0,3,2:T(8,128)(2,1)} %copy-done.4) | copy-start | bytes 3145732
  131.8 13.5 %copy-start.30 = (bf16[1,8,1,64,64]{4,3,2,1,0:T(8,128)(2,1)S(1)}, bf16[1,8,1,64,64]{4,3,2,1,0:T(8,128)(2,1)}, u32[]{:S(2)}) copy-start(bf16[1,8,1,64,64]{4,3,2,1,0:T(8,128)(2,1)} %get-tuple-element.104) | copy-start | bytes 196612
  154.2 0.7 copy-start.39
  154.2 0.7 copy-start.40
  154.2 92.7 %all-gather.7.cloned.1.call-start = ((), (), s32[]{:S(2)}) async-start(), calls=%async_computation.6 | async-start | bytes 3145728 | tf_op jit(solution)/shard_map/all_gather | solution.py:272
  211.8 1.8 copy-start.36
  213.6 82.9 %reduce-scatter.7.cloned.1.call-start = ((), (), s32[]{:S(2)}) async-start(), calls=%async_computation.7 | async-start | bytes 3145728 | tf_op jit(solution)/shard_map/reduce_scatter | solution.py:279
  246.9 10.9 %copy-start.44 = (bf16[2048,1024]{1,0:T(8,128)(2,1)S(1)}, bf16[2048,1024]{1,0:T(8,128)(2,1)}, u32[]{:S(2)}) copy-start(bf16[2048,1024]{1,0:T(8,128)(2,1)} %param.30) | copy-start | bytes 12582916
  254.4 3.4 copy-start.51
  257.8 6.7 copy-start.41
  257.8 6.7 copy-start.42
  257.8 6.8 copy-start.43
  264.4 73.1 %all-gather.9.cloned.1.call-start = ((), (), s32[]{:S(2)}) async-start(), calls=%async_computation.8 | async-start | bytes 3145728 | tf_op jit(solution)/shard_map/all_gather | solution.py:295
  296.4 3.4 copy-start.15
  304.3 86.4 %reduce-scatter.9.cloned.1.call-start = ((), (), s32[]{:S(2)}) async-start(), calls=%async_computation.9 | async-start | bytes 3145728 | tf_op jit(solution)/shard_map/reduce_scatter | solution.py:304
  337.5 15.5 %copy-start.45 = (bf16[1024,2048]{1,0:T(8,128)(2,1)S(1)}, bf16[1024,2048]{1,0:T(8,128)(2,1)}, u32[]{:S(2)}) copy-start(bf16[1024,2048]{1,0:T(8,128)(2,1)} %param.28) | copy-start | bytes 12582916
  351.0 2.0 copy-start.50
  358.7 72.5 %all-gather.11.cloned.1.call-start = ((), (), s32[]{:S(2)}) async-start(), calls=%async_computation.10 | async-start | bytes 3145728 | tf_op jit(solution)/shard_map/all_gather | solution.py:316
  390.7 4.0 copy-start.6
  390.7 4.0 copy-start.22
  394.7 3.3 copy-start.33
  395.5 1.3 copy-start.7
  398.0 346.6 %reduce-scatter.11.cloned.1.call-start = ((), (), s32[]{:S(2)}) async-start(), calls=%async_computation.11 | async-start | bytes 3145728 | tf_op jit(solution)/shard_map/reduce_scatter | solution.py:355
  438.6 1.3 copy-start.11
  458.2 25.1 %slice-start = ((s8[14680064]{0:T(1024)(128)(4,1)}), s8[4194304]{0:T(1024)(128)(4,1)S(1)}, s32[]{:S(2)}) async-start(s8[14680064]{0:T(1024)(128)(4,1)} %bitcast.247), calls=%async_computation.13 | async-start | bytes 8388608
  458.2 25.1 %slice-start.1 = ((s8[14680064]{0:T(1024)(128)(4,1)}), s8[4194304]{0:T(1024)(128)(4,1)S(1)}, s32[]{:S(2)}) async-start(s8[14680064]{0:T(1024)(128)(4,1)} %bitcast.247), calls=%async_computation.14 | async-start | bytes 8388608
  458.2 25.1 %slice-start.2 = ((s8[14680064]{0:T(1024)(128)(4,1)}), s8[2097152]{0:T(1024)(128)(4,1)S(1)}, s32[]{:S(2)}) async-start(s8[14680064]{0:T(1024)(128)(4,1)} %bitcast.247), calls=%async_computation.15 | async-start | bytes 4194304
  468.0 15.3 %slice-start.3 = ((s8[14680064]{0:T(1024)(128)(4,1)}), s8[4194304]{0:T(1024)(128)(4,1)S(1)}, s32[]{:S(2)}) async-start(s8[14680064]{0:T(1024)(128)(4,1)} %bitcast.247), calls=%async_computation.16 | async-start | bytes 8388608
  490.6 9.8 %copy-start.32 = (f32[2,8,64]{2,1,0:T(8,128)S(1)}, f32[2,8,64]{2,1,0:T(8,128)}, u32[]{:S(2)}) copy-start(f32[2,8,64]{2,1,0:T(8,128)} %copy-done.31) | copy-start | bytes 12292
  499.2 6.2 copy-start.3
  499.2 6.2 copy-start.14
  507.1 1.2 copy-start.17
  507.1 2.0 copy-start.25
  507.2 2.0 copy-start.27
  528.9 8.8 copy-start.18
  531.6 6.1 copy-start.48
  581.1 4.9 copy-start.20
  625.9 6.6 copy-start.46
  632.5 276.7 %all-reduce.5.cloned.1.call-start = ((), (), s32[]{:S(2)}) async-start(), calls=%async_computation.12 | async-start | bytes 25165824 | tf_op jit(solution)/shard_map/psum | solution.py:373
  632.5 8.7 copy-start.47
  641.2 12.0 %copy-start.16 = (bf16[1024,512]{1,0:T(8,128)(2,1)S(1)}, bf16[1024,512]{1,0:T(8,128)(2,1)}, u32[]{:S(2)}) copy-start(bf16[1024,512]{1,0:T(8,128)(2,1)} %convert_element_type.244) | copy-start | bytes 3145732
  641.2 12.0 %copy-start.23 = (bf16[1024,1,1024]{2,0,1:T(8,128)(2,1)S(1)}, bf16[1024,1,1024]{2,0,1:T(8,128)(2,1)}, u32[]{:S(2)}) copy-start(bf16[1024,1,1024]{2,0,1:T(8,128)(2,1)} %all-gather.11.cloned.1.call-done) | copy-start | bytes 6291460
  653.2 2.3 copy-start.10
  653.2 2.3 copy-start.19
  653.2 4.5 copy-start.21
  662.3 0.7 copy-start.34
  662.3 0.7 copy-start.35
  662.3 45.0 %copy-start.37 = (bf16[2048]{0:T(1024)(128)(2,1)S(1)}, bf16[2048]{0:T(1024)(128)(2,1)}, u32[]{:S(2)}) copy-start(bf16[2048]{0:T(1024)(128)(2,1)} %get-tuple-element.113) | copy-start | bytes 12292
  662.3 82.3 %copy-start.8 = (f32[512,1,1024]{2,0,1:T(8,128)S(1)}, f32[512,1,1024]{2,0,1:T(8,128)}, u32[]{:S(2)}) copy-start(f32[512,1,1024]{2,0,1:T(8,128)} %copy-done.7) | copy-start | bytes 6291460
  909.2 5.3 copy-start.29
  909.2 6.9 copy-start.28
  917.7 6.8 copy-start.12
  924.5 4.4 copy-start.1
  (1 other events, 0.7 us)
Sparse Core Ops, SparseCore 0:
  9.6 35.7 all-gather.4
  154.3 54.2 reduce-scatter.4
  213.7 33.1 all-gather.6
  264.6 31.8 reduce-scatter.6
  304.4 33.1 all-gather.8
  358.9 31.8 reduce-scatter.8
  398.1 33.1 all-gather.10
  632.6 31.8 reduce-scatter.10
  670.7 238.4 all-reduce.4
where the time goes:
time: 947 us; the launch traced here: 936 us
  waiting for transfers between devices  414 us (44%)
  matrix products  193 us (20%)
  local copies, waits for them, and re-layouts  161 us (17%)
  blocking collectives  77.1 us (8%)
  other arithmetic  75.5 us (8%)
  between operations  15 us (2%)
    psum x1, waiting for transfers between devices, local(): lax.psum(grad_query_w.astype(jnp.bfloat16), 'dp').astype(jnp.float32)  162 us
    reduce_scatter x1, waiting for transfers between devices, local(): lax.psum_scatter(jnp.dot(piece, out_w, preferred_element_type=jnp.float32...  53.8 us
    another operation x6, local copies, waits for them, and re-layouts  44.4 us
    psum x1, blocking collectives, local(): lax.psum((grad_out_b, grad_gain_attn, grad_shift_attn, grad_down_b, grad_...  41.6 us
    psum x1, blocking collectives, local(): lax.psum(grad_query_b.astype(jnp.bfloat16), 'dp').astype(jnp.float32)  35.5 us
    all_gather x1, waiting for transfers between devices, local(): seq_rows = lax.all_gather(hidden_in, 'tensor', axis=0, tiled=True)  34.6 us
    all_gather x1, waiting for transfers between devices, local(): dmlp_rows = lax.all_gather(dmlp, 'tensor', axis=0, tiled=True)  33.2 us
    all_gather x1, waiting for transfers between devices, local(): ffn_rows = lax.all_gather(hidden_low, 'tensor', axis=0, tiled=True)  33.2 us
  transfers between devices with their start and end apart: 9, of which 8 were waited for; matrix products, arithmetic and copies ran while one was open for 4% of the time, Pallas kernels for 0%

commit v1 on v0

v1 whole, which is shorter than its diff:
```python
import functools
import math

import jax
import jax.numpy as jnp
from jax import lax
from jax.experimental import pallas as pl
from jax.experimental.pallas import tpu as pltpu
from jax.sharding import PartitionSpec as P

HD = 64
BLOCK = 64
NEG = -1e30
EPS = 1e-12
GELU_C = math.sqrt(2.0 / math.pi)
CHUNKS = 2
LOW = jnp.bfloat16


def dot_on(left, right, left_dim, right_dim):
    return lax.dot_general(
        left,
        right,
        (((left_dim,), (right_dim,)), ((), ())),
        preferred_element_type=jnp.float32,
    )


def lane_masks(width, value):
    lane = lax.broadcasted_iota(jnp.int32, (1, width), 1) // HD
    return [jnp.where(lane == h, value, 0.0).astype(LOW) for h in range(width // HD)]


def stack_heads(rows, masks):
    return jnp.concatenate([rows * m for m in masks], 0)


def unstack_heads(stacked, heads):
    lane = lax.broadcasted_iota(jnp.int32, (1, stacked.shape[1]), 1) // HD
    out = stacked[:BLOCK]
    for h in range(1, heads):
        out = jnp.where(lane == h, stacked[h * BLOCK : (h + 1) * BLOCK], out)
    return out


def block_at(index):
    return pl.ds(pl.multiple_of(index * BLOCK, BLOCK), BLOCK)


class Plan:
    def __init__(self, chunk, chunks, ranks, length, rand, heads):
        self.blocks = length // BLOCK
        self.rank_blocks = self.blocks // ranks
        self.chunk_blocks = self.rank_blocks // chunks
        self.chunk = chunk
        self.rand = rand
        self.heads = heads
        taken = [
            j * self.rank_blocks + chunk * self.chunk_blocks + r
            for j in range(ranks)
            for r in range(self.chunk_blocks)
        ]
        self.ends = [b for b in taken if b in (0, self.blocks - 1)]
        middles = [b for b in taken if b not in self.ends]
        self.ranges = []
        for b in middles:
            if self.ranges and self.ranges[-1][1] == b:
                self.ranges[-1][1] = b + 1
            else:
                self.ranges.append([b, b + 1])

    def local(self, block, first):
        return lax.rem(block - first + self.blocks, self.blocks)

    def inner(self, local):
        part = lax.div(local, self.rank_blocks)
        rest = local - part * self.rank_blocks
        return part * self.chunk_blocks + rest - self.chunk * self.chunk_blocks

    def fixed(self, block, first):
        wanted = (jnp.int32(0), jnp.int32(self.blocks - 1), block - 1, block, block + 1)
        return [self.local(w, first) for w in wanted]

    def random(self, rb_ref, group, block, first):
        return [
            [
                self.local(rb_ref[group * self.heads + h, (block - 1) * self.rand + r], first)
                for h in range(self.heads)
            ]
            for r in range(self.rand)
        ]

    def run(self, one, unroll):
        for low, high in self.ranges:
            count = high - low
            main = count - count % unroll
            if main > unroll:

                @pl.loop(0, main // unroll)
                def _(step, low=low):
                    for u in range(unroll):
                        one(low + step * unroll + u)
            else:
                main = 0
            for x in range(main, count):
                one(jnp.int32(low + x))


def pick_tiles(ref, fixed, rands):
    width = ref.shape[1]
    column = min(128, width)
    per = column // HD
    lane = lax.broadcasted_iota(jnp.int32, (1, column), 1) // HD
    parts = [ref[block_at(f), :] for f in fixed]
    for per_head in rands:
        columns = []
        for c in range(width // column):
            tile = None
            for p in range(per):
                x = ref[block_at(per_head[c * per + p]), c * column : (c + 1) * column]
                tile = x if tile is None else jnp.where(lane == p, x, tile)
            columns.append(tile)
        parts.append(jnp.concatenate(columns, 1) if len(columns) > 1 else columns[0])
    return jnp.concatenate(parts, 0)


def attend_kernel(plan, unroll, first_ref, rb_ref, q_ref, k_ref, v_ref, o_ref, lse_ref):
    group = pl.program_id(0)
    first = first_ref[0]
    heads = plan.heads
    masks = lane_masks(q_ref.shape[1], HD**-0.5)

    def finish(scores, values, place):
        top = jnp.max(scores, 1, keepdims=True)
        weights = jnp.exp(scores - top)
        total = jnp.sum(weights, 1, keepdims=True)
        out = dot_on(weights.astype(LOW), values, 1, 0) * (1.0 / total)
        o_ref[block_at(place), :] = unstack_heads(out, heads).astype(LOW)
        wide = jnp.broadcast_to(top + jnp.log(total), (heads * BLOCK, 128))
        lse_ref[0, pl.ds(place, 1), :] = jnp.transpose(wide)[0:1, :]

    def one(block):
        fixed = plan.fixed(block, first)
        rands = plan.random(rb_ref, group, block, first)
        queries = stack_heads(q_ref[block_at(fixed[3]), :], masks)
        scores = dot_on(queries, pick_tiles(k_ref, fixed, rands), 1, 1)
        lane = lax.broadcasted_iota(jnp.int32, (1, 2 * BLOCK), 1)
        drop = ((block == 1) & (lane < BLOCK)) | (
            (block == plan.blocks - 2) & (lane >= BLOCK)
        )
        scores = jnp.concatenate(
            [jnp.where(drop, NEG, scores[:, : 2 * BLOCK]), scores[:, 2 * BLOCK :]], 1
        )
        finish(scores, pick_tiles(v_ref, fixed, rands), plan.inner(fixed[3]))

    plan.run(one, unroll)
    for b in plan.ends:
        local = plan.local(jnp.int32(b), first)
        queries = stack_heads(q_ref[block_at(local), :], masks)
        finish(dot_on(queries, k_ref[...], 1, 1), v_ref[...], plan.inner(local))


def attend_back_kernel(plan, unroll, started, last, first_ref, rb_ref, q_ref, k_ref, v_ref, *refs):
    do_ref, lse_ref, *refs = refs
    if started:
        dk_in, dv_in, *refs = refs
    dq_ref, dk_ref, dv_ref, *refs = refs
    dk_acc, dv_acc = refs if last else (dk_ref, dv_ref)
    group = pl.program_id(0)
    first = first_ref[0]
    heads = plan.heads
    width = q_ref.shape[1]
    query_masks, out_masks = lane_masks(width, HD**-0.5), lane_masks(width, 1.0)
    column = min(128, width)
    per = column // HD
    lane = lax.broadcasted_iota(jnp.int32, (1, column), 1) // HD
    if started:
        dk_acc[...] = dk_in[...]
        dv_acc[...] = dv_in[...]
    else:
        dk_acc[...] = jnp.zeros_like(dk_acc)
        dv_acc[...] = jnp.zeros_like(dv_acc)

    def core(scores, keys, values, queries, douts, place):
        probs = jnp.exp(scores - lse_ref[0, pl.ds(place, 1), :])
        dprobs = dot_on(values, douts, 1, 1)
        row_dot = jnp.sum(probs * dprobs, 0, keepdims=True)
        dscores = (probs * (dprobs - row_dot)).astype(LOW)
        dv = dot_on(probs.astype(LOW), douts, 1, 0)
        dk = dot_on(dscores, queries, 1, 0)
        dq = unstack_heads(dot_on(dscores, keys, 0, 0), heads) * (HD**-0.5)
        dq_ref[block_at(place), :] = dq.astype(LOW)
        return dk, dv

    def add_tiles(acc, value, fixed, rands):
        for n, f in enumerate(fixed):
            acc[block_at(f), :] += value[n * BLOCK : (n + 1) * BLOCK]
        for r, per_head in enumerate(rands):
            tile = value[(5 + r) * BLOCK : (6 + r) * BLOCK]
            for h in range(heads):
                c = h // per
                cut = slice(c * column, (c + 1) * column)
                acc[block_at(per_head[h]), cut] += jnp.where(lane == h % per, tile[:, cut], 0.0)

    def one(block):
        fixed = plan.fixed(block, first)
        rands = plan.random(rb_ref, group, block, first)
        place = plan.inner(fixed[3])
        queries = stack_heads(q_ref[block_at(fixed[3]), :], query_masks)
        douts = stack_heads(do_ref[block_at(place), :], out_masks)
        keys = pick_tiles(k_ref, fixed, rands)
        values = pick_tiles(v_ref, fixed, rands)
        scores = dot_on(keys, queries, 1, 1)
        scores = jnp.concatenate(
            [
                jnp.where(block == 1, NEG, scores[:BLOCK]),
                jnp.where(block == plan.blocks - 2, NEG, scores[BLOCK : 2 * BLOCK]),
                scores[2 * BLOCK :],
            ],
            0,
        )
        dk, dv = core(scores, keys, values, queries, douts, place)
        add_tiles(dk_acc, dk, fixed, rands)
        add_tiles(dv_acc, dv, fixed, rands)

    for b in plan.ends:
        local = plan.local(jnp.int32(b), first)
        place = plan.inner(local)
        queries = stack_heads(q_ref[block_at(local), :], query_masks)
        douts = stack_heads(do_ref[block_at(place), :], out_masks)
        scores = dot_on(k_ref[...], queries, 1, 1)
        dk, dv = core(scores, k_ref[...], v_ref[...], queries, douts, place)
        dk_acc[...] += dk
        dv_acc[...] += dv
    plan.run(one, unroll)
    if last:
        dk_ref[...] = dk_acc[...].astype(LOW)
        dv_ref[...] = dv_acc[...].astype(LOW)


def group_width(channels):
    return min(256, channels)


def packed_specs(length, channels):
    width = group_width(channels)
    groups = channels // width
    return [
        pl.BlockSpec((length, width), lambda g, *_, n=n: (0, n * groups + g)) for n in range(3)
    ]


def attend(qkv, random_ids, first, chunk, chunks, ranks):
    length, channels = qkv.shape[0], qkv.shape[1] // 3
    width = group_width(channels)
    groups, heads = channels // width, width // HD
    plan = Plan(chunk, chunks, ranks, length, random_ids.shape[1] // (length // BLOCK - 2), heads)
    rows = length // chunks
    return pl.pallas_call(
        functools.partial(attend_kernel, plan, 4),
        grid_spec=pltpu.PrefetchScalarGridSpec(
            num_scalar_prefetch=2,
            grid=(groups,),
            in_specs=packed_specs(length, channels),
            out_specs=[
                pl.BlockSpec((rows, width), lambda g, *_: (0, g)),
                pl.BlockSpec((1, rows // BLOCK, width), lambda g, *_: (g, 0, 0)),
            ],
        ),
        out_shape=[
            jax.ShapeDtypeStruct((rows, channels), LOW),
            jax.ShapeDtypeStruct((groups, rows // BLOCK, width), jnp.float32),
        ],
        compiler_params=pltpu.CompilerParams(vmem_limit_bytes=24 << 20),
        cost_estimate=pl.CostEstimate(
            flops=6 << 30, bytes_accessed=8 * length * channels, transcendentals=0
        ),
        name="attend",
    )(first, random_ids, qkv, qkv, qkv)


def attend_back(qkv, dout, lse, random_ids, first, sums, chunk, chunks, ranks):
    length, channels = qkv.shape[0], qkv.shape[1] // 3
    width = group_width(channels)
    groups, heads = channels // width, width // HD
    plan = Plan(chunk, chunks, ranks, length, random_ids.shape[1] // (length // BLOCK - 2), heads)
    rows = length // chunks
    last = chunk == chunks - 1
    part = pl.BlockSpec((rows, width), lambda g, *_: (0, g))
    full = pl.BlockSpec((length, width), lambda g, *_: (0, g))
    sum_shape = jax.ShapeDtypeStruct((length, channels), LOW if last else jnp.float32)
    return pl.pallas_call(
        functools.partial(attend_back_kernel, plan, 3, bool(sums), last),
        grid_spec=pltpu.PrefetchScalarGridSpec(
            num_scalar_prefetch=2,
            grid=(groups,),
            in_specs=packed_specs(length, channels)
            + [part, pl.BlockSpec((1, rows // BLOCK, width), lambda g, *_: (g, 0, 0))]
            + [full] * len(sums),
            out_specs=[part, full, full],
            scratch_shapes=[pltpu.VMEM((length, width), jnp.float32)] * (2 if last else 0),
        ),
        out_shape=[jax.ShapeDtypeStruct((rows, channels), LOW), sum_shape, sum_shape],
        compiler_params=pltpu.CompilerParams(vmem_limit_bytes=32 << 20),
        cost_estimate=pl.CostEstimate(
            flops=12 << 30, bytes_accessed=16 * length * channels, transcendentals=0
        ),
        name="attend_back",
    )(first, random_ids, qkv, qkv, qkv, dout, lse, *sums)


def fetch(rows, ranks):
    parts = [rows]
    for s in range(1, ranks):
        parts.append(lax.ppermute(rows, "tensor", [((k + s) % ranks, k) for k in range(ranks)]))
    return parts


def share_sum(term, parts, ranks):
    moved = []
    for s in range(1, ranks):
        share = term(parts[s]).astype(LOW)
        moved.append(lax.ppermute(share, "tensor", [(k, (k + s) % ranks) for k in range(ranks)]))
    total = term(parts[0])
    for m in moved:
        total = total + m.astype(jnp.float32)
    return total


class Ring:
    def __init__(self, size):
        self.size = size
        self.chips = size // 2
        self.order = list(range(0, self.chips, 2)) + list(range(1, self.chips, 2))[::-1]
        self.ahead = self.chips // 2
        self.behind = self.chips - 1 - self.ahead
        index = lax.axis_index("dp")
        self.core = lax.rem(index, 2)
        chip = lax.div(index, 2)
        half = lax.div(chip, 2)
        self.place = jnp.where(lax.rem(chip, 2) == 0, half, self.chips - 1 - half)
        self.place_core = jnp.stack([self.core, self.place]).astype(jnp.int32)

    def shift(self, value, by):
        pairs = []
        for q in range(self.chips):
            source, target = self.order[q], self.order[(q + by) % self.chips]
            pairs += [(2 * source + c, 2 * target + c) for c in range(2)]
        return lax.ppermute(value, "dp", pairs)

    def mate(self, value):
        return lax.ppermute(value, "dp", [(i, i ^ 1) for i in range(self.size)])

    def fits(self, rows):
        return self.size % 4 == 0 and rows % (16 * self.size) == 0

    def total(self, grad):
        rows, columns = grad.shape
        chips, shard = self.chips, rows // self.size
        halves = grad.reshape(2, chips, shard, columns)
        given = lax.dynamic_index_in_dim(halves, 1 - self.core, 0, False)
        kept = lax.dynamic_index_in_dim(halves, self.core, 0, False)
        held = add_low(kept, self.mate(given))

        def take(offset):
            index = lax.rem(self.place + offset + 2 * chips, chips)
            return lax.dynamic_index_in_dim(held, index, 0, False)

        right, left = take(self.ahead), take(-self.behind)
        for j in range(1, self.ahead + 1):
            right = self.shift(right, 1)
            if j < self.ahead:
                right = add_low(right, take(self.ahead - j))
            if j <= self.behind:
                left = self.shift(left, -1)
                if j < self.behind:
                    left = add_low(left, take(j - self.behind))
        own = (
            take(0).astype(jnp.float32) + right.astype(jnp.float32) + left.astype(jnp.float32)
        ).astype(LOW)
        pieces = {0: own}
        right = left = own
        for j in range(1, self.ahead + 1):
            right = pieces[-j] = self.shift(right, 1)
            if j <= self.behind:
                left = pieces[j] = self.shift(left, -1)
        ordered = jnp.stack([pieces[o] for o in range(-self.ahead, self.behind + 1)])
        return self.place_pieces(ordered, self.mate(ordered))

    def place_pieces(self, mine, theirs):
        chips, shard, columns = mine.shape
        ahead = self.ahead

        def body(where_ref, mine_ref, theirs_ref, out_ref):
            step = pl.program_id(0)

            @pl.when(step < chips)
            def _():
                out_ref[...] = mine_ref[0].astype(jnp.float32)

            @pl.when(step >= chips)
            def _():
                out_ref[...] = theirs_ref[0].astype(jnp.float32)

        def target(i, where):
            core = jnp.where(i < chips, where[0], 1 - where[0])
            return (core * chips + lax.rem(where[1] - ahead + i + chips, chips), 0)

        return pl.pallas_call(
            body,
            grid_spec=pltpu.PrefetchScalarGridSpec(
                num_scalar_prefetch=1,
                grid=(2 * chips,),
                in_specs=[
                    pl.BlockSpec((1, shard, columns), lambda i, w: (jnp.minimum(i, chips - 1), 0, 0)),
                    pl.BlockSpec((1, shard, columns), lambda i, w: (jnp.maximum(i - chips, 0), 0, 0)),
                ],
                out_specs=pl.BlockSpec((shard, columns), target),
            ),
            out_shape=jax.ShapeDtypeStruct((2 * chips * shard, columns), jnp.float32),
            cost_estimate=pl.CostEstimate(
                flops=0, bytes_accessed=16 * chips * shard * columns, transcendentals=0
            ),
            name="place_pieces",
        )(self.place_core, mine, theirs)


def add_low(a, b):
    return (a.astype(jnp.float32) + b.astype(jnp.float32)).astype(LOW)


def dp_total(ring, grad):
    if ring.fits(grad.shape[0]):
        return ring.total(grad.astype(LOW))
    return lax.psum(grad.astype(LOW), "dp").astype(jnp.float32)


def small_total(both, dp_only, size, ranks):
    def fold(value, axis, count):
        if count & (count - 1):
            return lax.psum(value, axis)
        bit = 1
        while bit < count:
            value = value + lax.ppermute(value, axis, [(i, i ^ bit) for i in range(count)])
            bit *= 2
        return value

    lead = both.shape[0]
    both = fold(both, "tensor", ranks)
    total = fold(jnp.concatenate([both, dp_only]), "dp", size)
    return total[:lead], total[lead:]


def layer_norm(rows, gain, shift):
    centre = rows - jnp.mean(rows, -1, keepdims=True)
    inverse = lax.rsqrt(jnp.mean(centre * centre, -1, keepdims=True) + EPS)
    normed = centre * inverse
    return gain * normed + shift, normed, inverse


def norm_back(grad, normed, inverse, gain):
    scaled = grad * gain
    return inverse * (
        scaled
        - jnp.mean(scaled, -1, keepdims=True)
        - normed * jnp.mean(scaled * normed, -1, keepdims=True)
    )


def gelu_parts(values):
    tanh_val = jnp.tanh(GELU_C * (values + 0.044715 * values * values * values))
    output = 0.5 * values * (1.0 + tanh_val)
    slope = 0.5 * (1.0 + tanh_val) + 0.5 * values * (1.0 - tanh_val * tanh_val) * GELU_C * (
        1.0 + 3.0 * 0.044715 * values * values
    )
    return output, slope


def dot(a, b):
    return jnp.dot(a, b, preferred_element_type=jnp.float32)


def dot_nt(a, b):
    return dot_on(a, b, 1, 1)


def dot_tn(a, b):
    return dot_on(a, b, 0, 0)


def local(
    dp_size,
    ranks,
    hidden_in,
    query_w,
    key_w,
    value_w,
    query_b,
    value_b,
    out_w,
    out_b,
    gain_attn,
    shift_attn,
    up_w,
    up_b,
    down_w,
    down_b,
    gain_ffn,
    shift_ffn,
    random_blocks,
    cotangent,
):
    own_rows, seqs_here, width = hidden_in.shape
    channels = query_w.shape[1]
    length = own_rows * ranks
    chunks = CHUNKS
    piece = own_rows // chunks
    ring = Ring(dp_size)
    first = (lax.axis_index("tensor") * (own_rows // BLOCK)).reshape(1).astype(jnp.int32)
    random_ids = random_blocks.reshape(random_blocks.shape[0], -1)
    rows_in = hidden_in.reshape(own_rows, width)
    grad_out = cotangent.reshape(own_rows, width)

    flat = jnp.concatenate(fetch(rows_in, ranks), 0)
    qkv_w = jnp.concatenate([query_w, key_w, value_w], 1)
    qkv_b = jnp.concatenate([query_b, jnp.zeros_like(query_b), value_b])
    qkv = (dot(flat, qkv_w) + qkv_b).astype(LOW)

    contexts, lses = [], []
    for c in range(chunks):
        context, lse = attend(qkv, random_ids, first, c, chunks, ranks)
        contexts.append(context)
        lses.append(lse)

    state = []
    for c in range(chunks):
        span = slice(c * piece, (c + 1) * piece)
        parts = [contexts[c][j * piece : (j + 1) * piece] for j in range(ranks)]
        attn_out = share_sum(lambda x: dot(x, out_w), parts, ranks)
        resid = rows_in[span].astype(jnp.float32) + attn_out + out_b
        hidden, normed, inverse = layer_norm(resid, gain_attn, shift_attn)
        state.append(
            dict(span=span, attn_out=attn_out, resid=resid, hidden=hidden, n1=normed, i1=inverse)
        )
    for s in state:
        s["x"] = fetch(s["hidden"].astype(LOW), ranks)
    for s in state:
        ups = [dot(x, up_w) + up_b for x in s["x"]]
        both = [gelu_parts(u) for u in ups]
        s["act"] = [b[0].astype(LOW) for b in both]
        s["slope"] = [b[1] for b in both]
        s["mlp_out"] = share_sum(lambda x: dot(x, down_w), s["act"], ranks)
    for s in state:
        resid2 = s["hidden"] + s["mlp_out"] + down_b
        layer_out, n2, i2 = layer_norm(resid2, gain_ffn, shift_ffn)
        s["layer_out"] = layer_out.astype(LOW)
        g = grad_out[s["span"]].astype(jnp.float32)
        s["dresid2"] = norm_back(g, n2, i2, gain_ffn)
        s["sums2"] = [
            jnp.sum(s["dresid2"], 0),
            jnp.sum(g * n2, 0),
            jnp.sum(g, 0),
        ]
        s["dmlp"] = fetch(s["dresid2"].astype(LOW), ranks)
    for s in state:
        s["dup"] = [
            (dot_nt(d, down_w) * slope).astype(LOW) for d, slope in zip(s["dmlp"], s["slope"])
        ]
        part = share_sum(lambda x: dot_nt(x, up_w), s["dup"], ranks)
        s["dhidden"] = part + s["dresid2"]
    for s in state:
        s["dresid"] = norm_back(s["dhidden"], s["n1"], s["i1"], gain_attn)
        s["sums1"] = [
            jnp.sum(s["dresid"], 0),
            jnp.sum(s["dhidden"] * s["n1"], 0),
            jnp.sum(s["dhidden"], 0),
        ]
        s["dattn"] = fetch(s["dresid"].astype(LOW), ranks)

    def joined(name):
        return jnp.concatenate([x for s in state for x in s[name]], 0)

    dmlp_all, x_all, dattn_all = joined("dmlp"), joined("x"), joined("dattn")
    act_all, dup_all = joined("act"), joined("dup")
    grad_down_w = dp_total(ring, dot_tn(act_all, dmlp_all))
    grad_up_w = dp_total(ring, dot_tn(x_all, dup_all))
    grad_out_w = dp_total(ring, dot_tn(jnp.concatenate(contexts, 0), dattn_all))
    grad_up_b = jnp.sum(dup_all.astype(jnp.float32), 0)

    dq_parts, sums = [], []
    for c, s in enumerate(state):
        dcontext = jnp.concatenate([dot_nt(d, out_w).astype(LOW) for d in s["dattn"]], 0)
        dq, dk, dv = attend_back(
            qkv, dcontext, lses[c], random_ids, first, sums, c, chunks, ranks
        )
        dq_parts.append(dq)
        sums = [dk, dv]
    dq = jnp.concatenate(
        [dq_parts[c][j * piece : (j + 1) * piece] for j in range(ranks) for c in range(chunks)], 0
    )
    dqkv = jnp.concatenate([dq] + sums, 1)
    grad_qkv = dp_total(ring, dot_tn(flat, dqkv))
    grad_qkv_b = jnp.sum(dqkv.astype(jnp.float32), 0)
    dinput = share_sum(
        lambda x: dot_nt(x, qkv_w),
        [dqkv[j * own_rows : (j + 1) * own_rows] for j in range(ranks)],
        ranks,
    )
    grad_input = (dinput + jnp.concatenate([s["dresid"] for s in state], 0)).astype(LOW)

    def summed(name, n):
        return functools.reduce(jnp.add, [s[name][n] for s in state])

    squares = [
        functools.reduce(jnp.add, [jnp.sum(s[name] * s[name]) for s in state])
        for name in ("resid", "attn_out", "mlp_out")
    ]
    scalars = jnp.pad(jnp.stack(squares), (0, 125))
    both, dp_only = small_total(
        jnp.concatenate([summed(n, i) for n in ("sums1", "sums2") for i in range(3)] + [scalars]),
        jnp.concatenate([grad_qkv_b[:channels], grad_qkv_b[2 * channels :], grad_up_b]),
        dp_size,
        ranks,
    )
    vectors = [both[i * width : (i + 1) * width] for i in range(6)]
    entries = float(own_rows * ranks * dp_size * seqs_here * width)
    rms_stats = jnp.sqrt(both[6 * width : 6 * width + 3] / entries)
    layer_out = jnp.concatenate([s["layer_out"] for s in state], 0)
    shape = hidden_in.shape
    return (
        layer_out.reshape(shape),
        grad_input.reshape(shape),
        grad_qkv[:, :channels],
        grad_qkv[:, channels : 2 * channels],
        grad_qkv[:, 2 * channels :],
        dp_only[:channels],
        dp_only[channels : 2 * channels],
        grad_out_w,
        vectors[0],
        vectors[1],
        vectors[2],
        grad_up_w,
        dp_only[2 * channels :],
        grad_down_w,
        vectors[3],
        vectors[4],
        vectors[5],
        rms_stats,
    )


def solution(mesh):
    rows = P("tensor", "dp", None)
    columns, split, whole = P(None, "tensor"), P("tensor"), P()
    first = P("tensor", None)
    return jax.shard_map(
        functools.partial(local, mesh.shape["dp"], mesh.shape["tensor"]),
        mesh=mesh,
        in_specs=(
            rows,
            columns,
            columns,
            columns,
            split,
            split,
            first,
            whole,
            whole,
            whole,
            columns,
            split,
            first,
            whole,
            whole,
            whole,
            P("tensor", None, None),
            rows,
        ),
        out_specs=(
            rows,
            rows,
            columns,
            columns,
            columns,
            split,
            split,
            first,
            whole,
            whole,
            whole,
            columns,
            split,
            first,
            whole,
            whole,
            whole,
            whole,
        ),
        check_vma=False,
    )
```

time: 947 us -> 494 us (0.52)
  waiting for transfers between devices: 414 us -> 177 us
  local copies, waits for them, and re-layouts: 161 us -> 33.6 us
  matrix products: 193 us -> 87.5 us
  Pallas kernels: 0 us -> 78.2 us
  blocking collectives: 77.1 us -> 0 us
  starting transfers between devices: 0.37 us -> 72.5 us
  other arithmetic: 75.5 us -> 31.3 us
    ppermute x0 -> x83, waiting for transfers between devices: none -> 177 us  [the longest x56 93.7 us: shift(): return lax.ppermute(value, 'dp', pairs)]
    psum x1 -> x0, waiting for transfers between devices: 162 us -> none  [local(): lax.psum(grad_query_w.astype(jnp.bfloat16), 'dp').astype(jnp.float32)]
    all_gather x4 -> x0, waiting for transfers between devices: 134 us -> none  [the longest x1 34.6 us: local(): seq_rows = lax.all_gather(hidden_in, 'tensor', axis=0, tiled=True)]
    reduce_scatter x4 -> x0, waiting for transfers between devices: 118 us -> none  [the longest x1 53.8 us: local(): lax.psum_scatter(jnp.dot(piece, out_w, preferred_element_type=jnp.float32...]
    dot_general x32 -> x31, matrix products: 193 us -> 87.5 us  [the longest x18 49.8 us: dot_on(): lax.dot_general(left, right, (((left_dim,), (right_dim,)), ((), ())), pre...]
    pallas_call x0 -> x8, Pallas kernels: none -> 78.2 us  [the longest x4 44.5 us: place_pieces(): pl.pallas_call(body, grid_spec=pltpu.PrefetchScalarGridSpec(num_scalar_pr...]
    psum x2 -> x0, blocking collectives: 77.1 us -> none  [the longest x1 41.6 us: local(): lax.psum((grad_out_b, grad_gain_attn, grad_shift_attn, grad_down_b, grad_...]
    ppermute x0 -> x83, starting transfers between devices: none -> 72.5 us  [the longest x56 47.9 us: shift(): return lax.ppermute(value, 'dp', pairs)]
  transfers between devices with their start and end apart: 9 -> 83, of which waited for: 8 -> 40; matrix products, arithmetic and copies ran while one was open for 4% -> 26% of each run, Pallas kernels for 0% -> 11%
where the time goes in v1:
time: 494 us; the launch traced here: 486 us
  waiting for transfers between devices  177 us (36%)
  matrix products  87.5 us (18%)
  Pallas kernels  78.2 us (16%)
  starting transfers between devices  72.5 us (15%)
  local copies, waits for them, and re-layouts  33.6 us (7%)
  other arithmetic  31.3 us (6%)
  between operations  6.34 us (1%)
    ppermute x56, waiting for transfers between devices, shift(): return lax.ppermute(value, 'dp', pairs)  93.7 us
    ppermute x7, waiting for transfers between devices, fetch(): lax.ppermute(rows, 'tensor', [((k + s) % ranks, k) for k in range(ranks)])  55.4 us
    dot_general x18, matrix products, dot_on(): lax.dot_general(left, right, (((left_dim,), (right_dim,)), ((), ())), pre...  49.8 us
    ppermute x56, starting transfers between devices, shift(): return lax.ppermute(value, 'dp', pairs)  47.9 us
    pallas_call x4, Pallas kernels, place_pieces(): pl.pallas_call(body, grid_spec=pltpu.PrefetchScalarGridSpec(num_scalar_pr...  44.5 us
    dot_general x13, matrix products, dot(): return jnp.dot(a, b, preferred_element_type=jnp.float32)  37.7 us
    ppermute x7, waiting for transfers between devices, share_sum(): lax.ppermute(share, 'tensor', [(k, (k + s) % ranks) for k in range(ranks)])  26 us
    pallas_call x2, Pallas kernels, attend_back(): pl.pallas_call(functools.partial(attend_back_kernel, plan, 3, bool(sums),...  22.1 us
  transfers between devices with their start and end apart: 83, of which 40 were waited for; matrix products, arithmetic and copies ran while one was open for 26% of the time, Pallas kernels for 11%

profile of v1, /device:TPU:0, one launch (start us, length us, event | category | flops | bytes accessed | tf_op | source)
XLA Modules:
  0.0 486.1 jit_solution(10209316224764716483)
XLA Ops:
  0.7 3.0 collective-permute-start
  6.9 20.1 %collective-permute-done = bf16[512,1024]{1,0:T(8,128)(2,1)S(1)} collective-permute-done((bf16[512,1024]{1,0:T(8,128)(2,1)}, bf16[512,1024]{1,0:T(8,128)(2,1)S(1)}, u32[]{:S(2)}, u32[]{:S(2)}) %collective-permute-start) | collective-permute-done | bytes 1048608 | tf_op jit(solution)/shard_map/ppermute | solution.py:315
  27.1 4.4 add_convert_fusion.q_ref.k_ref.v_ref
  31.5 5.6 %attend.3 = (bf16[512,512]{1,0:T(8,128)(2,1)S(1)}, f32[2,8,256]{2,1,0:T(8,128)S(1)}) custom-call(s32[1]{0:T(128)} %bitcast.1.first_ref, s32[8,42]{1,0:T(8,128)S(1)} %copy.38.rb_ref, bf16[1024,1536]{1,0:T(8,128)(2,1)S(1)} %add_convert_fusion.q_ref.k_ref.v_ref, bf16[1024,1536]{1,0:T(8,128)(2,1)S(1)} %add_convert_fusion.q_ref.k_ref.v_ref, ...), custom_call_target="tpu_custom_call" | custom-call | flops 6442450944 | bytes 4194304 | tf_op jit(solution)/shard_map/attend/pallas_call | solution.py:259
  37.2 6.1 %attend.2 = (bf16[512,512]{1,0:T(8,128)(2,1)S(1)}, f32[2,8,256]{2,1,0:T(8,128)S(1)}) custom-call(s32[1]{0:T(128)} %bitcast.1.first_ref, s32[8,42]{1,0:T(8,128)S(1)} %copy.38.rb_ref, bf16[1024,1536]{1,0:T(8,128)(2,1)S(1)} %add_convert_fusion.q_ref.k_ref.v_ref, bf16[1024,1536]{1,0:T(8,128)(2,1)S(1)} %add_convert_fusion.q_ref.k_ref.v_ref, ...), custom_call_target="tpu_custom_call" | custom-call | flops 6442450944 | bytes 4194304 | tf_op jit(solution)/shard_map/attend/pallas_call | solution.py:259
  48.6 11.1 %collective-permute-done.4 = bf16[256,1024]{1,0:T(8,128)(2,1)} collective-permute-done((bf16[256,1024]{1,0:T(8,128)(2,1)}, bf16[256,1024]{1,0:T(8,128)(2,1)}, u32[]{:S(2)}, u32[]{:S(2)}) %collective-permute-start.4) | collective-permute-done | bytes 524320 | tf_op jit(solution)/shard_map/ppermute | solution.py:323
  59.7 9.5 %collective-permute-done.1 = bf16[256,1024]{1,0:T(8,128)(2,1)} collective-permute-done((bf16[256,1024]{1,0:T(8,128)(2,1)}, bf16[256,1024]{1,0:T(8,128)(2,1)}, u32[]{:S(2)}, u32[]{:S(2)}) %collective-permute-start.1) | collective-permute-done | bytes 524320 | tf_op jit(solution)/shard_map/ppermute | solution.py:323
  69.2 2.8 fusion.150
  76.7 5.7 %multiply_convert_fusion.1 = (bf16[256,2048]{1,0:T(8,128)(2,1)S(1)}, f32[256,2048]{1,0:T(8,128)}) fusion(f32[2048]{0:T(1024)S(1)} %convert_element_type.552, bf16[256,1024]{1,0:T(8,128)(2,1)} %get-tuple-element.135, bf16[1024,2048]{1,0:T(8,128)(2,1)} %param.28), kind=kOutput, calls=%fused_computation.90 | convolution fusion | flops 1078984704 | bytes 7872512 | tf_op jit(solution)/shard_map/dot_general | solution.py:480
  82.4 6.6 %collective-permute-done.5 = bf16[256,1024]{1,0:T(8,128)(2,1)} collective-permute-done((bf16[256,1024]{1,0:T(8,128)(2,1)}, bf16[256,1024]{1,0:T(8,128)(2,1)}, u32[]{:S(2)}, u32[]{:S(2)}) %collective-permute-start.5) | collective-permute-done | bytes 524320 | tf_op jit(solution)/shard_map/ppermute | solution.py:315
  89.0 4.1 multiply_convert_fusion
  96.7 3.5 collective-permute-done.2
  100.2 3.1 multiply_convert_fusion.2
  106.7 2.2 fusion.161
  110.3 4.4 multiply_convert_fusion.3
  114.8 5.3 %collective-permute-done.3 = bf16[256,1024]{1,0:T(8,128)(2,1)} collective-permute-done((bf16[256,1024]{1,0:T(8,128)(2,1)}, bf16[256,1024]{1,0:T(8,128)(2,1)}, u32[]{:S(2)}, u32[]{:S(2)}) %collective-permute-start.3) | collective-permute-done | bytes 524320 | tf_op jit(solution)/shard_map/ppermute | solution.py:323
  120.1 3.8 fusion.149
  131.0 4.3 fusion.16
  137.0 4.3 fusion.14
  142.6 2.3 maximum_bitcast_fusion
  145.0 3.6 fusion.162
  148.6 4.1 collective-permute-done.7
  152.7 3.7 fusion.15
  159.3 3.3 fusion.17
  166.0 5.9 %convolution_convert_fusion.1 = bf16[1024,2048]{1,0:T(8,128)(2,1)S(1)} fusion(bf16[256,1024]{1,0:T(8,128)(2,1)} %collective-permute-done.5, bf16[256,1024]{1,0:T(8,128)(2,1)} %get-tuple-element.135, bf16[256,1024]{1,0:T(8,128)(2,1)S(1)} %copy-done.45, bf16[256,1024]{1,0:T(8,128)(2,1)S(1)} %copy-done.23, bf16[256,2048]{1,0:T(8,128)(2,1)S(1)} %fusion.17, ...), kind=kOutput, calls=%fused_computation.18 | convolution fusion | flops 4322230272 | bytes 10485760 | tf_op jit(solution)/shard_map/dot_general | solution.py:21
  176.2 6.6 %fusion.10 = bf16[2048,1024]{1,0:T(8,128)(2,1)S(1)} fusion(bf16[256,2048]{1,0:T(8,128)(2,1)S(1)} %copy-done.52, bf16[256,2048]{1,0:T(8,128)(2,1)S(1)} %copy-done.50, bf16[256,2048]{1,0:T(8,128)(2,1)S(1)} %copy-done.54, bf16[256,2048]{1,0:T(8,128)(2,1)S(1)} %copy-done.47, bf16[256,1024]{1,0:T(8,128)(2,1)} %collective-permute-done.10, ...), kind=kOutput, calls=%fused_computation.16 | convolution fusion | flops 4322230272 | bytes 10485760 | tf_op jit(solution)/shard_map/dot_general | solution.py:21
  188.1 2.3 multiply_reduce_fusion.7
  190.4 3.0 fusion.148
  200.8 11.7 %collective-permute-done.9 = bf16[256,1024]{1,0:T(8,128)(2,1)S(1)} collective-permute-done((bf16[256,1024]{1,0:T(8,128)(2,1)S(1)}, bf16[256,1024]{1,0:T(8,128)(2,1)S(1)}, u32[]{:S(2)}, u32[]{:S(2)}) %collective-permute-start.9) | collective-permute-done | bytes 524320 | tf_op jit(solution)/shard_map/ppermute | solution.py:315
  212.4 9.4 %collective-permute-done.12 = bf16[256,1024]{1,0:T(8,128)(2,1)S(1)} collective-permute-done((bf16[256,1024]{1,0:T(8,128)(2,1)S(1)}, bf16[256,1024]{1,0:T(8,128)(2,1)S(1)}, u32[]{:S(2)}, u32[]{:S(2)}) %collective-permute-start.12) | collective-permute-done | bytes 524320 | tf_op jit(solution)/shard_map/ppermute | solution.py:315
  225.6 11.0 %attend_back.2 = (bf16[512,512]{1,0:T(8,128)(2,1)S(1)}, f32[1024,512]{1,0:T(8,128)S(1)}, f32[1024,512]{1,0:T(8,128)S(1)}) custom-call(s32[1]{0:T(128)} %bitcast.1.first_ref, s32[8,42]{1,0:T(8,128)S(1)} %copy.38.rb_ref, bf16[1024,1536]{1,0:T(8,128)(2,1)S(1)} %copy-done.2, bf16[1024,1536]{1,0:T(8,128)(2,1)S(1)} %copy-done.2, bf16[1024,1536]{1,0:T(8,128)(2,1)S(1)} %copy-done.2, ...), custom_call_target="tpu_custom_call" | custom-call | flops 12884901888 | bytes 8388608 | tf_op jit(solution)/shard_map/attend_back/pallas_call | solution.py:292
  236.6 11.1 %attend_back.3 = (bf16[512,512]{1,0:T(8,128)(2,1)S(1)}, bf16[1024,512]{1,0:T(8,128)(2,1)S(1)}, bf16[1024,512]{1,0:T(8,128)(2,1)S(1)}) custom-call(s32[1]{0:T(128)} %bitcast.1.first_ref, s32[8,42]{1,0:T(8,128)S(1)} %copy.38.rb_ref, bf16[1024,1536]{1,0:T(8,128)(2,1)S(1)} %copy-done.2, bf16[1024,1536]{1,0:T(8,128)(2,1)S(1)} %copy-done.2, ...), custom_call_target="tpu_custom_call" | custom-call | flops 12884901888 | bytes 8388608 | tf_op jit(solution)/shard_map/attend_back/pallas_call | solution.py:292
  247.8 7.0 %convert_reduce_fusion.1 = (f32[1536]{0:T(1024)S(1)}, bf16[1024,1536]{1,0:T(8,128)(2,1)S(1)}) fusion(bf16[1024,512]{1,0:T(8,128)(2,1)S(1)} %get-tuple-element.37, bf16[1024,512]{1,0:T(8,128)(2,1)S(1)} %get-tuple-element.36, bf16[256,512]{1,0:T(8,128)(2,1)S(1)} %get-tuple-element.120, bf16[256,512]{1,0:T(8,128)(2,1)S(1)} %get-tuple-element.118, ...), kind=kLoop, calls=%fused_computation.1 | loop fusion | flops 22018560 | bytes 6297600 | tf_op jit(solution)/shard_map/reduce_sum | solution.py:603
  261.6 3.8 convolution_convert_fusion
  271.0 3.0 collective-permute-start.34
  280.8 3.6 collective-permute-done.43
  285.2 3.4 collective-permute-done.44
  290.1 2.8 collective-permute-done.45
  293.2 2.8 fusion.8
  298.2 2.4 fusion.9
  302.7 2.7 collective-permute-done.68
  308.5 2.5 collective-permute-done.52
  311.5 9.3 %collective-permute-done.15 = bf16[64,1536]{1,0:T(8,128)(2,1)S(1)} collective-permute-done((bf16[64,1536]{1,0:T(8,128)(2,1)S(1)}, bf16[64,1536]{1,0:T(8,128)(2,1)S(1)}, u32[]{:S(2)}, u32[]{:S(2)}) %collective-permute-start.15) | collective-permute-done | bytes 196640 | tf_op jit(solution)/shard_map/ppermute | solution.py:349
  323.6 4.0 collective-permute-done.19
  327.6 2.6 collective-permute-start.73
  333.4 7.1 %collective-permute-done.17 = bf16[64,1536]{1,0:T(8,128)(2,1)S(1)} collective-permute-done((bf16[64,1536]{1,0:T(8,128)(2,1)S(1)}, bf16[64,1536]{1,0:T(8,128)(2,1)S(1)}, u32[]{:S(2)}, u32[]{:S(2)}) %collective-permute-start.17) | collective-permute-done | bytes 196640 | tf_op jit(solution)/shard_map/ppermute | solution.py:349
  345.0 5.4 %collective-permute-done.18 = bf16[64,1536]{1,0:T(8,128)(2,1)S(1)} collective-permute-done((bf16[64,1536]{1,0:T(8,128)(2,1)S(1)}, bf16[64,1536]{1,0:T(8,128)(2,1)S(1)}, u32[]{:S(2)}, u32[]{:S(2)}) %collective-permute-start.18) | collective-permute-done | bytes 196640 | tf_op jit(solution)/shard_map/ppermute | solution.py:349
  351.4 2.4 collective-permute-done.21
  356.2 3.9 collective-permute-done.22
  362.3 6.6 %collective-permute-done.23 = bf16[64,1536]{1,0:T(8,128)(2,1)S(1)} collective-permute-done((bf16[64,1536]{1,0:T(8,128)(2,1)S(1)}, bf16[64,1536]{1,0:T(8,128)(2,1)S(1)}, u32[]{:S(2)}, u32[]{:S(2)}) %collective-permute-start.23) | collective-permute-done | bytes 196640 | tf_op jit(solution)/shard_map/ppermute | solution.py:349
  373.1 3.5 collective-permute-done.24
  377.1 5.1 %collective-permute-done.75 = bf16[128,1024]{1,0:T(8,128)(2,1)S(1)} collective-permute-done((bf16[128,1024]{1,0:T(8,128)(2,1)S(1)}, bf16[128,1024]{1,0:T(8,128)(2,1)S(1)}, u32[]{:S(2)}, u32[]{:S(2)}) %collective-permute-start.75) | collective-permute-done | bytes 262176 | tf_op jit(solution)/shard_map/ppermute | solution.py:349
  383.4 3.0 collective-permute-done.25
  392.8 3.5 collective-permute-done.76
  401.6 4.6 collective-permute-done.77
  411.3 4.2 collective-permute-done.64
  418.7 3.2 collective-permute-done.81
  421.9 2.6 collective-permute-done.62
  431.1 2.8 fusion.83
  435.5 9.8 %place_pieces.5 = f32[512,1024]{1,0:T(8,128)} custom-call(s32[2]{0:T(128)} %pad_add_fusion.where_ref, bf16[8,32,1024]{2,1,0:T(8,128)(2,1)} %copy-done.22, bf16[8,32,1024]{2,1,0:T(8,128)(2,1)} %collective-permute-done.50.theirs_ref), custom_call_target="tpu_custom_call" | custom-call | bytes 4194304 | tf_op jit(solution)/shard_map/place_pieces/pallas_call | solution.py:409
  445.3 11.3 %place_pieces.4 = f32[1024,1536]{1,0:T(8,128)} custom-call(s32[2]{0:T(128)} %pad_add_fusion.where_ref, bf16[8,64,1536]{2,1,0:T(8,128)(2,1)} %bitcast_dynamic-update-slice_fusion.16.mine_ref, bf16[8,64,1536]{2,1,0:T(8,128)(2,1)} %collective-permute-done.29.theirs_ref), custom_call_target="tpu_custom_call" | custom-call | bytes 12582912 | tf_op jit(solution)/shard_map/place_pieces/pallas_call | solution.py:409
  456.6 5.7 %fusion.155 = (f32[1024,512]{1,0:T(8,128)}, f32[1024,512]{1,0:T(8,128)}, f32[1024,512]{1,0:T(8,128)}) fusion(f32[1024,1536]{1,0:T(8,128)} %place_pieces.4), kind=kLoop, calls=%fused_computation.328 | loop fusion | bytes 12582912 | tf_op jit(solution)/shard_map/slice | solution.py:635
  462.3 11.7 %place_pieces.6 = f32[1024,2048]{1,0:T(8,128)} custom-call(s32[2]{0:T(128)} %pad_add_fusion.where_ref, bf16[8,64,2048]{2,1,0:T(8,128)(2,1)} %bitcast_dynamic-update-slice_fusion.8.mine_ref, bf16[8,64,2048]{2,1,0:T(8,128)(2,1)} %collective-permute-done.66.theirs_ref), custom_call_target="tpu_custom_call" | custom-call | bytes 16777216 | tf_op jit(solution)/shard_map/place_pieces/pallas_call | solution.py:409
  474.0 11.7 %place_pieces.7 = f32[2048,1024]{1,0:T(8,128)} custom-call(s32[2]{0:T(128)} %pad_add_fusion.where_ref, bf16[8,128,1024]{2,1,0:T(8,128)(2,1)} %copy-done.17, bf16[8,128,1024]{2,1,0:T(8,128)(2,1)} %collective-permute-done.82.theirs_ref), custom_call_target="tpu_custom_call" | custom-call | bytes 16777216 | tf_op jit(solution)/shard_map/place_pieces/pallas_call | solution.py:409
  (388 shorter events, 133.7 us)
Async XLA Ops:
  0.7 26.4 %collective-permute-start = (bf16[512,1024]{1,0:T(8,128)(2,1)}, bf16[512,1024]{1,0:T(8,128)(2,1)S(1)}, u32[]{:S(2)}, u32[]{:S(2)}) collective-permute-start(bf16[512,1024]{1,0:T(8,128)(2,1)} %bitcast.295), channel_id=1, source_target_pairs={{1,0},{0,1},{3,2},{2,3},{5,4},{4,5},{7,6},{6,7},{9,8},{8,9},{11,10... | collective-permute-start | bytes 3145736 | tf_op jit(solution)/shard_map/ppermute | solution.py:315
  44.6 15.2 %collective-permute-start.4 = (bf16[256,1024]{1,0:T(8,128)(2,1)}, bf16[256,1024]{1,0:T(8,128)(2,1)}, u32[]{:S(2)}, u32[]{:S(2)}) collective-permute-start(bf16[256,1024]{1,0:T(8,128)(2,1)} %convolution_convert_fusion.2), channel_id=1, source_target_pairs={{0,1},{1,0},{2,3},{3,2},{4,5},{5,4},{6,7},{7,6},{8,9},{9,8},{10,11... | collective-permute-start | bytes 1572872 | tf_op jit(solution)/shard_map/ppermute | solution.py:323
  47.6 21.7 %collective-permute-start.1 = (bf16[256,1024]{1,0:T(8,128)(2,1)}, bf16[256,1024]{1,0:T(8,128)(2,1)}, u32[]{:S(2)}, u32[]{:S(2)}) collective-permute-start(bf16[256,1024]{1,0:T(8,128)(2,1)} %convolution_convert_fusion.3), channel_id=1, source_target_pairs={{0,1},{1,0},{2,3},{3,2},{4,5},{5,4},{6,7},{7,6},{8,9},{9,8},{10,11... | collective-permute-start | bytes 1572872 | tf_op jit(solution)/shard_map/ppermute | solution.py:323
  73.8 15.2 %collective-permute-start.5 = (bf16[256,1024]{1,0:T(8,128)(2,1)}, bf16[256,1024]{1,0:T(8,128)(2,1)}, u32[]{:S(2)}, u32[]{:S(2)}) collective-permute-start(bf16[256,1024]{1,0:T(8,128)(2,1)} %get-tuple-element.135), channel_id=1, source_target_pairs={{1,0},{0,1},{3,2},{2,3},{5,4},{4,5},{7,6},{6,7},{9,8},{8,9},{11,10... | collective-permute-start | bytes 1572872 | tf_op jit(solution)/shard_map/ppermute | solution.py:315
  76.0 24.1 %collective-permute-start.2 = (bf16[256,1024]{1,0:T(8,128)(2,1)}, bf16[256,1024]{1,0:T(8,128)(2,1)S(1)}, u32[]{:S(2)}, u32[]{:S(2)}) collective-permute-start(bf16[256,1024]{1,0:T(8,128)(2,1)} %get-tuple-element.134), channel_id=1, source_target_pairs={{1,0},{0,1},{3,2},{2,3},{5,4},{4,5},{7,6},{6,7},{9,8},{8,9},{11,10... | collective-permute-start | bytes 1572872 | tf_op jit(solution)/shard_map/ppermute | solution.py:315
  95.2 19.5 %collective-permute-start.6 = (bf16[256,1024]{1,0:T(8,128)(2,1)}, bf16[256,1024]{1,0:T(8,128)(2,1)}, u32[]{:S(2)}, u32[]{:S(2)}) collective-permute-start(bf16[256,1024]{1,0:T(8,128)(2,1)} %convolution_convert_fusion.6), channel_id=1, source_target_pairs={{0,1},{1,0},{2,3},{3,2},{4,5},{5,4},{6,7},{7,6},{8,9},{9,8},{10,11... | collective-permute-start | bytes 1572872 | tf_op jit(solution)/shard_map/ppermute | solution.py:323
  105.3 14.7 %collective-permute-start.3 = (bf16[256,1024]{1,0:T(8,128)(2,1)}, bf16[256,1024]{1,0:T(8,128)(2,1)}, u32[]{:S(2)}, u32[]{:S(2)}) collective-permute-start(bf16[256,1024]{1,0:T(8,128)(2,1)} %convolution_convert_fusion.7), channel_id=1, source_target_pairs={{0,1},{1,0},{2,3},{3,2},{4,5},{5,4},{6,7},{7,6},{8,9},{9,8},{10,11... | collective-permute-start | bytes 1572872 | tf_op jit(solution)/shard_map/ppermute | solution.py:323
  129.9 29.4 %collective-permute-start.10 = (bf16[256,1024]{1,0:T(8,128)(2,1)}, bf16[256,1024]{1,0:T(8,128)(2,1)}, u32[]{:S(2)}, u32[]{:S(2)}) collective-permute-start(bf16[256,1024]{1,0:T(8,128)(2,1)} %convert_element_type.582), channel_id=1, source_target_pairs={{1,0},{0,1},{3,2},{2,3},{5,4},{4,5},{7,6},{6,7},{9,8},{8,9},{11,10... | collective-permute-start | bytes 1572872 | tf_op jit(solution)/shard_map/ppermute | solution.py:315
  136.1 16.6 %collective-permute-start.7 = (bf16[256,1024]{1,0:T(8,128)(2,1)}, bf16[256,1024]{1,0:T(8,128)(2,1)}, u32[]{:S(2)}, u32[]{:S(2)}) collective-permute-start(bf16[256,1024]{1,0:T(8,128)(2,1)} %convert_element_type.572), channel_id=1, source_target_pairs={{1,0},{0,1},{3,2},{2,3},{5,4},{4,5},{7,6},{6,7},{9,8},{8,9},{11,10... | collective-permute-start | bytes 1572872 | tf_op jit(solution)/shard_map/ppermute | solution.py:315
  158.5 28.7 %collective-permute-start.8 = (bf16[256,1024]{1,0:T(8,128)(2,1)}, bf16[256,1024]{1,0:T(8,128)(2,1)S(1)}, u32[]{:S(2)}, u32[]{:S(2)}) collective-permute-start(bf16[256,1024]{1,0:T(8,128)(2,1)} %convolution_convert_fusion.5), channel_id=1, source_target_pairs={{0,1},{1,0},{2,3},{3,2},{4,5},{5,4},{6,7},{7,6},{8,9},{9,8},{10,11... | collective-permute-start | bytes 1572872 | tf_op jit(solution)/shard_map/ppermute | solution.py:323
  164.7 25.7 %collective-permute-start.11 = (bf16[256,1024]{1,0:T(8,128)(2,1)}, bf16[256,1024]{1,0:T(8,128)(2,1)S(1)}, u32[]{:S(2)}, u32[]{:S(2)}) collective-permute-start(bf16[256,1024]{1,0:T(8,128)(2,1)} %convolution_convert_fusion.4), channel_id=1, source_target_pairs={{0,1},{1,0},{2,3},{3,2},{4,5},{5,4},{6,7},{7,6},{8,9},{9,8},{10,11... | collective-permute-start | bytes 1572872 | tf_op jit(solution)/shard_map/ppermute | solution.py:323
  186.0 107.2 %collective-permute-start.67 = (bf16[8,128,1024]{2,1,0:T(8,128)(2,1)}, bf16[8,128,1024]{2,1,0:T(8,128)(2,1)}, u32[]{:S(2)}, u32[]{:S(2)}) collective-permute-start(bf16[8,128,1024]{2,1,0:T(8,128)(2,1)} %dynamic-slice_bitcast_fusion), channel_id=1, source_target_pairs={{0,2},{2,0},{4,6},{6,4},{8,10},{10,8},{12,14},{14,12},{16,18},{18,... | collective-permute-start | bytes 6291464 | tf_op jit(solution)/shard_map/ppermute | solution.py:352
  186.0 112.2 %collective-permute-start.51 = (bf16[8,64,2048]{2,1,0:T(8,128)(2,1)}, bf16[8,64,2048]{2,1,0:T(8,128)(2,1)}, u32[]{:S(2)}, u32[]{:S(2)}) collective-permute-start(bf16[8,64,2048]{2,1,0:T(8,128)(2,1)} %dynamic-slice_bitcast_fusion.1), channel_id=1, source_target_pairs={{0,2},{2,0},{4,6},{6,4},{8,10},{10,8},{12,14},{14,12},{16,18},{18,... | collective-permute-start | bytes 6291464 | tf_op jit(solution)/shard_map/ppermute | solution.py:352
  197.5 14.9 %collective-permute-start.9 = (bf16[256,1024]{1,0:T(8,128)(2,1)S(1)}, bf16[256,1024]{1,0:T(8,128)(2,1)S(1)}, u32[]{:S(2)}, u32[]{:S(2)}) collective-permute-start(bf16[256,1024]{1,0:T(8,128)(2,1)S(1)} %convert_element_type.577), channel_id=1, source_target_pairs={{1,0},{0,1},{3,2},{2,3},{5,4},{4,5},{7,6},{6,7},{9,8},{8,9},{11,10... | collective-permute-start | bytes 1572872 | tf_op jit(solution)/shard_map/ppermute | solution.py:315
  198.8 23.0 %collective-permute-start.12 = (bf16[256,1024]{1,0:T(8,128)(2,1)S(1)}, bf16[256,1024]{1,0:T(8,128)(2,1)S(1)}, u32[]{:S(2)}, u32[]{:S(2)}) collective-permute-start(bf16[256,1024]{1,0:T(8,128)(2,1)S(1)} %convert_element_type.587), channel_id=1, source_target_pairs={{1,0},{0,1},{3,2},{2,3},{5,4},{4,5},{7,6},{6,7},{9,8},{8,9},{11,10... | collective-permute-start | bytes 1572872 | tf_op jit(solution)/shard_map/ppermute | solution.py:315
  223.2 32.3 %collective-permute-start.35 = (bf16[8,32,1024]{2,1,0:T(8,128)(2,1)S(1)}, bf16[8,32,1024]{2,1,0:T(8,128)(2,1)S(1)}, u32[]{:S(2)}, u32[]{:S(2)}) collective-permute-start(bf16[8,32,1024]{2,1,0:T(8,128)(2,1)S(1)} %dynamic-slice_bitcast_fusion.3), channel_id=1, source_target_pairs={{0,2},{2,0},{4,6},{6,4},{8,10},{10,8},{12,14},{14,12},{16,18},{18,... | collective-permute-start | bytes 1572872 | tf_op jit(solution)/shard_map/ppermute | solution.py:352
  257.3 8.1 %collective-permute-start.32 = (f32[9344]{0:T(1024)S(1)}, f32[9344]{0:T(1024)S(1)}, u32[]{:S(2)}, u32[]{:S(2)}) collective-permute-start(f32[9344]{0:T(1024)S(1)} %fusion.142), channel_id=1, source_target_pairs={{0,4},{2,6},{4,0},{6,2},{8,12},{10,14},{12,8},{14,10},{16,20},{18,... | collective-permute-start | bytes 112136 | tf_op jit(solution)/shard_map/ppermute | solution.py:444
  257.9 9.2 %collective-permute-start.40 = (bf16[32,1024]{1,0:T(8,128)(2,1)S(1)}, bf16[32,1024]{1,0:T(8,128)(2,1)S(1)}, u32[]{:S(2)}, u32[]{:S(2)}) collective-permute-start(bf16[32,1024]{1,0:T(8,128)(2,1)S(1)} %get-tuple-element.116), channel_id=1, source_target_pairs={{0,4},{2,6},{8,0},{10,2},{16,8},{18,10},{24,16},{26,18},{28,24},{3... | collective-permute-start | bytes 196616 | tf_op jit(solution)/shard_map/ppermute | solution.py:349
  276.3 29.6 %collective-permute-start.14 = (bf16[8,64,1536]{2,1,0:T(8,128)(2,1)S(1)}, bf16[8,64,1536]{2,1,0:T(8,128)(2,1)S(1)}, u32[]{:S(2)}, u32[]{:S(2)}) collective-permute-start(bf16[8,64,1536]{2,1,0:T(8,128)(2,1)S(1)} %dynamic-slice_bitcast_fusion.2), channel_id=1, source_target_pairs={{0,2},{2,0},{4,6},{6,4},{8,10},{10,8},{12,14},{14,12},{16,18},{18,... | collective-permute-start | bytes 4718600 | tf_op jit(solution)/shard_map/ppermute | solution.py:352
  292.9 8.2 %collective-permute-start.46 = (bf16[32,1024]{1,0:T(8,128)(2,1)S(1)}, bf16[32,1024]{1,0:T(8,128)(2,1)S(1)}, u32[]{:S(2)}, u32[]{:S(2)}) collective-permute-start(bf16[32,1024]{1,0:T(8,128)(2,1)S(1)} %collective-permute-done.45), channel_id=1, source_target_pairs={{0,8},{2,10},{8,16},{10,18},{16,24},{18,26},{24,28},{26,30},{28,20... | collective-permute-start | bytes 196616 | tf_op jit(solution)/shard_map/ppermute | solution.py:349
  296.1 9.3 %collective-permute-start.68 = (bf16[128,1024]{1,0:T(8,128)(2,1)S(1)}, bf16[128,1024]{1,0:T(8,128)(2,1)S(1)}, u32[]{:S(2)}, u32[]{:S(2)}) collective-permute-start(bf16[128,1024]{1,0:T(8,128)(2,1)S(1)} %get-tuple-element.85), channel_id=1, source_target_pairs={{0,8},{2,10},{8,16},{10,18},{16,24},{18,26},{24,28},{26,30},{28,20... | collective-permute-start | bytes 786440 | tf_op jit(solution)/shard_map/ppermute | solution.py:349
  296.6 26.0 %collective-permute-start.72 = (bf16[128,1024]{1,0:T(8,128)(2,1)S(1)}, bf16[128,1024]{1,0:T(8,128)(2,1)S(1)}, u32[]{:S(2)}, u32[]{:S(2)}) collective-permute-start(bf16[128,1024]{1,0:T(8,128)(2,1)S(1)} %get-tuple-element.86), channel_id=1, source_target_pairs={{0,4},{2,6},{8,0},{10,2},{16,8},{18,10},{24,16},{26,18},{28,24},{3... | collective-permute-start | bytes 786440 | tf_op jit(solution)/shard_map/ppermute | solution.py:349
  300.6 10.4 %collective-permute-start.52 = (bf16[64,2048]{1,0:T(8,128)(2,1)S(1)}, bf16[64,2048]{1,0:T(8,128)(2,1)S(1)}, u32[]{:S(2)}, u32[]{:S(2)}) collective-permute-start(bf16[64,2048]{1,0:T(8,128)(2,1)S(1)} %get-tuple-element.91), channel_id=1, source_target_pairs={{0,8},{2,10},{8,16},{10,18},{16,24},{18,26},{24,28},{26,30},{28,20... | collective-permute-start | bytes 786440 | tf_op jit(solution)/shard_map/ppermute | solution.py:349
  301.1 30.1 %collective-permute-start.56 = (bf16[64,2048]{1,0:T(8,128)(2,1)S(1)}, bf16[64,2048]{1,0:T(8,128)(2,1)S(1)}, u32[]{:S(2)}, u32[]{:S(2)}) collective-permute-start(bf16[64,2048]{1,0:T(8,128)(2,1)S(1)} %get-tuple-element.92), channel_id=1, source_target_pairs={{0,4},{2,6},{8,0},{10,2},{16,8},{18,10},{24,16},{26,18},{28,24},{3... | collective-permute-start | bytes 786440 | tf_op jit(solution)/shard_map/ppermute | solution.py:349
  305.5 17.5 %collective-permute-start.69 = (bf16[128,1024]{1,0:T(8,128)(2,1)S(1)}, bf16[128,1024]{1,0:T(8,128)(2,1)S(1)}, u32[]{:S(2)}, u32[]{:S(2)}) collective-permute-start(bf16[128,1024]{1,0:T(8,128)(2,1)S(1)} %fusion.106), channel_id=1, source_target_pairs={{0,8},{2,10},{8,16},{10,18},{16,24},{18,26},{24,28},{26,30},{28,20... | collective-permute-start | bytes 786440 | tf_op jit(solution)/shard_map/ppermute | solution.py:349
  306.4 14.5 %collective-permute-start.15 = (bf16[64,1536]{1,0:T(8,128)(2,1)S(1)}, bf16[64,1536]{1,0:T(8,128)(2,1)S(1)}, u32[]{:S(2)}, u32[]{:S(2)}) collective-permute-start(bf16[64,1536]{1,0:T(8,128)(2,1)S(1)} %get-tuple-element.101), channel_id=1, source_target_pairs={{0,8},{2,10},{8,16},{10,18},{16,24},{18,26},{24,28},{26,30},{28,20... | collective-permute-start | bytes 589832 | tf_op jit(solution)/shard_map/ppermute | solution.py:349
  311.1 21.8 %collective-permute-start.53 = (bf16[64,2048]{1,0:T(8,128)(2,1)S(1)}, bf16[64,2048]{1,0:T(8,128)(2,1)S(1)}, u32[]{:S(2)}, u32[]{:S(2)}) collective-permute-start(bf16[64,2048]{1,0:T(8,128)(2,1)S(1)} %fusion.113), channel_id=1, source_target_pairs={{0,8},{2,10},{8,16},{10,18},{16,24},{18,26},{24,28},{26,30},{28,20... | collective-permute-start | bytes 786440 | tf_op jit(solution)/shard_map/ppermute | solution.py:349
  322.6 8.1 %collective-permute-start.16 = (bf16[64,1536]{1,0:T(8,128)(2,1)S(1)}, bf16[64,1536]{1,0:T(8,128)(2,1)S(1)}, u32[]{:S(2)}, u32[]{:S(2)}) collective-permute-start(bf16[64,1536]{1,0:T(8,128)(2,1)S(1)} %fusion.120), channel_id=1, source_target_pairs={{0,8},{2,10},{8,16},{10,18},{16,24},{18,26},{24,28},{26,30},{28,20... | collective-permute-start | bytes 589832 | tf_op jit(solution)/shard_map/ppermute | solution.py:349
  323.2 19.5 %collective-permute-start.70 = (bf16[128,1024]{1,0:T(8,128)(2,1)S(1)}, bf16[128,1024]{1,0:T(8,128)(2,1)S(1)}, u32[]{:S(2)}, u32[]{:S(2)}) collective-permute-start(bf16[128,1024]{1,0:T(8,128)(2,1)S(1)} %get-tuple-element.83), channel_id=1, source_target_pairs={{0,8},{2,10},{8,16},{10,18},{16,24},{18,26},{24,28},{26,30},{28,20... | collective-permute-start | bytes 786440 | tf_op jit(solution)/shard_map/ppermute | solution.py:349
  327.6 16.8 %collective-permute-start.73 = (bf16[128,1024]{1,0:T(8,128)(2,1)S(1)}, bf16[128,1024]{1,0:T(8,128)(2,1)S(1)}, u32[]{:S(2)}, u32[]{:S(2)}) collective-permute-start(bf16[128,1024]{1,0:T(8,128)(2,1)S(1)} %get-tuple-element.84), channel_id=1, source_target_pairs={{0,4},{2,6},{8,0},{10,2},{16,8},{18,10},{24,16},{26,18},{28,24},{3... | collective-permute-start | bytes 786440 | tf_op jit(solution)/shard_map/ppermute | solution.py:349
  330.8 9.7 %collective-permute-start.17 = (bf16[64,1536]{1,0:T(8,128)(2,1)S(1)}, bf16[64,1536]{1,0:T(8,128)(2,1)S(1)}, u32[]{:S(2)}, u32[]{:S(2)}) collective-permute-start(bf16[64,1536]{1,0:T(8,128)(2,1)S(1)} %get-tuple-element.99), channel_id=1, source_target_pairs={{0,8},{2,10},{8,16},{10,18},{16,24},{18,26},{24,28},{26,30},{28,20... | collective-permute-start | bytes 589832 | tf_op jit(solution)/shard_map/ppermute | solution.py:349
  331.2 11.0 %collective-permute-start.20 = (bf16[64,1536]{1,0:T(8,128)(2,1)S(1)}, bf16[64,1536]{1,0:T(8,128)(2,1)S(1)}, u32[]{:S(2)}, u32[]{:S(2)}) collective-permute-start(bf16[64,1536]{1,0:T(8,128)(2,1)S(1)} %get-tuple-element.100), channel_id=1, source_target_pairs={{0,4},{2,6},{8,0},{10,2},{16,8},{18,10},{24,16},{26,18},{28,24},{3... | collective-permute-start | bytes 589832 | tf_op jit(solution)/shard_map/ppermute | solution.py:349
  333.0 21.0 %collective-permute-start.54 = (bf16[64,2048]{1,0:T(8,128)(2,1)S(1)}, bf16[64,2048]{1,0:T(8,128)(2,1)S(1)}, u32[]{:S(2)}, u32[]{:S(2)}) collective-permute-start(bf16[64,2048]{1,0:T(8,128)(2,1)S(1)} %get-tuple-element.89), channel_id=1, source_target_pairs={{0,8},{2,10},{8,16},{10,18},{16,24},{18,26},{24,28},{26,30},{28,20... | collective-permute-start | bytes 786440 | tf_op jit(solution)/shard_map/ppermute | solution.py:349
  340.5 13.5 %collective-permute-start.57 = (bf16[64,2048]{1,0:T(8,128)(2,1)S(1)}, bf16[64,2048]{1,0:T(8,128)(2,1)S(1)}, u32[]{:S(2)}, u32[]{:S(2)}) collective-permute-start(bf16[64,2048]{1,0:T(8,128)(2,1)S(1)} %get-tuple-element.90), channel_id=1, source_target_pairs={{0,4},{2,6},{8,0},{10,2},{16,8},{18,10},{24,16},{26,18},{28,24},{3... | collective-permute-start | bytes 786440 | tf_op jit(solution)/shard_map/ppermute | solution.py:349
  342.3 8.0 %collective-permute-start.18 = (bf16[64,1536]{1,0:T(8,128)(2,1)S(1)}, bf16[64,1536]{1,0:T(8,128)(2,1)S(1)}, u32[]{:S(2)}, u32[]{:S(2)}) collective-permute-start(bf16[64,1536]{1,0:T(8,128)(2,1)S(1)} %get-tuple-element.97), channel_id=1, source_target_pairs={{0,8},{2,10},{8,16},{10,18},{16,24},{18,26},{24,28},{26,30},{28,20... | collective-permute-start | bytes 589832 | tf_op jit(solution)/shard_map/ppermute | solution.py:349
  342.7 11.2 %collective-permute-start.21 = (bf16[64,1536]{1,0:T(8,128)(2,1)S(1)}, bf16[64,1536]{1,0:T(8,128)(2,1)S(1)}, u32[]{:S(2)}, u32[]{:S(2)}) collective-permute-start(bf16[64,1536]{1,0:T(8,128)(2,1)S(1)} %get-tuple-element.98), channel_id=1, source_target_pairs={{0,4},{2,6},{8,0},{10,2},{16,8},{18,10},{24,16},{26,18},{28,24},{3... | collective-permute-start | bytes 589832 | tf_op jit(solution)/shard_map/ppermute | solution.py:349
  344.6 16.8 %collective-permute-start.71 = (bf16[128,1024]{1,0:T(8,128)(2,1)S(1)}, bf16[128,1024]{1,0:T(8,128)(2,1)S(1)}, u32[]{:S(2)}, u32[]{:S(2)}) collective-permute-start(bf16[128,1024]{1,0:T(8,128)(2,1)S(1)} %get-tuple-element.81), channel_id=1, source_target_pairs={{0,8},{2,10},{8,16},{10,18},{16,24},{18,26},{24,28},{26,30},{28,20... | collective-permute-start | bytes 786440 | tf_op jit(solution)/shard_map/ppermute | solution.py:349
  350.3 18.8 %collective-permute-start.74 = (bf16[128,1024]{1,0:T(8,128)(2,1)S(1)}, bf16[128,1024]{1,0:T(8,128)(2,1)S(1)}, u32[]{:S(2)}, u32[]{:S(2)}) collective-permute-start(bf16[128,1024]{1,0:T(8,128)(2,1)S(1)} %get-tuple-element.82), channel_id=1, source_target_pairs={{0,4},{2,6},{8,0},{10,2},{16,8},{18,10},{24,16},{26,18},{28,24},{3... | collective-permute-start | bytes 786440 | tf_op jit(solution)/shard_map/ppermute | solution.py:349
  354.1 16.9 %collective-permute-start.55 = (bf16[64,2048]{1,0:T(8,128)(2,1)S(1)}, bf16[64,2048]{1,0:T(8,128)(2,1)S(1)}, u32[]{:S(2)}, u32[]{:S(2)}) collective-permute-start(bf16[64,2048]{1,0:T(8,128)(2,1)S(1)} %get-tuple-element.87), channel_id=1, source_target_pairs={{0,8},{2,10},{8,16},{10,18},{16,24},{18,26},{24,28},{26,30},{28,20... | collective-permute-start | bytes 786440 | tf_op jit(solution)/shard_map/ppermute | solution.py:349
  355.4 16.0 %collective-permute-start.58 = (bf16[64,2048]{1,0:T(8,128)(2,1)S(1)}, bf16[64,2048]{1,0:T(8,128)(2,1)S(1)}, u32[]{:S(2)}, u32[]{:S(2)}) collective-permute-start(bf16[64,2048]{1,0:T(8,128)(2,1)S(1)} %get-tuple-element.88), channel_id=1, source_target_pairs={{0,4},{2,6},{8,0},{10,2},{16,8},{18,10},{24,16},{26,18},{28,24},{3... | collective-permute-start | bytes 786440 | tf_op jit(solution)/shard_map/ppermute | solution.py:349
  360.2 8.7 %collective-permute-start.23 = (bf16[64,1536]{1,0:T(8,128)(2,1)S(1)}, bf16[64,1536]{1,0:T(8,128)(2,1)S(1)}, u32[]{:S(2)}, u32[]{:S(2)}) collective-permute-start(bf16[64,1536]{1,0:T(8,128)(2,1)S(1)} %collective-permute-done.22), channel_id=1, source_target_pairs={{0,8},{2,10},{8,16},{10,18},{16,24},{18,26},{24,28},{26,30},{28,20... | collective-permute-start | bytes 589832 | tf_op jit(solution)/shard_map/ppermute | solution.py:349
  361.4 29.4 %collective-permute-start.47 = (bf16[32,1024]{1,0:T(8,128)(2,1)S(1)}, bf16[32,1024]{1,0:T(8,128)(2,1)S(1)}, u32[]{:S(2)}, u32[]{:S(2)}) collective-permute-start(bf16[32,1024]{1,0:T(8,128)(2,1)S(1)} %fusion.135), channel_id=1, source_target_pairs={{0,4},{2,6},{8,0},{10,2},{16,8},{18,10},{24,16},{26,18},{28,24},{3... | collective-permute-start | bytes 196616 | tf_op jit(solution)/shard_map/ppermute | solution.py:349
  369.3 29.7 %collective-permute-start.79 = (bf16[128,1024]{1,0:T(8,128)(2,1)S(1)}, bf16[128,1024]{1,0:T(8,128)(2,1)S(1)}, u32[]{:S(2)}, u32[]{:S(2)}) collective-permute-start(bf16[128,1024]{1,0:T(8,128)(2,1)S(1)} %fusion.108), channel_id=1, source_target_pairs={{0,4},{2,6},{8,0},{10,2},{16,8},{18,10},{24,16},{26,18},{28,24},{3... | collective-permute-start | bytes 786440 | tf_op jit(solution)/shard_map/ppermute | solution.py:349
  371.1 11.2 %collective-permute-start.75 = (bf16[128,1024]{1,0:T(8,128)(2,1)S(1)}, bf16[128,1024]{1,0:T(8,128)(2,1)S(1)}, u32[]{:S(2)}, u32[]{:S(2)}) collective-permute-start(bf16[128,1024]{1,0:T(8,128)(2,1)S(1)} %fusion.108), channel_id=1, source_target_pairs={{0,8},{2,10},{8,16},{10,18},{16,24},{18,26},{24,28},{26,30},{28,20... | collective-permute-start | bytes 786440 | tf_op jit(solution)/shard_map/ppermute | solution.py:349
  371.4 11.2 %collective-permute-start.26 = (bf16[64,1536]{1,0:T(8,128)(2,1)S(1)}, bf16[64,1536]{1,0:T(8,128)(2,1)S(1)}, u32[]{:S(2)}, u32[]{:S(2)}) collective-permute-start(bf16[64,1536]{1,0:T(8,128)(2,1)S(1)} %fusion.122), channel_id=1, source_target_pairs={{0,4},{2,6},{8,0},{10,2},{16,8},{18,10},{24,16},{26,18},{28,24},{3... | collective-permute-start | bytes 589832 | tf_op jit(solution)/shard_map/ppermute | solution.py:349
  376.6 9.8 %collective-permute-start.25 = (bf16[64,1536]{1,0:T(8,128)(2,1)S(1)}, bf16[64,1536]{1,0:T(8,128)(2,1)S(1)}, u32[]{:S(2)}, u32[]{:S(2)}) collective-permute-start(bf16[64,1536]{1,0:T(8,128)(2,1)S(1)} %collective-permute-done.24), channel_id=1, source_target_pairs={{0,8},{2,10},{8,16},{10,18},{16,24},{18,26},{24,28},{26,30},{28,20... | collective-permute-start | bytes 589832 | tf_op jit(solution)/shard_map/ppermute | solution.py:349
  382.3 9.8 %collective-permute-start.59 = (bf16[64,2048]{1,0:T(8,128)(2,1)S(1)}, bf16[64,2048]{1,0:T(8,128)(2,1)S(1)}, u32[]{:S(2)}, u32[]{:S(2)}) collective-permute-start(bf16[64,2048]{1,0:T(8,128)(2,1)S(1)} %fusion.115), channel_id=1, source_target_pairs={{0,8},{2,10},{8,16},{10,18},{16,24},{18,26},{24,28},{26,30},{28,20... | collective-permute-start | bytes 786440 | tf_op jit(solution)/shard_map/ppermute | solution.py:349
  382.6 13.7 %collective-permute-start.76 = (bf16[128,1024]{1,0:T(8,128)(2,1)S(1)}, bf16[128,1024]{1,0:T(8,128)(2,1)S(1)}, u32[]{:S(2)}, u32[]{:S(2)}) collective-permute-start(bf16[128,1024]{1,0:T(8,128)(2,1)S(1)} %collective-permute-done.75), channel_id=1, source_target_pairs={{0,8},{2,10},{8,16},{10,18},{16,24},{18,26},{24,28},{26,30},{28,20... | collective-permute-start | bytes 786440 | tf_op jit(solution)/shard_map/ppermute | solution.py:349
  386.5 10.7 %collective-permute-start.27 = (bf16[64,1536]{1,0:T(8,128)(2,1)S(1)}, bf16[64,1536]{1,0:T(8,128)(2,1)S(1)}, u32[]{:S(2)}, u32[]{:S(2)}) collective-permute-start(bf16[64,1536]{1,0:T(8,128)(2,1)S(1)} %collective-permute-done.26), channel_id=1, source_target_pairs={{0,4},{2,6},{8,0},{10,2},{16,8},{18,10},{24,16},{26,18},{28,24},{3... | collective-permute-start | bytes 589832 | tf_op jit(solution)/shard_map/ppermute | solution.py:349
  390.8 9.2 %collective-permute-start.63 = (bf16[64,2048]{1,0:T(8,128)(2,1)S(1)}, bf16[64,2048]{1,0:T(8,128)(2,1)S(1)}, u32[]{:S(2)}, u32[]{:S(2)}) collective-permute-start(bf16[64,2048]{1,0:T(8,128)(2,1)S(1)} %fusion.115), channel_id=1, source_target_pairs={{0,4},{2,6},{8,0},{10,2},{16,8},{18,10},{24,16},{26,18},{28,24},{3... | collective-permute-start | bytes 786440 | tf_op jit(solution)/shard_map/ppermute | solution.py:349
  392.1 8.5 %collective-permute-start.60 = (bf16[64,2048]{1,0:T(8,128)(2,1)S(1)}, bf16[64,2048]{1,0:T(8,128)(2,1)S(1)}, u32[]{:S(2)}, u32[]{:S(2)}) collective-permute-start(bf16[64,2048]{1,0:T(8,128)(2,1)S(1)} %collective-permute-done.59), channel_id=1, source_target_pairs={{0,8},{2,10},{8,16},{10,18},{16,24},{18,26},{24,28},{26,30},{28,20... | collective-permute-start | bytes 786440 | tf_op jit(solution)/shard_map/ppermute | solution.py:349
  396.3 9.9 %collective-permute-start.77 = (bf16[128,1024]{1,0:T(8,128)(2,1)S(1)}, bf16[128,1024]{1,0:T(8,128)(2,1)S(1)}, u32[]{:S(2)}, u32[]{:S(2)}) collective-permute-start(bf16[128,1024]{1,0:T(8,128)(2,1)S(1)} %collective-permute-done.76), channel_id=1, source_target_pairs={{0,8},{2,10},{8,16},{10,18},{16,24},{18,26},{24,28},{26,30},{28,20... | collective-permute-start | bytes 786440 | tf_op jit(solution)/shard_map/ppermute | solution.py:349
  397.2 9.4 %collective-permute-start.28 = (bf16[64,1536]{1,0:T(8,128)(2,1)S(1)}, bf16[64,1536]{1,0:T(8,128)(2,1)S(1)}, u32[]{:S(2)}, u32[]{:S(2)}) collective-permute-start(bf16[64,1536]{1,0:T(8,128)(2,1)S(1)} %collective-permute-done.27), channel_id=1, source_target_pairs={{0,4},{2,6},{8,0},{10,2},{16,8},{18,10},{24,16},{26,18},{28,24},{3... | collective-permute-start | bytes 589832 | tf_op jit(solution)/shard_map/ppermute | solution.py:349
  399.0 9.8 %collective-permute-start.48 = (bf16[32,1024]{1,0:T(8,128)(2,1)S(1)}, bf16[32,1024]{1,0:T(8,128)(2,1)S(1)}, u32[]{:S(2)}, u32[]{:S(2)}) collective-permute-start(bf16[32,1024]{1,0:T(8,128)(2,1)S(1)} %collective-permute-done.47), channel_id=1, source_target_pairs={{0,4},{2,6},{8,0},{10,2},{16,8},{18,10},{24,16},{26,18},{28,24},{3... | collective-permute-start | bytes 196616 | tf_op jit(solution)/shard_map/ppermute | solution.py:349
  400.0 10.6 %collective-permute-start.80 = (bf16[128,1024]{1,0:T(8,128)(2,1)S(1)}, bf16[128,1024]{1,0:T(8,128)(2,1)S(1)}, u32[]{:S(2)}, u32[]{:S(2)}) collective-permute-start(bf16[128,1024]{1,0:T(8,128)(2,1)S(1)} %collective-permute-done.79), channel_id=1, source_target_pairs={{0,4},{2,6},{8,0},{10,2},{16,8},{18,10},{24,16},{26,18},{28,24},{3... | collective-permute-start | bytes 786440 | tf_op jit(solution)/shard_map/ppermute | solution.py:349
  400.5 15.0 %collective-permute-start.64 = (bf16[64,2048]{1,0:T(8,128)(2,1)S(1)}, bf16[64,2048]{1,0:T(8,128)(2,1)S(1)}, u32[]{:S(2)}, u32[]{:S(2)}) collective-permute-start(bf16[64,2048]{1,0:T(8,128)(2,1)S(1)} %collective-permute-done.63), channel_id=1, source_target_pairs={{0,4},{2,6},{8,0},{10,2},{16,8},{18,10},{24,16},{26,18},{28,24},{3... | collective-permute-start | bytes 786440 | tf_op jit(solution)/shard_map/ppermute | solution.py:349
  406.2 10.0 %collective-permute-start.61 = (bf16[64,2048]{1,0:T(8,128)(2,1)S(1)}, bf16[64,2048]{1,0:T(8,128)(2,1)S(1)}, u32[]{:S(2)}, u32[]{:S(2)}) collective-permute-start(bf16[64,2048]{1,0:T(8,128)(2,1)S(1)} %collective-permute-done.60), channel_id=1, source_target_pairs={{0,8},{2,10},{8,16},{10,18},{16,24},{18,26},{24,28},{26,30},{28,20... | collective-permute-start | bytes 786440 | tf_op jit(solution)/shard_map/ppermute | solution.py:349
  406.5 11.6 %collective-permute-start.78 = (bf16[128,1024]{1,0:T(8,128)(2,1)S(1)}, bf16[128,1024]{1,0:T(8,128)(2,1)S(1)}, u32[]{:S(2)}, u32[]{:S(2)}) collective-permute-start(bf16[128,1024]{1,0:T(8,128)(2,1)S(1)} %collective-permute-done.77), channel_id=1, source_target_pairs={{0,8},{2,10},{8,16},{10,18},{16,24},{18,26},{24,28},{26,30},{28,20... | collective-permute-start | bytes 786440 | tf_op jit(solution)/shard_map/ppermute | solution.py:349
  408.8 22.3 %collective-permute-start.13 = (bf16[512,1024]{1,0:T(8,128)(2,1)S(1)}, bf16[512,1024]{1,0:T(8,128)(2,1)S(1)}, u32[]{:S(2)}, u32[]{:S(2)}) collective-permute-start(bf16[512,1024]{1,0:T(8,128)(2,1)S(1)} %fusion.65), channel_id=1, source_target_pairs={{0,1},{1,0},{2,3},{3,2},{4,5},{5,4},{6,7},{7,6},{8,9},{9,8},{10,11... | collective-permute-start | bytes 3145736 | tf_op jit(solution)/shard_map/ppermute | solution.py:323
  410.6 20.3 %collective-permute-start.49 = (bf16[32,1024]{1,0:T(8,128)(2,1)S(1)}, bf16[32,1024]{1,0:T(8,128)(2,1)S(1)}, u32[]{:S(2)}, u32[]{:S(2)}) collective-permute-start(bf16[32,1024]{1,0:T(8,128)(2,1)S(1)} %collective-permute-done.48), channel_id=1, source_target_pairs={{0,4},{2,6},{8,0},{10,2},{16,8},{18,10},{24,16},{26,18},{28,24},{3... | collective-permute-start | bytes 196616 | tf_op jit(solution)/shard_map/ppermute | solution.py:349
  416.2 13.5 %collective-permute-start.65 = (bf16[64,2048]{1,0:T(8,128)(2,1)S(1)}, bf16[64,2048]{1,0:T(8,128)(2,1)S(1)}, u32[]{:S(2)}, u32[]{:S(2)}) collective-permute-start(bf16[64,2048]{1,0:T(8,128)(2,1)S(1)} %collective-permute-done.64), channel_id=1, source_target_pairs={{0,4},{2,6},{8,0},{10,2},{16,8},{18,10},{24,16},{26,18},{28,24},{3... | collective-permute-start | bytes 786440 | tf_op jit(solution)/shard_map/ppermute | solution.py:349
  421.9 23.4 %collective-permute-start.29 = (bf16[8,64,1536]{2,1,0:T(8,128)(2,1)}, bf16[8,64,1536]{2,1,0:T(8,128)(2,1)}, u32[]{:S(2)}, u32[]{:S(2)}) collective-permute-start(bf16[8,64,1536]{2,1,0:T(8,128)(2,1)} %bitcast_dynamic-update-slice_fusion.16.mine_ref), channel_id=1, source_target_pairs={{0,2},{2,0},{4,6},{6,4},{8,10},{10,8},{12,14},{14,12},{16,18},{18,... | collective-permute-start | bytes 4718600 | tf_op jit(solution)/shard_map/ppermute | solution.py:352
  424.5 49.5 %collective-permute-start.82 = (bf16[8,128,1024]{2,1,0:T(8,128)(2,1)S(1)}, bf16[8,128,1024]{2,1,0:T(8,128)(2,1)}, u32[]{:S(2)}, u32[]{:S(2)}) collective-permute-start(bf16[8,128,1024]{2,1,0:T(8,128)(2,1)S(1)} %bitcast_dynamic-update-slice_fusion.mine_ref), channel_id=1, source_target_pairs={{0,2},{2,0},{4,6},{6,4},{8,10},{10,8},{12,14},{14,12},{16,18},{18,... | collective-permute-start | bytes 6291464 | tf_op jit(solution)/shard_map/ppermute | solution.py:352
  430.4 31.9 %collective-permute-start.66 = (bf16[8,64,2048]{2,1,0:T(8,128)(2,1)}, bf16[8,64,2048]{2,1,0:T(8,128)(2,1)}, u32[]{:S(2)}, u32[]{:S(2)}) collective-permute-start(bf16[8,64,2048]{2,1,0:T(8,128)(2,1)} %bitcast_dynamic-update-slice_fusion.8.mine_ref), channel_id=1, source_target_pairs={{0,2},{2,0},{4,6},{6,4},{8,10},{10,8},{12,14},{14,12},{16,18},{18,... | collective-permute-start | bytes 6291464 | tf_op jit(solution)/shard_map/ppermute | solution.py:352
  (77 other events, 504.4 us)

commit v2 on v1

v2 whole, which is shorter than its diff:
```python
import functools
import math

import jax
import jax.numpy as jnp
from jax import lax
from jax.experimental import pallas as pl
from jax.experimental.pallas import tpu as pltpu
from jax.sharding import PartitionSpec as P

HD = 64
BLOCK = 64
NEG = -1e30
EPS = 1e-12
GELU_C = math.sqrt(2.0 / math.pi)
CHUNKS = 2
LOW = jnp.bfloat16
FIRST, CORE, MATE, PLACE = range(4)
COST = pl.CostEstimate(flops=1024, bytes_accessed=1024, transcendentals=0)


def dot_on(left, right, left_dim, right_dim):
    return lax.dot_general(
        left,
        right,
        (((left_dim,), (right_dim,)), ((), ())),
        preferred_element_type=jnp.float32,
    )


def lane_masks(width, value):
    lane = lax.broadcasted_iota(jnp.int32, (1, width), 1) // HD
    return [jnp.where(lane == h, value, 0.0).astype(LOW) for h in range(width // HD)]


def stack_heads(rows, masks):
    return jnp.concatenate([rows * m for m in masks], 0)


def unstack_heads(stacked, heads):
    lane = lax.broadcasted_iota(jnp.int32, (1, stacked.shape[1]), 1) // HD
    out = stacked[:BLOCK]
    for h in range(1, heads):
        out = jnp.where(lane == h, stacked[h * BLOCK : (h + 1) * BLOCK], out)
    return out


def block_at(index):
    return pl.ds(pl.multiple_of(index * BLOCK, BLOCK), BLOCK)


class Plan:
    def __init__(self, chunk, chunks, ranks, length, rand, heads):
        self.blocks = length // BLOCK
        self.rank_blocks = self.blocks // ranks
        self.chunk_blocks = self.rank_blocks // chunks
        self.chunk = chunk
        self.rand = rand
        self.heads = heads
        taken = [
            j * self.rank_blocks + chunk * self.chunk_blocks + r
            for j in range(ranks)
            for r in range(self.chunk_blocks)
        ]
        self.ends = [b for b in taken if b in (0, self.blocks - 1)]
        middles = [b for b in taken if b not in self.ends]
        self.ranges = []
        for b in middles:
            if self.ranges and self.ranges[-1][1] == b:
                self.ranges[-1][1] = b + 1
            else:
                self.ranges.append([b, b + 1])

    def local(self, block, first):
        return lax.rem(block - first + self.blocks, self.blocks)

    def inner(self, local):
        part = lax.div(local, self.rank_blocks)
        rest = local - part * self.rank_blocks
        return part * self.chunk_blocks + rest - self.chunk * self.chunk_blocks

    def fixed(self, block, first):
        wanted = (jnp.int32(0), jnp.int32(self.blocks - 1), block - 1, block, block + 1)
        return [self.local(w, first) for w in wanted]

    def random(self, rb_ref, group, block, first):
        return [
            [
                self.local(rb_ref[group * self.heads + h, (block - 1) * self.rand + r], first)
                for h in range(self.heads)
            ]
            for r in range(self.rand)
        ]

    def run(self, one, unroll):
        for low, high in self.ranges:
            count = high - low
            main = count - count % unroll
            if main > unroll:

                @pl.loop(0, main // unroll)
                def _(step, low=low):
                    for u in range(unroll):
                        one(low + step * unroll + u)
            else:
                main = 0
            for x in range(main, count):
                one(jnp.int32(low + x))


def pick_tiles(ref, fixed, rands):
    width = ref.shape[1]
    column = min(128, width)
    per = column // HD
    lane = lax.broadcasted_iota(jnp.int32, (1, column), 1) // HD
    parts = [ref[block_at(f), :] for f in fixed]
    for per_head in rands:
        columns = []
        for c in range(width // column):
            tile = None
            for p in range(per):
                x = ref[block_at(per_head[c * per + p]), c * column : (c + 1) * column]
                tile = x if tile is None else jnp.where(lane == p, x, tile)
            columns.append(tile)
        parts.append(jnp.concatenate(columns, 1) if len(columns) > 1 else columns[0])
    return jnp.concatenate(parts, 0)


def attend_kernel(plan, unroll, table_ref, rb_ref, q_ref, k_ref, v_ref, o_ref, lse_ref):
    group = pl.program_id(0)
    first = table_ref[FIRST]
    heads = plan.heads
    masks = lane_masks(q_ref.shape[1], HD**-0.5)

    def finish(scores, values, place):
        top = jnp.max(scores, 1, keepdims=True)
        weights = jnp.exp(scores - top)
        total = jnp.sum(weights, 1, keepdims=True)
        out = dot_on(weights.astype(LOW), values, 1, 0) * (1.0 / total)
        o_ref[block_at(place), :] = unstack_heads(out, heads).astype(LOW)
        wide = jnp.broadcast_to(top + jnp.log(total), (heads * BLOCK, 128))
        lse_ref[0, pl.ds(place, 1), :] = jnp.transpose(wide)[0:1, :]

    def one(block):
        fixed = plan.fixed(block, first)
        rands = plan.random(rb_ref, group, block, first)
        queries = stack_heads(q_ref[block_at(fixed[3]), :], masks)
        scores = dot_on(queries, pick_tiles(k_ref, fixed, rands), 1, 1)
        lane = lax.broadcasted_iota(jnp.int32, (1, 2 * BLOCK), 1)
        drop = ((block == 1) & (lane < BLOCK)) | (
            (block == plan.blocks - 2) & (lane >= BLOCK)
        )
        scores = jnp.concatenate(
            [jnp.where(drop, NEG, scores[:, : 2 * BLOCK]), scores[:, 2 * BLOCK :]], 1
        )
        finish(scores, pick_tiles(v_ref, fixed, rands), plan.inner(fixed[3]))

    plan.run(one, unroll)
    for b in plan.ends:
        local = plan.local(jnp.int32(b), first)
        queries = stack_heads(q_ref[block_at(local), :], masks)
        finish(dot_on(queries, k_ref[...], 1, 1), v_ref[...], plan.inner(local))


def attend_back_kernel(plan, unroll, earlier, last, table_ref, rb_ref, q_ref, k_ref, v_ref, *refs):
    do_ref, lse_ref, *refs = refs
    dq_in, refs = refs[:earlier], refs[earlier:]
    if earlier:
        dk_in, dv_in, *refs = refs
    if last:
        all_ref, bias_ref, dq_ref, dk_acc, dv_acc = refs
    else:
        dq_ref, dk_acc, dv_acc = refs
    group = pl.program_id(0)
    first = table_ref[FIRST]
    heads = plan.heads
    width = q_ref.shape[1]
    query_masks, out_masks = lane_masks(width, HD**-0.5), lane_masks(width, 1.0)
    column = min(128, width)
    per = column // HD
    lane = lax.broadcasted_iota(jnp.int32, (1, column), 1) // HD
    if earlier:
        dk_acc[...] = dk_in[...]
        dv_acc[...] = dv_in[...]
    else:
        dk_acc[...] = jnp.zeros_like(dk_acc)
        dv_acc[...] = jnp.zeros_like(dv_acc)

    def core(scores, keys, values, queries, douts, place):
        probs = jnp.exp(scores - lse_ref[0, pl.ds(place, 1), :])
        dprobs = dot_on(values, douts, 1, 1)
        row_dot = jnp.sum(probs * dprobs, 0, keepdims=True)
        dscores = (probs * (dprobs - row_dot)).astype(LOW)
        dv = dot_on(probs.astype(LOW), douts, 1, 0)
        dk = dot_on(dscores, queries, 1, 0)
        dq = unstack_heads(dot_on(dscores, keys, 0, 0), heads) * (HD**-0.5)
        dq_ref[block_at(place), :] = dq.astype(LOW)
        return dk, dv

    def add_tiles(acc, value, fixed, rands):
        for n, f in enumerate(fixed):
            acc[block_at(f), :] += value[n * BLOCK : (n + 1) * BLOCK]
        for r, per_head in enumerate(rands):
            tile = value[(5 + r) * BLOCK : (6 + r) * BLOCK]
            for h in range(heads):
                c = h // per
                cut = slice(c * column, (c + 1) * column)
                acc[block_at(per_head[h]), cut] += jnp.where(lane == h % per, tile[:, cut], 0.0)

    def one(block):
        fixed = plan.fixed(block, first)
        rands = plan.random(rb_ref, group, block, first)
        place = plan.inner(fixed[3])
        queries = stack_heads(q_ref[block_at(fixed[3]), :], query_masks)
        douts = stack_heads(do_ref[block_at(place), :], out_masks)
        keys = pick_tiles(k_ref, fixed, rands)
        values = pick_tiles(v_ref, fixed, rands)
        scores = dot_on(keys, queries, 1, 1)
        scores = jnp.concatenate(
            [
                jnp.where(block == 1, NEG, scores[:BLOCK]),
                jnp.where(block == plan.blocks - 2, NEG, scores[BLOCK : 2 * BLOCK]),
                scores[2 * BLOCK :],
            ],
            0,
        )
        dk, dv = core(scores, keys, values, queries, douts, place)
        add_tiles(dk_acc, dk, fixed, rands)
        add_tiles(dv_acc, dv, fixed, rands)

    for b in plan.ends:
        local = plan.local(jnp.int32(b), first)
        place = plan.inner(local)
        queries = stack_heads(q_ref[block_at(local), :], query_masks)
        douts = stack_heads(do_ref[block_at(place), :], out_masks)
        scores = dot_on(k_ref[...], queries, 1, 1)
        dk, dv = core(scores, k_ref[...], v_ref[...], queries, douts, place)
        dk_acc[...] += dk
        dv_acc[...] += dv
    plan.run(one, unroll)
    if last:
        channels = all_ref.shape[1] // 3
        rows = plan.chunk_blocks * BLOCK
        chunks = earlier + 1
        for at in range(0, channels, width):

            @pl.when(group * width == at)
            def _(at=at):
                for c, source in enumerate([*dq_in, dq_ref]):
                    for j in range(plan.blocks // plan.rank_blocks):
                        low = (j * chunks + c) * rows
                        all_ref[low : low + rows, at : at + width] = source[j * rows : (j + 1) * rows]
                for n, acc in ((1, dk_acc), (2, dv_acc)):
                    cut = n * channels + at
                    all_ref[:, cut : cut + width] = acc[...].astype(LOW)
                for n in (0, 2):
                    cut = slice(n * channels + at, n * channels + at + width)
                    total = jnp.sum(all_ref[:, cut].astype(jnp.float32), 0, keepdims=True)
                    cut = slice(n // 2 * channels + at, n // 2 * channels + at + width)
                    bias_ref[:, cut] = jnp.broadcast_to(total, (8, width))


def group_width(channels):
    return min(256, channels)


def packed_specs(length, channels):
    width = group_width(channels)
    groups = channels // width
    return [
        pl.BlockSpec((length, width), lambda g, *_, n=n: (0, n * groups + g)) for n in range(3)
    ]


def attend(qkv, random_ids, table, chunk, chunks, ranks):
    length, channels = qkv.shape[0], qkv.shape[1] // 3
    width = group_width(channels)
    groups, heads = channels // width, width // HD
    plan = Plan(chunk, chunks, ranks, length, random_ids.shape[1] // (length // BLOCK - 2), heads)
    rows = length // chunks
    return pl.pallas_call(
        functools.partial(attend_kernel, plan, 4),
        grid_spec=pltpu.PrefetchScalarGridSpec(
            num_scalar_prefetch=2,
            grid=(groups,),
            in_specs=packed_specs(length, channels),
            out_specs=[
                pl.BlockSpec((rows, width), lambda g, *_: (0, g)),
                pl.BlockSpec((1, rows // BLOCK, width), lambda g, *_: (g, 0, 0)),
            ],
        ),
        out_shape=[
            jax.ShapeDtypeStruct((rows, channels), LOW),
            jax.ShapeDtypeStruct((groups, rows // BLOCK, width), jnp.float32),
        ],
        compiler_params=pltpu.CompilerParams(vmem_limit_bytes=12 << 20),
        cost_estimate=COST,
        name="attend",
    )(table, random_ids, qkv, qkv, qkv)


def attend_back(qkv, dout, lse, random_ids, table, earlier, sums, chunk, chunks, ranks):
    length, channels = qkv.shape[0], qkv.shape[1] // 3
    width = group_width(channels)
    groups, heads = channels // width, width // HD
    plan = Plan(chunk, chunks, ranks, length, random_ids.shape[1] // (length // BLOCK - 2), heads)
    rows = length // chunks
    last = chunk == chunks - 1
    part = pl.BlockSpec((rows, width), lambda g, *_: (0, g))
    full = pl.BlockSpec((length, width), lambda g, *_: (0, g))
    sum_shape = jax.ShapeDtypeStruct((length, channels), jnp.float32)
    if last:
        bias = (8, 2 * channels)
        out_specs = [pl.BlockSpec(shape, lambda g, *_: (0, 0)) for shape in (qkv.shape, bias)]
        out_shape = [
            jax.ShapeDtypeStruct(qkv.shape, LOW),
            jax.ShapeDtypeStruct(bias, jnp.float32),
        ]
        scratch = [pltpu.VMEM((rows, width), LOW)] + [pltpu.VMEM((length, width), jnp.float32)] * 2
    else:
        out_specs = [part, full, full]
        out_shape = [jax.ShapeDtypeStruct((rows, channels), LOW), sum_shape, sum_shape]
        scratch = []
    return pl.pallas_call(
        functools.partial(attend_back_kernel, plan, 3, len(earlier), last),
        grid_spec=pltpu.PrefetchScalarGridSpec(
            num_scalar_prefetch=2,
            grid=(groups,),
            in_specs=packed_specs(length, channels)
            + [part, pl.BlockSpec((1, rows // BLOCK, width), lambda g, *_: (g, 0, 0))]
            + [part] * len(earlier)
            + [full] * len(sums),
            out_specs=out_specs,
            scratch_shapes=scratch,
        ),
        out_shape=out_shape,
        compiler_params=pltpu.CompilerParams(vmem_limit_bytes=(28 if last else 18) << 20),
        cost_estimate=COST,
        name="attend_back",
    )(table, random_ids, qkv, qkv, qkv, dout, lse, *earlier, *sums)


class Order:
    def __init__(self):
        self.token = None

    def tie(self, values):
        if self.token is None:
            return values
        values, self.token = lax.optimization_barrier((values, self.token))
        return values

    def run(self, function, *values):
        out = function(*self.tie(values))
        self.token = min(jax.tree.leaves(out), key=lambda leaf: leaf.size)
        return out


def fetch(rows, ranks):
    return [
        lax.ppermute(rows, "tensor", [((k + s) % ranks, k) for k in range(ranks)])
        for s in range(1, ranks)
    ]


def hand_over(shares, ranks):
    return [
        lax.ppermute(share, "tensor", [(k, (k + s) % ranks) for k in range(ranks)])
        for s, share in enumerate(shares, 1)
    ]


def plus(own, moved):
    for m in moved:
        own = own + m.astype(jnp.float32)
    return own


class Ring:
    def __init__(self, size):
        self.size = size
        self.chips = size // 2
        self.order = list(range(0, self.chips, 2)) + list(range(1, self.chips, 2))[::-1]
        self.ahead = self.chips // 2
        self.behind = self.chips - 1 - self.ahead

    def table(self, own_blocks):
        index = lax.axis_index("dp")
        core, chip = lax.rem(index, 2), lax.div(index, 2)
        half = lax.div(chip, 2)
        place = jnp.where(lax.rem(chip, 2) == 0, half, self.chips - 1 - half)
        first = lax.axis_index("tensor") * own_blocks
        return jnp.stack([first, core, 1 - core, place]).astype(jnp.int32)

    def shift(self, value, by):
        pairs = []
        for q in range(self.chips):
            source, target = self.order[q], self.order[(q + by) % self.chips]
            pairs += [(2 * source + c, 2 * target + c) for c in range(2)]
        return lax.ppermute(value, "dp", pairs)

    def mate(self, value):
        return lax.ppermute(value, "dp", [(i, i ^ 1) for i in range(self.size)])

    def add(self, table, kept, moved, offset, *more):
        chips, rows, columns = kept.shape
        block = rows // 2 if rows % 32 == 0 else rows

        def body(table_ref, kept_ref, moved_ref, *refs):
            *refs, out_ref = refs
            total = kept_ref[0].astype(jnp.float32) + moved_ref[0].astype(jnp.float32)
            for ref in refs:
                total = total + ref[...].astype(jnp.float32)
            out_ref[...] = total.astype(LOW)

        shard = pl.BlockSpec(
            (1, block, columns),
            lambda i, t: (lax.rem(t[PLACE] + offset + 2 * chips, chips), i, 0),
        )
        part = pl.BlockSpec((block, columns), lambda i, t: (i, 0))
        return pl.pallas_call(
            body,
            grid_spec=pltpu.PrefetchScalarGridSpec(
                num_scalar_prefetch=1,
                grid=(rows // block,),
                in_specs=[shard, shard] + [part] * len(more),
                out_specs=part,
            ),
            out_shape=jax.ShapeDtypeStruct((rows, columns), LOW),
            compiler_params=pltpu.CompilerParams(vmem_limit_bytes=8 << 20),
            cost_estimate=COST,
            name="ring_add",
        )(table, kept, moved, *more)

    def steps(self, order, table, kept, moved, results):
        def add(offset, *more):
            return order.run(
                lambda t, k, m, *more: self.add(t, k, m, offset, *more), table, kept, moved, *more
            )

        right = add(self.ahead)
        left = add(-self.behind)
        for j in range(1, self.ahead + 1):
            right = self.shift(right, 1)
            if j <= self.behind:
                left = self.shift(left, -1)
            yield
            if j < self.ahead:
                right = add(self.ahead - j, right)
            if j < self.behind:
                left = add(j - self.behind, left)
        own = add(0, right, left)
        mine, theirs = {0: own}, {0: self.mate(own)}
        right = left = own
        for j in range(1, self.ahead + 1):
            right = self.shift(right, 1)
            if j <= self.behind:
                left = self.shift(left, -1)
            yield
            right, left = order.tie((right, left))
            mine[-j], theirs[-j] = right, self.mate(right)
            if j <= self.behind:
                mine[j], theirs[j] = left, self.mate(left)
        yield
        offsets = range(-self.ahead, self.behind + 1)
        results += [side[o] for side in (mine, theirs) for o in offsets]

    def place_pieces(self, table, pieces, outs):
        shard, columns = pieces[0].shape
        chips, ahead = self.chips, self.ahead

        def body(table_ref, *refs):
            piece_refs, out_refs = refs[: 2 * chips], refs[2 * chips :]

            def put(sources):
                for i, source in enumerate(sources):
                    slot = lax.rem(table_ref[PLACE] - ahead + i + chips, chips)
                    for ref, (_, moves) in zip(out_refs, outs):
                        for own_rows, own_columns, rows, cut in moves:
                            ref[0, slot, own_rows, own_columns] = source[rows, cut].astype(
                                jnp.float32
                            )

            @pl.when(pl.program_id(0) == 0)
            def _():
                put(piece_refs[:chips])

            @pl.when(pl.program_id(0) == 1)
            def _():
                put(piece_refs[chips:])

        def target(i, t):
            return (jnp.where(i == 0, t[CORE], t[MATE]), 0, 0, 0)

        shapes = [(chips, *shape) for shape, _ in outs]
        results = pl.pallas_call(
            body,
            grid_spec=pltpu.PrefetchScalarGridSpec(
                num_scalar_prefetch=1,
                grid=(2,),
                in_specs=[
                    pl.BlockSpec(
                        (shard, columns), lambda i, w: (0, 0), pipeline_mode=pl.Buffered(1)
                    )
                ]
                * (2 * chips),
                out_specs=[pl.BlockSpec((1, *shape), target) for shape in shapes],
            ),
            out_shape=[jax.ShapeDtypeStruct((2, *shape), jnp.float32) for shape in shapes],
            compiler_params=pltpu.CompilerParams(vmem_limit_bytes=44 << 20),
            cost_estimate=COST,
            name="place_pieces",
        )(table, *pieces)
        return [out.reshape(-1, out.shape[-1]) for out in results]


class Share:
    def __init__(self, size, shape, rows, at):
        self.shard = shape[0] // size
        self.columns = shape[1]
        self.moves = []
        if self.shard <= rows:
            wide = self.columns // (rows // self.shard)
            for i in range(rows // self.shard):
                there = slice(i * self.shard, (i + 1) * self.shard)
                cut = slice(i * wide, (i + 1) * wide)
                self.moves.append((slice(0, self.shard), cut, there, slice(at, at + wide)))
            self.end = at + wide
        else:
            for i in range(self.shard // rows):
                low = at + i * self.columns
                here = slice(i * rows, (i + 1) * rows)
                self.moves.append(
                    (here, slice(0, self.columns), slice(0, rows), slice(low, low + self.columns))
                )
            self.end = at + (self.shard // rows) * self.columns


def grad_halves(table, cores, chips, rows, shares, sides):
    columns = shares[-1].end
    halves = [share.shard * chips for share in shares]
    steps = min(halves) // 128
    per = chips // steps
    arrays, where = [], []
    for lefts, rights in sides:
        place = []
        for array, low, count in [*lefts, *rights]:
            known = [n for n, other in enumerate(arrays) if other is array]
            if not known:
                arrays.append(array)
            place.append((known[0] if known else len(arrays) - 1, slice(low, low + count)))
        where.append((place[: len(lefts)], place[len(lefts) :]))

    def body(table_ref, *refs):
        refs, out_refs = refs[: len(arrays)], refs[len(arrays) :]

        @pl.loop(0, len(cores) * steps)
        def _(at):
            n_out = lax.div(at, steps)
            step = lax.rem(at, steps)
            core = table_ref[cores[0]]
            if len(cores) == 2:
                core = jnp.where(n_out == 0, core, table_ref[cores[1]])
            grads = []
            for half, (left, right) in zip(halves, where):
                tile = half // steps
                low = pl.multiple_of((core * steps + step) * tile, tile)
                grad = None
                for (n, n_rows), (m, m_rows) in zip(left, right):
                    term = dot_on(refs[n][n_rows, pl.ds(low, tile)], refs[m][m_rows, :], 0, 0)
                    grad = term if grad is None else grad + term
                grads.append(grad.astype(LOW))

            def put(ref):
                for grad, share in zip(grads, shares):
                    for n in range(per):
                        for own_rows, own_columns, there, cut in share.moves:
                            first = n * share.shard
                            ref[step * per + n, there, cut] = grad[
                                first + own_rows.start : first + own_rows.stop, own_columns
                            ]

            for n, ref in enumerate(out_refs):
                if len(out_refs) == 1:
                    put(ref)
                else:
                    pl.when(n_out == n)(functools.partial(put, ref))

    vmem = pl.BlockSpec(memory_space=pltpu.VMEM)
    return pl.pallas_call(
        body,
        in_specs=[pl.BlockSpec(memory_space=pltpu.SMEM)] + [vmem] * len(arrays),
        out_specs=[vmem] * len(cores),
        out_shape=[jax.ShapeDtypeStruct((chips, rows, columns), LOW)] * len(cores),
        compiler_params=pltpu.CompilerParams(vmem_limit_bytes=32 << 20),
        cost_estimate=COST,
        name="grad_halves",
    )(table, *arrays)


def add_low(a, b):
    return (a.astype(jnp.float32) + b.astype(jnp.float32)).astype(LOW)


def fold_sum(order, value, axis, count):
    bit = 1
    while bit < count:
        moved = lax.ppermute(value, axis, [(i, i ^ bit) for i in range(count)])
        yield
        value = order.run(jnp.add, value, moved)
        bit *= 2
    return value


def small_total(order, both, dp_only, size, ranks, results):
    lead = both.shape[0]
    both = yield from fold_sum(order, both, "tensor", ranks)
    total = yield from fold_sum(order, jnp.concatenate([both, dp_only]), "dp", size)
    results += [total[:lead], total[lead:]]


def dp_sum(order, value, size, results):
    total = yield from fold_sum(order, value, "dp", size)
    results.append(total)


def row_kernel(name, body, rows, arrays, vectors, out_types, sum_rows):
    block = min(128, rows)
    n = len(arrays) + len(vectors)

    def kernel(*refs):
        values, sums = body(*[r[...].astype(jnp.float32) for r in refs[:n]])
        for ref, value in zip(refs[n:-1], values, strict=True):
            ref[...] = value.astype(ref.dtype)
        sums = [jnp.sum(v, 0, keepdims=True) for v in sums]
        sums = jnp.concatenate(sums + [jnp.zeros_like(sums[0])] * (sum_rows - len(sums)), 0)

        @pl.when(pl.program_id(0) == 0)
        def _():
            refs[-1][...] = sums

        @pl.when(pl.program_id(0) > 0)
        def _():
            refs[-1][...] += sums

    width = vectors[0].shape[-1]
    in_specs = [
        pl.BlockSpec((block, a.shape[1]), lambda i, at=low // block: (at + i, 0))
        for a, low in arrays
    ]
    in_specs += [pl.BlockSpec((1, width), lambda i: (0, 0))] * len(vectors)
    out_specs = [pl.BlockSpec((block, w), lambda i: (i, 0)) for w, _ in out_types]
    return pl.pallas_call(
        kernel,
        grid=(rows // block,),
        in_specs=in_specs,
        out_specs=out_specs + [pl.BlockSpec((sum_rows, width), lambda i: (0, 0))],
        out_shape=[jax.ShapeDtypeStruct((rows, w), t) for w, t in out_types]
        + [jax.ShapeDtypeStruct((sum_rows, width), jnp.float32)],
        compiler_params=pltpu.CompilerParams(vmem_limit_bytes=12 << 20),
        cost_estimate=COST,
        name=name,
    )(*[a for a, _ in arrays], *vectors)


def product(x, low, rows, weights, transposed, out_type):
    inner = x.shape[1]
    outer = weights.shape[0 if transposed else 1]
    tile = min(512, outer)

    def body(x_ref, w_ref, out_ref):
        out_ref[...] = dot_on(x_ref[...], w_ref[...], 1, 1 if transposed else 0).astype(out_type)

    if transposed:
        spec = pl.BlockSpec((tile, inner), lambda i: (i, 0))
    else:
        spec = pl.BlockSpec((inner, tile), lambda i: (0, i))
    return pl.pallas_call(
        body,
        grid=(outer // tile,),
        in_specs=[pl.BlockSpec((rows, inner), lambda i: (low // rows, 0)), spec],
        out_specs=pl.BlockSpec((rows, tile), lambda i: (0, i)),
        out_shape=jax.ShapeDtypeStruct((rows, outer), out_type),
        compiler_params=pltpu.CompilerParams(vmem_limit_bytes=10 << 20),
        cost_estimate=COST,
        name="product",
    )(x, weights)


def ffn_forward(x, up_w, up_b, down_w, out_type):
    rows, width = x.shape
    units = up_w.shape[1]
    tile = min(512, units)
    steps = units // tile

    def body(x_ref, up_ref, b_ref, down_ref, act_ref, slope_ref, out_ref, acc_ref):
        step = pl.program_id(0)
        up = dot_on(x_ref[...], up_ref[...], 1, 0) + b_ref[...].astype(jnp.float32)
        act, slope = gelu_parts(up)
        act = act.astype(LOW)
        act_ref[...] = act
        slope_ref[...] = slope.astype(LOW)
        accumulate(step, steps, dot_on(act, down_ref[...], 1, 0), acc_ref, out_ref)

    part = pl.BlockSpec((rows, tile), lambda i: (0, i))
    whole = pl.BlockSpec((rows, width), lambda i: (0, 0))
    return pl.pallas_call(
        body,
        grid=(steps,),
        in_specs=[
            whole,
            pl.BlockSpec((width, tile), lambda i: (0, i)),
            pl.BlockSpec((1, tile), lambda i: (0, i)),
            pl.BlockSpec((tile, width), lambda i: (i, 0)),
        ],
        out_specs=[part, part, whole],
        out_shape=[jax.ShapeDtypeStruct((rows, units), LOW)] * 2
        + [jax.ShapeDtypeStruct((rows, width), out_type)],
        scratch_shapes=[pltpu.VMEM((rows, width), jnp.float32)],
        compiler_params=pltpu.CompilerParams(vmem_limit_bytes=16 << 20),
        cost_estimate=COST,
        name="ffn_forward",
    )(x, up_w, up_b, down_w)


def ffn_back(grad, slope, down_w, up_w, out_type):
    rows, width = grad.shape
    units = up_w.shape[1]
    tile = min(512, units)
    steps = units // tile

    def body(g_ref, slope_ref, down_ref, up_ref, dup_ref, out_ref, acc_ref):
        step = pl.program_id(0)
        dact = dot_on(g_ref[...], down_ref[...], 1, 1)
        dup = (dact * slope_ref[...].astype(jnp.float32)).astype(LOW)
        dup_ref[...] = dup
        accumulate(step, steps, dot_on(dup, up_ref[...], 1, 1), acc_ref, out_ref)

    part = pl.BlockSpec((rows, tile), lambda i: (0, i))
    whole = pl.BlockSpec((rows, width), lambda i: (0, 0))
    return pl.pallas_call(
        body,
        grid=(steps,),
        in_specs=[
            whole,
            part,
            pl.BlockSpec((tile, width), lambda i: (i, 0)),
            pl.BlockSpec((width, tile), lambda i: (0, i)),
        ],
        out_specs=[part, whole],
        out_shape=[
            jax.ShapeDtypeStruct((rows, units), LOW),
            jax.ShapeDtypeStruct((rows, width), out_type),
        ],
        scratch_shapes=[pltpu.VMEM((rows, width), jnp.float32)],
        compiler_params=pltpu.CompilerParams(vmem_limit_bytes=16 << 20),
        cost_estimate=COST,
        name="ffn_back",
    )(grad, slope, down_w, up_w)


def accumulate(step, steps, term, acc_ref, out_ref):
    if steps == 1:
        out_ref[...] = term.astype(out_ref.dtype)
        return

    @pl.when(step == 0)
    def _():
        acc_ref[...] = term

    @pl.when((step > 0) & (step < steps - 1))
    def _():
        acc_ref[...] += term

    @pl.when(step == steps - 1)
    def _():
        out_ref[...] = (acc_ref[...] + term).astype(out_ref.dtype)


def mean(rows):
    return jnp.mean(rows, -1, keepdims=True)


def normalise(rows):
    centre = rows - mean(rows)
    inverse = lax.rsqrt(mean(centre * centre) + EPS)
    return centre * inverse, inverse


def norm_back(grad, normed, inverse, gain):
    scaled = grad * gain
    return inverse * (scaled - mean(scaled) - normed * mean(scaled * normed))


def gelu_parts(values):
    square = values * values
    rate = -2.0 * GELU_C
    gate = 1.0 / (1.0 + jnp.exp(values * (rate + rate * 0.044715 * square)))
    output = values * gate
    slope = gate + output * (1.0 - gate) * (2.0 * GELU_C + 6.0 * GELU_C * 0.044715 * square)
    return output, slope


def dot(a, b):
    return jnp.dot(a, b, preferred_element_type=jnp.float32)


def dot_nt(a, b):
    return dot_on(a, b, 1, 1)


def dot_tn(a, b):
    return dot_on(a, b, 0, 0)


def column_sums(rows):
    ones = jnp.ones((8, rows.shape[0]), LOW)
    return dot(ones, rows)[0]


def local(
    dp_size,
    ranks,
    hidden_in,
    query_w,
    key_w,
    value_w,
    query_b,
    value_b,
    out_w,
    out_b,
    gain_attn,
    shift_attn,
    up_w,
    up_b,
    down_w,
    down_b,
    gain_ffn,
    shift_ffn,
    random_blocks,
    cotangent,
):
    own_rows, seqs_here, width = hidden_in.shape
    channels, hidden_units = query_w.shape[1], up_w.shape[1]
    length = own_rows * ranks
    chunks = CHUNKS
    piece = own_rows // chunks
    every = range(chunks)
    others = range(1, ranks)
    ring = Ring(dp_size)
    rows_in = hidden_in.reshape(own_rows, width)
    grad_out = cotangent.reshape(own_rows, width)
    lows = [c * piece for c in every]
    order = Order()
    run, tie = order.run, order.tie

    far_rows = fetch(rows_in, ranks)

    def project(x, *w):
        return (dot(x, w[0]) + w[1]).astype(LOW)

    def set_up(ids, q_w, k_w, v_w, q_b, v_b, *vectors):
        return (
            ring.table(own_rows // BLOCK),
            ids.reshape(ids.shape[0], -1),
            jnp.concatenate([q_w, k_w, v_w], 1),
            jnp.concatenate([q_b, jnp.zeros_like(q_b), v_b]).astype(jnp.float32),
            [v.reshape(1, -1) for v in vectors],
        )

    table, random_ids, qkv_w, qkv_b, vectors = run(
        set_up,
        random_blocks,
        query_w,
        key_w,
        value_w,
        query_b,
        value_b,
        out_b,
        gain_attn,
        shift_attn,
        up_b,
        down_b,
        gain_ffn,
        shift_ffn,
    )
    out_b, gain_attn, shift_attn, up_b, down_b, gain_ffn, shift_ffn = vectors
    near = run(project, rows_in, qkv_w, qkv_b)
    qkv = run(
        lambda n, w, b, *x: jnp.concatenate([n] + [project(p, w, b) for p in x], 0),
        near,
        qkv_w,
        qkv_b,
        *far_rows,
    )

    contexts, lses, attn_moved, attn_own = [], [], [], []
    for c in every:
        context, lse = run(lambda v: attend(v, random_ids, table, c, chunks, ranks), qkv)
        contexts.append(context)
        lses.append(lse)
        shares = [
            run(lambda x: product(x, j * piece, piece, out_w, False, LOW), context) for j in others
        ]
        attn_moved.append(hand_over(shares, ranks))
    for c in every:
        attn_own.append(
            run(lambda x: product(x, 0, piece, out_w, False, jnp.float32), contexts[c])
        )

    low_rows = (width, LOW)

    def norm_one(low, own, *moved):
        def body(*values):
            *terms, source, bias, gain, shift = values
            attn_out = functools.reduce(jnp.add, terms)
            resid = source + attn_out + bias
            normed, inverse = normalise(resid)
            hidden = gain * normed + shift
            inverse = jnp.broadcast_to(inverse, (inverse.shape[0], 128))
            return [hidden, normed, inverse], [resid * resid, attn_out * attn_out]

        return row_kernel(
            "norm_one",
            body,
            piece,
            [(own, 0)] + [(m, 0) for m in moved] + [(rows_in, low)],
            [out_b, gain_attn, shift_attn],
            [low_rows, low_rows, (128, jnp.float32)],
            8,
        )

    x, n1, i1, squares, acts, slopes, mlp_moved, mlp_own = ([] for _ in range(8))
    for c in every:
        low, n, i, sq = run(functools.partial(norm_one, lows[c]), attn_own[c], *attn_moved[c])
        n1.append(n)
        i1.append(i)
        squares.append(sq)
        x.append([low] + fetch(low, ranks))
        act, slope, own = run(lambda v: ffn_forward(v, up_w, up_b, down_w, jnp.float32), low)
        acts.append([act])
        slopes.append([slope])
        mlp_own.append(own)
    for c in every:
        shares = []
        for j in others:
            act, slope, share = run(lambda v: ffn_forward(v, up_w, up_b, down_w, LOW), x[c][j])
            acts[c].append(act)
            slopes[c].append(slope)
            shares.append(share)
        mlp_moved.append(hand_over(shares, ranks))

    def norm_two(low, own, h, *moved):
        def body(*values):
            *terms, before, g, bias, gain, shift = values
            mlp_out = functools.reduce(jnp.add, terms)
            normed, inverse = normalise(before + mlp_out + bias)
            back = norm_back(g, normed, inverse, gain)
            sums = [back, g * normed, g, mlp_out * mlp_out]
            return [back, gain * normed + shift], sums

        return row_kernel(
            "norm_two",
            body,
            piece,
            [(own, 0)] + [(m, 0) for m in moved] + [(h, 0), (grad_out, low)],
            [down_b, gain_ffn, shift_ffn],
            [low_rows, low_rows],
            8,
        )

    dmlp, layer_out, sums2 = [], [], []
    for c in every:
        low, out, sums = run(
            functools.partial(norm_two, lows[c]), mlp_own[c], x[c][0], *mlp_moved[c]
        )
        layer_out.append(out)
        sums2.append(sums)
        dmlp.append([low] + fetch(low, ranks))

    dups, dhid_moved, dhid_own = [], [], []
    for c in every:
        dup, own = run(
            lambda d, s: ffn_back(d, s, down_w, up_w, jnp.float32), dmlp[c][0], slopes[c][0]
        )
        dups.append([dup])
        dhid_own.append(own)
    for c in every:
        shares = []
        for j in others:
            dup, share = run(
                lambda d, s: ffn_back(d, s, down_w, up_w, LOW), dmlp[c][j], slopes[c][j]
            )
            dups[c].append(dup)
            shares.append(share)
        dhid_moved.append(hand_over(shares, ranks))

    under_way = []

    def advance(*names):
        for name in names or [n for n, _ in under_way]:
            for entry in [e for e in under_way if e[0] == name]:
                if next(entry[1], "end") == "end":
                    under_way.remove(entry)

    def begin(name, rows, shares, sides, between):
        results = []
        leaves, tree = jax.tree.flatten(sides)
        arrays = list({id(x): x for x in leaves if not isinstance(x, int)}.values())

        def halves(*cores):
            def call(*tied):
                known = {id(x): t for x, t in zip(arrays, tied)}
                found = [x if isinstance(x, int) else known[id(x)] for x in leaves]
                sides = jax.tree.unflatten(tree, found)
                return grad_halves(table, cores, ring.chips, rows, shares, sides)

            return run(call, *arrays)

        if between is None:
            given, kept = halves(MATE, CORE)
            moved = ring.mate(given)
        else:
            moved = ring.mate(halves(MATE)[0])
            between()
            (kept,) = halves(CORE)
        under_way.append((name, ring.steps(order, table, kept, moved, results)))
        return results

    def pieces_of(parts):
        return [(p, 0, piece) for part in parts for p in part]

    ffn_rows = hidden_units // dp_size
    down_share = Share(dp_size, (hidden_units, width), ffn_rows, 0)
    up_share = Share(dp_size, (width, hidden_units), ffn_rows, down_share.end)
    ffn = begin(
        "ffn",
        ffn_rows,
        [down_share, up_share],
        [
            (pieces_of(acts), pieces_of(dmlp)),
            (pieces_of(x), pieces_of(dups)),
        ],
        None,
    )

    def norm_one_back(own, d2, n, i, *moved):
        def body(*values):
            *terms, normed, inverse, gain = values
            dhidden = functools.reduce(jnp.add, terms)
            back = norm_back(dhidden, normed, inverse[:, :1], gain)
            return [back], [back, dhidden * normed, dhidden]

        return row_kernel(
            "norm_one_back",
            body,
            piece,
            [(a, 0) for a in (own, *moved, d2, n, i)],
            [gain_attn],
            [low_rows],
            8,
        )

    dattn, sums1, dcontexts = [], [], []
    for c in every:
        low, sums = run(
            norm_one_back, dhid_own[c], dmlp[c][0], n1[c], i1[c], *dhid_moved[c]
        )
        sums1.append(sums)
        dattn.append([low] + fetch(low, ranks))
        advance("ffn")
    for c in every:
        dcontexts.append(run(lambda d: product(d, 0, piece, out_w, True, LOW), dattn[c][0]))
    grad_up_b = run(
        lambda *d: functools.reduce(jnp.add, [column_sums(p) for p in d]),
        *[p for part in dups for p in part],
    )

    def gather_sums(squares, one, two):
        one, two, squares = sum(one), sum(two), sum(squares)
        scalars = jnp.stack([jnp.sum(squares[0]), jnp.sum(squares[1]), jnp.sum(two[3])])
        rows = [one[i] for i in range(3)] + [two[i] for i in range(3)]
        return jnp.concatenate(rows + [jnp.pad(scalars, (0, 125))])

    small = []
    both = run(gather_sums, squares, sums1, sums2)
    under_way.append(("small", small_total(order, both, grad_up_b, dp_size, ranks, small)))

    dq_parts, sums = [], []
    for c in every:
        dcontext = run(
            lambda near, *far: jnp.concatenate(
                [near] + [product(d, 0, piece, out_w, True, LOW) for d in far], 0
            ),
            dcontexts[c],
            *dattn[c][1:],
        )
        advance("ffn", "small")
        dq, *sums = run(
            lambda v, d, l, e, s: jax.tree.leaves(
                attend_back(v, d, l, random_ids, table, e, s, c, chunks, ranks)
            ),
            qkv,
            dcontext,
            lses[c],
            dq_parts,
            sums,
        )
        dq_parts.append(dq)
        if c < chunks - 1:
            advance("ffn", "small")
    dqkv, bias_sums = dq, sums[0]

    attn_rows = width // dp_size
    attn_shares = [Share(dp_size, (width, 3 * channels), attn_rows, 0)]
    attn_sides = [
        (
            [(x, 0, own_rows) for x in [rows_in] + far_rows],
            [(dqkv, j * own_rows, own_rows) for j in range(ranks)],
        )
    ]
    with_out = channels % 256 == 0
    if with_out:
        attn_shares.append(Share(dp_size, (channels, width), attn_rows, attn_shares[0].end))
        attn_sides.append(
            (
                [(contexts[c], j * piece, piece) for c in every for j in range(ranks)],
                [(dattn[c][j], 0, piece) for c in every for j in range(ranks)],
            )
        )
    dinput_moved = []

    def send_dinput():
        shares = [
            run(lambda d: product(d, j * own_rows, own_rows, qkv_w, True, LOW), dqkv)
            for j in others
        ]
        dinput_moved.extend(hand_over(shares, ranks))

    attn = begin("attn", attn_rows, attn_shares, attn_sides, send_dinput)
    qkv_b_sums = []
    advance("attn", "ffn")
    under_way.append(
        ("qkv_b", dp_sum(order, bias_sums[0], dp_size, qkv_b_sums))
    )
    advance("attn")
    dinput_own = run(lambda d: product(d, 0, own_rows, qkv_w, True, jnp.float32), dqkv)
    advance("ffn", "attn", "qkv_b")
    grad_input = run(
        lambda own, d, *m: (plus(own, m) + jnp.concatenate(d, 0)).astype(LOW),
        dinput_own,
        [d[0] for d in dattn],
        *dinput_moved,
    )
    totals = {}
    entries = float(own_rows * ranks * dp_size * seqs_here * width)

    def spread(both):
        vectors = [both[i * width : (i + 1) * width] for i in range(6)]
        return vectors, jnp.sqrt(both[6 * width : 6 * width + 3] / entries)

    ffn_outs = [((g.shard, g.columns), g.moves) for g in (down_share, up_share)]
    while under_way:
        advance()
        names = {n for n, _ in under_way}
        if "ffn" not in names and "ffn" not in totals:
            totals["ffn"] = run(lambda *p: ring.place_pieces(table, p, ffn_outs), *ffn)
        if "small" not in names and "small" not in totals:
            totals["small"] = run(spread, small[0])
    everything = slice(0, attn_rows)
    attn_outs = []
    for i in range(3):
        cut = slice(i * channels, (i + 1) * channels)
        attn_outs.append(
            ((attn_rows, channels), [(everything, slice(0, channels), everything, cut)])
        )
    if with_out:
        attn_outs.append(((attn_shares[1].shard, width), attn_shares[1].moves))
    grad_q, grad_k, grad_v, *rest = run(lambda *p: ring.place_pieces(table, p, attn_outs), *attn)
    if with_out:
        (grad_out_w,) = rest
    else:
        partial = sum(
            dot_tn(contexts[c], jnp.concatenate(dattn[c], 0)) for c in every
        )
        grad_out_w = lax.psum(partial.astype(LOW), "dp").astype(jnp.float32)
    grad_down_w, grad_up_w = totals["ffn"]
    vectors, rms_stats = totals["small"]
    biases = [qkv_b_sums[0][:channels], qkv_b_sums[0][channels:], small[1]]
    shape = hidden_in.shape
    return (
        jnp.concatenate(layer_out, 0).reshape(shape),
        grad_input.reshape(shape),
        grad_q,
        grad_k,
        grad_v,
        biases[0],
        biases[1],
        grad_out_w,
        vectors[0],
        vectors[1],
        vectors[2],
        grad_up_w,
        biases[2],
        grad_down_w,
        vectors[3],
        vectors[4],
        vectors[5],
        rms_stats,
    )


def solution(mesh):
    rows = P("tensor", "dp", None)
    columns, split, whole = P(None, "tensor"), P("tensor"), P()
    first = P("tensor", None)
    return jax.shard_map(
        functools.partial(local, mesh.shape["dp"], mesh.shape["tensor"]),
        mesh=mesh,
        in_specs=(
            rows,
            columns,
            columns,
            columns,
            split,
            split,
            first,
            whole,
            whole,
            whole,
            columns,
            split,
            first,
            whole,
            whole,
            whole,
            P("tensor", None, None),
            rows,
        ),
        out_specs=(
            rows,
            rows,
            columns,
            columns,
            columns,
            split,
            split,
            first,
            whole,
            whole,
            whole,
            columns,
            split,
            first,
            whole,
            whole,
            whole,
            whole,
        ),
        check_vma=False,
    )
```

time: 494 us -> 372 us (0.75)
  matrix products: 87.5 us -> 4.63 us
  Pallas kernels: 78.2 us -> 127 us
  other arithmetic: 31.3 us -> 7.48 us
  local copies, waits for them, and re-layouts: 33.6 us -> 11.3 us
  waiting for transfers between devices: 177 us -> 155 us
  starting transfers between devices: 72.5 us -> 60.5 us
    pallas_call x2 -> x45, Pallas kernels: 22.1 us -> 105 us  [the longest x2 22.3 us: attend_back(): pl.pallas_call(functools.partial(attend_back_kernel, plan, 3, len(earlier...]
    dot_general x18 -> x0, matrix products: 49.8 us -> none  [dot_on(): lax.dot_general(left, right, (((left_dim,), (right_dim,)), ((), ())), pre...]
    ppermute x12 -> x16, waiting for transfers between devices: 26.1 us -> 63.2 us  [the longest x7 37.1 us: hand_over(): lax.ppermute(share, 'tensor', [(k, (k + s) % ranks) for k in range(ranks)])]
    pallas_call x4 -> x2, Pallas kernels: 44.5 us -> 11.3 us  [place_pieces(): pl.pallas_call(body, grid_spec=pltpu.PrefetchScalarGridSpec(num_scalar_pr...]
    dot_general x13 -> x6, matrix products: 37.7 us -> 4.63 us  [dot(): return jnp.dot(a, b, preferred_element_type=jnp.float32)]
    ppermute x56 -> x28, waiting for transfers between devices: 93.7 us -> 61.9 us  [shift(): return lax.ppermute(value, 'dp', pairs)]
    ppermute x7, waiting for transfers between devices: 55.4 us -> 29.2 us  [fetch(): lax.ppermute(rows, 'tensor', [((k + s) % ranks, k) for k in range(ranks)])]
    ppermute x56 -> x28, starting transfers between devices: 47.9 us -> 30.2 us  [shift(): return lax.ppermute(value, 'dp', pairs)]
  transfers between devices with their start and end apart: 83 -> 69, of which waited for: 40 -> 32; matrix products, arithmetic and copies ran while one was open for 26% -> 4% of each run, Pallas kernels for 11% -> 23%
where the time goes in v2:
time: 372 us; the launch traced here: 368 us
  waiting for transfers between devices  155 us (42%)
  Pallas kernels  127 us (34%)
  starting transfers between devices  60.5 us (16%)
  local copies, waits for them, and re-layouts  11.3 us (3%)
  other arithmetic  7.48 us (2%)
  matrix products  4.63 us (1%)
    ppermute x28, waiting for transfers between devices, shift(): return lax.ppermute(value, 'dp', pairs)  61.9 us
    ppermute x7, waiting for transfers between devices, hand_over(): lax.ppermute(share, 'tensor', [(k, (k + s) % ranks) for k in range(ranks)])  37.1 us
    ppermute x28, starting transfers between devices, shift(): return lax.ppermute(value, 'dp', pairs)  30.2 us
    ppermute x7, waiting for transfers between devices, fetch(): lax.ppermute(rows, 'tensor', [((k + s) % ranks, k) for k in range(ranks)])  29.2 us
    ppermute x9, waiting for transfers between devices, fold_sum(): moved = lax.ppermute(value, axis, [(i, i ^ bit) for i in range(count)])  26.1 us
    pallas_call x2, Pallas kernels, attend_back(): pl.pallas_call(functools.partial(attend_back_kernel, plan, 3, len(earlier...  22.3 us
    pallas_call x4, Pallas kernels, ffn_forward(): pl.pallas_call(body, grid=(steps,), in_specs=[whole, pl.BlockSpec((width,...  20.3 us
    pallas_call x3, Pallas kernels, grad_halves(): pl.pallas_call(body, in_specs=[pl.BlockSpec(memory_space=pltpu.SMEM)] + [...  18.1 us
  transfers between devices with their start and end apart: 69, of which 32 were waited for; matrix products, arithmetic and copies ran while one was open for 4% of the time, Pallas kernels for 23%

profile of v2, /device:TPU:0, one launch (start us, length us, event | category | flops | bytes accessed | tf_op | source)
XLA Modules:
  0.0 368.0 jit_solution(9313860968506366610)
XLA Ops:
  0.7 3.0 collective-permute-start
  8.1 1.8 fusion
  10.0 17.1 %collective-permute-done.refs_1_ = bf16[512,1024]{1,0:T(8,128)(2,1)S(1)} collective-permute-done((bf16[512,1024]{1,0:T(8,128)(2,1)}, bf16[512,1024]{1,0:T(8,128)(2,1)S(1)}, u32[]{:S(2)}, u32[]{:S(2)}) %collective-permute-start) | collective-permute-done | bytes 1048608 | tf_op jit(solution)/shard_map/ppermute | solution.py:361
  27.0 1.8 fusion.1
  29.1 5.8 %attend.2 = (bf16[512,512]{1,0:T(8,128)(2,1)S(1)}, f32[2,8,256]{2,1,0:T(8,128)S(1)}) custom-call(s32[4]{0:T(128)S(1)} %pad_add_fusion.table_ref, s32[8,42]{1,0:T(8,128)S(1)} %copy.38.rb_ref, bf16[1024,1536]{1,0:T(8,128)(2,1)S(1)} %pad_maximum_fusion.q_ref.k_ref.v_ref, bf16[1024,1536]{1,0:T(8,128)(2,1)S(1)} %pad_maximum_fusion.q_ref.k_ref.v_ref, ...), custom_call_target="tpu_custom_call" | custom-call | flops 1024 | bytes 1024 | tf_op jit(solution)/shard_map/attend/pallas_call | solution.py:281
  35.8 1.8 collective-permute-start.1
  37.5 5.6 %attend.3 = (bf16[512,512]{1,0:T(8,128)(2,1)S(1)}, f32[2,8,256]{2,1,0:T(8,128)S(1)}) custom-call(s32[4]{0:T(128)S(1)} %pad_add_fusion.table_ref, s32[8,42]{1,0:T(8,128)S(1)} %copy.38.rb_ref, bf16[1024,1536]{1,0:T(8,128)(2,1)S(1)} %pad_maximum_fusion.q_ref.k_ref.v_ref, bf16[1024,1536]{1,0:T(8,128)(2,1)S(1)} %pad_maximum_fusion.q_ref.k_ref.v_ref, ...), custom_call_target="tpu_custom_call" | custom-call | flops 1024 | bytes 1024 | tf_op jit(solution)/shard_map/attend/pallas_call | solution.py:281
  46.0 4.7 %collective-permute-done.1.refs_1_ = bf16[256,1024]{1,0:T(8,128)(2,1)S(1)} collective-permute-done((bf16[256,1024]{1,0:T(8,128)(2,1)S(1)}, bf16[256,1024]{1,0:T(8,128)(2,1)S(1)}, u32[]{:S(2)}, u32[]{:S(2)}) %collective-permute-start.1) | collective-permute-done | bytes 524320 | tf_op jit(solution)/shard_map/ppermute | solution.py:368
  52.3 1.7 collective-permute-start.2
  54.0 5.1 %ffn_forward.4 = (bf16[256,2048]{1,0:T(8,128)(2,1)S(1)}, bf16[256,2048]{1,0:T(8,128)(2,1)S(1)}, f32[256,1024]{1,0:T(8,128)S(1)}) custom-call(bf16[256,1024]{1,0:T(8,128)(2,1)S(1)} %get-tuple-element.385.x_ref.refs_2_.refs_8_, bf16[1024,2048]{1,0:T(8,128)(2,1)S(1)} %copy-done, bf16[1,2048]{1,0:T(2,128)(2,1)S(1)} %reshape.100.b_ref, ...), custom_call_target="tpu_custom_call" | custom-call | flops 1024 | bytes 1024 | tf_op jit(solution)/shard_map/ffn_forward/pallas_call | solution.py:707
  59.1 2.8 collective-permute-done.3.refs_1_
  63.5 1.7 collective-permute-start.5
  65.3 5.1 %ffn_forward.5 = (bf16[256,2048]{1,0:T(8,128)(2,1)S(1)}, bf16[256,2048]{1,0:T(8,128)(2,1)S(1)}, f32[256,1024]{1,0:T(8,128)S(1)}) custom-call(bf16[256,1024]{1,0:T(8,128)(2,1)S(1)} %get-tuple-element.387.x_ref.refs_2_.refs_10_, bf16[1024,2048]{1,0:T(8,128)(2,1)S(1)} %copy-done, bf16[1,2048]{1,0:T(2,128)(2,1)S(1)} %reshape.100.b_ref, ...), custom_call_target="tpu_custom_call" | custom-call | flops 1024 | bytes 1024 | tf_op jit(solution)/shard_map/ffn_forward/pallas_call | solution.py:707
  70.4 2.8 collective-permute-done.2.x_ref.refs_9_
  73.1 5.1 %ffn_forward.6 = (bf16[256,2048]{1,0:T(8,128)(2,1)S(1)}, bf16[256,2048]{1,0:T(8,128)(2,1)S(1)}, bf16[256,1024]{1,0:T(8,128)(2,1)S(1)}) custom-call(bf16[256,1024]{1,0:T(8,128)(2,1)S(1)} %collective-permute-done.2.x_ref.refs_9_, bf16[1024,2048]{1,0:T(8,128)(2,1)S(1)} %copy-done, bf16[1,2048]{1,0:T(2,128)(2,1)S(1)} %reshape.100.b_ref, ...), custom_call_target="tpu_custom_call" | custom-call | flops 1024 | bytes 1024 | tf_op jit(solution)/shard_map/ffn_forward/pallas_call | solution.py:707
  78.3 1.8 collective-permute-start.4
  80.1 4.3 %collective-permute-done.5.x_ref.refs_11_ = bf16[256,1024]{1,0:T(8,128)(2,1)S(1)} collective-permute-done((bf16[256,1024]{1,0:T(8,128)(2,1)S(1)}, bf16[256,1024]{1,0:T(8,128)(2,1)S(1)}, u32[]{:S(2)}, u32[]{:S(2)}) %collective-permute-start.5) | collective-permute-done | bytes 524320 | tf_op jit(solution)/shard_map/ppermute | solution.py:361
  84.4 5.1 %ffn_forward.7 = (bf16[256,2048]{1,0:T(8,128)(2,1)S(1)}, bf16[256,2048]{1,0:T(8,128)(2,1)S(1)}, bf16[256,1024]{1,0:T(8,128)(2,1)S(1)}) custom-call(bf16[256,1024]{1,0:T(8,128)(2,1)S(1)} %collective-permute-done.5.x_ref.refs_11_, bf16[1024,2048]{1,0:T(8,128)(2,1)S(1)} %copy-done, bf16[1,2048]{1,0:T(2,128)(2,1)S(1)} %reshape.100.b_ref, ...), custom_call_target="tpu_custom_call" | custom-call | flops 1024 | bytes 1024 | tf_op jit(solution)/shard_map/ffn_forward/pallas_call | solution.py:707
  89.5 1.8 collective-permute-start.6
  91.3 4.3 %collective-permute-done.4.refs_1_ = bf16[256,1024]{1,0:T(8,128)(2,1)S(1)} collective-permute-done((bf16[256,1024]{1,0:T(8,128)(2,1)S(1)}, bf16[256,1024]{1,0:T(8,128)(2,1)S(1)}, u32[]{:S(2)}, u32[]{:S(2)}) %collective-permute-start.4) | collective-permute-done | bytes 524320 | tf_op jit(solution)/shard_map/ppermute | solution.py:368
  98.0 1.7 collective-permute-start.8
  99.8 7.1 %collective-permute-done.6.refs_1_ = bf16[256,1024]{1,0:T(8,128)(2,1)S(1)} collective-permute-done((bf16[256,1024]{1,0:T(8,128)(2,1)S(1)}, bf16[256,1024]{1,0:T(8,128)(2,1)S(1)}, u32[]{:S(2)}, u32[]{:S(2)}) %collective-permute-start.6) | collective-permute-done | bytes 524320 | tf_op jit(solution)/shard_map/ppermute | solution.py:368
  108.0 1.8 collective-permute-start.7
  109.8 4.2 %ffn_back.4 = (bf16[256,2048]{1,0:T(8,128)(2,1)S(1)}, f32[256,1024]{1,0:T(8,128)S(1)}) custom-call(bf16[256,1024]{1,0:T(8,128)(2,1)S(1)} %get-tuple-element.399.g_ref.refs_4_.refs_2_, bf16[256,2048]{1,0:T(8,128)(2,1)S(1)} %get-tuple-element.354.slope_ref, bf16[2048,1024]{1,0:T(8,128)(2,1)S(1)} %copy-done.1, bf16[1024,2048]{1,0:T(8,128)(2,1)S(1)} %copy-done), custom_call_target="tpu_custom_call" | custom-call | flops 1024 | bytes 1024 | tf_op jit(solution)/shard_map/ffn_back/pallas_call | solution.py:741
  114.1 4.2 %ffn_back.5 = (bf16[256,2048]{1,0:T(8,128)(2,1)S(1)}, f32[256,1024]{1,0:T(8,128)S(1)}) custom-call(bf16[256,1024]{1,0:T(8,128)(2,1)S(1)} %get-tuple-element.411.g_ref.refs_6_.refs_2_, bf16[256,2048]{1,0:T(8,128)(2,1)S(1)} %get-tuple-element.357.slope_ref, bf16[2048,1024]{1,0:T(8,128)(2,1)S(1)} %copy-done.1, bf16[1024,2048]{1,0:T(8,128)(2,1)S(1)} %copy-done), custom_call_target="tpu_custom_call" | custom-call | flops 1024 | bytes 1024 | tf_op jit(solution)/shard_map/ffn_back/pallas_call | solution.py:741
  118.3 4.2 %ffn_back.6 = (bf16[256,2048]{1,0:T(8,128)(2,1)S(1)}, bf16[256,1024]{1,0:T(8,128)(2,1)S(1)}) custom-call(bf16[256,1024]{1,0:T(8,128)(2,1)S(1)} %collective-permute-done.8.g_ref.refs_5_, bf16[256,2048]{1,0:T(8,128)(2,1)S(1)} %get-tuple-element.364.slope_ref, bf16[2048,1024]{1,0:T(8,128)(2,1)S(1)} %copy-done.1, bf16[1024,2048]{1,0:T(8,128)(2,1)S(1)} %copy-done), custom_call_target="tpu_custom_call" | custom-call | flops 1024 | bytes 1024 | tf_op jit(solution)/shard_map/ffn_back/pallas_call | solution.py:741
  122.5 5.0 %collective-permute-done.7.g_ref.refs_7_ = bf16[256,1024]{1,0:T(8,128)(2,1)S(1)} collective-permute-done((bf16[256,1024]{1,0:T(8,128)(2,1)S(1)}, bf16[256,1024]{1,0:T(8,128)(2,1)S(1)}, u32[]{:S(2)}, u32[]{:S(2)}) %collective-permute-start.7) | collective-permute-done | bytes 524320 | tf_op jit(solution)/shard_map/ppermute | solution.py:361
  127.6 4.2 %ffn_back.7 = (bf16[256,2048]{1,0:T(8,128)(2,1)S(1)}, bf16[256,1024]{1,0:T(8,128)(2,1)S(1)}) custom-call(bf16[256,1024]{1,0:T(8,128)(2,1)S(1)} %collective-permute-done.7.g_ref.refs_7_, bf16[256,2048]{1,0:T(8,128)(2,1)S(1)} %get-tuple-element.367.slope_ref, bf16[2048,1024]{1,0:T(8,128)(2,1)S(1)} %copy-done.1, bf16[1024,2048]{1,0:T(8,128)(2,1)S(1)} %copy-done), custom_call_target="tpu_custom_call" | custom-call | flops 1024 | bytes 1024 | tf_op jit(solution)/shard_map/ffn_back/pallas_call | solution.py:741
  135.0 11.8 %grad_halves.3 = (bf16[8,128,2048]{2,1,0:T(8,128)(2,1)S(1)}, bf16[8,128,2048]{2,1,0:T(8,128)(2,1)S(1)}) custom-call(s32[4]{0:T(128)S(1)} %pad_add_fusion.table_ref, bf16[256,2048]{1,0:T(8,128)(2,1)S(1)} %get-tuple-element.377.refs_0_, bf16[256,2048]{1,0:T(8,128)(2,1)S(1)} %copy-done.10, bf16[256,2048]{1,0:T(8,128)(2,1)S(1)} %copy-done.8, ...), custom_call_target="tpu_custom_call" | custom-call | flops 1024 | bytes 1024 | tf_op jit(solution)/shard_map/grad_halves/pallas_call | solution.py:590
  149.0 12.9 %collective-permute-done.11.refs_1_ = bf16[256,1024]{1,0:T(8,128)(2,1)S(1)} collective-permute-done((bf16[256,1024]{1,0:T(8,128)(2,1)}, bf16[256,1024]{1,0:T(8,128)(2,1)S(1)}, u32[]{:S(2)}, u32[]{:S(2)}) %collective-permute-start.11) | collective-permute-done | bytes 524320 | tf_op jit(solution)/shard_map/ppermute | solution.py:368
  167.9 5.3 %collective-permute-done.9.refs_1_ = bf16[256,1024]{1,0:T(8,128)(2,1)S(1)} collective-permute-done((bf16[256,1024]{1,0:T(8,128)(2,1)S(1)}, bf16[256,1024]{1,0:T(8,128)(2,1)S(1)}, u32[]{:S(2)}, u32[]{:S(2)}) %collective-permute-start.9) | collective-permute-done | bytes 524320 | tf_op jit(solution)/shard_map/ppermute | solution.py:368
  174.0 2.6 collective-permute-done.13.refs_0_
  184.8 2.0 constant_dynamic-update-slice_fusion.5
  187.4 4.2 %collective-permute-done.16.refs_0_ = bf16[128,2048]{1,0:T(8,128)(2,1)S(1)} collective-permute-done((bf16[128,2048]{1,0:T(8,128)(2,1)S(1)}, bf16[128,2048]{1,0:T(8,128)(2,1)S(1)}, u32[]{:S(2)}, u32[]{:S(2)}) %collective-permute-start.16) | collective-permute-done | bytes 524320 | tf_op jit(solution)/shard_map/ppermute | solution.py:400
  196.8 10.8 %attend_back.2 = (bf16[512,512]{1,0:T(8,128)(2,1)S(1)}, f32[1024,512]{1,0:T(8,128)S(1)}, f32[1024,512]{1,0:T(8,128)S(1)}) custom-call(s32[4]{0:T(128)S(1)} %pad_add_fusion.table_ref, s32[8,42]{1,0:T(8,128)S(1)} %copy.38.rb_ref, bf16[1024,1536]{1,0:T(8,128)(2,1)S(1)} %pad_maximum_fusion.q_ref.k_ref.v_ref, ...), custom_call_target="tpu_custom_call" | custom-call | flops 1024 | bytes 1024 | tf_op jit(solution)/shard_map/attend_back/pallas_call | solution.py:324
  210.6 3.3 collective-permute-done.15
  214.6 3.9 %collective-permute-done.21.refs_0_ = bf16[128,2048]{1,0:T(8,128)(2,1)S(1)} collective-permute-done((bf16[128,2048]{1,0:T(8,128)(2,1)S(1)}, bf16[128,2048]{1,0:T(8,128)(2,1)S(1)}, u32[]{:S(2)}, u32[]{:S(2)}) %collective-permute-start.21) | collective-permute-done | bytes 524320 | tf_op jit(solution)/shard_map/ppermute | solution.py:400
  219.5 11.4 %attend_back.3 = (bf16[1024,1536]{1,0:T(8,128)(2,1)S(1)}, f32[8,1024]{1,0:T(8,128)S(1)}) custom-call(s32[4]{0:T(128)S(1)} %pad_add_fusion.table_ref, s32[8,42]{1,0:T(8,128)S(1)} %copy.38.rb_ref, bf16[1024,1536]{1,0:T(8,128)(2,1)S(1)} %pad_maximum_fusion.q_ref.k_ref.v_ref, bf16[1024,1536]{1,0:T(8,128)(2,1)S(1)} %pad_maximum_fusion.q_ref.k_ref.v_ref, ...), custom_call_target="tpu_custom_call" | custom-call | flops 1024 | bytes 1024 | tf_op jit(solution)/shard_map/attend_back/pallas_call | solution.py:324
  231.0 3.1 grad_halves.4
  236.3 2.1 product.18
  238.9 3.1 grad_halves.5.kept_ref
  243.4 5.1 %collective-permute-done.42.refs_5_ = bf16[128,2048]{1,0:T(8,128)(2,1)S(1)} collective-permute-done((bf16[128,2048]{1,0:T(8,128)(2,1)S(1)}, bf16[128,2048]{1,0:T(8,128)(2,1)S(1)}, u32[]{:S(2)}, u32[]{:S(2)}) %collective-permute-start.42) | collective-permute-done | bytes 524320 | tf_op jit(solution)/shard_map/ppermute | solution.py:400
  253.9 14.7 %collective-permute-done.25.refs_0_ = bf16[64,2048]{1,0:T(8,128)(2,1)S(1)} collective-permute-done((bf16[64,2048]{1,0:T(8,128)(2,1)S(1)}, bf16[64,2048]{1,0:T(8,128)(2,1)S(1)}, u32[]{:S(2)}, u32[]{:S(2)}) %collective-permute-start.25) | collective-permute-done | bytes 262176 | tf_op jit(solution)/shard_map/ppermute | solution.py:400
  270.5 2.2 product.19
  276.4 11.6 %collective-permute-done.30 = f32[8320]{0:T(1024)S(1)} collective-permute-done((f32[8320]{0:T(1024)S(1)}, f32[8320]{0:T(1024)S(1)}, u32[]{:S(2)}, u32[]{:S(2)}) %collective-permute-start.30) | collective-permute-done | bytes 33312 | tf_op jit(solution)/shard_map/ppermute | solution.py:608
  288.8 3.2 collective-permute-done.33
  292.4 2.4 collective-permute-done.27.refs_0_
  296.1 2.3 collective-permute-done.29.refs_0_
  300.3 2.0 collective-permute-start.32
  304.0 2.1 collective-permute-start.47
  306.1 3.1 collective-permute-done.32.refs_1_
  309.3 2.2 collective-permute-done.31.refs_0_
  312.2 2.1 collective-permute-start.35
  314.5 7.7 %collective-permute-done.47.refs_0_ = bf16[128,2048]{1,0:T(8,128)(2,1)S(1)} collective-permute-done((bf16[128,2048]{1,0:T(8,128)(2,1)S(1)}, bf16[128,2048]{1,0:T(8,128)(2,1)S(1)}, u32[]{:S(2)}, u32[]{:S(2)}) %collective-permute-start.47) | collective-permute-done | bytes 524320 | tf_op jit(solution)/shard_map/ppermute | solution.py:400
  322.2 1.7 collective-permute-start.38
  323.9 1.9 collective-permute-done.38
  326.4 8.1 %collective-permute-done.34.refs_3_ = bf16[64,2048]{1,0:T(8,128)(2,1)S(1)} collective-permute-done((bf16[64,2048]{1,0:T(8,128)(2,1)S(1)}, bf16[64,2048]{1,0:T(8,128)(2,1)S(1)}, u32[]{:S(2)}, u32[]{:S(2)}) %collective-permute-start.34) | collective-permute-done | bytes 262176 | tf_op jit(solution)/shard_map/ppermute | solution.py:400
  334.9 1.8 collective-permute-start.39
  338.2 1.8 collective-permute-start.40
  340.1 7.1 %place_pieces.2 = (f32[2,8,128,1024]{3,2,1,0:T(8,128)}, f32[2,8,64,2048]{3,2,1,0:T(8,128)}) custom-call(s32[4]{0:T(128)S(1)} %pad_add_fusion.table_ref, bf16[128,2048]{1,0:T(8,128)(2,1)S(1)} %collective-permute-done.47.refs_0_, bf16[128,2048]{1,0:T(8,128)(2,1)S(1)} %collective-permute-done.45.refs_1_, bf16[128,2048]{1,0:T(8,128)(2,1)S(1)} %collective-permute-done.43.refs_2_, ...), custom_call_target="tpu_custom_call" | custom-call | flops 1024 | bytes 1024 | tf_op jit(solution)/shard_map/place_pieces/pallas_call | solution.py:496
  347.9 1.8 collective-permute-start.58
  349.7 4.6 %collective-permute-done.59 = f32[1024]{0:T(1024)S(1)} collective-permute-done((f32[1024]{0:T(1024)S(1)}, f32[1024]{0:T(1024)S(1)}, u32[]{:S(2)}, u32[]{:S(2)}) %collective-permute-start.59) | collective-permute-done | bytes 4128 | tf_op jit(solution)/shard_map/ppermute | solution.py:608
  358.2 2.7 collective-permute-done.60.refs_0_
  363.6 4.2 %place_pieces.3 = (f32[2,8,64,512]{3,2,1,0:T(8,128)}, f32[2,8,64,512]{3,2,1,0:T(8,128)}, f32[2,8,64,512]{3,2,1,0:T(8,128)}, f32[2,8,32,1024]{3,2,1,0:T(8,128)}) custom-call(s32[4]{0:T(128)S(1)} %pad_add_fusion.table_ref, bf16[64,2048]{1,0:T(8,128)(2,1)S(1)} %collective-permute-done.60.refs_0_, bf16[64,2048]{1,0:T(8,128)(2,1)S(1)} %collective-permute-done.57.refs_1_, ...), custom_call_target="tpu_custom_call" | custom-call | flops 1024 | bytes 1024 | tf_op jit(solution)/shard_map/place_pieces/pallas_call | solution.py:496
  (251 shorter events, 77.3 us)
Async XLA Ops:
  0.7 26.4 %collective-permute-start = (bf16[512,1024]{1,0:T(8,128)(2,1)}, bf16[512,1024]{1,0:T(8,128)(2,1)S(1)}, u32[]{:S(2)}, u32[]{:S(2)}) collective-permute-start(bf16[512,1024]{1,0:T(8,128)(2,1)} %bitcast.36), channel_id=1, source_target_pairs={{1,0},{0,1},{3,2},{2,3},{5,4},{4,5},{7,6},{6,7},{9,8},{8,9},{11,10... | collective-permute-start | bytes 3145736 | tf_op jit(solution)/shard_map/ppermute | solution.py:361
  35.8 14.9 %collective-permute-start.1 = (bf16[256,1024]{1,0:T(8,128)(2,1)S(1)}, bf16[256,1024]{1,0:T(8,128)(2,1)S(1)}, u32[]{:S(2)}, u32[]{:S(2)}) collective-permute-start(bf16[256,1024]{1,0:T(8,128)(2,1)S(1)} %product.10), channel_id=1, source_target_pairs={{0,1},{1,0},{2,3},{3,2},{4,5},{5,4},{6,7},{7,6},{8,9},{9,8},{10,11... | collective-permute-start | bytes 1572872 | tf_op jit(solution)/shard_map/ppermute | solution.py:368
  43.9 18.0 %collective-permute-start.3 = (bf16[256,1024]{1,0:T(8,128)(2,1)S(1)}, bf16[256,1024]{1,0:T(8,128)(2,1)S(1)}, u32[]{:S(2)}, u32[]{:S(2)}) collective-permute-start(bf16[256,1024]{1,0:T(8,128)(2,1)S(1)} %product.11), channel_id=1, source_target_pairs={{0,1},{1,0},{2,3},{3,2},{4,5},{5,4},{6,7},{7,6},{8,9},{9,8},{10,11... | collective-permute-start | bytes 1572872 | tf_op jit(solution)/shard_map/ppermute | solution.py:368
  52.3 20.9 %collective-permute-start.2 = (bf16[256,1024]{1,0:T(8,128)(2,1)S(1)}, bf16[256,1024]{1,0:T(8,128)(2,1)S(1)}, u32[]{:S(2)}, u32[]{:S(2)}) collective-permute-start(bf16[256,1024]{1,0:T(8,128)(2,1)S(1)} %get-tuple-element.385.x_ref.refs_2_.refs_8_), channel_id=1, source_target_pairs={{1,0},{0,1},{3,2},{2,3},{5,4},{4,5},{7,6},{6,7},{9,8},{8,9},{11,10... | collective-permute-start | bytes 1572872 | tf_op jit(solution)/shard_map/ppermute | solution.py:361
  63.5 20.9 %collective-permute-start.5 = (bf16[256,1024]{1,0:T(8,128)(2,1)S(1)}, bf16[256,1024]{1,0:T(8,128)(2,1)S(1)}, u32[]{:S(2)}, u32[]{:S(2)}) collective-permute-start(bf16[256,1024]{1,0:T(8,128)(2,1)S(1)} %get-tuple-element.387.x_ref.refs_2_.refs_10_), channel_id=1, source_target_pairs={{1,0},{0,1},{3,2},{2,3},{5,4},{4,5},{7,6},{6,7},{9,8},{8,9},{11,10... | collective-permute-start | bytes 1572872 | tf_op jit(solution)/shard_map/ppermute | solution.py:361
  78.3 17.3 %collective-permute-start.4 = (bf16[256,1024]{1,0:T(8,128)(2,1)S(1)}, bf16[256,1024]{1,0:T(8,128)(2,1)S(1)}, u32[]{:S(2)}, u32[]{:S(2)}) collective-permute-start(bf16[256,1024]{1,0:T(8,128)(2,1)S(1)} %get-tuple-element.336), channel_id=1, source_target_pairs={{0,1},{1,0},{2,3},{3,2},{4,5},{5,4},{6,7},{7,6},{8,9},{9,8},{10,11... | collective-permute-start | bytes 1572872 | tf_op jit(solution)/shard_map/ppermute | solution.py:368
  89.5 17.4 %collective-permute-start.6 = (bf16[256,1024]{1,0:T(8,128)(2,1)S(1)}, bf16[256,1024]{1,0:T(8,128)(2,1)S(1)}, u32[]{:S(2)}, u32[]{:S(2)}) collective-permute-start(bf16[256,1024]{1,0:T(8,128)(2,1)S(1)} %get-tuple-element.338), channel_id=1, source_target_pairs={{0,1},{1,0},{2,3},{3,2},{4,5},{5,4},{6,7},{7,6},{8,9},{9,8},{10,11... | collective-permute-start | bytes 1572872 | tf_op jit(solution)/shard_map/ppermute | solution.py:368
  98.0 20.3 %collective-permute-start.8 = (bf16[256,1024]{1,0:T(8,128)(2,1)S(1)}, bf16[256,1024]{1,0:T(8,128)(2,1)S(1)}, u32[]{:S(2)}, u32[]{:S(2)}) collective-permute-start(bf16[256,1024]{1,0:T(8,128)(2,1)S(1)} %get-tuple-element.399.g_ref.refs_4_.refs_2_), channel_id=1, source_target_pairs={{1,0},{0,1},{3,2},{2,3},{5,4},{4,5},{7,6},{6,7},{9,8},{8,9},{11,10... | collective-permute-start | bytes 1572872 | tf_op jit(solution)/shard_map/ppermute | solution.py:361
  108.0 19.5 %collective-permute-start.7 = (bf16[256,1024]{1,0:T(8,128)(2,1)S(1)}, bf16[256,1024]{1,0:T(8,128)(2,1)S(1)}, u32[]{:S(2)}, u32[]{:S(2)}) collective-permute-start(bf16[256,1024]{1,0:T(8,128)(2,1)S(1)} %get-tuple-element.411.g_ref.refs_6_.refs_2_), channel_id=1, source_target_pairs={{1,0},{0,1},{3,2},{2,3},{5,4},{4,5},{7,6},{6,7},{9,8},{8,9},{11,10... | collective-permute-start | bytes 1572872 | tf_op jit(solution)/shard_map/ppermute | solution.py:361
  146.8 16.0 %collective-permute-start.10 = (bf16[8,128,2048]{2,1,0:T(8,128)(2,1)S(1)}, bf16[8,128,2048]{2,1,0:T(8,128)(2,1)S(1)}, u32[]{:S(2)}, u32[]{:S(2)}) collective-permute-start(bf16[8,128,2048]{2,1,0:T(8,128)(2,1)S(1)} %get-tuple-element.394), channel_id=1, source_target_pairs={{0,2},{2,0},{4,6},{6,4},{8,10},{10,8},{12,14},{14,12},{16,18},{18,... | collective-permute-start | bytes 12582920 | tf_op jit(solution)/shard_map/ppermute | solution.py:403
  146.9 15.0 %collective-permute-start.11 = (bf16[256,1024]{1,0:T(8,128)(2,1)}, bf16[256,1024]{1,0:T(8,128)(2,1)S(1)}, u32[]{:S(2)}, u32[]{:S(2)}) collective-permute-start(bf16[256,1024]{1,0:T(8,128)(2,1)} %copy-done.27), channel_id=1, source_target_pairs={{0,1},{1,0},{2,3},{3,2},{4,5},{5,4},{6,7},{7,6},{8,9},{9,8},{10,11... | collective-permute-start | bytes 1572872 | tf_op jit(solution)/shard_map/ppermute | solution.py:368
  148.4 24.7 %collective-permute-start.9 = (bf16[256,1024]{1,0:T(8,128)(2,1)S(1)}, bf16[256,1024]{1,0:T(8,128)(2,1)S(1)}, u32[]{:S(2)}, u32[]{:S(2)}) collective-permute-start(bf16[256,1024]{1,0:T(8,128)(2,1)S(1)} %copy-done.26), channel_id=1, source_target_pairs={{0,1},{1,0},{2,3},{3,2},{4,5},{5,4},{6,7},{7,6},{8,9},{9,8},{10,11... | collective-permute-start | bytes 1572872 | tf_op jit(solution)/shard_map/ppermute | solution.py:368
  163.6 13.1 %collective-permute-start.13 = (bf16[128,2048]{1,0:T(8,128)(2,1)S(1)}, bf16[128,2048]{1,0:T(8,128)(2,1)S(1)}, u32[]{:S(2)}, u32[]{:S(2)}) collective-permute-start(bf16[128,2048]{1,0:T(8,128)(2,1)S(1)} %ring_add.16), channel_id=1, source_target_pairs={{0,8},{2,10},{8,16},{10,18},{16,24},{18,26},{24,28},{26,30},{28,20... | collective-permute-start | bytes 1572872 | tf_op jit(solution)/shard_map/ppermute | solution.py:400
  165.9 12.8 %collective-permute-start.12 = (bf16[128,2048]{1,0:T(8,128)(2,1)S(1)}, bf16[128,2048]{1,0:T(8,128)(2,1)S(1)}, u32[]{:S(2)}, u32[]{:S(2)}) collective-permute-start(bf16[128,2048]{1,0:T(8,128)(2,1)S(1)} %ring_add.17), channel_id=1, source_target_pairs={{0,4},{2,6},{8,0},{10,2},{16,8},{18,10},{24,16},{26,18},{28,24},{3... | collective-permute-start | bytes 1572872 | tf_op jit(solution)/shard_map/ppermute | solution.py:400
  166.4 20.4 %collective-permute-start.17 = (bf16[256,1024]{1,0:T(8,128)(2,1)S(1)}, bf16[256,1024]{1,0:T(8,128)(2,1)S(1)}, u32[]{:S(2)}, u32[]{:S(2)}) collective-permute-start(bf16[256,1024]{1,0:T(8,128)(2,1)S(1)} %get-tuple-element.522.x_ref.refs_5_), channel_id=1, source_target_pairs={{1,0},{0,1},{3,2},{2,3},{5,4},{4,5},{7,6},{6,7},{9,8},{8,9},{11,10... | collective-permute-start | bytes 1572872 | tf_op jit(solution)/shard_map/ppermute | solution.py:361
  179.5 16.0 %collective-permute-start.19 = (bf16[128,2048]{1,0:T(8,128)(2,1)S(1)}, bf16[128,2048]{1,0:T(8,128)(2,1)S(1)}, u32[]{:S(2)}, u32[]{:S(2)}) collective-permute-start(bf16[128,2048]{1,0:T(8,128)(2,1)S(1)} %ring_add.19), channel_id=1, source_target_pairs={{0,4},{2,6},{8,0},{10,2},{16,8},{18,10},{24,16},{26,18},{28,24},{3... | collective-permute-start | bytes 1572872 | tf_op jit(solution)/shard_map/ppermute | solution.py:400
  180.0 11.6 %collective-permute-start.16 = (bf16[128,2048]{1,0:T(8,128)(2,1)S(1)}, bf16[128,2048]{1,0:T(8,128)(2,1)S(1)}, u32[]{:S(2)}, u32[]{:S(2)}) collective-permute-start(bf16[128,2048]{1,0:T(8,128)(2,1)S(1)} %ring_add.18), channel_id=1, source_target_pairs={{0,8},{2,10},{8,16},{10,18},{16,24},{18,26},{24,28},{26,30},{28,20... | collective-permute-start | bytes 1572872 | tf_op jit(solution)/shard_map/ppermute | solution.py:400
  192.4 15.3 %collective-permute-start.18 = (bf16[128,2048]{1,0:T(8,128)(2,1)S(1)}, bf16[128,2048]{1,0:T(8,128)(2,1)S(1)}, u32[]{:S(2)}, u32[]{:S(2)}) collective-permute-start(bf16[128,2048]{1,0:T(8,128)(2,1)S(1)} %ring_add.20), channel_id=1, source_target_pairs={{0,8},{2,10},{8,16},{10,18},{16,24},{18,26},{24,28},{26,30},{28,20... | collective-permute-start | bytes 1572872 | tf_op jit(solution)/shard_map/ppermute | solution.py:400
  194.0 20.0 %collective-permute-start.14 = (bf16[256,1024]{1,0:T(8,128)(2,1)S(1)}, bf16[256,1024]{1,0:T(8,128)(2,1)S(1)}, u32[]{:S(2)}, u32[]{:S(2)}) collective-permute-start(bf16[256,1024]{1,0:T(8,128)(2,1)S(1)} %get-tuple-element.523.x_ref.refs_7_), channel_id=1, source_target_pairs={{1,0},{0,1},{3,2},{2,3},{5,4},{4,5},{7,6},{6,7},{9,8},{8,9},{11,10... | collective-permute-start | bytes 1572872 | tf_op jit(solution)/shard_map/ppermute | solution.py:361
  196.3 18.3 %collective-permute-start.22 = (bf16[128,2048]{1,0:T(8,128)(2,1)S(1)}, bf16[128,2048]{1,0:T(8,128)(2,1)S(1)}, u32[]{:S(2)}, u32[]{:S(2)}) collective-permute-start(bf16[128,2048]{1,0:T(8,128)(2,1)S(1)} %ring_add.21), channel_id=1, source_target_pairs={{0,4},{2,6},{8,0},{10,2},{16,8},{18,10},{24,16},{26,18},{28,24},{3... | collective-permute-start | bytes 1572872 | tf_op jit(solution)/shard_map/ppermute | solution.py:400
  208.5 9.9 %collective-permute-start.21 = (bf16[128,2048]{1,0:T(8,128)(2,1)S(1)}, bf16[128,2048]{1,0:T(8,128)(2,1)S(1)}, u32[]{:S(2)}, u32[]{:S(2)}) collective-permute-start(bf16[128,2048]{1,0:T(8,128)(2,1)S(1)} %ring_add.22), channel_id=1, source_target_pairs={{0,8},{2,10},{8,16},{10,18},{16,24},{18,26},{24,28},{26,30},{28,20... | collective-permute-start | bytes 1572872 | tf_op jit(solution)/shard_map/ppermute | solution.py:400
  210.1 3.9 %collective-permute-start.15 = (f32[6272]{0:T(1024)S(1)}, f32[6272]{0:T(1024)S(1)}, u32[]{:S(2)}, u32[]{:S(2)}) collective-permute-start(f32[6272]{0:T(1024)S(1)} %constant_dynamic-update-slice_fusion.5), channel_id=1, source_target_pairs={{0,1},{1,0},{2,3},{3,2},{4,5},{5,4},{6,7},{7,6},{8,9},{9,8},{10,11... | collective-permute-start | bytes 75272 | tf_op jit(solution)/shard_map/ppermute | solution.py:608
  214.0 5.5 %collective-permute-start.20 = (f32[8320]{0:T(1024)S(1)}, f32[8320]{0:T(1024)S(1)}, u32[]{:S(2)}, u32[]{:S(2)}) collective-permute-start(f32[8320]{0:T(1024)S(1)} %pad_maximum_fusion.3), channel_id=1, source_target_pairs={{0,2},{2,0},{4,6},{6,4},{8,10},{10,8},{12,14},{14,12},{16,18},{18,... | collective-permute-start | bytes 99848 | tf_op jit(solution)/shard_map/ppermute | solution.py:608
  234.1 8.0 %collective-permute-start.23 = (bf16[8,64,2048]{2,1,0:T(8,128)(2,1)S(1)}, bf16[8,64,2048]{2,1,0:T(8,128)(2,1)S(1)}, u32[]{:S(2)}, u32[]{:S(2)}) collective-permute-start(bf16[8,64,2048]{2,1,0:T(8,128)(2,1)S(1)} %grad_halves.4), channel_id=1, source_target_pairs={{0,2},{2,0},{4,6},{6,4},{8,10},{10,8},{12,14},{14,12},{16,18},{18,... | collective-permute-start | bytes 6291464 | tf_op jit(solution)/shard_map/ppermute | solution.py:403
  234.2 14.3 %collective-permute-start.42 = (bf16[128,2048]{1,0:T(8,128)(2,1)S(1)}, bf16[128,2048]{1,0:T(8,128)(2,1)S(1)}, u32[]{:S(2)}, u32[]{:S(2)}) collective-permute-start(bf16[128,2048]{1,0:T(8,128)(2,1)S(1)} %ring_add.23.refs_4_), channel_id=1, source_target_pairs={{0,4},{2,6},{8,0},{10,2},{16,8},{18,10},{24,16},{26,18},{28,24},{3... | collective-permute-start | bytes 1572872 | tf_op jit(solution)/shard_map/ppermute | solution.py:400
  235.9 14.0 %collective-permute-start.41 = (bf16[128,2048]{1,0:T(8,128)(2,1)S(1)}, bf16[128,2048]{1,0:T(8,128)(2,1)S(1)}, u32[]{:S(2)}, u32[]{:S(2)}) collective-permute-start(bf16[128,2048]{1,0:T(8,128)(2,1)S(1)} %ring_add.23.refs_4_), channel_id=1, source_target_pairs={{0,8},{2,10},{8,16},{10,18},{16,24},{18,26},{24,28},{26,30},{28,20... | collective-permute-start | bytes 1572872 | tf_op jit(solution)/shard_map/ppermute | solution.py:400
  238.3 57.2 %collective-permute-start.26 = (bf16[512,1024]{1,0:T(8,128)(2,1)S(1)}, bf16[512,1024]{1,0:T(8,128)(2,1)S(1)}, u32[]{:S(2)}, u32[]{:S(2)}) collective-permute-start(bf16[512,1024]{1,0:T(8,128)(2,1)S(1)} %product.18), channel_id=1, source_target_pairs={{0,1},{1,0},{2,3},{3,2},{4,5},{5,4},{6,7},{7,6},{8,9},{9,8},{10,11... | collective-permute-start | bytes 3145736 | tf_op jit(solution)/shard_map/ppermute | solution.py:368
  249.9 22.8 %collective-permute-start.43 = (bf16[128,2048]{1,0:T(8,128)(2,1)S(1)}, bf16[128,2048]{1,0:T(8,128)(2,1)S(1)}, u32[]{:S(2)}, u32[]{:S(2)}) collective-permute-start(bf16[128,2048]{1,0:T(8,128)(2,1)S(1)} %collective-permute-done.41.refs_3_), channel_id=1, source_target_pairs={{0,8},{2,10},{8,16},{10,18},{16,24},{18,26},{24,28},{26,30},{28,20... | collective-permute-start | bytes 1572872 | tf_op jit(solution)/shard_map/ppermute | solution.py:400
  250.3 22.4 %collective-permute-start.44 = (bf16[128,2048]{1,0:T(8,128)(2,1)S(1)}, bf16[128,2048]{1,0:T(8,128)(2,1)S(1)}, u32[]{:S(2)}, u32[]{:S(2)}) collective-permute-start(bf16[128,2048]{1,0:T(8,128)(2,1)S(1)} %collective-permute-done.42.refs_5_), channel_id=1, source_target_pairs={{0,4},{2,6},{8,0},{10,2},{16,8},{18,10},{24,16},{26,18},{28,24},{3... | collective-permute-start | bytes 1572872 | tf_op jit(solution)/shard_map/ppermute | solution.py:400
  251.9 16.8 %collective-permute-start.25 = (bf16[64,2048]{1,0:T(8,128)(2,1)S(1)}, bf16[64,2048]{1,0:T(8,128)(2,1)S(1)}, u32[]{:S(2)}, u32[]{:S(2)}) collective-permute-start(bf16[64,2048]{1,0:T(8,128)(2,1)S(1)} %ring_add.24), channel_id=1, source_target_pairs={{0,8},{2,10},{8,16},{10,18},{16,24},{18,26},{24,28},{26,30},{28,20... | collective-permute-start | bytes 786440 | tf_op jit(solution)/shard_map/ppermute | solution.py:400
  252.3 17.5 %collective-permute-start.24 = (bf16[64,2048]{1,0:T(8,128)(2,1)S(1)}, bf16[64,2048]{1,0:T(8,128)(2,1)S(1)}, u32[]{:S(2)}, u32[]{:S(2)}) collective-permute-start(bf16[64,2048]{1,0:T(8,128)(2,1)S(1)} %ring_add.25), channel_id=1, source_target_pairs={{0,4},{2,6},{8,0},{10,2},{16,8},{18,10},{24,16},{26,18},{28,24},{3... | collective-permute-start | bytes 786440 | tf_op jit(solution)/shard_map/ppermute | solution.py:400
  269.3 18.7 %collective-permute-start.28 = (bf16[64,2048]{1,0:T(8,128)(2,1)S(1)}, bf16[64,2048]{1,0:T(8,128)(2,1)S(1)}, u32[]{:S(2)}, u32[]{:S(2)}) collective-permute-start(bf16[64,2048]{1,0:T(8,128)(2,1)S(1)} %ring_add.26), channel_id=1, source_target_pairs={{0,8},{2,10},{8,16},{10,18},{16,24},{18,26},{24,28},{26,30},{28,20... | collective-permute-start | bytes 786440 | tf_op jit(solution)/shard_map/ppermute | solution.py:400
  272.7 27.6 %collective-permute-start.45 = (bf16[128,2048]{1,0:T(8,128)(2,1)S(1)}, bf16[128,2048]{1,0:T(8,128)(2,1)S(1)}, u32[]{:S(2)}, u32[]{:S(2)}) collective-permute-start(bf16[128,2048]{1,0:T(8,128)(2,1)S(1)} %collective-permute-done.43.refs_2_), channel_id=1, source_target_pairs={{0,8},{2,10},{8,16},{10,18},{16,24},{18,26},{24,28},{26,30},{28,20... | collective-permute-start | bytes 1572872 | tf_op jit(solution)/shard_map/ppermute | solution.py:400
  274.3 28.0 %collective-permute-start.46 = (bf16[128,2048]{1,0:T(8,128)(2,1)S(1)}, bf16[128,2048]{1,0:T(8,128)(2,1)S(1)}, u32[]{:S(2)}, u32[]{:S(2)}) collective-permute-start(bf16[128,2048]{1,0:T(8,128)(2,1)S(1)} %collective-permute-done.44.refs_6_), channel_id=1, source_target_pairs={{0,4},{2,6},{8,0},{10,2},{16,8},{18,10},{24,16},{26,18},{28,24},{3... | collective-permute-start | bytes 1572872 | tf_op jit(solution)/shard_map/ppermute | solution.py:400
  274.8 13.3 %collective-permute-start.30 = (f32[8320]{0:T(1024)S(1)}, f32[8320]{0:T(1024)S(1)}, u32[]{:S(2)}, u32[]{:S(2)}) collective-permute-start(f32[8320]{0:T(1024)S(1)} %add.86), channel_id=1, source_target_pairs={{0,4},{2,6},{4,0},{6,2},{8,12},{10,14},{12,8},{14,10},{16,20},{18,... | collective-permute-start | bytes 99848 | tf_op jit(solution)/shard_map/ppermute | solution.py:608
  288.1 4.0 %collective-permute-start.33 = (f32[8320]{0:T(1024)S(1)}, f32[8320]{0:T(1024)S(1)}, u32[]{:S(2)}, u32[]{:S(2)}) collective-permute-start(f32[8320]{0:T(1024)S(1)} %add.89), channel_id=1, source_target_pairs={{0,8},{2,10},{4,12},{6,14},{8,0},{10,2},{12,4},{14,6},{16,24},{18,... | collective-permute-start | bytes 99848 | tf_op jit(solution)/shard_map/ppermute | solution.py:608
  288.1 6.7 %collective-permute-start.27 = (bf16[64,2048]{1,0:T(8,128)(2,1)S(1)}, bf16[64,2048]{1,0:T(8,128)(2,1)S(1)}, u32[]{:S(2)}, u32[]{:S(2)}) collective-permute-start(bf16[64,2048]{1,0:T(8,128)(2,1)S(1)} %ring_add.27), channel_id=1, source_target_pairs={{0,4},{2,6},{8,0},{10,2},{16,8},{18,10},{24,16},{26,18},{28,24},{3... | collective-permute-start | bytes 786440 | tf_op jit(solution)/shard_map/ppermute | solution.py:400
  292.0 6.4 %collective-permute-start.29 = (bf16[64,2048]{1,0:T(8,128)(2,1)S(1)}, bf16[64,2048]{1,0:T(8,128)(2,1)S(1)}, u32[]{:S(2)}, u32[]{:S(2)}) collective-permute-start(bf16[64,2048]{1,0:T(8,128)(2,1)S(1)} %ring_add.28), channel_id=1, source_target_pairs={{0,8},{2,10},{8,16},{10,18},{16,24},{18,26},{24,28},{26,30},{28,20... | collective-permute-start | bytes 786440 | tf_op jit(solution)/shard_map/ppermute | solution.py:400
  294.8 5.4 %collective-permute-start.37 = (f32[1024]{0:T(1024)S(1)}, f32[1024]{0:T(1024)S(1)}, u32[]{:S(2)}, u32[]{:S(2)}) collective-permute-start(f32[1024]{0:T(1024)S(1)} %bitcast.46), channel_id=1, source_target_pairs={{0,2},{2,0},{4,6},{6,4},{8,10},{10,8},{12,14},{14,12},{16,18},{18,... | collective-permute-start | bytes 12296 | tf_op jit(solution)/shard_map/ppermute | solution.py:608
  295.6 16.6 %collective-permute-start.52 = (bf16[128,2048]{1,0:T(8,128)(2,1)S(1)}, bf16[128,2048]{1,0:T(8,128)(2,1)S(1)}, u32[]{:S(2)}, u32[]{:S(2)}) collective-permute-start(bf16[128,2048]{1,0:T(8,128)(2,1)S(1)} %ring_add.23.refs_4_), channel_id=1, source_target_pairs={{0,2},{2,0},{4,6},{6,4},{8,10},{10,8},{12,14},{14,12},{16,18},{18,... | collective-permute-start | bytes 1572872 | tf_op jit(solution)/shard_map/ppermute | solution.py:403
  298.4 5.6 %collective-permute-start.36 = (f32[8320]{0:T(1024)S(1)}, f32[8320]{0:T(1024)S(1)}, u32[]{:S(2)}, u32[]{:S(2)}) collective-permute-start(f32[8320]{0:T(1024)S(1)} %add.90), channel_id=1, source_target_pairs={{0,16},{2,18},{4,20},{6,22},{8,24},{10,26},{12,28},{14,30},{16,0},... | collective-permute-start | bytes 99848 | tf_op jit(solution)/shard_map/ppermute | solution.py:608
  300.2 14.1 %collective-permute-start.51 = (bf16[128,2048]{1,0:T(8,128)(2,1)S(1)}, bf16[128,2048]{1,0:T(8,128)(2,1)S(1)}, u32[]{:S(2)}, u32[]{:S(2)}) collective-permute-start(bf16[128,2048]{1,0:T(8,128)(2,1)S(1)} %collective-permute-done.41.refs_3_), channel_id=1, source_target_pairs={{0,2},{2,0},{4,6},{6,4},{8,10},{10,8},{12,14},{14,12},{16,18},{18,... | collective-permute-start | bytes 1572872 | tf_op jit(solution)/shard_map/ppermute | solution.py:403
  300.3 9.0 %collective-permute-start.32 = (bf16[64,2048]{1,0:T(8,128)(2,1)S(1)}, bf16[64,2048]{1,0:T(8,128)(2,1)S(1)}, u32[]{:S(2)}, u32[]{:S(2)}) collective-permute-start(bf16[64,2048]{1,0:T(8,128)(2,1)S(1)} %ring_add.29), channel_id=1, source_target_pairs={{0,4},{2,6},{8,0},{10,2},{16,8},{18,10},{24,16},{26,18},{28,24},{3... | collective-permute-start | bytes 786440 | tf_op jit(solution)/shard_map/ppermute | solution.py:400
  302.3 9.1 %collective-permute-start.31 = (bf16[64,2048]{1,0:T(8,128)(2,1)S(1)}, bf16[64,2048]{1,0:T(8,128)(2,1)S(1)}, u32[]{:S(2)}, u32[]{:S(2)}) collective-permute-start(bf16[64,2048]{1,0:T(8,128)(2,1)S(1)} %ring_add.30), channel_id=1, source_target_pairs={{0,8},{2,10},{8,16},{10,18},{16,24},{18,26},{24,28},{26,30},{28,20... | collective-permute-start | bytes 786440 | tf_op jit(solution)/shard_map/ppermute | solution.py:400
  304.0 18.2 %collective-permute-start.47 = (bf16[128,2048]{1,0:T(8,128)(2,1)S(1)}, bf16[128,2048]{1,0:T(8,128)(2,1)S(1)}, u32[]{:S(2)}, u32[]{:S(2)}) collective-permute-start(bf16[128,2048]{1,0:T(8,128)(2,1)S(1)} %collective-permute-done.45.refs_1_), channel_id=1, source_target_pairs={{0,8},{2,10},{8,16},{10,18},{16,24},{18,26},{24,28},{26,30},{28,20... | collective-permute-start | bytes 1572872 | tf_op jit(solution)/shard_map/ppermute | solution.py:400
  309.2 14.7 %collective-permute-start.53 = (bf16[128,2048]{1,0:T(8,128)(2,1)S(1)}, bf16[128,2048]{1,0:T(8,128)(2,1)S(1)}, u32[]{:S(2)}, u32[]{:S(2)}) collective-permute-start(bf16[128,2048]{1,0:T(8,128)(2,1)S(1)} %collective-permute-done.42.refs_5_), channel_id=1, source_target_pairs={{0,2},{2,0},{4,6},{6,4},{8,10},{10,8},{12,14},{14,12},{16,18},{18,... | collective-permute-start | bytes 1572872 | tf_op jit(solution)/shard_map/ppermute | solution.py:403
  311.4 14.4 %collective-permute-start.50 = (bf16[128,2048]{1,0:T(8,128)(2,1)S(1)}, bf16[128,2048]{1,0:T(8,128)(2,1)S(1)}, u32[]{:S(2)}, u32[]{:S(2)}) collective-permute-start(bf16[128,2048]{1,0:T(8,128)(2,1)S(1)} %collective-permute-done.43.refs_2_), channel_id=1, source_target_pairs={{0,2},{2,0},{4,6},{6,4},{8,10},{10,8},{12,14},{14,12},{16,18},{18,... | collective-permute-start | bytes 1572872 | tf_op jit(solution)/shard_map/ppermute | solution.py:403
  312.2 14.1 %collective-permute-start.35 = (bf16[64,2048]{1,0:T(8,128)(2,1)S(1)}, bf16[64,2048]{1,0:T(8,128)(2,1)S(1)}, u32[]{:S(2)}, u32[]{:S(2)}) collective-permute-start(bf16[64,2048]{1,0:T(8,128)(2,1)S(1)} %ring_add.31.refs_4_), channel_id=1, source_target_pairs={{0,4},{2,6},{8,0},{10,2},{16,8},{18,10},{24,16},{26,18},{28,24},{3... | collective-permute-start | bytes 786440 | tf_op jit(solution)/shard_map/ppermute | solution.py:400
  314.3 20.6 %collective-permute-start.54 = (bf16[128,2048]{1,0:T(8,128)(2,1)S(1)}, bf16[128,2048]{1,0:T(8,128)(2,1)S(1)}, u32[]{:S(2)}, u32[]{:S(2)}) collective-permute-start(bf16[128,2048]{1,0:T(8,128)(2,1)S(1)} %collective-permute-done.44.refs_6_), channel_id=1, source_target_pairs={{0,2},{2,0},{4,6},{6,4},{8,10},{10,8},{12,14},{14,12},{16,18},{18,... | collective-permute-start | bytes 1572872 | tf_op jit(solution)/shard_map/ppermute | solution.py:403
  322.2 3.6 collective-permute-start.38
  323.9 16.1 %collective-permute-start.49 = (bf16[128,2048]{1,0:T(8,128)(2,1)S(1)}, bf16[128,2048]{1,0:T(8,128)(2,1)S(1)}, u32[]{:S(2)}, u32[]{:S(2)}) collective-permute-start(bf16[128,2048]{1,0:T(8,128)(2,1)S(1)} %collective-permute-done.45.refs_1_), channel_id=1, source_target_pairs={{0,2},{2,0},{4,6},{6,4},{8,10},{10,8},{12,14},{14,12},{16,18},{18,... | collective-permute-start | bytes 1572872 | tf_op jit(solution)/shard_map/ppermute | solution.py:403
  325.8 14.3 %collective-permute-start.55 = (bf16[128,2048]{1,0:T(8,128)(2,1)S(1)}, bf16[128,2048]{1,0:T(8,128)(2,1)S(1)}, u32[]{:S(2)}, u32[]{:S(2)}) collective-permute-start(bf16[128,2048]{1,0:T(8,128)(2,1)S(1)} %collective-permute-done.46.refs_7_), channel_id=1, source_target_pairs={{0,2},{2,0},{4,6},{6,4},{8,10},{10,8},{12,14},{14,12},{16,18},{18,... | collective-permute-start | bytes 1572872 | tf_op jit(solution)/shard_map/ppermute | solution.py:403
  325.8 14.3 %collective-permute-start.48 = (bf16[128,2048]{1,0:T(8,128)(2,1)S(1)}, bf16[128,2048]{1,0:T(8,128)(2,1)S(1)}, u32[]{:S(2)}, u32[]{:S(2)}) collective-permute-start(bf16[128,2048]{1,0:T(8,128)(2,1)S(1)} %collective-permute-done.47.refs_0_), channel_id=1, source_target_pairs={{0,2},{2,0},{4,6},{6,4},{8,10},{10,8},{12,14},{14,12},{16,18},{18,... | collective-permute-start | bytes 1572872 | tf_op jit(solution)/shard_map/ppermute | solution.py:403
  326.3 8.3 %collective-permute-start.34 = (bf16[64,2048]{1,0:T(8,128)(2,1)S(1)}, bf16[64,2048]{1,0:T(8,128)(2,1)S(1)}, u32[]{:S(2)}, u32[]{:S(2)}) collective-permute-start(bf16[64,2048]{1,0:T(8,128)(2,1)S(1)} %ring_add.31.refs_4_), channel_id=1, source_target_pairs={{0,8},{2,10},{8,16},{10,18},{16,24},{18,26},{24,28},{26,30},{28,20... | collective-permute-start | bytes 786440 | tf_op jit(solution)/shard_map/ppermute | solution.py:400
  334.9 12.8 %collective-permute-start.39 = (bf16[64,2048]{1,0:T(8,128)(2,1)S(1)}, bf16[64,2048]{1,0:T(8,128)(2,1)S(1)}, u32[]{:S(2)}, u32[]{:S(2)}) collective-permute-start(bf16[64,2048]{1,0:T(8,128)(2,1)S(1)} %collective-permute-done.34.refs_3_), channel_id=1, source_target_pairs={{0,8},{2,10},{8,16},{10,18},{16,24},{18,26},{24,28},{26,30},{28,20... | collective-permute-start | bytes 786440 | tf_op jit(solution)/shard_map/ppermute | solution.py:400
  338.2 9.5 %collective-permute-start.40 = (bf16[64,2048]{1,0:T(8,128)(2,1)S(1)}, bf16[64,2048]{1,0:T(8,128)(2,1)S(1)}, u32[]{:S(2)}, u32[]{:S(2)}) collective-permute-start(bf16[64,2048]{1,0:T(8,128)(2,1)S(1)} %collective-permute-done.35.refs_5_), channel_id=1, source_target_pairs={{0,4},{2,6},{8,0},{10,2},{16,8},{18,10},{24,16},{26,18},{28,24},{3... | collective-permute-start | bytes 786440 | tf_op jit(solution)/shard_map/ppermute | solution.py:400
  347.7 6.9 %collective-permute-start.57 = (bf16[64,2048]{1,0:T(8,128)(2,1)S(1)}, bf16[64,2048]{1,0:T(8,128)(2,1)S(1)}, u32[]{:S(2)}, u32[]{:S(2)}) collective-permute-start(bf16[64,2048]{1,0:T(8,128)(2,1)S(1)} %collective-permute-done.39.refs_2_), channel_id=1, source_target_pairs={{0,8},{2,10},{8,16},{10,18},{16,24},{18,26},{24,28},{26,30},{28,20... | collective-permute-start | bytes 786440 | tf_op jit(solution)/shard_map/ppermute | solution.py:400
  347.9 6.7 %collective-permute-start.58 = (bf16[64,2048]{1,0:T(8,128)(2,1)S(1)}, bf16[64,2048]{1,0:T(8,128)(2,1)S(1)}, u32[]{:S(2)}, u32[]{:S(2)}) collective-permute-start(bf16[64,2048]{1,0:T(8,128)(2,1)S(1)} %collective-permute-done.40.refs_6_), channel_id=1, source_target_pairs={{0,4},{2,6},{8,0},{10,2},{16,8},{18,10},{24,16},{26,18},{28,24},{3... | collective-permute-start | bytes 786440 | tf_op jit(solution)/shard_map/ppermute | solution.py:400
  349.7 4.6 %collective-permute-start.59 = (f32[1024]{0:T(1024)S(1)}, f32[1024]{0:T(1024)S(1)}, u32[]{:S(2)}, u32[]{:S(2)}) collective-permute-start(f32[1024]{0:T(1024)S(1)} %add.94), channel_id=1, source_target_pairs={{0,16},{2,18},{4,20},{6,22},{8,24},{10,26},{12,28},{14,30},{16,0},... | collective-permute-start | bytes 12296 | tf_op jit(solution)/shard_map/ppermute | solution.py:608
  354.6 6.4 %collective-permute-start.60 = (bf16[64,2048]{1,0:T(8,128)(2,1)S(1)}, bf16[64,2048]{1,0:T(8,128)(2,1)S(1)}, u32[]{:S(2)}, u32[]{:S(2)}) collective-permute-start(bf16[64,2048]{1,0:T(8,128)(2,1)S(1)} %collective-permute-done.57.refs_1_), channel_id=1, source_target_pairs={{0,8},{2,10},{8,16},{10,18},{16,24},{18,26},{24,28},{26,30},{28,20... | collective-permute-start | bytes 786440 | tf_op jit(solution)/shard_map/ppermute | solution.py:400
  355.6 5.4 %collective-permute-start.65 = (bf16[64,2048]{1,0:T(8,128)(2,1)S(1)}, bf16[64,2048]{1,0:T(8,128)(2,1)S(1)}, u32[]{:S(2)}, u32[]{:S(2)}) collective-permute-start(bf16[64,2048]{1,0:T(8,128)(2,1)S(1)} %ring_add.31.refs_4_), channel_id=1, source_target_pairs={{0,2},{2,0},{4,6},{6,4},{8,10},{10,8},{12,14},{14,12},{16,18},{18,... | collective-permute-start | bytes 786440 | tf_op jit(solution)/shard_map/ppermute | solution.py:403
  355.6 5.9 %collective-permute-start.64 = (bf16[64,2048]{1,0:T(8,128)(2,1)S(1)}, bf16[64,2048]{1,0:T(8,128)(2,1)S(1)}, u32[]{:S(2)}, u32[]{:S(2)}) collective-permute-start(bf16[64,2048]{1,0:T(8,128)(2,1)S(1)} %collective-permute-done.34.refs_3_), channel_id=1, source_target_pairs={{0,2},{2,0},{4,6},{6,4},{8,10},{10,8},{12,14},{14,12},{16,18},{18,... | collective-permute-start | bytes 786440 | tf_op jit(solution)/shard_map/ppermute | solution.py:403
  356.1 5.5 %collective-permute-start.66 = (bf16[64,2048]{1,0:T(8,128)(2,1)S(1)}, bf16[64,2048]{1,0:T(8,128)(2,1)S(1)}, u32[]{:S(2)}, u32[]{:S(2)}) collective-permute-start(bf16[64,2048]{1,0:T(8,128)(2,1)S(1)} %collective-permute-done.35.refs_5_), channel_id=1, source_target_pairs={{0,2},{2,0},{4,6},{6,4},{8,10},{10,8},{12,14},{14,12},{16,18},{18,... | collective-permute-start | bytes 786440 | tf_op jit(solution)/shard_map/ppermute | solution.py:403
  357.7 5.4 %collective-permute-start.63 = (bf16[64,2048]{1,0:T(8,128)(2,1)S(1)}, bf16[64,2048]{1,0:T(8,128)(2,1)S(1)}, u32[]{:S(2)}, u32[]{:S(2)}) collective-permute-start(bf16[64,2048]{1,0:T(8,128)(2,1)S(1)} %collective-permute-done.39.refs_2_), channel_id=1, source_target_pairs={{0,2},{2,0},{4,6},{6,4},{8,10},{10,8},{12,14},{14,12},{16,18},{18,... | collective-permute-start | bytes 786440 | tf_op jit(solution)/shard_map/ppermute | solution.py:403
  (41 other events, 343.0 us)

commit v3 on v2

--- a/solution.py
+++ b/solution.py
@@ -402,92 +402,125 @@
     def mate(self, value):
         return lax.ppermute(value, "dp", [(i, i ^ 1) for i in range(self.size)])
 
-    def add(self, table, kept, moved, offset, *more):
+    def add(self, table, kept, moved, offset, part, pair, *more):
         chips, rows, columns = kept.shape
         block = rows // 2 if rows % 32 == 0 else rows
+        steps = rows // block if part is None else 1
 
         def body(table_ref, kept_ref, moved_ref, *refs):
             *refs, out_ref = refs
             total = kept_ref[0].astype(jnp.float32) + moved_ref[0].astype(jnp.float32)
-            for ref in refs:
-                total = total + ref[...].astype(jnp.float32)
+            for ref, (array, half) in zip(refs, more):
+                term = ref[...].astype(jnp.float32)
+                if array.shape[0] < rows and part is None:
+                    term = jnp.where(pl.program_id(0) == half, term, 0.0)
+                total = total + term
             out_ref[...] = total.astype(LOW)
+            if pair is not None and part != 1:
+
+                @pl.when(pl.program_id(0) == 0)
+                def _():
+                    out_ref[0:16, pair:] = two_parts(total[0:8, pair:] + total[8:16, pair:])
 
         shard = pl.BlockSpec(
             (1, block, columns),
-            lambda i, t: (lax.rem(t[PLACE] + offset + 2 * chips, chips), i, 0),
-        )
-        part = pl.BlockSpec((block, columns), lambda i, t: (i, 0))
+            lambda i, t: (lax.rem(t[PLACE] + offset + 2 * chips, chips), i + (part or 0), 0),
+        )
+        each = pl.BlockSpec((block, columns), lambda i, t: (i, 0))
+        fixed = pl.BlockSpec((block, columns), lambda i, t: (0, 0))
         return pl.pallas_call(
             body,
             grid_spec=pltpu.PrefetchScalarGridSpec(
                 num_scalar_prefetch=1,
-                grid=(rows // block,),
-                in_specs=[shard, shard] + [part] * len(more),
-                out_specs=part,
+                grid=(steps,),
+                in_specs=[shard, shard] + [fixed if a.shape[0] < rows else each for a, _ in more],
+                out_specs=each,
             ),
-            out_shape=jax.ShapeDtypeStruct((rows, columns), LOW),
+            out_shape=jax.ShapeDtypeStruct((block * steps, columns), LOW),
             compiler_params=pltpu.CompilerParams(vmem_limit_bytes=8 << 20),
             cost_estimate=COST,
             name="ring_add",
-        )(table, kept, moved, *more)
-
-    def steps(self, order, table, kept, moved, results):
-        def add(offset, *more):
+        )(table, kept, moved, *[a for a, _ in more])
+
+    def steps(self, order, table, kept, moved, results, pair=None):
+        ahead = self.ahead
+        rows = kept.shape[1]
+        split = rows % 32 == 0
+
+        def add(offset, part, *more):
+            halves = [h for _, h in more]
             return order.run(
-                lambda t, k, m, *more: self.add(t, k, m, offset, *more), table, kept, moved, *more
+                lambda t, k, m, *more: self.add(t, k, m, offset, part, pair, *zip(more, halves)),
+                table,
+                kept,
+                moved,
+                *[a for a, _ in more],
             )
 
-        right = add(self.ahead)
-        left = add(-self.behind)
-        for j in range(1, self.ahead + 1):
+        right = add(ahead, 0 if split else None)
+        left = add(-ahead, 1) if split else None
+        for j in range(1, ahead + 1):
             right = self.shift(right, 1)
-            if j <= self.behind:
-                left = self.shift(left, -1)
+            left = None if left is None else self.shift(left, -1)
             yield
-            if j < self.ahead:
-                right = add(self.ahead - j, right)
-            if j < self.behind:
-                left = add(j - self.behind, left)
-        own = add(0, right, left)
-        mine, theirs = {0: own}, {0: self.mate(own)}
+            if j < ahead:
+                right = add(ahead - j, None, (right, 0))
+                left = add(j - ahead, None, *([] if left is None else [(left, 1)]))
+        own = add(0, None, (right, 0), (left, 0))
+        mine, theirs = {0: own}, {0: order.tie(self.mate(own))}
         right = left = own
-        for j in range(1, self.ahead + 1):
+        for j in range(1, ahead + 1):
+            if j == ahead and split:
+                half = rows // 2
+                right, left = order.run(lambda r, l: (r[:half], l[half:]), right, left)
             right = self.shift(right, 1)
-            if j <= self.behind:
-                left = self.shift(left, -1)
+            left = self.shift(left, -1) if j < ahead or split else None
             yield
             right, left = order.tie((right, left))
-            mine[-j], theirs[-j] = right, self.mate(right)
-            if j <= self.behind:
-                mine[j], theirs[j] = left, self.mate(left)
-        yield
-        offsets = range(-self.ahead, self.behind + 1)
-        results += [side[o] for side in (mine, theirs) for o in offsets]
+            mine[-j], mine[j] = right, left
+            theirs[-j] = self.mate(right)
+            theirs[j] = None if left is None else self.mate(left)
+        offsets = range(-ahead, ahead + 1)
+        results += [[side[o] for o in offsets] for side in (mine, theirs)]
 
     def place_pieces(self, table, pieces, outs):
-        shard, columns = pieces[0].shape
         chips, ahead = self.chips, self.ahead
+        size = pieces[0][ahead].shape[0]
+        arrays, places = [], []
+        for side in pieces:
+            entries = []
+            for offset, array in zip(range(-ahead, ahead + 1), side):
+                if array is not None:
+                    first = size - array.shape[0] if offset == ahead else 0
+                    entries.append((offset, len(arrays), first, array.shape[0]))
+                    arrays.append(array)
+            places.append(entries)
 
         def body(table_ref, *refs):
-            piece_refs, out_refs = refs[: 2 * chips], refs[2 * chips :]
-
-            def put(sources):
-                for i, source in enumerate(sources):
-                    slot = lax.rem(table_ref[PLACE] - ahead + i + chips, chips)
+            piece_refs, out_refs = refs[: len(arrays)], refs[len(arrays) :]
+
+            def put(entries):
+                for offset, at, first, count in entries:
+                    slot = lax.rem(table_ref[PLACE] + offset + chips, chips)
                     for ref, (_, moves) in zip(out_refs, outs):
                         for own_rows, own_columns, rows, cut in moves:
-                            ref[0, slot, own_rows, own_columns] = source[rows, cut].astype(
-                                jnp.float32
+                            if isinstance(rows, tuple):
+                                if first == 0:
+                                    both = [piece_refs[at][r, cut].astype(jnp.float32) for r in rows]
+                                    ref[0, slot, own_rows, own_columns] = both[0] + both[1]
+                                continue
+                            low, high = max(rows.start, first), min(rows.stop, first + count)
+                            if low >= high:
+                                continue
+                            there = slice(
+                                own_rows.start + low - rows.start,
+                                own_rows.start + high - rows.start,
                             )
-
-            @pl.when(pl.program_id(0) == 0)
-            def _():
-                put(piece_refs[:chips])
-
-            @pl.when(pl.program_id(0) == 1)
-            def _():
-                put(piece_refs[chips:])
+                            value = piece_refs[at][low - first : high - first, cut]
+                            ref[0, slot, there, own_columns] = value.astype(jnp.float32)
+
+            for i, entries in enumerate(places):
+                pl.when(pl.program_id(0) == i)(functools.partial(put, entries))
 
         def target(i, t):
             return (jnp.where(i == 0, t[CORE], t[MATE]), 0, 0, 0)
@@ -499,23 +532,22 @@
                 num_scalar_prefetch=1,
                 grid=(2,),
                 in_specs=[
-                    pl.BlockSpec(
-                        (shard, columns), lambda i, w: (0, 0), pipeline_mode=pl.Buffered(1)
-                    )
-                ]
-                * (2 * chips),
+                    pl.BlockSpec(a.shape, lambda i, w: (0, 0), pipeline_mode=pl.Buffered(1))
+                    for a in arrays
+                ],
                 out_specs=[pl.BlockSpec((1, *shape), target) for shape in shapes],
             ),
             out_shape=[jax.ShapeDtypeStruct((2, *shape), jnp.float32) for shape in shapes],
-            compiler_params=pltpu.CompilerParams(vmem_limit_bytes=44 << 20),
+            compiler_params=pltpu.CompilerParams(vmem_limit_bytes=40 << 20),
             cost_estimate=COST,
             name="place_pieces",
-        )(table, *pieces)
+        )(table, *arrays)
         return [out.reshape(-1, out.shape[-1]) for out in results]
 
 
 class Share:
     def __init__(self, size, shape, rows, at):
+        self.array = 0
         self.shard = shape[0] // size
         self.columns = shape[1]
         self.moves = []
@@ -536,28 +568,38 @@
             self.end = at + (self.shard // rows) * self.columns
 
 
-def grad_halves(table, cores, chips, rows, shares, sides):
-    columns = shares[-1].end
+def two_parts(values):
+    high = values.astype(LOW)
+    low = (values - high.astype(jnp.float32)).astype(LOW)
+    return jnp.concatenate([high, low], 0)
+
+
+def grad_halves(table, cores, chips, rows, shares, sides, extra=None):
+    count = max(share.array for share in shares) + 1
+    columns = [max(share.end for share in shares if share.array == n) for n in range(count)]
     halves = [share.shard * chips for share in shares]
     steps = min(halves) // 128
     per = chips // steps
-    arrays, where = [], []
+    arrays, where = [] if extra is None else [extra], []
+    at = columns[0]
+    if extra is not None:
+        columns[0] += 128
     for lefts, rights in sides:
         place = []
-        for array, low, count in [*lefts, *rights]:
+        for array, low, size in [*lefts, *rights]:
             known = [n for n, other in enumerate(arrays) if other is array]
             if not known:
                 arrays.append(array)
-            place.append((known[0] if known else len(arrays) - 1, slice(low, low + count)))
+            place.append((known[0] if known else len(arrays) - 1, slice(low, low + size)))
         where.append((place[: len(lefts)], place[len(lefts) :]))
 
     def body(table_ref, *refs):
         refs, out_refs = refs[: len(arrays)], refs[len(arrays) :]
 
         @pl.loop(0, len(cores) * steps)
-        def _(at):
-            n_out = lax.div(at, steps)
-            step = lax.rem(at, steps)
+        def _(turn):
+            n_out = lax.div(turn, steps)
+            step = lax.rem(turn, steps)
             core = table_ref[cores[0]]
             if len(cores) == 2:
                 core = jnp.where(n_out == 0, core, table_ref[cores[1]])
@@ -571,8 +613,17 @@
                     grad = term if grad is None else grad + term
                 grads.append(grad.astype(LOW))
 
-            def put(ref):
+            def put(core_refs):
+                for n in range(per if extra is not None else 0):
+                    row = refs[0][pl.ds(core * chips + step * per + n, 1), :]
+                    lines = [row[:, k * 128 : (k + 1) * 128] for k in range(row.shape[1] // 128)]
+                    block = two_parts(jnp.concatenate(lines, 0))
+                    if rows > 16:
+                        fill = jnp.zeros((rows - 16, 128), LOW)
+                        block = jnp.concatenate([block, fill], 0)
+                    core_refs[0][step * per + n, :, at : at + 128] = block
                 for grad, share in zip(grads, shares):
+                    ref = core_refs[share.array]
                     for n in range(per):
                         for own_rows, own_columns, there, cut in share.moves:
                             first = n * share.shard
@@ -580,48 +631,24 @@
                                 first + own_rows.start : first + own_rows.stop, own_columns
                             ]
 
-            for n, ref in enumerate(out_refs):
-                if len(out_refs) == 1:
-                    put(ref)
+            for n in range(len(cores)):
+                core_refs = out_refs[n * count : (n + 1) * count]
+                if len(cores) == 1:
+                    put(core_refs)
                 else:
-                    pl.when(n_out == n)(functools.partial(put, ref))
+                    pl.when(n_out == n)(functools.partial(put, core_refs))
 
     vmem = pl.BlockSpec(memory_space=pltpu.VMEM)
-    return pl.pallas_call(
+    outs = pl.pallas_call(
         body,
         in_specs=[pl.BlockSpec(memory_space=pltpu.SMEM)] + [vmem] * len(arrays),
-        out_specs=[vmem] * len(cores),
-        out_shape=[jax.ShapeDtypeStruct((chips, rows, columns), LOW)] * len(cores),
-        compiler_params=pltpu.CompilerParams(vmem_limit_bytes=32 << 20),
+        out_specs=[vmem] * (len(cores) * count),
+        out_shape=[jax.ShapeDtypeStruct((chips, rows, c), LOW) for c in columns] * len(cores),
+        compiler_params=pltpu.CompilerParams(vmem_limit_bytes=16 << 20),
         cost_estimate=COST,
         name="grad_halves",
     )(table, *arrays)
-
-
-def add_low(a, b):
-    return (a.astype(jnp.float32) + b.astype(jnp.float32)).astype(LOW)
-
-
-def fold_sum(order, value, axis, count):
-    bit = 1
-    while bit < count:
-        moved = lax.ppermute(value, axis, [(i, i ^ bit) for i in range(count)])
-        yield
-        value = order.run(jnp.add, value, moved)
-        bit *= 2
-    return value
-
-
-def small_total(order, both, dp_only, size, ranks, results):
-    lead = both.shape[0]
-    both = yield from fold_sum(order, both, "tensor", ranks)
-    total = yield from fold_sum(order, jnp.concatenate([both, dp_only]), "dp", size)
-    results += [total[:lead], total[lead:]]
-
-
-def dp_sum(order, value, size, results):
-    total = yield from fold_sum(order, value, "dp", size)
-    results.append(total)
+    return [outs[n] for n in range(len(cores))]
 
 
 def row_kernel(name, body, rows, arrays, vectors, out_types, sum_rows):
@@ -663,28 +690,90 @@
     )(*[a for a, _ in arrays], *vectors)
 
 
-def product(x, low, rows, weights, transposed, out_type):
+def product(x, low, rows, weights, transposed, out_type, into=None, parts=1, part=0):
     inner = x.shape[1]
     outer = weights.shape[0 if transposed else 1]
     tile = min(512, outer)
 
-    def body(x_ref, w_ref, out_ref):
-        out_ref[...] = dot_on(x_ref[...], w_ref[...], 1, 1 if transposed else 0).astype(out_type)
+    def body(x_ref, w_ref, *refs):
+        refs[-1][...] = dot_on(x_ref[...], w_ref[...], 1, 1 if transposed else 0).astype(out_type)
 
     if transposed:
         spec = pl.BlockSpec((tile, inner), lambda i: (i, 0))
     else:
         spec = pl.BlockSpec((inner, tile), lambda i: (0, i))
+    more = [] if into is None else [into]
     return pl.pallas_call(
         body,
         grid=(outer // tile,),
-        in_specs=[pl.BlockSpec((rows, inner), lambda i: (low // rows, 0)), spec],
-        out_specs=pl.BlockSpec((rows, tile), lambda i: (0, i)),
-        out_shape=jax.ShapeDtypeStruct((rows, outer), out_type),
+        in_specs=[pl.BlockSpec((rows, inner), lambda i: (low // rows, 0)), spec]
+        + [pl.BlockSpec(memory_space=pl.ANY)] * len(more),
+        out_specs=pl.BlockSpec((rows, tile), lambda i: (part, i)),
+        out_shape=jax.ShapeDtypeStruct((rows * parts, outer), out_type),
+        input_output_aliases={2: 0} if more else {},
         compiler_params=pltpu.CompilerParams(vmem_limit_bytes=10 << 20),
         cost_estimate=COST,
         name="product",
-    )(x, weights)
+    )(x, weights, *more)
+
+
+def sum_kernel(one, two, squares):
+    flat = [*one, *two, *squares]
+    width = one[0].shape[1]
+
+    def body(*refs):
+        *refs, out_ref = refs
+
+        def total(count):
+            nonlocal refs
+            mine, refs = refs[:count], refs[count:]
+            return functools.reduce(jnp.add, [r[...] for r in mine])
+
+        first, second, third = (total(len(g)) for g in (one, two, squares))
+        lane = lax.broadcasted_iota(jnp.int32, (1, width), 1)
+        row = jnp.zeros((1, width), jnp.float32)
+        for n, source in enumerate((third[0:1], third[1:2], second[3:4])):
+            row = jnp.where(lane == n, jnp.sum(source, 1, keepdims=True), row)
+        out_ref[...] = jnp.concatenate([first[0:3], second[0:3], row, jnp.zeros_like(row)], 0)
+
+    vmem = pl.BlockSpec(memory_space=pltpu.VMEM)
+    return pl.pallas_call(
+        body,
+        in_specs=[vmem] * len(flat),
+        out_specs=vmem,
+        out_shape=jax.ShapeDtypeStruct((8, width), jnp.float32),
+        compiler_params=pltpu.CompilerParams(vmem_limit_bytes=4 << 20),
+        cost_estimate=COST,
+        name="sum_kernel",
+    )(*flat)
+
+
+def row_values(size, norms, up_sums, biases):
+    width = norms[0].shape[1]
+    up_rows = -(-up_sums[0].shape[1] // width)
+    flat = [*norms, *up_sums, biases]
+
+    def body(*refs):
+        *refs, out_ref = refs
+        out_ref[...] = jnp.zeros_like(out_ref)
+        out_ref[0:8, :] = functools.reduce(jnp.add, [r[...] for r in refs[: len(norms)]])
+        ups = functools.reduce(jnp.add, [r[...] for r in refs[len(norms) : -1]])
+        for n in range(up_rows):
+            part = ups[:, n * width : (n + 1) * width]
+            out_ref[8 + n : 9 + n, 0 : part.shape[1]] = part
+        bias = refs[-1][0:1]
+        out_ref[8 + up_rows : 9 + up_rows, 0 : bias.shape[1]] = bias
+
+    vmem = pl.BlockSpec(memory_space=pltpu.VMEM)
+    return pl.pallas_call(
+        body,
+        in_specs=[vmem] * len(flat),
+        out_specs=vmem,
+        out_shape=jax.ShapeDtypeStruct((size, width), jnp.float32),
+        compiler_params=pltpu.CompilerParams(vmem_limit_bytes=4 << 20),
+        cost_estimate=COST,
+        name="row_values",
+    )(*flat)
 
 
 def ffn_forward(x, up_w, up_b, down_w, out_type):
@@ -729,11 +818,12 @@
     tile = min(512, units)
     steps = units // tile
 
-    def body(g_ref, slope_ref, down_ref, up_ref, dup_ref, out_ref, acc_ref):
+    def body(g_ref, slope_ref, down_ref, up_ref, dup_ref, sum_ref, out_ref, acc_ref):
         step = pl.program_id(0)
         dact = dot_on(g_ref[...], down_ref[...], 1, 1)
         dup = (dact * slope_ref[...].astype(jnp.float32)).astype(LOW)
         dup_ref[...] = dup
+        sum_ref[...] = jnp.sum(dup.astype(jnp.float32), 0, keepdims=True)
         accumulate(step, steps, dot_on(dup, up_ref[...], 1, 1), acc_ref, out_ref)
 
     part = pl.BlockSpec((rows, tile), lambda i: (0, i))
@@ -747,9 +837,10 @@
             pl.BlockSpec((tile, width), lambda i: (i, 0)),
             pl.BlockSpec((width, tile), lambda i: (0, i)),
         ],
-        out_specs=[part, whole],
+        out_specs=[part, pl.BlockSpec((1, tile), lambda i: (0, i)), whole],
         out_shape=[
             jax.ShapeDtypeStruct((rows, units), LOW),
+            jax.ShapeDtypeStruct((1, units), jnp.float32),
             jax.ShapeDtypeStruct((rows, width), out_type),
         ],
         scratch_shapes=[pltpu.VMEM((rows, width), jnp.float32)],
@@ -978,20 +1069,22 @@
         sums2.append(sums)
         dmlp.append([low] + fetch(low, ranks))
 
-    dups, dhid_moved, dhid_own = [], [], []
+    dups, dhid_moved, dhid_own, up_sums = [], [], [], []
     for c in every:
-        dup, own = run(
+        dup, total, own = run(
             lambda d, s: ffn_back(d, s, down_w, up_w, jnp.float32), dmlp[c][0], slopes[c][0]
         )
         dups.append([dup])
+        up_sums.append(total)
         dhid_own.append(own)
     for c in every:
         shares = []
         for j in others:
-            dup, share = run(
+            dup, total, share = run(
                 lambda d, s: ffn_back(d, s, down_w, up_w, LOW), dmlp[c][j], slopes[c][j]
             )
             dups[c].append(dup)
+            up_sums.append(total)
             shares.append(share)
         dhid_moved.append(hand_over(shares, ranks))
 
@@ -1003,29 +1096,25 @@
                 if next(entry[1], "end") == "end":
                     under_way.remove(entry)
 
-    def begin(name, rows, shares, sides, between):
-        results = []
-        leaves, tree = jax.tree.flatten(sides)
-        arrays = list({id(x): x for x in leaves if not isinstance(x, int)}.values())
-
-        def halves(*cores):
-            def call(*tied):
-                known = {id(x): t for x, t in zip(arrays, tied)}
-                found = [x if isinstance(x, int) else known[id(x)] for x in leaves]
-                sides = jax.tree.unflatten(tree, found)
-                return grad_halves(table, cores, ring.chips, rows, shares, sides)
-
-            return run(call, *arrays)
-
-        if between is None:
-            given, kept = halves(MATE, CORE)
-            moved = ring.mate(given)
-        else:
-            moved = ring.mate(halves(MATE)[0])
-            between()
-            (kept,) = halves(CORE)
-        under_way.append((name, ring.steps(order, table, kept, moved, results)))
-        return results
+    class Grads:
+        def __init__(self, rows, shares, sides, extra=None):
+            self.rows, self.shares, self.extra = rows, shares, extra
+            self.leaves, self.tree = jax.tree.flatten(sides)
+            leaves = [x for x in self.leaves if not isinstance(x, int)]
+            self.arrays = list({id(x): x for x in leaves}.values())
+            self.results = []
+
+        def halves(self, *cores):
+            def call(t, extra, *tied):
+                known = {id(x): v for x, v in zip(self.arrays, tied)}
+                found = [x if isinstance(x, int) else known[id(x)] for x in self.leaves]
+                sides = jax.tree.unflatten(self.tree, found)
+                return grad_halves(t, cores, ring.chips, self.rows, self.shares, sides, extra)
+
+            return run(call, table, self.extra, *self.arrays)
+
+        def ring(self, name, kept, moved, pair=None):
+            under_way.append((name, ring.steps(order, table, kept, moved, self.results, pair)))
 
     def pieces_of(parts):
         return [(p, 0, piece) for part in parts for p in part]
@@ -1033,16 +1122,12 @@
     ffn_rows = hidden_units // dp_size
     down_share = Share(dp_size, (hidden_units, width), ffn_rows, 0)
     up_share = Share(dp_size, (width, hidden_units), ffn_rows, down_share.end)
-    ffn = begin(
-        "ffn",
+    ffn = Grads(
         ffn_rows,
         [down_share, up_share],
-        [
-            (pieces_of(acts), pieces_of(dmlp)),
-            (pieces_of(x), pieces_of(dups)),
-        ],
-        None,
+        [(pieces_of(acts), pieces_of(dmlp)), (pieces_of(x), pieces_of(dups))],
     )
+    ffn_given, ffn_kept = ffn.halves(MATE, CORE)
 
     def norm_one_back(own, d2, n, i, *moved):
         def body(*values):
@@ -1068,34 +1153,26 @@
         )
         sums1.append(sums)
         dattn.append([low] + fetch(low, ranks))
-        advance("ffn")
+    ffn_moved = ring.mate(tie(ffn_given))
     for c in every:
-        dcontexts.append(run(lambda d: product(d, 0, piece, out_w, True, LOW), dattn[c][0]))
-    grad_up_b = run(
-        lambda *d: functools.reduce(jnp.add, [column_sums(p) for p in d]),
-        *[p for part in dups for p in part],
-    )
-
-    def gather_sums(squares, one, two):
-        one, two, squares = sum(one), sum(two), sum(squares)
-        scalars = jnp.stack([jnp.sum(squares[0]), jnp.sum(squares[1]), jnp.sum(two[3])])
-        rows = [one[i] for i in range(3)] + [two[i] for i in range(3)]
-        return jnp.concatenate(rows + [jnp.pad(scalars, (0, 125))])
-
-    small = []
-    both = run(gather_sums, squares, sums1, sums2)
-    under_way.append(("small", small_total(order, both, grad_up_b, dp_size, ranks, small)))
+        dcontexts.append(
+            run(lambda d: product(d, 0, piece, out_w, True, LOW, None, ranks, 0), dattn[c][0])
+        )
+    norms = run(sum_kernel, sums1, sums2, squares)
+    norms = [norms] + fetch(norms, ranks)
+    ffn.ring("ffn", ffn_kept, ffn_moved)
+    advance("ffn")
 
     dq_parts, sums = [], []
     for c in every:
-        dcontext = run(
-            lambda near, *far: jnp.concatenate(
-                [near] + [product(d, 0, piece, out_w, True, LOW) for d in far], 0
-            ),
-            dcontexts[c],
-            *dattn[c][1:],
-        )
-        advance("ffn", "small")
+        dcontext = dcontexts[c]
+        for j in others:
+            dcontext = run(
+                lambda d, whole: product(d, 0, piece, out_w, True, LOW, whole, ranks, j),
+                dattn[c][j],
+                dcontext,
+            )
+        advance("ffn")
         dq, *sums = run(
             lambda v, d, l, e, s: jax.tree.leaves(
                 attend_back(v, d, l, random_ids, table, e, s, c, chunks, ranks)
@@ -1107,8 +1184,6 @@
             sums,
         )
         dq_parts.append(dq)
-        if c < chunks - 1:
-            advance("ffn", "small")
     dqkv, bias_sums = dq, sums[0]
 
     attn_rows = width // dp_size
@@ -1128,24 +1203,21 @@
                 [(dattn[c][j], 0, piece) for c in every for j in range(ranks)],
             )
         )
-    dinput_moved = []
-
-    def send_dinput():
-        shares = [
-            run(lambda d: product(d, j * own_rows, own_rows, qkv_w, True, LOW), dqkv)
-            for j in others
-        ]
-        dinput_moved.extend(hand_over(shares, ranks))
-
-    attn = begin("attn", attn_rows, attn_shares, attn_sides, send_dinput)
-    qkv_b_sums = []
-    advance("attn", "ffn")
-    under_way.append(
-        ("qkv_b", dp_sum(order, bias_sums[0], dp_size, qkv_b_sums))
-    )
+    values = run(functools.partial(row_values, dp_size), norms, up_sums, bias_sums)
+    pair = attn_shares[-1].end
+    attn = Grads(attn_rows, attn_shares, attn_sides, values)
+    (given,) = attn.halves(MATE)
+    advance("ffn")
+    moved = ring.mate(tie(given))
+    shares = [
+        run(lambda d: product(d, j * own_rows, own_rows, qkv_w, True, LOW), dqkv) for j in others
+    ]
+    dinput_moved = hand_over(shares, ranks)
+    (kept,) = attn.halves(CORE)
+    attn.ring("attn", kept, moved, pair)
     advance("attn")
     dinput_own = run(lambda d: product(d, 0, own_rows, qkv_w, True, jnp.float32), dqkv)
-    advance("ffn", "attn", "qkv_b")
+    advance("ffn", "attn")
     grad_input = run(
         lambda own, d, *m: (plus(own, m) + jnp.concatenate(d, 0)).astype(LOW),
         dinput_own,
@@ -1154,19 +1226,24 @@
     )
     totals = {}
     entries = float(own_rows * ranks * dp_size * seqs_here * width)
-
-    def spread(both):
-        vectors = [both[i * width : (i + 1) * width] for i in range(6)]
-        return vectors, jnp.sqrt(both[6 * width : 6 * width + 3] / entries)
-
     ffn_outs = [((g.shard, g.columns), g.moves) for g in (down_share, up_share)]
+    up_rows = -(-hidden_units // width)
+
+    def spread(value):
+        value = value.reshape(dp_size, width)
+        return (
+            [value[i] for i in range(6)],
+            jnp.sqrt(value[6, :3] / entries),
+            value[8 + up_rows, :channels],
+            value[8 + up_rows, channels : 2 * channels],
+            value[8 : 8 + up_rows].reshape(-1)[:hidden_units],
+        )
+
     while under_way:
         advance()
         names = {n for n, _ in under_way}
         if "ffn" not in names and "ffn" not in totals:
-            totals["ffn"] = run(lambda *p: ring.place_pieces(table, p, ffn_outs), *ffn)
-        if "small" not in names and "small" not in totals:
-            totals["small"] = run(spread, small[0])
+            totals["ffn"] = run(lambda *p: ring.place_pieces(table, p, ffn_outs), *ffn.results)
     everything = slice(0, attn_rows)
     attn_outs = []
     for i in range(3):
@@ -1174,9 +1251,13 @@
         attn_outs.append(
             ((attn_rows, channels), [(everything, slice(0, channels), everything, cut)])
         )
+    lines = slice(0, 8)
+    attn_outs.append(
+        ((8, 128), [(lines, slice(0, 128), (lines, slice(8, 16)), slice(pair, pair + 128))])
+    )
     if with_out:
         attn_outs.append(((attn_shares[1].shard, width), attn_shares[1].moves))
-    grad_q, grad_k, grad_v, *rest = run(lambda *p: ring.place_pieces(table, p, attn_outs), *attn)
+    grad_q, grad_k, grad_v, value, *rest = run(lambda *p: ring.place_pieces(table, p, attn_outs), *attn.results)
     if with_out:
         (grad_out_w,) = rest
     else:
@@ -1185,8 +1266,7 @@
         )
         grad_out_w = lax.psum(partial.astype(LOW), "dp").astype(jnp.float32)
     grad_down_w, grad_up_w = totals["ffn"]
-    vectors, rms_stats = totals["small"]
-    biases = [qkv_b_sums[0][:channels], qkv_b_sums[0][channels:], small[1]]
+    vectors, rms_stats, *biases = spread(value)
     shape = hidden_in.shape
     return (
         jnp.concatenate(layer_out, 0).reshape(shape),

time: 372 us -> 340 us (0.914)
  waiting for transfers between devices: 155 us -> 131 us
  local copies, waits for them, and re-layouts: 11.3 us -> 5.64 us
  Pallas kernels: 127 us -> 131 us
    ppermute x9 -> x0, waiting for transfers between devices: 26.1 us -> none  [fold_sum(): moved = lax.ppermute(value, axis, [(i, i ^ bit) for i in range(count)])]
    ppermute x7, waiting for transfers between devices: 37.1 us -> 20.5 us  [hand_over(): lax.ppermute(share, 'tensor', [(k, (k + s) % ranks) for k in range(ranks)])]
    ppermute x28 -> x32, waiting for transfers between devices: 61.9 us -> 70.9 us  [shift(): return lax.ppermute(value, 'dp', pairs)]
    ppermute x18 -> x20, waiting for transfers between devices: 0.45 us -> 6.8 us  [mate(): return lax.ppermute(value, 'dp', [(i, i ^ 1) for i in range(self.size)])]
    ppermute x9 -> x0, starting transfers between devices: 5.39 us -> none  [fold_sum(): moved = lax.ppermute(value, axis, [(i, i ^ bit) for i in range(count)])]
    unnamed x81 -> x32, local copies, waits for them, and re-layouts: 9.27 us -> 4.17 us
    ppermute x7 -> x8, waiting for transfers between devices: 29.2 us -> 32.9 us  [fetch(): lax.ppermute(rows, 'tensor', [((k + s) % ranks, k) for k in range(ranks)])]
    ppermute x28 -> x32, starting transfers between devices: 30.2 us -> 33.4 us  [shift(): return lax.ppermute(value, 'dp', pairs)]
  transfers between devices with their start and end apart: 69 -> 67, of which waited for: 32 -> 28; matrix products, arithmetic and copies ran while one was open for 4% -> 3% of each run, Pallas kernels for 23% -> 35%
where the time goes in v3:
time: 340 us; the launch traced here: 337 us
  waiting for transfers between devices  131 us (39%)
  Pallas kernels  131 us (39%)
  starting transfers between devices  59.7 us (18%)
  local copies, waits for them, and re-layouts  5.64 us (2%)
  other arithmetic  4.12 us (1%)
  matrix products  3.58 us (1%)
    ppermute x32, waiting for transfers between devices, shift(): return lax.ppermute(value, 'dp', pairs)  70.9 us
    ppermute x32, starting transfers between devices, shift(): return lax.ppermute(value, 'dp', pairs)  33.4 us
    ppermute x8, waiting for transfers between devices, fetch(): lax.ppermute(rows, 'tensor', [((k + s) % ranks, k) for k in range(ranks)])  32.9 us
    pallas_call x2, Pallas kernels, attend_back(): pl.pallas_call(functools.partial(attend_back_kernel, plan, 3, len(earlier...  22.4 us
    ppermute x7, waiting for transfers between devices, hand_over(): lax.ppermute(share, 'tensor', [(k, (k + s) % ranks) for k in range(ranks)])  20.5 us
    pallas_call x4, Pallas kernels, ffn_forward(): pl.pallas_call(body, grid=(steps,), in_specs=[whole, pl.BlockSpec((width,...  20.2 us
    pallas_call x3, Pallas kernels, grad_halves(): pl.pallas_call(body, in_specs=[pl.BlockSpec(memory_space=pltpu.SMEM)] + [...  20.1 us
    pallas_call x4, Pallas kernels, ffn_back(): pl.pallas_call(body, grid=(steps,), in_specs=[whole, part, pl.BlockSpec((...  17 us
  transfers between devices with their start and end apart: 67, of which 28 were waited for; matrix products, arithmetic and copies ran while one was open for 3% of the time, Pallas kernels for 35%

profile of v3, /device:TPU:0, one launch (start us, length us, event | category | flops | bytes accessed | tf_op | source)
XLA Modules:
  0.0 336.7 jit_solution(7582225389969943785)
XLA Ops:
  0.7 3.0 collective-permute-start
  8.1 1.8 fusion
  9.9 17.1 %collective-permute-done.refs_2_ = bf16[512,1024]{1,0:T(8,128)(2,1)S(1)} collective-permute-done((bf16[512,1024]{1,0:T(8,128)(2,1)}, bf16[512,1024]{1,0:T(8,128)(2,1)S(1)}, u32[]{:S(2)}, u32[]{:S(2)}) %collective-permute-start) | collective-permute-done | bytes 1048608 | tf_op jit(solution)/shard_map/ppermute | solution.py:361
  27.0 1.8 fusion.1
  29.1 5.8 %attend.2 = (bf16[512,512]{1,0:T(8,128)(2,1)S(1)}, f32[2,8,256]{2,1,0:T(8,128)S(1)}) custom-call(s32[4]{0:T(128)S(1)} %pad_add_fusion.table_ref, s32[8,42]{1,0:T(8,128)S(1)} %copy.40.rb_ref, bf16[1024,1536]{1,0:T(8,128)(2,1)S(1)} %pad_maximum_fusion.q_ref.k_ref.v_ref, bf16[1024,1536]{1,0:T(8,128)(2,1)S(1)} %pad_maximum_fusion.q_ref.k_ref.v_ref, ...), custom_call_target="tpu_custom_call" | custom-call | flops 1024 | bytes 1024 | tf_op jit(solution)/shard_map/attend/pallas_call | solution.py:281
  35.7 1.8 collective-permute-start.1
  37.5 5.6 %attend.3 = (bf16[512,512]{1,0:T(8,128)(2,1)S(1)}, f32[2,8,256]{2,1,0:T(8,128)S(1)}) custom-call(s32[4]{0:T(128)S(1)} %pad_add_fusion.table_ref, s32[8,42]{1,0:T(8,128)S(1)} %copy.40.rb_ref, bf16[1024,1536]{1,0:T(8,128)(2,1)S(1)} %pad_maximum_fusion.q_ref.k_ref.v_ref, bf16[1024,1536]{1,0:T(8,128)(2,1)S(1)} %pad_maximum_fusion.q_ref.k_ref.v_ref, ...), custom_call_target="tpu_custom_call" | custom-call | flops 1024 | bytes 1024 | tf_op jit(solution)/shard_map/attend/pallas_call | solution.py:281
  45.9 4.7 %collective-permute-done.1.refs_1_ = bf16[256,1024]{1,0:T(8,128)(2,1)S(1)} collective-permute-done((bf16[256,1024]{1,0:T(8,128)(2,1)S(1)}, bf16[256,1024]{1,0:T(8,128)(2,1)S(1)}, u32[]{:S(2)}, u32[]{:S(2)}) %collective-permute-start.1) | collective-permute-done | bytes 524320 | tf_op jit(solution)/shard_map/ppermute | solution.py:368
  51.4 1.8 collective-permute-start.2
  53.2 5.0 %ffn_forward.4 = (bf16[256,2048]{1,0:T(8,128)(2,1)S(1)}, bf16[256,2048]{1,0:T(8,128)(2,1)S(1)}, f32[256,1024]{1,0:T(8,128)S(1)}) custom-call(bf16[256,1024]{1,0:T(8,128)(2,1)S(1)} %get-tuple-element.410.x_ref.refs_2_.refs_8_, bf16[1024,2048]{1,0:T(8,128)(2,1)S(1)} %copy-done, bf16[1,2048]{1,0:T(2,128)(2,1)S(1)} %reshape.103.b_ref, ...), custom_call_target="tpu_custom_call" | custom-call | flops 1024 | bytes 1024 | tf_op jit(solution)/shard_map/ffn_forward/pallas_call | solution.py:796
  58.2 3.6 %collective-permute-done.3.refs_1_ = bf16[256,1024]{1,0:T(8,128)(2,1)S(1)} collective-permute-done((bf16[256,1024]{1,0:T(8,128)(2,1)S(1)}, bf16[256,1024]{1,0:T(8,128)(2,1)S(1)}, u32[]{:S(2)}, u32[]{:S(2)}) %collective-permute-start.3) | collective-permute-done | bytes 524320 | tf_op jit(solution)/shard_map/ppermute | solution.py:368
  62.6 1.8 collective-permute-start.5
  64.4 5.0 %ffn_forward.5 = (bf16[256,2048]{1,0:T(8,128)(2,1)S(1)}, bf16[256,2048]{1,0:T(8,128)(2,1)S(1)}, f32[256,1024]{1,0:T(8,128)S(1)}) custom-call(bf16[256,1024]{1,0:T(8,128)(2,1)S(1)} %get-tuple-element.412.x_ref.refs_2_.refs_10_, bf16[1024,2048]{1,0:T(8,128)(2,1)S(1)} %copy-done, bf16[1,2048]{1,0:T(2,128)(2,1)S(1)} %reshape.103.b_ref, ...), custom_call_target="tpu_custom_call" | custom-call | flops 1024 | bytes 1024 | tf_op jit(solution)/shard_map/ffn_forward/pallas_call | solution.py:796
  69.5 3.6 %collective-permute-done.2.x_ref.refs_9_ = bf16[256,1024]{1,0:T(8,128)(2,1)S(1)} collective-permute-done((bf16[256,1024]{1,0:T(8,128)(2,1)S(1)}, bf16[256,1024]{1,0:T(8,128)(2,1)S(1)}, u32[]{:S(2)}, u32[]{:S(2)}) %collective-permute-start.2) | collective-permute-done | bytes 524320 | tf_op jit(solution)/shard_map/ppermute | solution.py:361
  73.1 5.1 %ffn_forward.6 = (bf16[256,2048]{1,0:T(8,128)(2,1)S(1)}, bf16[256,2048]{1,0:T(8,128)(2,1)S(1)}, bf16[256,1024]{1,0:T(8,128)(2,1)S(1)}) custom-call(bf16[256,1024]{1,0:T(8,128)(2,1)S(1)} %collective-permute-done.2.x_ref.refs_9_, bf16[1024,2048]{1,0:T(8,128)(2,1)S(1)} %copy-done, bf16[1,2048]{1,0:T(2,128)(2,1)S(1)} %reshape.103.b_ref, ...), custom_call_target="tpu_custom_call" | custom-call | flops 1024 | bytes 1024 | tf_op jit(solution)/shard_map/ffn_forward/pallas_call | solution.py:796
  78.2 1.8 collective-permute-start.4
  80.0 4.3 %collective-permute-done.5.x_ref.refs_11_ = bf16[256,1024]{1,0:T(8,128)(2,1)S(1)} collective-permute-done((bf16[256,1024]{1,0:T(8,128)(2,1)S(1)}, bf16[256,1024]{1,0:T(8,128)(2,1)S(1)}, u32[]{:S(2)}, u32[]{:S(2)}) %collective-permute-start.5) | collective-permute-done | bytes 524320 | tf_op jit(solution)/shard_map/ppermute | solution.py:361
  84.3 5.1 %ffn_forward.7 = (bf16[256,2048]{1,0:T(8,128)(2,1)S(1)}, bf16[256,2048]{1,0:T(8,128)(2,1)S(1)}, bf16[256,1024]{1,0:T(8,128)(2,1)S(1)}) custom-call(bf16[256,1024]{1,0:T(8,128)(2,1)S(1)} %collective-permute-done.5.x_ref.refs_11_, bf16[1024,2048]{1,0:T(8,128)(2,1)S(1)} %copy-done, bf16[1,2048]{1,0:T(2,128)(2,1)S(1)} %reshape.103.b_ref, ...), custom_call_target="tpu_custom_call" | custom-call | flops 1024 | bytes 1024 | tf_op jit(solution)/shard_map/ffn_forward/pallas_call | solution.py:796
  89.4 1.8 collective-permute-start.6
  91.2 4.3 %collective-permute-done.4.refs_1_ = bf16[256,1024]{1,0:T(8,128)(2,1)S(1)} collective-permute-done((bf16[256,1024]{1,0:T(8,128)(2,1)S(1)}, bf16[256,1024]{1,0:T(8,128)(2,1)S(1)}, u32[]{:S(2)}, u32[]{:S(2)}) %collective-permute-start.4) | collective-permute-done | bytes 524320 | tf_op jit(solution)/shard_map/ppermute | solution.py:368
  95.5 1.6 norm_two.2
  97.1 1.8 collective-permute-start.8
  98.9 7.9 %collective-permute-done.6.refs_1_ = bf16[256,1024]{1,0:T(8,128)(2,1)S(1)} collective-permute-done((bf16[256,1024]{1,0:T(8,128)(2,1)S(1)}, bf16[256,1024]{1,0:T(8,128)(2,1)S(1)}, u32[]{:S(2)}, u32[]{:S(2)}) %collective-permute-start.6) | collective-permute-done | bytes 524320 | tf_op jit(solution)/shard_map/ppermute | solution.py:368
  108.0 1.8 collective-permute-start.7
  109.8 4.3 %ffn_back.4 = (bf16[256,2048]{1,0:T(8,128)(2,1)S(1)}, f32[1,2048]{1,0:T(1,128)S(1)}, f32[256,1024]{1,0:T(8,128)S(1)}) custom-call(bf16[256,1024]{1,0:T(8,128)(2,1)S(1)} %get-tuple-element.421.g_ref.refs_4_.refs_2_, bf16[256,2048]{1,0:T(8,128)(2,1)S(1)} %get-tuple-element.372.slope_ref, bf16[2048,1024]{1,0:T(8,128)(2,1)S(1)} %copy-done.1, ...), custom_call_target="tpu_custom_call" | custom-call | flops 1024 | bytes 1024 | tf_op jit(solution)/shard_map/ffn_back/pallas_call | solution.py:831
  114.0 4.3 %ffn_back.5 = (bf16[256,2048]{1,0:T(8,128)(2,1)S(1)}, f32[1,2048]{1,0:T(1,128)S(1)}, f32[256,1024]{1,0:T(8,128)S(1)}) custom-call(bf16[256,1024]{1,0:T(8,128)(2,1)S(1)} %get-tuple-element.427.g_ref.refs_6_.refs_2_, bf16[256,2048]{1,0:T(8,128)(2,1)S(1)} %get-tuple-element.375.slope_ref, bf16[2048,1024]{1,0:T(8,128)(2,1)S(1)} %copy-done.1, ...), custom_call_target="tpu_custom_call" | custom-call | flops 1024 | bytes 1024 | tf_op jit(solution)/shard_map/ffn_back/pallas_call | solution.py:831
  118.3 4.2 %ffn_back.6 = (bf16[256,2048]{1,0:T(8,128)(2,1)S(1)}, f32[1,2048]{1,0:T(1,128)S(1)}, bf16[256,1024]{1,0:T(8,128)(2,1)S(1)}) custom-call(bf16[256,1024]{1,0:T(8,128)(2,1)S(1)} %collective-permute-done.8.g_ref.refs_5_, bf16[256,2048]{1,0:T(8,128)(2,1)S(1)} %get-tuple-element.383.slope_ref, bf16[2048,1024]{1,0:T(8,128)(2,1)S(1)} %copy-done.1, ...), custom_call_target="tpu_custom_call" | custom-call | flops 1024 | bytes 1024 | tf_op jit(solution)/shard_map/ffn_back/pallas_call | solution.py:831
  124.1 5.2 %collective-permute-done.7.g_ref.refs_7_ = bf16[256,1024]{1,0:T(8,128)(2,1)S(1)} collective-permute-done((bf16[256,1024]{1,0:T(8,128)(2,1)S(1)}, bf16[256,1024]{1,0:T(8,128)(2,1)S(1)}, u32[]{:S(2)}, u32[]{:S(2)}) %collective-permute-start.7) | collective-permute-done | bytes 524320 | tf_op jit(solution)/shard_map/ppermute | solution.py:361
  129.2 4.2 %ffn_back.7 = (bf16[256,2048]{1,0:T(8,128)(2,1)S(1)}, f32[1,2048]{1,0:T(1,128)S(1)}, bf16[256,1024]{1,0:T(8,128)(2,1)S(1)}) custom-call(bf16[256,1024]{1,0:T(8,128)(2,1)S(1)} %collective-permute-done.7.g_ref.refs_7_, bf16[256,2048]{1,0:T(8,128)(2,1)S(1)} %get-tuple-element.386.slope_ref, bf16[2048,1024]{1,0:T(8,128)(2,1)S(1)} %copy-done.1, ...), custom_call_target="tpu_custom_call" | custom-call | flops 1024 | bytes 1024 | tf_op jit(solution)/shard_map/ffn_back/pallas_call | solution.py:831
  133.5 1.8 collective-permute-start.9
  135.3 13.8 %grad_halves.3 = (bf16[8,128,2048]{2,1,0:T(8,128)(2,1)}, bf16[8,128,2048]{2,1,0:T(8,128)(2,1)S(1)}) custom-call(s32[4]{0:T(128)S(1)} %pad_add_fusion.table_ref, bf16[256,2048]{1,0:T(8,128)(2,1)S(1)} %get-tuple-element.402.refs_0_, bf16[256,2048]{1,0:T(8,128)(2,1)S(1)} %get-tuple-element.403.refs_1_, bf16[256,2048]{1,0:T(8,128)(2,1)S(1)} %get-tuple-element.404.refs_2_, ...), custom_call_target="tpu_custom_call" | custom-call | flops 1024 | bytes 1024 | tf_op jit(solution)/shard_map/grad_halves/pallas_call | solution.py:642
  153.5 4.9 %collective-permute-done.13.moved_ref = bf16[8,128,2048]{2,1,0:T(8,128)(2,1)S(1)} collective-permute-done((bf16[8,128,2048]{2,1,0:T(8,128)(2,1)}, bf16[8,128,2048]{2,1,0:T(8,128)(2,1)S(1)}, u32[]{:S(2)}, u32[]{:S(2)}) %collective-permute-start.13) | collective-permute-done | bytes 4194336 | tf_op jit(solution)/shard_map/ppermute | solution.py:403
  159.0 1.6 collective-permute-start.15
  163.1 2.7 collective-permute-done.12.x_ref.refs_7_
  168.2 1.6 collective-permute-start.17
  171.1 10.8 %attend_back.2 = (bf16[512,512]{1,0:T(8,128)(2,1)S(1)}, f32[1024,512]{1,0:T(8,128)S(1)}, f32[1024,512]{1,0:T(8,128)S(1)}) custom-call(s32[4]{0:T(128)S(1)} %pad_add_fusion.table_ref, s32[8,42]{1,0:T(8,128)S(1)} %copy.40.rb_ref, bf16[1024,1536]{1,0:T(8,128)(2,1)S(1)} %pad_maximum_fusion.q_ref.k_ref.v_ref, ...), custom_call_target="tpu_custom_call" | custom-call | flops 1024 | bytes 1024 | tf_op jit(solution)/shard_map/attend_back/pallas_call | solution.py:324
  183.3 1.6 collective-permute-start.20
  187.6 11.6 %attend_back.3 = (bf16[1024,1536]{1,0:T(8,128)(2,1)S(1)}, f32[8,1024]{1,0:T(8,128)S(1)}) custom-call(s32[4]{0:T(128)S(1)} %pad_add_fusion.table_ref, s32[8,42]{1,0:T(8,128)S(1)} %copy.40.rb_ref, bf16[1024,1536]{1,0:T(8,128)(2,1)S(1)} %pad_maximum_fusion.q_ref.k_ref.v_ref, bf16[1024,1536]{1,0:T(8,128)(2,1)S(1)} %pad_maximum_fusion.q_ref.k_ref.v_ref, ...), custom_call_target="tpu_custom_call" | custom-call | flops 1024 | bytes 1024 | tf_op jit(solution)/shard_map/attend_back/pallas_call | solution.py:324
  199.2 3.1 grad_halves.5
  204.0 2.1 product.18
  208.9 3.1 grad_halves.4.kept_ref
  213.2 2.2 product.19
  215.4 5.5 %collective-permute-done.32.refs_1_ = bf16[128,2048]{1,0:T(8,128)(2,1)S(1)} collective-permute-done((bf16[128,2048]{1,0:T(8,128)(2,1)S(1)}, bf16[128,2048]{1,0:T(8,128)(2,1)S(1)}, u32[]{:S(2)}, u32[]{:S(2)}) %collective-permute-start.32) | collective-permute-done | bytes 524320 | tf_op jit(solution)/shard_map/ppermute | solution.py:400
  223.0 1.6 collective-permute-start.34
  227.1 13.1 %collective-permute-done.24.refs_0_ = bf16[32,2176]{1,0:T(8,128)(2,1)S(1)} collective-permute-done((bf16[32,2176]{1,0:T(8,128)(2,1)S(1)}, bf16[32,2176]{1,0:T(8,128)(2,1)S(1)}, u32[]{:S(2)}, u32[]{:S(2)}) %collective-permute-start.24) | collective-permute-done | bytes 139296 | tf_op jit(solution)/shard_map/ppermute | solution.py:400
  241.6 1.6 add_convert_fusion
  243.7 1.6 collective-permute-start.36
  245.7 1.6 collective-permute-start.28
  247.3 13.6 %collective-permute-done.25.refs_0_ = bf16[64,2176]{1,0:T(8,128)(2,1)S(1)} collective-permute-done((bf16[64,2176]{1,0:T(8,128)(2,1)S(1)}, bf16[64,2176]{1,0:T(8,128)(2,1)S(1)}, u32[]{:S(2)}, u32[]{:S(2)}) %collective-permute-start.25) | collective-permute-done | bytes 278560 | tf_op jit(solution)/shard_map/ppermute | solution.py:400
  264.9 1.6 collective-permute-start.38
  266.4 12.7 %collective-permute-done.26.refs_0_ = bf16[64,2176]{1,0:T(8,128)(2,1)S(1)} collective-permute-done((bf16[64,2176]{1,0:T(8,128)(2,1)S(1)}, bf16[64,2176]{1,0:T(8,128)(2,1)S(1)}, u32[]{:S(2)}, u32[]{:S(2)}) %collective-permute-start.26) | collective-permute-done | bytes 278560 | tf_op jit(solution)/shard_map/ppermute | solution.py:400
  280.5 1.8 collective-permute-start.30
  283.4 1.6 collective-permute-start.44
  285.0 3.6 %collective-permute-done.30.refs_1_ = bf16[64,2176]{1,0:T(8,128)(2,1)S(1)} collective-permute-done((bf16[64,2176]{1,0:T(8,128)(2,1)S(1)}, bf16[64,2176]{1,0:T(8,128)(2,1)S(1)}, u32[]{:S(2)}, u32[]{:S(2)}) %collective-permute-start.30) | collective-permute-done | bytes 278560 | tf_op jit(solution)/shard_map/ppermute | solution.py:400
  291.2 1.6 collective-permute-start.40
  293.2 1.7 collective-permute-done.43.refs_0_
  295.5 4.8 %collective-permute-done.40.refs_5_ = bf16[64,2176]{1,0:T(8,128)(2,1)S(1)} collective-permute-done((bf16[64,2176]{1,0:T(8,128)(2,1)S(1)}, bf16[64,2176]{1,0:T(8,128)(2,1)S(1)}, u32[]{:S(2)}, u32[]{:S(2)}) %collective-permute-start.40) | collective-permute-done | bytes 278560 | tf_op jit(solution)/shard_map/ppermute | solution.py:400
  302.0 1.6 collective-permute-start.42
  305.2 7.1 %place_pieces.2 = (f32[2,8,128,1024]{3,2,1,0:T(8,128)}, f32[2,8,64,2048]{3,2,1,0:T(8,128)}) custom-call(s32[4]{0:T(128)S(1)} %pad_add_fusion.table_ref, bf16[64,2048]{1,0:T(8,128)(2,1)S(1)} %collective-permute-done.43.refs_0_, bf16[128,2048]{1,0:T(8,128)(2,1)S(1)} %collective-permute-done.37.refs_1_, bf16[128,2048]{1,0:T(8,128)(2,1)S(1)} %collective-permute-done.35.refs_2_, ...), custom_call_target="tpu_custom_call" | custom-call | flops 1024 | bytes 1024 | tf_op jit(solution)/shard_map/place_pieces/pallas_call | solution.py:529
  312.7 1.6 collective-permute-start.55
  314.8 6.2 %collective-permute-done.54.refs_1_ = bf16[64,2176]{1,0:T(8,128)(2,1)S(1)} collective-permute-done((bf16[64,2176]{1,0:T(8,128)(2,1)S(1)}, bf16[64,2176]{1,0:T(8,128)(2,1)S(1)}, u32[]{:S(2)}, u32[]{:S(2)}) %collective-permute-start.54) | collective-permute-done | bytes 278560 | tf_op jit(solution)/shard_map/ppermute | solution.py:400
  321.2 1.6 collective-permute-start.57
  323.3 3.8 %collective-permute-done.57.refs_8_ = bf16[32,2176]{1,0:T(8,128)(2,1)S(1)} collective-permute-done((bf16[32,2176]{1,0:T(8,128)(2,1)S(1)}, bf16[32,2176]{1,0:T(8,128)(2,1)S(1)}, u32[]{:S(2)}, u32[]{:S(2)}) %collective-permute-start.57) | collective-permute-done | bytes 139296 | tf_op jit(solution)/shard_map/ppermute | solution.py:400
  329.9 4.2 %place_pieces.3 = (f32[2,8,64,512]{3,2,1,0:T(8,128)}, f32[2,8,64,512]{3,2,1,0:T(8,128)}, f32[2,8,64,512]{3,2,1,0:T(8,128)}, f32[2,8,8,128]{3,2,1,0:T(8,128)S(1)}, f32[2,8,32,1024]{3,2,1,0:T(8,128)}) custom-call(s32[4]{0:T(128)S(1)} %pad_add_fusion.table_ref, bf16[32,2176]{1,0:T(8,128)(2,1)S(1)} %collective-permute-done.56.refs_0_, ...), custom_call_target="tpu_custom_call" | custom-call | flops 1024 | bytes 1024 | tf_op jit(solution)/shard_map/place_pieces/pallas_call | solution.py:529
  (180 shorter events, 59.9 us)
Async XLA Ops:
  0.7 26.4 %collective-permute-start = (bf16[512,1024]{1,0:T(8,128)(2,1)}, bf16[512,1024]{1,0:T(8,128)(2,1)S(1)}, u32[]{:S(2)}, u32[]{:S(2)}) collective-permute-start(bf16[512,1024]{1,0:T(8,128)(2,1)} %bitcast.41), channel_id=1, source_target_pairs={{1,0},{0,1},{3,2},{2,3},{5,4},{4,5},{7,6},{6,7},{9,8},{8,9},{11,10... | collective-permute-start | bytes 3145736 | tf_op jit(solution)/shard_map/ppermute | solution.py:361
  35.7 14.9 %collective-permute-start.1 = (bf16[256,1024]{1,0:T(8,128)(2,1)S(1)}, bf16[256,1024]{1,0:T(8,128)(2,1)S(1)}, u32[]{:S(2)}, u32[]{:S(2)}) collective-permute-start(bf16[256,1024]{1,0:T(8,128)(2,1)S(1)} %product.10), channel_id=1, source_target_pairs={{0,1},{1,0},{2,3},{3,2},{4,5},{5,4},{6,7},{7,6},{8,9},{9,8},{10,11... | collective-permute-start | bytes 1572872 | tf_op jit(solution)/shard_map/ppermute | solution.py:368
  43.8 18.0 %collective-permute-start.3 = (bf16[256,1024]{1,0:T(8,128)(2,1)S(1)}, bf16[256,1024]{1,0:T(8,128)(2,1)S(1)}, u32[]{:S(2)}, u32[]{:S(2)}) collective-permute-start(bf16[256,1024]{1,0:T(8,128)(2,1)S(1)} %product.11), channel_id=1, source_target_pairs={{0,1},{1,0},{2,3},{3,2},{4,5},{5,4},{6,7},{7,6},{8,9},{9,8},{10,11... | collective-permute-start | bytes 1572872 | tf_op jit(solution)/shard_map/ppermute | solution.py:368
  51.4 21.7 %collective-permute-start.2 = (bf16[256,1024]{1,0:T(8,128)(2,1)S(1)}, bf16[256,1024]{1,0:T(8,128)(2,1)S(1)}, u32[]{:S(2)}, u32[]{:S(2)}) collective-permute-start(bf16[256,1024]{1,0:T(8,128)(2,1)S(1)} %get-tuple-element.410.x_ref.refs_2_.refs_8_), channel_id=1, source_target_pairs={{1,0},{0,1},{3,2},{2,3},{5,4},{4,5},{7,6},{6,7},{9,8},{8,9},{11,10... | collective-permute-start | bytes 1572872 | tf_op jit(solution)/shard_map/ppermute | solution.py:361
  62.6 21.7 %collective-permute-start.5 = (bf16[256,1024]{1,0:T(8,128)(2,1)S(1)}, bf16[256,1024]{1,0:T(8,128)(2,1)S(1)}, u32[]{:S(2)}, u32[]{:S(2)}) collective-permute-start(bf16[256,1024]{1,0:T(8,128)(2,1)S(1)} %get-tuple-element.412.x_ref.refs_2_.refs_10_), channel_id=1, source_target_pairs={{1,0},{0,1},{3,2},{2,3},{5,4},{4,5},{7,6},{6,7},{9,8},{8,9},{11,10... | collective-permute-start | bytes 1572872 | tf_op jit(solution)/shard_map/ppermute | solution.py:361
  78.2 17.3 %collective-permute-start.4 = (bf16[256,1024]{1,0:T(8,128)(2,1)S(1)}, bf16[256,1024]{1,0:T(8,128)(2,1)S(1)}, u32[]{:S(2)}, u32[]{:S(2)}) collective-permute-start(bf16[256,1024]{1,0:T(8,128)(2,1)S(1)} %get-tuple-element.354), channel_id=1, source_target_pairs={{0,1},{1,0},{2,3},{3,2},{4,5},{5,4},{6,7},{7,6},{8,9},{9,8},{10,11... | collective-permute-start | bytes 1572872 | tf_op jit(solution)/shard_map/ppermute | solution.py:368
  89.4 17.4 %collective-permute-start.6 = (bf16[256,1024]{1,0:T(8,128)(2,1)S(1)}, bf16[256,1024]{1,0:T(8,128)(2,1)S(1)}, u32[]{:S(2)}, u32[]{:S(2)}) collective-permute-start(bf16[256,1024]{1,0:T(8,128)(2,1)S(1)} %get-tuple-element.356), channel_id=1, source_target_pairs={{0,1},{1,0},{2,3},{3,2},{4,5},{5,4},{6,7},{7,6},{8,9},{9,8},{10,11... | collective-permute-start | bytes 1572872 | tf_op jit(solution)/shard_map/ppermute | solution.py:368
  97.1 21.2 %collective-permute-start.8 = (bf16[256,1024]{1,0:T(8,128)(2,1)S(1)}, bf16[256,1024]{1,0:T(8,128)(2,1)S(1)}, u32[]{:S(2)}, u32[]{:S(2)}) collective-permute-start(bf16[256,1024]{1,0:T(8,128)(2,1)S(1)} %get-tuple-element.421.g_ref.refs_4_.refs_2_), channel_id=1, source_target_pairs={{1,0},{0,1},{3,2},{2,3},{5,4},{4,5},{7,6},{6,7},{9,8},{8,9},{11,10... | collective-permute-start | bytes 1572872 | tf_op jit(solution)/shard_map/ppermute | solution.py:361
  108.0 21.3 %collective-permute-start.7 = (bf16[256,1024]{1,0:T(8,128)(2,1)S(1)}, bf16[256,1024]{1,0:T(8,128)(2,1)S(1)}, u32[]{:S(2)}, u32[]{:S(2)}) collective-permute-start(bf16[256,1024]{1,0:T(8,128)(2,1)S(1)} %get-tuple-element.427.g_ref.refs_6_.refs_2_), channel_id=1, source_target_pairs={{1,0},{0,1},{3,2},{2,3},{5,4},{4,5},{7,6},{6,7},{9,8},{8,9},{11,10... | collective-permute-start | bytes 1572872 | tf_op jit(solution)/shard_map/ppermute | solution.py:361
  122.5 26.6 %collective-permute-start.10 = (bf16[256,1024]{1,0:T(8,128)(2,1)S(1)}, bf16[256,1024]{1,0:T(8,128)(2,1)S(1)}, u32[]{:S(2)}, u32[]{:S(2)}) collective-permute-start(bf16[256,1024]{1,0:T(8,128)(2,1)S(1)} %get-tuple-element.391), channel_id=1, source_target_pairs={{0,1},{1,0},{2,3},{3,2},{4,5},{5,4},{6,7},{7,6},{8,9},{9,8},{10,11... | collective-permute-start | bytes 1572872 | tf_op jit(solution)/shard_map/ppermute | solution.py:368
  133.5 16.5 %collective-permute-start.9 = (bf16[256,1024]{1,0:T(8,128)(2,1)S(1)}, bf16[256,1024]{1,0:T(8,128)(2,1)S(1)}, u32[]{:S(2)}, u32[]{:S(2)}) collective-permute-start(bf16[256,1024]{1,0:T(8,128)(2,1)S(1)} %get-tuple-element.387), channel_id=1, source_target_pairs={{0,1},{1,0},{2,3},{3,2},{4,5},{5,4},{6,7},{7,6},{8,9},{9,8},{10,11... | collective-permute-start | bytes 1572872 | tf_op jit(solution)/shard_map/ppermute | solution.py:368
  150.9 7.4 %collective-permute-start.13 = (bf16[8,128,2048]{2,1,0:T(8,128)(2,1)}, bf16[8,128,2048]{2,1,0:T(8,128)(2,1)S(1)}, u32[]{:S(2)}, u32[]{:S(2)}) collective-permute-start(bf16[8,128,2048]{2,1,0:T(8,128)(2,1)} %get-tuple-element.435), channel_id=1, source_target_pairs={{0,2},{2,0},{4,6},{6,4},{8,10},{10,8},{12,14},{14,12},{16,18},{18,... | collective-permute-start | bytes 12582920 | tf_op jit(solution)/shard_map/ppermute | solution.py:403
  151.0 14.8 %collective-permute-start.12 = (bf16[256,1024]{1,0:T(8,128)(2,1)S(1)}, bf16[256,1024]{1,0:T(8,128)(2,1)S(1)}, u32[]{:S(2)}, u32[]{:S(2)}) collective-permute-start(bf16[256,1024]{1,0:T(8,128)(2,1)S(1)} %get-tuple-element.539.x_ref.refs_6_), channel_id=1, source_target_pairs={{1,0},{0,1},{3,2},{2,3},{5,4},{4,5},{7,6},{6,7},{9,8},{8,9},{11,10... | collective-permute-start | bytes 1572872 | tf_op jit(solution)/shard_map/ppermute | solution.py:361
  159.0 8.4 %collective-permute-start.15 = (bf16[64,2048]{1,0:T(8,128)(2,1)S(1)}, bf16[64,2048]{1,0:T(8,128)(2,1)S(1)}, u32[]{:S(2)}, u32[]{:S(2)}) collective-permute-start(bf16[64,2048]{1,0:T(8,128)(2,1)S(1)} %ring_add.18), channel_id=1, source_target_pairs={{0,8},{2,10},{8,16},{10,18},{16,24},{18,26},{24,28},{26,30},{28,20... | collective-permute-start | bytes 786440 | tf_op jit(solution)/shard_map/ppermute | solution.py:400
  161.2 8.6 %collective-permute-start.14 = (bf16[64,2048]{1,0:T(8,128)(2,1)S(1)}, bf16[64,2048]{1,0:T(8,128)(2,1)S(1)}, u32[]{:S(2)}, u32[]{:S(2)}) collective-permute-start(bf16[64,2048]{1,0:T(8,128)(2,1)S(1)} %ring_add.19), channel_id=1, source_target_pairs={{0,4},{2,6},{8,0},{10,2},{16,8},{18,10},{24,16},{26,18},{28,24},{3... | collective-permute-start | bytes 786440 | tf_op jit(solution)/shard_map/ppermute | solution.py:400
  161.7 20.3 %collective-permute-start.11 = (bf16[256,1024]{1,0:T(8,128)(2,1)S(1)}, bf16[256,1024]{1,0:T(8,128)(2,1)S(1)}, u32[]{:S(2)}, u32[]{:S(2)}) collective-permute-start(bf16[256,1024]{1,0:T(8,128)(2,1)S(1)} %get-tuple-element.540.x_ref.refs_8_), channel_id=1, source_target_pairs={{1,0},{0,1},{3,2},{2,3},{5,4},{4,5},{7,6},{6,7},{9,8},{8,9},{11,10... | collective-permute-start | bytes 1572872 | tf_op jit(solution)/shard_map/ppermute | solution.py:361
  168.2 14.3 %collective-permute-start.17 = (bf16[128,2048]{1,0:T(8,128)(2,1)S(1)}, bf16[128,2048]{1,0:T(8,128)(2,1)S(1)}, u32[]{:S(2)}, u32[]{:S(2)}) collective-permute-start(bf16[128,2048]{1,0:T(8,128)(2,1)S(1)} %ring_add.20), channel_id=1, source_target_pairs={{0,8},{2,10},{8,16},{10,18},{16,24},{18,26},{24,28},{26,30},{28,20... | collective-permute-start | bytes 1572872 | tf_op jit(solution)/shard_map/ppermute | solution.py:400
  170.6 14.3 %collective-permute-start.16 = (bf16[128,2048]{1,0:T(8,128)(2,1)S(1)}, bf16[128,2048]{1,0:T(8,128)(2,1)S(1)}, u32[]{:S(2)}, u32[]{:S(2)}) collective-permute-start(bf16[128,2048]{1,0:T(8,128)(2,1)S(1)} %ring_add.21), channel_id=1, source_target_pairs={{0,4},{2,6},{8,0},{10,2},{16,8},{18,10},{24,16},{26,18},{28,24},{3... | collective-permute-start | bytes 1572872 | tf_op jit(solution)/shard_map/ppermute | solution.py:400
  183.3 19.1 %collective-permute-start.20 = (bf16[128,2048]{1,0:T(8,128)(2,1)S(1)}, bf16[128,2048]{1,0:T(8,128)(2,1)S(1)}, u32[]{:S(2)}, u32[]{:S(2)}) collective-permute-start(bf16[128,2048]{1,0:T(8,128)(2,1)S(1)} %ring_add.22), channel_id=1, source_target_pairs={{0,8},{2,10},{8,16},{10,18},{16,24},{18,26},{24,28},{26,30},{28,20... | collective-permute-start | bytes 1572872 | tf_op jit(solution)/shard_map/ppermute | solution.py:400
  185.7 17.4 %collective-permute-start.19 = (bf16[128,2048]{1,0:T(8,128)(2,1)S(1)}, bf16[128,2048]{1,0:T(8,128)(2,1)S(1)}, u32[]{:S(2)}, u32[]{:S(2)}) collective-permute-start(bf16[128,2048]{1,0:T(8,128)(2,1)S(1)} %ring_add.23), channel_id=1, source_target_pairs={{0,4},{2,6},{8,0},{10,2},{16,8},{18,10},{24,16},{26,18},{28,24},{3... | collective-permute-start | bytes 1572872 | tf_op jit(solution)/shard_map/ppermute | solution.py:400
  186.2 13.0 %collective-permute-start.18 = (f32[8,1024]{1,0:T(8,128)S(1)}, f32[8,1024]{1,0:T(8,128)S(1)}, u32[]{:S(2)}, u32[]{:S(2)}) collective-permute-start(f32[8,1024]{1,0:T(8,128)S(1)} %sum_kernel.1.refs_0_), channel_id=1, source_target_pairs={{1,0},{0,1},{3,2},{2,3},{5,4},{4,5},{7,6},{6,7},{9,8},{8,9},{11,10... | collective-permute-start | bytes 98312 | tf_op jit(solution)/shard_map/ppermute | solution.py:361
  203.9 8.1 %collective-permute-start.21 = (bf16[8,64,2176]{2,1,0:T(8,128)(2,1)S(1)}, bf16[8,64,2176]{2,1,0:T(8,128)(2,1)S(1)}, u32[]{:S(2)}, u32[]{:S(2)}) collective-permute-start(bf16[8,64,2176]{2,1,0:T(8,128)(2,1)S(1)} %grad_halves.5), channel_id=1, source_target_pairs={{0,2},{2,0},{4,6},{6,4},{8,10},{10,8},{12,14},{14,12},{16,18},{18,... | collective-permute-start | bytes 6684680 | tf_op jit(solution)/shard_map/ppermute | solution.py:403
  206.1 35.5 %collective-permute-start.22 = (bf16[512,1024]{1,0:T(8,128)(2,1)S(1)}, bf16[512,1024]{1,0:T(8,128)(2,1)S(1)}, u32[]{:S(2)}, u32[]{:S(2)}) collective-permute-start(bf16[512,1024]{1,0:T(8,128)(2,1)S(1)} %product.18), channel_id=1, source_target_pairs={{0,1},{1,0},{2,3},{3,2},{4,5},{5,4},{6,7},{7,6},{8,9},{9,8},{10,11... | collective-permute-start | bytes 3145736 | tf_op jit(solution)/shard_map/ppermute | solution.py:368
  206.9 14.0 %collective-permute-start.32 = (bf16[128,2048]{1,0:T(8,128)(2,1)S(1)}, bf16[128,2048]{1,0:T(8,128)(2,1)S(1)}, u32[]{:S(2)}, u32[]{:S(2)}) collective-permute-start(bf16[128,2048]{1,0:T(8,128)(2,1)S(1)} %ring_add.25), channel_id=1, source_target_pairs={{0,4},{2,6},{8,0},{10,2},{16,8},{18,10},{24,16},{26,18},{28,24},{3... | collective-permute-start | bytes 1572872 | tf_op jit(solution)/shard_map/ppermute | solution.py:400
  208.4 13.7 %collective-permute-start.31 = (bf16[128,2048]{1,0:T(8,128)(2,1)S(1)}, bf16[128,2048]{1,0:T(8,128)(2,1)S(1)}, u32[]{:S(2)}, u32[]{:S(2)}) collective-permute-start(bf16[128,2048]{1,0:T(8,128)(2,1)S(1)} %ring_add.24), channel_id=1, source_target_pairs={{0,8},{2,10},{8,16},{10,18},{16,24},{18,26},{24,28},{26,30},{28,20... | collective-permute-start | bytes 1572872 | tf_op jit(solution)/shard_map/ppermute | solution.py:400
  223.0 20.2 %collective-permute-start.34 = (bf16[128,2048]{1,0:T(8,128)(2,1)S(1)}, bf16[128,2048]{1,0:T(8,128)(2,1)S(1)}, u32[]{:S(2)}, u32[]{:S(2)}) collective-permute-start(bf16[128,2048]{1,0:T(8,128)(2,1)S(1)} %ring_add.34.refs_4_), channel_id=1, source_target_pairs={{0,4},{2,6},{8,0},{10,2},{16,8},{18,10},{24,16},{26,18},{28,24},{3... | collective-permute-start | bytes 1572872 | tf_op jit(solution)/shard_map/ppermute | solution.py:400
  224.6 18.6 %collective-permute-start.33 = (bf16[128,2048]{1,0:T(8,128)(2,1)S(1)}, bf16[128,2048]{1,0:T(8,128)(2,1)S(1)}, u32[]{:S(2)}, u32[]{:S(2)}) collective-permute-start(bf16[128,2048]{1,0:T(8,128)(2,1)S(1)} %ring_add.34.refs_4_), channel_id=1, source_target_pairs={{0,8},{2,10},{8,16},{10,18},{16,24},{18,26},{24,28},{26,30},{28,20... | collective-permute-start | bytes 1572872 | tf_op jit(solution)/shard_map/ppermute | solution.py:400
  225.1 15.1 %collective-permute-start.24 = (bf16[32,2176]{1,0:T(8,128)(2,1)S(1)}, bf16[32,2176]{1,0:T(8,128)(2,1)S(1)}, u32[]{:S(2)}, u32[]{:S(2)}) collective-permute-start(bf16[32,2176]{1,0:T(8,128)(2,1)S(1)} %ring_add.26), channel_id=1, source_target_pairs={{0,8},{2,10},{8,16},{10,18},{16,24},{18,26},{24,28},{26,30},{28,20... | collective-permute-start | bytes 417800 | tf_op jit(solution)/shard_map/ppermute | solution.py:400
  225.6 15.3 %collective-permute-start.23 = (bf16[32,2176]{1,0:T(8,128)(2,1)S(1)}, bf16[32,2176]{1,0:T(8,128)(2,1)S(1)}, u32[]{:S(2)}, u32[]{:S(2)}) collective-permute-start(bf16[32,2176]{1,0:T(8,128)(2,1)S(1)} %ring_add.27), channel_id=1, source_target_pairs={{0,4},{2,6},{8,0},{10,2},{16,8},{18,10},{24,16},{26,18},{28,24},{3... | collective-permute-start | bytes 417800 | tf_op jit(solution)/shard_map/ppermute | solution.py:400
  243.2 19.1 %collective-permute-start.35 = (bf16[128,2048]{1,0:T(8,128)(2,1)S(1)}, bf16[128,2048]{1,0:T(8,128)(2,1)S(1)}, u32[]{:S(2)}, u32[]{:S(2)}) collective-permute-start(bf16[128,2048]{1,0:T(8,128)(2,1)S(1)} %collective-permute-done.33.refs_3_), channel_id=1, source_target_pairs={{0,8},{2,10},{8,16},{10,18},{16,24},{18,26},{24,28},{26,30},{28,20... | collective-permute-start | bytes 1572872 | tf_op jit(solution)/shard_map/ppermute | solution.py:400
  243.7 18.6 %collective-permute-start.36 = (bf16[128,2048]{1,0:T(8,128)(2,1)S(1)}, bf16[128,2048]{1,0:T(8,128)(2,1)S(1)}, u32[]{:S(2)}, u32[]{:S(2)}) collective-permute-start(bf16[128,2048]{1,0:T(8,128)(2,1)S(1)} %collective-permute-done.34.refs_5_), channel_id=1, source_target_pairs={{0,4},{2,6},{8,0},{10,2},{16,8},{18,10},{24,16},{26,18},{28,24},{3... | collective-permute-start | bytes 1572872 | tf_op jit(solution)/shard_map/ppermute | solution.py:400
  245.3 15.6 %collective-permute-start.25 = (bf16[64,2176]{1,0:T(8,128)(2,1)S(1)}, bf16[64,2176]{1,0:T(8,128)(2,1)S(1)}, u32[]{:S(2)}, u32[]{:S(2)}) collective-permute-start(bf16[64,2176]{1,0:T(8,128)(2,1)S(1)} %ring_add.28), channel_id=1, source_target_pairs={{0,8},{2,10},{8,16},{10,18},{16,24},{18,26},{24,28},{26,30},{28,20... | collective-permute-start | bytes 835592 | tf_op jit(solution)/shard_map/ppermute | solution.py:400
  245.7 15.9 %collective-permute-start.28 = (bf16[64,2176]{1,0:T(8,128)(2,1)S(1)}, bf16[64,2176]{1,0:T(8,128)(2,1)S(1)}, u32[]{:S(2)}, u32[]{:S(2)}) collective-permute-start(bf16[64,2176]{1,0:T(8,128)(2,1)S(1)} %ring_add.29), channel_id=1, source_target_pairs={{0,4},{2,6},{8,0},{10,2},{16,8},{18,10},{24,16},{26,18},{28,24},{3... | collective-permute-start | bytes 835592 | tf_op jit(solution)/shard_map/ppermute | solution.py:400
  262.3 20.5 %collective-permute-start.37 = (bf16[128,2048]{1,0:T(8,128)(2,1)S(1)}, bf16[128,2048]{1,0:T(8,128)(2,1)S(1)}, u32[]{:S(2)}, u32[]{:S(2)}) collective-permute-start(bf16[128,2048]{1,0:T(8,128)(2,1)S(1)} %collective-permute-done.35.refs_2_), channel_id=1, source_target_pairs={{0,8},{2,10},{8,16},{10,18},{16,24},{18,26},{24,28},{26,30},{28,20... | collective-permute-start | bytes 1572872 | tf_op jit(solution)/shard_map/ppermute | solution.py:400
  262.8 16.3 %collective-permute-start.26 = (bf16[64,2176]{1,0:T(8,128)(2,1)S(1)}, bf16[64,2176]{1,0:T(8,128)(2,1)S(1)}, u32[]{:S(2)}, u32[]{:S(2)}) collective-permute-start(bf16[64,2176]{1,0:T(8,128)(2,1)S(1)} %ring_add.30), channel_id=1, source_target_pairs={{0,8},{2,10},{8,16},{10,18},{16,24},{18,26},{24,28},{26,30},{28,20... | collective-permute-start | bytes 835592 | tf_op jit(solution)/shard_map/ppermute | solution.py:400
  264.2 15.6 %collective-permute-start.29 = (bf16[64,2176]{1,0:T(8,128)(2,1)S(1)}, bf16[64,2176]{1,0:T(8,128)(2,1)S(1)}, u32[]{:S(2)}, u32[]{:S(2)}) collective-permute-start(bf16[64,2176]{1,0:T(8,128)(2,1)S(1)} %ring_add.32), channel_id=1, source_target_pairs={{0,4},{2,6},{8,0},{10,2},{16,8},{18,10},{24,16},{26,18},{28,24},{3... | collective-permute-start | bytes 835592 | tf_op jit(solution)/shard_map/ppermute | solution.py:400
  264.9 18.5 %collective-permute-start.38 = (bf16[128,2048]{1,0:T(8,128)(2,1)S(1)}, bf16[128,2048]{1,0:T(8,128)(2,1)S(1)}, u32[]{:S(2)}, u32[]{:S(2)}) collective-permute-start(bf16[128,2048]{1,0:T(8,128)(2,1)S(1)} %collective-permute-done.36.refs_6_), channel_id=1, source_target_pairs={{0,4},{2,6},{8,0},{10,2},{16,8},{18,10},{24,16},{26,18},{28,24},{3... | collective-permute-start | bytes 1572872 | tf_op jit(solution)/shard_map/ppermute | solution.py:400
  280.5 8.1 %collective-permute-start.30 = (bf16[64,2176]{1,0:T(8,128)(2,1)S(1)}, bf16[64,2176]{1,0:T(8,128)(2,1)S(1)}, u32[]{:S(2)}, u32[]{:S(2)}) collective-permute-start(bf16[64,2176]{1,0:T(8,128)(2,1)S(1)} %ring_add.33), channel_id=1, source_target_pairs={{0,4},{2,6},{8,0},{10,2},{16,8},{18,10},{24,16},{26,18},{28,24},{3... | collective-permute-start | bytes 835592 | tf_op jit(solution)/shard_map/ppermute | solution.py:400
  282.4 8.0 %collective-permute-start.27 = (bf16[64,2176]{1,0:T(8,128)(2,1)S(1)}, bf16[64,2176]{1,0:T(8,128)(2,1)S(1)}, u32[]{:S(2)}, u32[]{:S(2)}) collective-permute-start(bf16[64,2176]{1,0:T(8,128)(2,1)S(1)} %ring_add.31), channel_id=1, source_target_pairs={{0,8},{2,10},{8,16},{10,18},{16,24},{18,26},{24,28},{26,30},{28,20... | collective-permute-start | bytes 835592 | tf_op jit(solution)/shard_map/ppermute | solution.py:400
  282.8 8.3 %collective-permute-start.49 = (bf16[128,2048]{1,0:T(8,128)(2,1)S(1)}, bf16[128,2048]{1,0:T(8,128)(2,1)S(1)}, u32[]{:S(2)}, u32[]{:S(2)}) collective-permute-start(bf16[128,2048]{1,0:T(8,128)(2,1)S(1)} %ring_add.34.refs_4_), channel_id=1, source_target_pairs={{0,2},{2,0},{4,6},{6,4},{8,10},{10,8},{12,14},{14,12},{16,18},{18,... | collective-permute-start | bytes 1572872 | tf_op jit(solution)/shard_map/ppermute | solution.py:403
  282.8 9.9 %collective-permute-start.48 = (bf16[128,2048]{1,0:T(8,128)(2,1)S(1)}, bf16[128,2048]{1,0:T(8,128)(2,1)S(1)}, u32[]{:S(2)}, u32[]{:S(2)}) collective-permute-start(bf16[128,2048]{1,0:T(8,128)(2,1)S(1)} %collective-permute-done.33.refs_3_), channel_id=1, source_target_pairs={{0,2},{2,0},{4,6},{6,4},{8,10},{10,8},{12,14},{14,12},{16,18},{18,... | collective-permute-start | bytes 1572872 | tf_op jit(solution)/shard_map/ppermute | solution.py:403
  283.4 9.9 %collective-permute-start.44 = (bf16[64,2048]{1,0:T(8,128)(2,1)S(1)}, bf16[64,2048]{1,0:T(8,128)(2,1)S(1)}, u32[]{:S(2)}, u32[]{:S(2)}) collective-permute-start(bf16[64,2048]{1,0:T(8,128)(2,1)S(1)} %slice.43), channel_id=1, source_target_pairs={{0,4},{2,6},{8,0},{10,2},{16,8},{18,10},{24,16},{26,18},{28,24},{3... | collective-permute-start | bytes 786440 | tf_op jit(solution)/shard_map/ppermute | solution.py:400
  288.6 6.4 %collective-permute-start.43 = (bf16[64,2048]{1,0:T(8,128)(2,1)S(1)}, bf16[64,2048]{1,0:T(8,128)(2,1)S(1)}, u32[]{:S(2)}, u32[]{:S(2)}) collective-permute-start(bf16[64,2048]{1,0:T(8,128)(2,1)S(1)} %slice.42), channel_id=1, source_target_pairs={{0,8},{2,10},{8,16},{10,18},{16,24},{18,26},{24,28},{26,30},{28,20... | collective-permute-start | bytes 786440 | tf_op jit(solution)/shard_map/ppermute | solution.py:400
  290.4 4.6 %collective-permute-start.50 = (bf16[128,2048]{1,0:T(8,128)(2,1)S(1)}, bf16[128,2048]{1,0:T(8,128)(2,1)S(1)}, u32[]{:S(2)}, u32[]{:S(2)}) collective-permute-start(bf16[128,2048]{1,0:T(8,128)(2,1)S(1)} %collective-permute-done.34.refs_5_), channel_id=1, source_target_pairs={{0,2},{2,0},{4,6},{6,4},{8,10},{10,8},{12,14},{14,12},{16,18},{18,... | collective-permute-start | bytes 1572872 | tf_op jit(solution)/shard_map/ppermute | solution.py:403
  291.2 9.1 %collective-permute-start.40 = (bf16[64,2176]{1,0:T(8,128)(2,1)S(1)}, bf16[64,2176]{1,0:T(8,128)(2,1)S(1)}, u32[]{:S(2)}, u32[]{:S(2)}) collective-permute-start(bf16[64,2176]{1,0:T(8,128)(2,1)S(1)} %ring_add.35.refs_4_), channel_id=1, source_target_pairs={{0,4},{2,6},{8,0},{10,2},{16,8},{18,10},{24,16},{26,18},{28,24},{3... | collective-permute-start | bytes 835592 | tf_op jit(solution)/shard_map/ppermute | solution.py:400
  292.8 8.8 %collective-permute-start.39 = (bf16[64,2176]{1,0:T(8,128)(2,1)S(1)}, bf16[64,2176]{1,0:T(8,128)(2,1)S(1)}, u32[]{:S(2)}, u32[]{:S(2)}) collective-permute-start(bf16[64,2176]{1,0:T(8,128)(2,1)S(1)} %ring_add.35.refs_4_), channel_id=1, source_target_pairs={{0,8},{2,10},{8,16},{10,18},{16,24},{18,26},{24,28},{26,30},{28,20... | collective-permute-start | bytes 835592 | tf_op jit(solution)/shard_map/ppermute | solution.py:400
  293.2 8.3 %collective-permute-start.47 = (bf16[128,2048]{1,0:T(8,128)(2,1)S(1)}, bf16[128,2048]{1,0:T(8,128)(2,1)S(1)}, u32[]{:S(2)}, u32[]{:S(2)}) collective-permute-start(bf16[128,2048]{1,0:T(8,128)(2,1)S(1)} %collective-permute-done.35.refs_2_), channel_id=1, source_target_pairs={{0,2},{2,0},{4,6},{6,4},{8,10},{10,8},{12,14},{14,12},{16,18},{18,... | collective-permute-start | bytes 1572872 | tf_op jit(solution)/shard_map/ppermute | solution.py:403
  295.0 7.1 %collective-permute-start.51 = (bf16[128,2048]{1,0:T(8,128)(2,1)S(1)}, bf16[128,2048]{1,0:T(8,128)(2,1)S(1)}, u32[]{:S(2)}, u32[]{:S(2)}) collective-permute-start(bf16[128,2048]{1,0:T(8,128)(2,1)S(1)} %collective-permute-done.36.refs_6_), channel_id=1, source_target_pairs={{0,2},{2,0},{4,6},{6,4},{8,10},{10,8},{12,14},{14,12},{16,18},{18,... | collective-permute-start | bytes 1572872 | tf_op jit(solution)/shard_map/ppermute | solution.py:403
  295.0 8.6 %collective-permute-start.45 = (bf16[64,2048]{1,0:T(8,128)(2,1)S(1)}, bf16[64,2048]{1,0:T(8,128)(2,1)S(1)}, u32[]{:S(2)}, u32[]{:S(2)}) collective-permute-start(bf16[64,2048]{1,0:T(8,128)(2,1)S(1)} %collective-permute-done.43.refs_0_), channel_id=1, source_target_pairs={{0,2},{2,0},{4,6},{6,4},{8,10},{10,8},{12,14},{14,12},{16,18},{18,... | collective-permute-start | bytes 786440 | tf_op jit(solution)/shard_map/ppermute | solution.py:403
  300.3 4.9 %collective-permute-start.46 = (bf16[128,2048]{1,0:T(8,128)(2,1)S(1)}, bf16[128,2048]{1,0:T(8,128)(2,1)S(1)}, u32[]{:S(2)}, u32[]{:S(2)}) collective-permute-start(bf16[128,2048]{1,0:T(8,128)(2,1)S(1)} %collective-permute-done.37.refs_1_), channel_id=1, source_target_pairs={{0,2},{2,0},{4,6},{6,4},{8,10},{10,8},{12,14},{14,12},{16,18},{18,... | collective-permute-start | bytes 1572872 | tf_op jit(solution)/shard_map/ppermute | solution.py:403
  301.6 3.6 %collective-permute-start.52 = (bf16[128,2048]{1,0:T(8,128)(2,1)S(1)}, bf16[128,2048]{1,0:T(8,128)(2,1)S(1)}, u32[]{:S(2)}, u32[]{:S(2)}) collective-permute-start(bf16[128,2048]{1,0:T(8,128)(2,1)S(1)} %collective-permute-done.38.refs_7_), channel_id=1, source_target_pairs={{0,2},{2,0},{4,6},{6,4},{8,10},{10,8},{12,14},{14,12},{16,18},{18,... | collective-permute-start | bytes 1572872 | tf_op jit(solution)/shard_map/ppermute | solution.py:403
  301.6 10.6 %collective-permute-start.41 = (bf16[64,2176]{1,0:T(8,128)(2,1)S(1)}, bf16[64,2176]{1,0:T(8,128)(2,1)S(1)}, u32[]{:S(2)}, u32[]{:S(2)}) collective-permute-start(bf16[64,2176]{1,0:T(8,128)(2,1)S(1)} %collective-permute-done.39.refs_3_), channel_id=1, source_target_pairs={{0,8},{2,10},{8,16},{10,18},{16,24},{18,26},{24,28},{26,30},{28,20... | collective-permute-start | bytes 835592 | tf_op jit(solution)/shard_map/ppermute | solution.py:400
  302.0 10.2 %collective-permute-start.42 = (bf16[64,2176]{1,0:T(8,128)(2,1)S(1)}, bf16[64,2176]{1,0:T(8,128)(2,1)S(1)}, u32[]{:S(2)}, u32[]{:S(2)}) collective-permute-start(bf16[64,2176]{1,0:T(8,128)(2,1)S(1)} %collective-permute-done.40.refs_5_), channel_id=1, source_target_pairs={{0,4},{2,6},{8,0},{10,2},{16,8},{18,10},{24,16},{26,18},{28,24},{3... | collective-permute-start | bytes 835592 | tf_op jit(solution)/shard_map/ppermute | solution.py:400
  312.2 8.7 %collective-permute-start.54 = (bf16[64,2176]{1,0:T(8,128)(2,1)S(1)}, bf16[64,2176]{1,0:T(8,128)(2,1)S(1)}, u32[]{:S(2)}, u32[]{:S(2)}) collective-permute-start(bf16[64,2176]{1,0:T(8,128)(2,1)S(1)} %collective-permute-done.41.refs_2_), channel_id=1, source_target_pairs={{0,8},{2,10},{8,16},{10,18},{16,24},{18,26},{24,28},{26,30},{28,20... | collective-permute-start | bytes 835592 | tf_op jit(solution)/shard_map/ppermute | solution.py:400
  312.7 8.4 %collective-permute-start.55 = (bf16[64,2176]{1,0:T(8,128)(2,1)S(1)}, bf16[64,2176]{1,0:T(8,128)(2,1)S(1)}, u32[]{:S(2)}, u32[]{:S(2)}) collective-permute-start(bf16[64,2176]{1,0:T(8,128)(2,1)S(1)} %collective-permute-done.42.refs_6_), channel_id=1, source_target_pairs={{0,4},{2,6},{8,0},{10,2},{16,8},{18,10},{24,16},{26,18},{28,24},{3... | collective-permute-start | bytes 835592 | tf_op jit(solution)/shard_map/ppermute | solution.py:400
  314.3 8.5 %collective-permute-start.62 = (bf16[64,2176]{1,0:T(8,128)(2,1)S(1)}, bf16[64,2176]{1,0:T(8,128)(2,1)S(1)}, u32[]{:S(2)}, u32[]{:S(2)}) collective-permute-start(bf16[64,2176]{1,0:T(8,128)(2,1)S(1)} %ring_add.35.refs_4_), channel_id=1, source_target_pairs={{0,2},{2,0},{4,6},{6,4},{8,10},{10,8},{12,14},{14,12},{16,18},{18,... | collective-permute-start | bytes 835592 | tf_op jit(solution)/shard_map/ppermute | solution.py:403
  314.3 9.0 %collective-permute-start.61 = (bf16[64,2176]{1,0:T(8,128)(2,1)S(1)}, bf16[64,2176]{1,0:T(8,128)(2,1)S(1)}, u32[]{:S(2)}, u32[]{:S(2)}) collective-permute-start(bf16[64,2176]{1,0:T(8,128)(2,1)S(1)} %collective-permute-done.39.refs_3_), channel_id=1, source_target_pairs={{0,2},{2,0},{4,6},{6,4},{8,10},{10,8},{12,14},{14,12},{16,18},{18,... | collective-permute-start | bytes 835592 | tf_op jit(solution)/shard_map/ppermute | solution.py:403
  314.8 13.1 %collective-permute-start.63 = (bf16[64,2176]{1,0:T(8,128)(2,1)S(1)}, bf16[64,2176]{1,0:T(8,128)(2,1)S(1)}, u32[]{:S(2)}, u32[]{:S(2)}) collective-permute-start(bf16[64,2176]{1,0:T(8,128)(2,1)S(1)} %collective-permute-done.40.refs_5_), channel_id=1, source_target_pairs={{0,2},{2,0},{4,6},{6,4},{8,10},{10,8},{12,14},{14,12},{16,18},{18,... | collective-permute-start | bytes 835592 | tf_op jit(solution)/shard_map/ppermute | solution.py:403
  321.0 7.5 %collective-permute-start.60 = (bf16[64,2176]{1,0:T(8,128)(2,1)S(1)}, bf16[64,2176]{1,0:T(8,128)(2,1)S(1)}, u32[]{:S(2)}, u32[]{:S(2)}) collective-permute-start(bf16[64,2176]{1,0:T(8,128)(2,1)S(1)} %collective-permute-done.41.refs_2_), channel_id=1, source_target_pairs={{0,2},{2,0},{4,6},{6,4},{8,10},{10,8},{12,14},{14,12},{16,18},{18,... | collective-permute-start | bytes 835592 | tf_op jit(solution)/shard_map/ppermute | solution.py:403
  321.2 6.0 %collective-permute-start.57 = (bf16[32,2176]{1,0:T(8,128)(2,1)S(1)}, bf16[32,2176]{1,0:T(8,128)(2,1)S(1)}, u32[]{:S(2)}, u32[]{:S(2)}) collective-permute-start(bf16[32,2176]{1,0:T(8,128)(2,1)S(1)} %slice.45), channel_id=1, source_target_pairs={{0,4},{2,6},{8,0},{10,2},{16,8},{18,10},{24,16},{26,18},{28,24},{3... | collective-permute-start | bytes 417800 | tf_op jit(solution)/shard_map/ppermute | solution.py:400
  322.8 5.1 %collective-permute-start.56 = (bf16[32,2176]{1,0:T(8,128)(2,1)S(1)}, bf16[32,2176]{1,0:T(8,128)(2,1)S(1)}, u32[]{:S(2)}, u32[]{:S(2)}) collective-permute-start(bf16[32,2176]{1,0:T(8,128)(2,1)S(1)} %slice.44), channel_id=1, source_target_pairs={{0,8},{2,10},{8,16},{10,18},{16,24},{18,26},{24,28},{26,30},{28,20... | collective-permute-start | bytes 417800 | tf_op jit(solution)/shard_map/ppermute | solution.py:400
  323.3 6.2 %collective-permute-start.64 = (bf16[64,2176]{1,0:T(8,128)(2,1)S(1)}, bf16[64,2176]{1,0:T(8,128)(2,1)S(1)}, u32[]{:S(2)}, u32[]{:S(2)}) collective-permute-start(bf16[64,2176]{1,0:T(8,128)(2,1)S(1)} %collective-permute-done.42.refs_6_), channel_id=1, source_target_pairs={{0,2},{2,0},{4,6},{6,4},{8,10},{10,8},{12,14},{14,12},{16,18},{18,... | collective-permute-start | bytes 835592 | tf_op jit(solution)/shard_map/ppermute | solution.py:403
  327.1 2.7 collective-permute-start.59
  327.9 2.0 collective-permute-start.65
  (16 other events, 129.7 us)

commit v4 on v3

--- a/solution.py
+++ b/solution.py
@@ -486,6 +486,9 @@
     def place_pieces(self, table, pieces, outs):
         chips, ahead = self.chips, self.ahead
         size = pieces[0][ahead].shape[0]
+        cuts = [move[3] for _, moves in outs for move in moves]
+        first_lane = min(cut.start for cut in cuts)
+        wide = max(cut.stop for cut in cuts) - first_lane
         arrays, places = [], []
         for side in pieces:
             entries = []
@@ -504,9 +507,10 @@
                     slot = lax.rem(table_ref[PLACE] + offset + chips, chips)
                     for ref, (_, moves) in zip(out_refs, outs):
                         for own_rows, own_columns, rows, cut in moves:
+                            lanes = slice(cut.start - first_lane, cut.stop - first_lane)
                             if isinstance(rows, tuple):
                                 if first == 0:
-                                    both = [piece_refs[at][r, cut].astype(jnp.float32) for r in rows]
+                                    both = [piece_refs[at][r, lanes].astype(jnp.float32) for r in rows]
                                     ref[0, slot, own_rows, own_columns] = both[0] + both[1]
                                 continue
                             low, high = max(rows.start, first), min(rows.stop, first + count)
@@ -516,7 +520,7 @@
                                 own_rows.start + low - rows.start,
                                 own_rows.start + high - rows.start,
                             )
-                            value = piece_refs[at][low - first : high - first, cut]
+                            value = piece_refs[at][low - first : high - first, lanes]
                             ref[0, slot, there, own_columns] = value.astype(jnp.float32)
 
             for i, entries in enumerate(places):
@@ -532,7 +536,11 @@
                 num_scalar_prefetch=1,
                 grid=(2,),
                 in_specs=[
-                    pl.BlockSpec(a.shape, lambda i, w: (0, 0), pipeline_mode=pl.Buffered(1))
+                    pl.BlockSpec(
+                        (a.shape[0], wide),
+                        lambda i, w: (0, first_lane // wide),
+                        pipeline_mode=pl.Buffered(1),
+                    )
                     for a in arrays
                 ],
                 out_specs=[pl.BlockSpec((1, *shape), target) for shape in shapes],
@@ -1241,9 +1249,12 @@
 
     while under_way:
         advance()
-        names = {n for n, _ in under_way}
-        if "ffn" not in names and "ffn" not in totals:
-            totals["ffn"] = run(lambda *p: ring.place_pieces(table, p, ffn_outs), *ffn.results)
+        for n, name in enumerate(("down", "up")):
+            if ffn.results and name not in totals:
+                (totals[name],) = run(
+                    lambda *p: ring.place_pieces(table, p, [ffn_outs[n]]), *ffn.results
+                )
+                break
     everything = slice(0, attn_rows)
     attn_outs = []
     for i in range(3):
@@ -1265,7 +1276,7 @@
             dot_tn(contexts[c], jnp.concatenate(dattn[c], 0)) for c in every
         )
         grad_out_w = lax.psum(partial.astype(LOW), "dp").astype(jnp.float32)
-    grad_down_w, grad_up_w = totals["ffn"]
+    grad_down_w, grad_up_w = totals["down"], totals["up"]
     vectors, rms_stats, *biases = spread(value)
     shape = hidden_in.shape
     return (

time: 340 us -> 339 us (level)
  waiting for transfers between devices: 131 us -> 127 us
    ppermute x32, waiting for transfers between devices: 70.9 us -> 67.3 us  [shift(): return lax.ppermute(value, 'dp', pairs)]
    pallas_call x2 -> x3, Pallas kernels: 11.3 us -> 13.3 us  [place_pieces(): pl.pallas_call(body, grid_spec=pltpu.PrefetchScalarGridSpec(num_scalar_pr...]
  transfers between devices with their start and end apart: 67 -> 67, of which waited for: 28 -> 30; matrix products, arithmetic and copies ran while one was open for 3% -> 3% of each run, Pallas kernels for 35% -> 36%
where the time goes in v4:
time: 339 us; the launch traced here: 335 us
  Pallas kernels  133 us (39%)
  waiting for transfers between devices  127 us (37%)
  starting transfers between devices  59.6 us (18%)
  local copies, waits for them, and re-layouts  5.64 us (2%)
  other arithmetic  4.12 us (1%)
  matrix products  3.58 us (1%)
    ppermute x32, waiting for transfers between devices, shift(): return lax.ppermute(value, 'dp', pairs)  67.3 us
    ppermute x32, starting transfers between devices, shift(): return lax.ppermute(value, 'dp', pairs)  33.3 us
    ppermute x8, waiting for transfers between devices, fetch(): lax.ppermute(rows, 'tensor', [((k + s) % ranks, k) for k in range(ranks)])  32.9 us
    pallas_call x2, Pallas kernels, attend_back(): pl.pallas_call(functools.partial(attend_back_kernel, plan, 3, len(earlier...  22.4 us
    ppermute x7, waiting for transfers between devices, hand_over(): lax.ppermute(share, 'tensor', [(k, (k + s) % ranks) for k in range(ranks)])  20.4 us
    pallas_call x4, Pallas kernels, ffn_forward(): pl.pallas_call(body, grid=(steps,), in_specs=[whole, pl.BlockSpec((width,...  20.3 us
    pallas_call x3, Pallas kernels, grad_halves(): pl.pallas_call(body, in_specs=[pl.BlockSpec(memory_space=pltpu.SMEM)] + [...  20.1 us
    pallas_call x4, Pallas kernels, ffn_back(): pl.pallas_call(body, grid=(steps,), in_specs=[whole, part, pl.BlockSpec((...  17 us
  transfers between devices with their start and end apart: 67, of which 30 were waited for; matrix products, arithmetic and copies ran while one was open for 3% of the time, Pallas kernels for 36%

profile of v4, /device:TPU:0, one launch (start us, length us, event | category | flops | bytes accessed | tf_op | source)
XLA Modules:
  0.0 335.1 jit_solution(17141413390788618885)
XLA Ops:
  0.7 3.0 collective-permute-start
  8.1 1.8 fusion
  9.9 17.1 %collective-permute-done.refs_2_ = bf16[512,1024]{1,0:T(8,128)(2,1)S(1)} collective-permute-done((bf16[512,1024]{1,0:T(8,128)(2,1)}, bf16[512,1024]{1,0:T(8,128)(2,1)S(1)}, u32[]{:S(2)}, u32[]{:S(2)}) %collective-permute-start) | collective-permute-done | bytes 1048608 | tf_op jit(solution)/shard_map/ppermute | solution.py:361
  27.0 1.8 fusion.1
  29.1 5.8 %attend.2 = (bf16[512,512]{1,0:T(8,128)(2,1)S(1)}, f32[2,8,256]{2,1,0:T(8,128)S(1)}) custom-call(s32[4]{0:T(128)S(1)} %pad_add_fusion.table_ref, s32[8,42]{1,0:T(8,128)S(1)} %copy.40.rb_ref, bf16[1024,1536]{1,0:T(8,128)(2,1)S(1)} %pad_maximum_fusion.q_ref.k_ref.v_ref, bf16[1024,1536]{1,0:T(8,128)(2,1)S(1)} %pad_maximum_fusion.q_ref.k_ref.v_ref, ...), custom_call_target="tpu_custom_call" | custom-call | flops 1024 | bytes 1024 | tf_op jit(solution)/shard_map/attend/pallas_call | solution.py:281
  35.7 1.8 collective-permute-start.1
  37.5 5.6 %attend.3 = (bf16[512,512]{1,0:T(8,128)(2,1)S(1)}, f32[2,8,256]{2,1,0:T(8,128)S(1)}) custom-call(s32[4]{0:T(128)S(1)} %pad_add_fusion.table_ref, s32[8,42]{1,0:T(8,128)S(1)} %copy.40.rb_ref, bf16[1024,1536]{1,0:T(8,128)(2,1)S(1)} %pad_maximum_fusion.q_ref.k_ref.v_ref, bf16[1024,1536]{1,0:T(8,128)(2,1)S(1)} %pad_maximum_fusion.q_ref.k_ref.v_ref, ...), custom_call_target="tpu_custom_call" | custom-call | flops 1024 | bytes 1024 | tf_op jit(solution)/shard_map/attend/pallas_call | solution.py:281
  45.9 4.7 %collective-permute-done.1.refs_1_ = bf16[256,1024]{1,0:T(8,128)(2,1)S(1)} collective-permute-done((bf16[256,1024]{1,0:T(8,128)(2,1)S(1)}, bf16[256,1024]{1,0:T(8,128)(2,1)S(1)}, u32[]{:S(2)}, u32[]{:S(2)}) %collective-permute-start.1) | collective-permute-done | bytes 524320 | tf_op jit(solution)/shard_map/ppermute | solution.py:368
  51.4 1.8 collective-permute-start.2
  53.2 5.0 %ffn_forward.4 = (bf16[256,2048]{1,0:T(8,128)(2,1)S(1)}, bf16[256,2048]{1,0:T(8,128)(2,1)S(1)}, f32[256,1024]{1,0:T(8,128)S(1)}) custom-call(bf16[256,1024]{1,0:T(8,128)(2,1)S(1)} %get-tuple-element.408.x_ref.refs_2_.refs_8_, bf16[1024,2048]{1,0:T(8,128)(2,1)S(1)} %copy-done, bf16[1,2048]{1,0:T(2,128)(2,1)S(1)} %reshape.103.b_ref, ...), custom_call_target="tpu_custom_call" | custom-call | flops 1024 | bytes 1024 | tf_op jit(solution)/shard_map/ffn_forward/pallas_call | solution.py:804
  58.3 3.6 %collective-permute-done.3.refs_1_ = bf16[256,1024]{1,0:T(8,128)(2,1)S(1)} collective-permute-done((bf16[256,1024]{1,0:T(8,128)(2,1)S(1)}, bf16[256,1024]{1,0:T(8,128)(2,1)S(1)}, u32[]{:S(2)}, u32[]{:S(2)}) %collective-permute-start.3) | collective-permute-done | bytes 524320 | tf_op jit(solution)/shard_map/ppermute | solution.py:368
  62.7 1.8 collective-permute-start.5
  64.5 5.1 %ffn_forward.5 = (bf16[256,2048]{1,0:T(8,128)(2,1)S(1)}, bf16[256,2048]{1,0:T(8,128)(2,1)S(1)}, f32[256,1024]{1,0:T(8,128)S(1)}) custom-call(bf16[256,1024]{1,0:T(8,128)(2,1)S(1)} %get-tuple-element.410.x_ref.refs_2_.refs_10_, bf16[1024,2048]{1,0:T(8,128)(2,1)S(1)} %copy-done, bf16[1,2048]{1,0:T(2,128)(2,1)S(1)} %reshape.103.b_ref, ...), custom_call_target="tpu_custom_call" | custom-call | flops 1024 | bytes 1024 | tf_op jit(solution)/shard_map/ffn_forward/pallas_call | solution.py:804
  69.5 3.6 %collective-permute-done.2.x_ref.refs_9_ = bf16[256,1024]{1,0:T(8,128)(2,1)S(1)} collective-permute-done((bf16[256,1024]{1,0:T(8,128)(2,1)S(1)}, bf16[256,1024]{1,0:T(8,128)(2,1)S(1)}, u32[]{:S(2)}, u32[]{:S(2)}) %collective-permute-start.2) | collective-permute-done | bytes 524320 | tf_op jit(solution)/shard_map/ppermute | solution.py:361
  73.1 5.1 %ffn_forward.6 = (bf16[256,2048]{1,0:T(8,128)(2,1)S(1)}, bf16[256,2048]{1,0:T(8,128)(2,1)S(1)}, bf16[256,1024]{1,0:T(8,128)(2,1)S(1)}) custom-call(bf16[256,1024]{1,0:T(8,128)(2,1)S(1)} %collective-permute-done.2.x_ref.refs_9_, bf16[1024,2048]{1,0:T(8,128)(2,1)S(1)} %copy-done, bf16[1,2048]{1,0:T(2,128)(2,1)S(1)} %reshape.103.b_ref, ...), custom_call_target="tpu_custom_call" | custom-call | flops 1024 | bytes 1024 | tf_op jit(solution)/shard_map/ffn_forward/pallas_call | solution.py:804
  78.2 1.8 collective-permute-start.4
  80.0 4.3 %collective-permute-done.5.x_ref.refs_11_ = bf16[256,1024]{1,0:T(8,128)(2,1)S(1)} collective-permute-done((bf16[256,1024]{1,0:T(8,128)(2,1)S(1)}, bf16[256,1024]{1,0:T(8,128)(2,1)S(1)}, u32[]{:S(2)}, u32[]{:S(2)}) %collective-permute-start.5) | collective-permute-done | bytes 524320 | tf_op jit(solution)/shard_map/ppermute | solution.py:361
  84.3 5.1 %ffn_forward.7 = (bf16[256,2048]{1,0:T(8,128)(2,1)S(1)}, bf16[256,2048]{1,0:T(8,128)(2,1)S(1)}, bf16[256,1024]{1,0:T(8,128)(2,1)S(1)}) custom-call(bf16[256,1024]{1,0:T(8,128)(2,1)S(1)} %collective-permute-done.5.x_ref.refs_11_, bf16[1024,2048]{1,0:T(8,128)(2,1)S(1)} %copy-done, bf16[1,2048]{1,0:T(2,128)(2,1)S(1)} %reshape.103.b_ref, ...), custom_call_target="tpu_custom_call" | custom-call | flops 1024 | bytes 1024 | tf_op jit(solution)/shard_map/ffn_forward/pallas_call | solution.py:804
  89.4 1.8 collective-permute-start.6
  91.3 4.3 %collective-permute-done.4.refs_1_ = bf16[256,1024]{1,0:T(8,128)(2,1)S(1)} collective-permute-done((bf16[256,1024]{1,0:T(8,128)(2,1)S(1)}, bf16[256,1024]{1,0:T(8,128)(2,1)S(1)}, u32[]{:S(2)}, u32[]{:S(2)}) %collective-permute-start.4) | collective-permute-done | bytes 524320 | tf_op jit(solution)/shard_map/ppermute | solution.py:368
  95.6 1.6 norm_two.2
  97.2 1.8 collective-permute-start.8
  99.0 7.8 %collective-permute-done.6.refs_1_ = bf16[256,1024]{1,0:T(8,128)(2,1)S(1)} collective-permute-done((bf16[256,1024]{1,0:T(8,128)(2,1)S(1)}, bf16[256,1024]{1,0:T(8,128)(2,1)S(1)}, u32[]{:S(2)}, u32[]{:S(2)}) %collective-permute-start.6) | collective-permute-done | bytes 524320 | tf_op jit(solution)/shard_map/ppermute | solution.py:368
  108.0 1.8 collective-permute-start.7
  109.8 4.3 %ffn_back.4 = (bf16[256,2048]{1,0:T(8,128)(2,1)S(1)}, f32[1,2048]{1,0:T(1,128)S(1)}, f32[256,1024]{1,0:T(8,128)S(1)}) custom-call(bf16[256,1024]{1,0:T(8,128)(2,1)S(1)} %get-tuple-element.419.g_ref.refs_4_.refs_2_, bf16[256,2048]{1,0:T(8,128)(2,1)S(1)} %get-tuple-element.370.slope_ref, bf16[2048,1024]{1,0:T(8,128)(2,1)S(1)} %copy-done.1, ...), custom_call_target="tpu_custom_call" | custom-call | flops 1024 | bytes 1024 | tf_op jit(solution)/shard_map/ffn_back/pallas_call | solution.py:839
  114.1 4.3 %ffn_back.5 = (bf16[256,2048]{1,0:T(8,128)(2,1)S(1)}, f32[1,2048]{1,0:T(1,128)S(1)}, f32[256,1024]{1,0:T(8,128)S(1)}) custom-call(bf16[256,1024]{1,0:T(8,128)(2,1)S(1)} %get-tuple-element.425.g_ref.refs_6_.refs_2_, bf16[256,2048]{1,0:T(8,128)(2,1)S(1)} %get-tuple-element.373.slope_ref, bf16[2048,1024]{1,0:T(8,128)(2,1)S(1)} %copy-done.1, ...), custom_call_target="tpu_custom_call" | custom-call | flops 1024 | bytes 1024 | tf_op jit(solution)/shard_map/ffn_back/pallas_call | solution.py:839
  118.3 4.2 %ffn_back.6 = (bf16[256,2048]{1,0:T(8,128)(2,1)S(1)}, f32[1,2048]{1,0:T(1,128)S(1)}, bf16[256,1024]{1,0:T(8,128)(2,1)S(1)}) custom-call(bf16[256,1024]{1,0:T(8,128)(2,1)S(1)} %collective-permute-done.8.g_ref.refs_5_, bf16[256,2048]{1,0:T(8,128)(2,1)S(1)} %get-tuple-element.381.slope_ref, bf16[2048,1024]{1,0:T(8,128)(2,1)S(1)} %copy-done.1, ...), custom_call_target="tpu_custom_call" | custom-call | flops 1024 | bytes 1024 | tf_op jit(solution)/shard_map/ffn_back/pallas_call | solution.py:839
  124.1 5.2 %collective-permute-done.7.g_ref.refs_7_ = bf16[256,1024]{1,0:T(8,128)(2,1)S(1)} collective-permute-done((bf16[256,1024]{1,0:T(8,128)(2,1)S(1)}, bf16[256,1024]{1,0:T(8,128)(2,1)S(1)}, u32[]{:S(2)}, u32[]{:S(2)}) %collective-permute-start.7) | collective-permute-done | bytes 524320 | tf_op jit(solution)/shard_map/ppermute | solution.py:361
  129.3 4.2 %ffn_back.7 = (bf16[256,2048]{1,0:T(8,128)(2,1)S(1)}, f32[1,2048]{1,0:T(1,128)S(1)}, bf16[256,1024]{1,0:T(8,128)(2,1)S(1)}) custom-call(bf16[256,1024]{1,0:T(8,128)(2,1)S(1)} %collective-permute-done.7.g_ref.refs_7_, bf16[256,2048]{1,0:T(8,128)(2,1)S(1)} %get-tuple-element.384.slope_ref, bf16[2048,1024]{1,0:T(8,128)(2,1)S(1)} %copy-done.1, ...), custom_call_target="tpu_custom_call" | custom-call | flops 1024 | bytes 1024 | tf_op jit(solution)/shard_map/ffn_back/pallas_call | solution.py:839
  133.5 1.8 collective-permute-start.9
  135.3 13.8 %grad_halves.3 = (bf16[8,128,2048]{2,1,0:T(8,128)(2,1)}, bf16[8,128,2048]{2,1,0:T(8,128)(2,1)S(1)}) custom-call(s32[4]{0:T(128)S(1)} %pad_add_fusion.table_ref, bf16[256,2048]{1,0:T(8,128)(2,1)S(1)} %get-tuple-element.400.refs_0_, bf16[256,2048]{1,0:T(8,128)(2,1)S(1)} %get-tuple-element.401.refs_1_, bf16[256,2048]{1,0:T(8,128)(2,1)S(1)} %get-tuple-element.402.refs_2_, ...), custom_call_target="tpu_custom_call" | custom-call | flops 1024 | bytes 1024 | tf_op jit(solution)/shard_map/grad_halves/pallas_call | solution.py:650
  153.5 4.9 %collective-permute-done.13.moved_ref = bf16[8,128,2048]{2,1,0:T(8,128)(2,1)S(1)} collective-permute-done((bf16[8,128,2048]{2,1,0:T(8,128)(2,1)}, bf16[8,128,2048]{2,1,0:T(8,128)(2,1)S(1)}, u32[]{:S(2)}, u32[]{:S(2)}) %collective-permute-start.13) | collective-permute-done | bytes 4194336 | tf_op jit(solution)/shard_map/ppermute | solution.py:403
  159.0 1.6 collective-permute-start.15
  163.1 2.7 collective-permute-done.12.x_ref.refs_7_
  168.2 1.6 collective-permute-start.17
  171.2 10.8 %attend_back.2 = (bf16[512,512]{1,0:T(8,128)(2,1)S(1)}, f32[1024,512]{1,0:T(8,128)S(1)}, f32[1024,512]{1,0:T(8,128)S(1)}) custom-call(s32[4]{0:T(128)S(1)} %pad_add_fusion.table_ref, s32[8,42]{1,0:T(8,128)S(1)} %copy.40.rb_ref, bf16[1024,1536]{1,0:T(8,128)(2,1)S(1)} %pad_maximum_fusion.q_ref.k_ref.v_ref, ...), custom_call_target="tpu_custom_call" | custom-call | flops 1024 | bytes 1024 | tf_op jit(solution)/shard_map/attend_back/pallas_call | solution.py:324
  183.3 1.6 collective-permute-start.20
  187.6 11.6 %attend_back.3 = (bf16[1024,1536]{1,0:T(8,128)(2,1)S(1)}, f32[8,1024]{1,0:T(8,128)S(1)}) custom-call(s32[4]{0:T(128)S(1)} %pad_add_fusion.table_ref, s32[8,42]{1,0:T(8,128)S(1)} %copy.40.rb_ref, bf16[1024,1536]{1,0:T(8,128)(2,1)S(1)} %pad_maximum_fusion.q_ref.k_ref.v_ref, bf16[1024,1536]{1,0:T(8,128)(2,1)S(1)} %pad_maximum_fusion.q_ref.k_ref.v_ref, ...), custom_call_target="tpu_custom_call" | custom-call | flops 1024 | bytes 1024 | tf_op jit(solution)/shard_map/attend_back/pallas_call | solution.py:324
  199.2 3.1 grad_halves.5
  204.0 2.1 product.18
  206.9 1.5 collective-permute-start.32
  208.9 3.1 grad_halves.4.kept_ref
  213.3 2.2 product.19
  215.4 5.5 %collective-permute-done.32.refs_1_ = bf16[128,2048]{1,0:T(8,128)(2,1)S(1)} collective-permute-done((bf16[128,2048]{1,0:T(8,128)(2,1)S(1)}, bf16[128,2048]{1,0:T(8,128)(2,1)S(1)}, u32[]{:S(2)}, u32[]{:S(2)}) %collective-permute-start.32) | collective-permute-done | bytes 524320 | tf_op jit(solution)/shard_map/ppermute | solution.py:400
  223.0 1.6 collective-permute-start.34
  227.1 13.1 %collective-permute-done.24.refs_0_ = bf16[32,2176]{1,0:T(8,128)(2,1)S(1)} collective-permute-done((bf16[32,2176]{1,0:T(8,128)(2,1)S(1)}, bf16[32,2176]{1,0:T(8,128)(2,1)S(1)}, u32[]{:S(2)}, u32[]{:S(2)}) %collective-permute-start.24) | collective-permute-done | bytes 139296 | tf_op jit(solution)/shard_map/ppermute | solution.py:400
  241.7 1.6 add_convert_fusion
  243.7 1.6 collective-permute-start.36
  245.7 1.6 collective-permute-start.28
  247.3 13.6 %collective-permute-done.25.refs_0_ = bf16[64,2176]{1,0:T(8,128)(2,1)S(1)} collective-permute-done((bf16[64,2176]{1,0:T(8,128)(2,1)S(1)}, bf16[64,2176]{1,0:T(8,128)(2,1)S(1)}, u32[]{:S(2)}, u32[]{:S(2)}) %collective-permute-start.25) | collective-permute-done | bytes 278560 | tf_op jit(solution)/shard_map/ppermute | solution.py:400
  264.9 1.6 collective-permute-start.38
  266.5 12.7 %collective-permute-done.26.refs_0_ = bf16[64,2176]{1,0:T(8,128)(2,1)S(1)} collective-permute-done((bf16[64,2176]{1,0:T(8,128)(2,1)S(1)}, bf16[64,2176]{1,0:T(8,128)(2,1)S(1)}, u32[]{:S(2)}, u32[]{:S(2)}) %collective-permute-start.26) | collective-permute-done | bytes 278560 | tf_op jit(solution)/shard_map/ppermute | solution.py:400
  280.6 1.9 collective-permute-start.30
  283.4 1.6 collective-permute-start.44
  285.1 3.6 %collective-permute-done.30.refs_1_ = bf16[64,2176]{1,0:T(8,128)(2,1)S(1)} collective-permute-done((bf16[64,2176]{1,0:T(8,128)(2,1)S(1)}, bf16[64,2176]{1,0:T(8,128)(2,1)S(1)}, u32[]{:S(2)}, u32[]{:S(2)}) %collective-permute-start.30) | collective-permute-done | bytes 278560 | tf_op jit(solution)/shard_map/ppermute | solution.py:400
  291.2 1.6 collective-permute-start.40
  293.3 1.7 collective-permute-done.43.refs_0_
  295.6 4.8 %collective-permute-done.40.refs_5_ = bf16[64,2176]{1,0:T(8,128)(2,1)S(1)} collective-permute-done((bf16[64,2176]{1,0:T(8,128)(2,1)S(1)}, bf16[64,2176]{1,0:T(8,128)(2,1)S(1)}, u32[]{:S(2)}, u32[]{:S(2)}) %collective-permute-start.40) | collective-permute-done | bytes 278560 | tf_op jit(solution)/shard_map/ppermute | solution.py:400
  302.1 1.6 collective-permute-start.42
  303.7 1.5 collective-permute-done.53.refs_17_
  305.2 4.6 %place_pieces.3 = f32[2,8,128,1024]{3,2,1,0:T(8,128)} custom-call(s32[4]{0:T(128)S(1)} %pad_add_fusion.table_ref, bf16[64,2048]{1,0:T(8,128)(2,1)S(1)} %collective-permute-done.43.refs_0_, bf16[128,2048]{1,0:T(8,128)(2,1)S(1)} %collective-permute-done.37.refs_1_, bf16[128,2048]{1,0:T(8,128)(2,1)S(1)} %collective-permute-done.35.refs_2_, ...), custom_call_target="tpu_custom_call" | custom-call | flops 1024 | bytes 1024 | tf_op jit(solution)/shard_map/place_pieces/pallas_call | solution.py:533
  313.4 4.6 %place_pieces.4 = f32[2,8,64,2048]{3,2,1,0:T(8,128)} custom-call(s32[4]{0:T(128)S(1)} %pad_add_fusion.table_ref, bf16[64,2048]{1,0:T(8,128)(2,1)S(1)} %collective-permute-done.43.refs_0_, bf16[128,2048]{1,0:T(8,128)(2,1)S(1)} %collective-permute-done.37.refs_1_, bf16[128,2048]{1,0:T(8,128)(2,1)S(1)} %collective-permute-done.35.refs_2_, ...), custom_call_target="tpu_custom_call" | custom-call | flops 1024 | bytes 1024 | tf_op jit(solution)/shard_map/place_pieces/pallas_call | solution.py:533
  321.6 3.6 %collective-permute-done.57.refs_8_ = bf16[32,2176]{1,0:T(8,128)(2,1)S(1)} collective-permute-done((bf16[32,2176]{1,0:T(8,128)(2,1)S(1)}, bf16[32,2176]{1,0:T(8,128)(2,1)S(1)}, u32[]{:S(2)}, u32[]{:S(2)}) %collective-permute-start.57) | collective-permute-done | bytes 139296 | tf_op jit(solution)/shard_map/ppermute | solution.py:400
  328.3 4.2 %place_pieces.5 = (f32[2,8,64,512]{3,2,1,0:T(8,128)}, f32[2,8,64,512]{3,2,1,0:T(8,128)}, f32[2,8,64,512]{3,2,1,0:T(8,128)}, f32[2,8,8,128]{3,2,1,0:T(8,128)S(1)}, f32[2,8,32,1024]{3,2,1,0:T(8,128)}) custom-call(s32[4]{0:T(128)S(1)} %pad_add_fusion.table_ref, bf16[32,2176]{1,0:T(8,128)(2,1)S(1)} %collective-permute-done.56.refs_0_, ...), custom_call_target="tpu_custom_call" | custom-call | flops 1024 | bytes 1024 | tf_op jit(solution)/shard_map/place_pieces/pallas_call | solution.py:533
  (181 shorter events, 62.7 us)
Async XLA Ops:
  0.7 26.4 %collective-permute-start = (bf16[512,1024]{1,0:T(8,128)(2,1)}, bf16[512,1024]{1,0:T(8,128)(2,1)S(1)}, u32[]{:S(2)}, u32[]{:S(2)}) collective-permute-start(bf16[512,1024]{1,0:T(8,128)(2,1)} %bitcast.41), channel_id=1, source_target_pairs={{1,0},{0,1},{3,2},{2,3},{5,4},{4,5},{7,6},{6,7},{9,8},{8,9},{11,10... | collective-permute-start | bytes 3145736 | tf_op jit(solution)/shard_map/ppermute | solution.py:361
  35.7 14.9 %collective-permute-start.1 = (bf16[256,1024]{1,0:T(8,128)(2,1)S(1)}, bf16[256,1024]{1,0:T(8,128)(2,1)S(1)}, u32[]{:S(2)}, u32[]{:S(2)}) collective-permute-start(bf16[256,1024]{1,0:T(8,128)(2,1)S(1)} %product.10), channel_id=1, source_target_pairs={{0,1},{1,0},{2,3},{3,2},{4,5},{5,4},{6,7},{7,6},{8,9},{9,8},{10,11... | collective-permute-start | bytes 1572872 | tf_op jit(solution)/shard_map/ppermute | solution.py:368
  43.9 18.0 %collective-permute-start.3 = (bf16[256,1024]{1,0:T(8,128)(2,1)S(1)}, bf16[256,1024]{1,0:T(8,128)(2,1)S(1)}, u32[]{:S(2)}, u32[]{:S(2)}) collective-permute-start(bf16[256,1024]{1,0:T(8,128)(2,1)S(1)} %product.11), channel_id=1, source_target_pairs={{0,1},{1,0},{2,3},{3,2},{4,5},{5,4},{6,7},{7,6},{8,9},{9,8},{10,11... | collective-permute-start | bytes 1572872 | tf_op jit(solution)/shard_map/ppermute | solution.py:368
  51.4 21.7 %collective-permute-start.2 = (bf16[256,1024]{1,0:T(8,128)(2,1)S(1)}, bf16[256,1024]{1,0:T(8,128)(2,1)S(1)}, u32[]{:S(2)}, u32[]{:S(2)}) collective-permute-start(bf16[256,1024]{1,0:T(8,128)(2,1)S(1)} %get-tuple-element.408.x_ref.refs_2_.refs_8_), channel_id=1, source_target_pairs={{1,0},{0,1},{3,2},{2,3},{5,4},{4,5},{7,6},{6,7},{9,8},{8,9},{11,10... | collective-permute-start | bytes 1572872 | tf_op jit(solution)/shard_map/ppermute | solution.py:361
  62.7 21.7 %collective-permute-start.5 = (bf16[256,1024]{1,0:T(8,128)(2,1)S(1)}, bf16[256,1024]{1,0:T(8,128)(2,1)S(1)}, u32[]{:S(2)}, u32[]{:S(2)}) collective-permute-start(bf16[256,1024]{1,0:T(8,128)(2,1)S(1)} %get-tuple-element.410.x_ref.refs_2_.refs_10_), channel_id=1, source_target_pairs={{1,0},{0,1},{3,2},{2,3},{5,4},{4,5},{7,6},{6,7},{9,8},{8,9},{11,10... | collective-permute-start | bytes 1572872 | tf_op jit(solution)/shard_map/ppermute | solution.py:361
  78.2 17.3 %collective-permute-start.4 = (bf16[256,1024]{1,0:T(8,128)(2,1)S(1)}, bf16[256,1024]{1,0:T(8,128)(2,1)S(1)}, u32[]{:S(2)}, u32[]{:S(2)}) collective-permute-start(bf16[256,1024]{1,0:T(8,128)(2,1)S(1)} %get-tuple-element.352), channel_id=1, source_target_pairs={{0,1},{1,0},{2,3},{3,2},{4,5},{5,4},{6,7},{7,6},{8,9},{9,8},{10,11... | collective-permute-start | bytes 1572872 | tf_op jit(solution)/shard_map/ppermute | solution.py:368
  89.4 17.4 %collective-permute-start.6 = (bf16[256,1024]{1,0:T(8,128)(2,1)S(1)}, bf16[256,1024]{1,0:T(8,128)(2,1)S(1)}, u32[]{:S(2)}, u32[]{:S(2)}) collective-permute-start(bf16[256,1024]{1,0:T(8,128)(2,1)S(1)} %get-tuple-element.354), channel_id=1, source_target_pairs={{0,1},{1,0},{2,3},{3,2},{4,5},{5,4},{6,7},{7,6},{8,9},{9,8},{10,11... | collective-permute-start | bytes 1572872 | tf_op jit(solution)/shard_map/ppermute | solution.py:368
  97.2 21.1 %collective-permute-start.8 = (bf16[256,1024]{1,0:T(8,128)(2,1)S(1)}, bf16[256,1024]{1,0:T(8,128)(2,1)S(1)}, u32[]{:S(2)}, u32[]{:S(2)}) collective-permute-start(bf16[256,1024]{1,0:T(8,128)(2,1)S(1)} %get-tuple-element.419.g_ref.refs_4_.refs_2_), channel_id=1, source_target_pairs={{1,0},{0,1},{3,2},{2,3},{5,4},{4,5},{7,6},{6,7},{9,8},{8,9},{11,10... | collective-permute-start | bytes 1572872 | tf_op jit(solution)/shard_map/ppermute | solution.py:361
  108.0 21.3 %collective-permute-start.7 = (bf16[256,1024]{1,0:T(8,128)(2,1)S(1)}, bf16[256,1024]{1,0:T(8,128)(2,1)S(1)}, u32[]{:S(2)}, u32[]{:S(2)}) collective-permute-start(bf16[256,1024]{1,0:T(8,128)(2,1)S(1)} %get-tuple-element.425.g_ref.refs_6_.refs_2_), channel_id=1, source_target_pairs={{1,0},{0,1},{3,2},{2,3},{5,4},{4,5},{7,6},{6,7},{9,8},{8,9},{11,10... | collective-permute-start | bytes 1572872 | tf_op jit(solution)/shard_map/ppermute | solution.py:361
  122.6 26.6 %collective-permute-start.10 = (bf16[256,1024]{1,0:T(8,128)(2,1)S(1)}, bf16[256,1024]{1,0:T(8,128)(2,1)S(1)}, u32[]{:S(2)}, u32[]{:S(2)}) collective-permute-start(bf16[256,1024]{1,0:T(8,128)(2,1)S(1)} %get-tuple-element.389), channel_id=1, source_target_pairs={{0,1},{1,0},{2,3},{3,2},{4,5},{5,4},{6,7},{7,6},{8,9},{9,8},{10,11... | collective-permute-start | bytes 1572872 | tf_op jit(solution)/shard_map/ppermute | solution.py:368
  133.5 16.5 %collective-permute-start.9 = (bf16[256,1024]{1,0:T(8,128)(2,1)S(1)}, bf16[256,1024]{1,0:T(8,128)(2,1)S(1)}, u32[]{:S(2)}, u32[]{:S(2)}) collective-permute-start(bf16[256,1024]{1,0:T(8,128)(2,1)S(1)} %get-tuple-element.385), channel_id=1, source_target_pairs={{0,1},{1,0},{2,3},{3,2},{4,5},{5,4},{6,7},{7,6},{8,9},{9,8},{10,11... | collective-permute-start | bytes 1572872 | tf_op jit(solution)/shard_map/ppermute | solution.py:368
  151.0 7.4 %collective-permute-start.13 = (bf16[8,128,2048]{2,1,0:T(8,128)(2,1)}, bf16[8,128,2048]{2,1,0:T(8,128)(2,1)S(1)}, u32[]{:S(2)}, u32[]{:S(2)}) collective-permute-start(bf16[8,128,2048]{2,1,0:T(8,128)(2,1)} %get-tuple-element.433), channel_id=1, source_target_pairs={{0,2},{2,0},{4,6},{6,4},{8,10},{10,8},{12,14},{14,12},{16,18},{18,... | collective-permute-start | bytes 12582920 | tf_op jit(solution)/shard_map/ppermute | solution.py:403
  151.0 14.8 %collective-permute-start.12 = (bf16[256,1024]{1,0:T(8,128)(2,1)S(1)}, bf16[256,1024]{1,0:T(8,128)(2,1)S(1)}, u32[]{:S(2)}, u32[]{:S(2)}) collective-permute-start(bf16[256,1024]{1,0:T(8,128)(2,1)S(1)} %get-tuple-element.537.x_ref.refs_6_), channel_id=1, source_target_pairs={{1,0},{0,1},{3,2},{2,3},{5,4},{4,5},{7,6},{6,7},{9,8},{8,9},{11,10... | collective-permute-start | bytes 1572872 | tf_op jit(solution)/shard_map/ppermute | solution.py:361
  159.0 8.4 %collective-permute-start.15 = (bf16[64,2048]{1,0:T(8,128)(2,1)S(1)}, bf16[64,2048]{1,0:T(8,128)(2,1)S(1)}, u32[]{:S(2)}, u32[]{:S(2)}) collective-permute-start(bf16[64,2048]{1,0:T(8,128)(2,1)S(1)} %ring_add.18), channel_id=1, source_target_pairs={{0,8},{2,10},{8,16},{10,18},{16,24},{18,26},{24,28},{26,30},{28,20... | collective-permute-start | bytes 786440 | tf_op jit(solution)/shard_map/ppermute | solution.py:400
  161.3 8.6 %collective-permute-start.14 = (bf16[64,2048]{1,0:T(8,128)(2,1)S(1)}, bf16[64,2048]{1,0:T(8,128)(2,1)S(1)}, u32[]{:S(2)}, u32[]{:S(2)}) collective-permute-start(bf16[64,2048]{1,0:T(8,128)(2,1)S(1)} %ring_add.19), channel_id=1, source_target_pairs={{0,4},{2,6},{8,0},{10,2},{16,8},{18,10},{24,16},{26,18},{28,24},{3... | collective-permute-start | bytes 786440 | tf_op jit(solution)/shard_map/ppermute | solution.py:400
  161.8 20.3 %collective-permute-start.11 = (bf16[256,1024]{1,0:T(8,128)(2,1)S(1)}, bf16[256,1024]{1,0:T(8,128)(2,1)S(1)}, u32[]{:S(2)}, u32[]{:S(2)}) collective-permute-start(bf16[256,1024]{1,0:T(8,128)(2,1)S(1)} %get-tuple-element.538.x_ref.refs_8_), channel_id=1, source_target_pairs={{1,0},{0,1},{3,2},{2,3},{5,4},{4,5},{7,6},{6,7},{9,8},{8,9},{11,10... | collective-permute-start | bytes 1572872 | tf_op jit(solution)/shard_map/ppermute | solution.py:361
  168.2 14.3 %collective-permute-start.17 = (bf16[128,2048]{1,0:T(8,128)(2,1)S(1)}, bf16[128,2048]{1,0:T(8,128)(2,1)S(1)}, u32[]{:S(2)}, u32[]{:S(2)}) collective-permute-start(bf16[128,2048]{1,0:T(8,128)(2,1)S(1)} %ring_add.20), channel_id=1, source_target_pairs={{0,8},{2,10},{8,16},{10,18},{16,24},{18,26},{24,28},{26,30},{28,20... | collective-permute-start | bytes 1572872 | tf_op jit(solution)/shard_map/ppermute | solution.py:400
  170.7 14.3 %collective-permute-start.16 = (bf16[128,2048]{1,0:T(8,128)(2,1)S(1)}, bf16[128,2048]{1,0:T(8,128)(2,1)S(1)}, u32[]{:S(2)}, u32[]{:S(2)}) collective-permute-start(bf16[128,2048]{1,0:T(8,128)(2,1)S(1)} %ring_add.21), channel_id=1, source_target_pairs={{0,4},{2,6},{8,0},{10,2},{16,8},{18,10},{24,16},{26,18},{28,24},{3... | collective-permute-start | bytes 1572872 | tf_op jit(solution)/shard_map/ppermute | solution.py:400
  183.3 19.0 %collective-permute-start.20 = (bf16[128,2048]{1,0:T(8,128)(2,1)S(1)}, bf16[128,2048]{1,0:T(8,128)(2,1)S(1)}, u32[]{:S(2)}, u32[]{:S(2)}) collective-permute-start(bf16[128,2048]{1,0:T(8,128)(2,1)S(1)} %ring_add.22), channel_id=1, source_target_pairs={{0,8},{2,10},{8,16},{10,18},{16,24},{18,26},{24,28},{26,30},{28,20... | collective-permute-start | bytes 1572872 | tf_op jit(solution)/shard_map/ppermute | solution.py:400
  185.7 17.4 %collective-permute-start.19 = (bf16[128,2048]{1,0:T(8,128)(2,1)S(1)}, bf16[128,2048]{1,0:T(8,128)(2,1)S(1)}, u32[]{:S(2)}, u32[]{:S(2)}) collective-permute-start(bf16[128,2048]{1,0:T(8,128)(2,1)S(1)} %ring_add.23), channel_id=1, source_target_pairs={{0,4},{2,6},{8,0},{10,2},{16,8},{18,10},{24,16},{26,18},{28,24},{3... | collective-permute-start | bytes 1572872 | tf_op jit(solution)/shard_map/ppermute | solution.py:400
  186.2 13.0 %collective-permute-start.18 = (f32[8,1024]{1,0:T(8,128)S(1)}, f32[8,1024]{1,0:T(8,128)S(1)}, u32[]{:S(2)}, u32[]{:S(2)}) collective-permute-start(f32[8,1024]{1,0:T(8,128)S(1)} %sum_kernel.1.refs_0_), channel_id=1, source_target_pairs={{1,0},{0,1},{3,2},{2,3},{5,4},{4,5},{7,6},{6,7},{9,8},{8,9},{11,10... | collective-permute-start | bytes 98312 | tf_op jit(solution)/shard_map/ppermute | solution.py:361
  204.0 8.1 %collective-permute-start.21 = (bf16[8,64,2176]{2,1,0:T(8,128)(2,1)S(1)}, bf16[8,64,2176]{2,1,0:T(8,128)(2,1)S(1)}, u32[]{:S(2)}, u32[]{:S(2)}) collective-permute-start(bf16[8,64,2176]{2,1,0:T(8,128)(2,1)S(1)} %grad_halves.5), channel_id=1, source_target_pairs={{0,2},{2,0},{4,6},{6,4},{8,10},{10,8},{12,14},{14,12},{16,18},{18,... | collective-permute-start | bytes 6684680 | tf_op jit(solution)/shard_map/ppermute | solution.py:403
  206.2 35.5 %collective-permute-start.22 = (bf16[512,1024]{1,0:T(8,128)(2,1)S(1)}, bf16[512,1024]{1,0:T(8,128)(2,1)S(1)}, u32[]{:S(2)}, u32[]{:S(2)}) collective-permute-start(bf16[512,1024]{1,0:T(8,128)(2,1)S(1)} %product.18), channel_id=1, source_target_pairs={{0,1},{1,0},{2,3},{3,2},{4,5},{5,4},{6,7},{7,6},{8,9},{9,8},{10,11... | collective-permute-start | bytes 3145736 | tf_op jit(solution)/shard_map/ppermute | solution.py:368
  206.9 14.0 %collective-permute-start.32 = (bf16[128,2048]{1,0:T(8,128)(2,1)S(1)}, bf16[128,2048]{1,0:T(8,128)(2,1)S(1)}, u32[]{:S(2)}, u32[]{:S(2)}) collective-permute-start(bf16[128,2048]{1,0:T(8,128)(2,1)S(1)} %ring_add.25), channel_id=1, source_target_pairs={{0,4},{2,6},{8,0},{10,2},{16,8},{18,10},{24,16},{26,18},{28,24},{3... | collective-permute-start | bytes 1572872 | tf_op jit(solution)/shard_map/ppermute | solution.py:400
  208.4 13.7 %collective-permute-start.31 = (bf16[128,2048]{1,0:T(8,128)(2,1)S(1)}, bf16[128,2048]{1,0:T(8,128)(2,1)S(1)}, u32[]{:S(2)}, u32[]{:S(2)}) collective-permute-start(bf16[128,2048]{1,0:T(8,128)(2,1)S(1)} %ring_add.24), channel_id=1, source_target_pairs={{0,8},{2,10},{8,16},{10,18},{16,24},{18,26},{24,28},{26,30},{28,20... | collective-permute-start | bytes 1572872 | tf_op jit(solution)/shard_map/ppermute | solution.py:400
  223.0 20.2 %collective-permute-start.34 = (bf16[128,2048]{1,0:T(8,128)(2,1)S(1)}, bf16[128,2048]{1,0:T(8,128)(2,1)S(1)}, u32[]{:S(2)}, u32[]{:S(2)}) collective-permute-start(bf16[128,2048]{1,0:T(8,128)(2,1)S(1)} %ring_add.34.refs_4_), channel_id=1, source_target_pairs={{0,4},{2,6},{8,0},{10,2},{16,8},{18,10},{24,16},{26,18},{28,24},{3... | collective-permute-start | bytes 1572872 | tf_op jit(solution)/shard_map/ppermute | solution.py:400
  224.7 18.6 %collective-permute-start.33 = (bf16[128,2048]{1,0:T(8,128)(2,1)S(1)}, bf16[128,2048]{1,0:T(8,128)(2,1)S(1)}, u32[]{:S(2)}, u32[]{:S(2)}) collective-permute-start(bf16[128,2048]{1,0:T(8,128)(2,1)S(1)} %ring_add.34.refs_4_), channel_id=1, source_target_pairs={{0,8},{2,10},{8,16},{10,18},{16,24},{18,26},{24,28},{26,30},{28,20... | collective-permute-start | bytes 1572872 | tf_op jit(solution)/shard_map/ppermute | solution.py:400
  225.1 15.1 %collective-permute-start.24 = (bf16[32,2176]{1,0:T(8,128)(2,1)S(1)}, bf16[32,2176]{1,0:T(8,128)(2,1)S(1)}, u32[]{:S(2)}, u32[]{:S(2)}) collective-permute-start(bf16[32,2176]{1,0:T(8,128)(2,1)S(1)} %ring_add.26), channel_id=1, source_target_pairs={{0,8},{2,10},{8,16},{10,18},{16,24},{18,26},{24,28},{26,30},{28,20... | collective-permute-start | bytes 417800 | tf_op jit(solution)/shard_map/ppermute | solution.py:400
  225.6 15.3 %collective-permute-start.23 = (bf16[32,2176]{1,0:T(8,128)(2,1)S(1)}, bf16[32,2176]{1,0:T(8,128)(2,1)S(1)}, u32[]{:S(2)}, u32[]{:S(2)}) collective-permute-start(bf16[32,2176]{1,0:T(8,128)(2,1)S(1)} %ring_add.27), channel_id=1, source_target_pairs={{0,4},{2,6},{8,0},{10,2},{16,8},{18,10},{24,16},{26,18},{28,24},{3... | collective-permute-start | bytes 417800 | tf_op jit(solution)/shard_map/ppermute | solution.py:400
  243.3 19.1 %collective-permute-start.35 = (bf16[128,2048]{1,0:T(8,128)(2,1)S(1)}, bf16[128,2048]{1,0:T(8,128)(2,1)S(1)}, u32[]{:S(2)}, u32[]{:S(2)}) collective-permute-start(bf16[128,2048]{1,0:T(8,128)(2,1)S(1)} %collective-permute-done.33.refs_3_), channel_id=1, source_target_pairs={{0,8},{2,10},{8,16},{10,18},{16,24},{18,26},{24,28},{26,30},{28,20... | collective-permute-start | bytes 1572872 | tf_op jit(solution)/shard_map/ppermute | solution.py:400
  243.7 18.7 %collective-permute-start.36 = (bf16[128,2048]{1,0:T(8,128)(2,1)S(1)}, bf16[128,2048]{1,0:T(8,128)(2,1)S(1)}, u32[]{:S(2)}, u32[]{:S(2)}) collective-permute-start(bf16[128,2048]{1,0:T(8,128)(2,1)S(1)} %collective-permute-done.34.refs_5_), channel_id=1, source_target_pairs={{0,4},{2,6},{8,0},{10,2},{16,8},{18,10},{24,16},{26,18},{28,24},{3... | collective-permute-start | bytes 1572872 | tf_op jit(solution)/shard_map/ppermute | solution.py:400
  245.3 15.6 %collective-permute-start.25 = (bf16[64,2176]{1,0:T(8,128)(2,1)S(1)}, bf16[64,2176]{1,0:T(8,128)(2,1)S(1)}, u32[]{:S(2)}, u32[]{:S(2)}) collective-permute-start(bf16[64,2176]{1,0:T(8,128)(2,1)S(1)} %ring_add.28), channel_id=1, source_target_pairs={{0,8},{2,10},{8,16},{10,18},{16,24},{18,26},{24,28},{26,30},{28,20... | collective-permute-start | bytes 835592 | tf_op jit(solution)/shard_map/ppermute | solution.py:400
  245.7 15.9 %collective-permute-start.28 = (bf16[64,2176]{1,0:T(8,128)(2,1)S(1)}, bf16[64,2176]{1,0:T(8,128)(2,1)S(1)}, u32[]{:S(2)}, u32[]{:S(2)}) collective-permute-start(bf16[64,2176]{1,0:T(8,128)(2,1)S(1)} %ring_add.29), channel_id=1, source_target_pairs={{0,4},{2,6},{8,0},{10,2},{16,8},{18,10},{24,16},{26,18},{28,24},{3... | collective-permute-start | bytes 835592 | tf_op jit(solution)/shard_map/ppermute | solution.py:400
  262.4 20.5 %collective-permute-start.37 = (bf16[128,2048]{1,0:T(8,128)(2,1)S(1)}, bf16[128,2048]{1,0:T(8,128)(2,1)S(1)}, u32[]{:S(2)}, u32[]{:S(2)}) collective-permute-start(bf16[128,2048]{1,0:T(8,128)(2,1)S(1)} %collective-permute-done.35.refs_2_), channel_id=1, source_target_pairs={{0,8},{2,10},{8,16},{10,18},{16,24},{18,26},{24,28},{26,30},{28,20... | collective-permute-start | bytes 1572872 | tf_op jit(solution)/shard_map/ppermute | solution.py:400
  262.9 16.3 %collective-permute-start.26 = (bf16[64,2176]{1,0:T(8,128)(2,1)S(1)}, bf16[64,2176]{1,0:T(8,128)(2,1)S(1)}, u32[]{:S(2)}, u32[]{:S(2)}) collective-permute-start(bf16[64,2176]{1,0:T(8,128)(2,1)S(1)} %ring_add.30), channel_id=1, source_target_pairs={{0,8},{2,10},{8,16},{10,18},{16,24},{18,26},{24,28},{26,30},{28,20... | collective-permute-start | bytes 835592 | tf_op jit(solution)/shard_map/ppermute | solution.py:400
  264.3 15.6 %collective-permute-start.29 = (bf16[64,2176]{1,0:T(8,128)(2,1)S(1)}, bf16[64,2176]{1,0:T(8,128)(2,1)S(1)}, u32[]{:S(2)}, u32[]{:S(2)}) collective-permute-start(bf16[64,2176]{1,0:T(8,128)(2,1)S(1)} %ring_add.32), channel_id=1, source_target_pairs={{0,4},{2,6},{8,0},{10,2},{16,8},{18,10},{24,16},{26,18},{28,24},{3... | collective-permute-start | bytes 835592 | tf_op jit(solution)/shard_map/ppermute | solution.py:400
  264.9 18.5 %collective-permute-start.38 = (bf16[128,2048]{1,0:T(8,128)(2,1)S(1)}, bf16[128,2048]{1,0:T(8,128)(2,1)S(1)}, u32[]{:S(2)}, u32[]{:S(2)}) collective-permute-start(bf16[128,2048]{1,0:T(8,128)(2,1)S(1)} %collective-permute-done.36.refs_6_), channel_id=1, source_target_pairs={{0,4},{2,6},{8,0},{10,2},{16,8},{18,10},{24,16},{26,18},{28,24},{3... | collective-permute-start | bytes 1572872 | tf_op jit(solution)/shard_map/ppermute | solution.py:400
  280.6 8.1 %collective-permute-start.30 = (bf16[64,2176]{1,0:T(8,128)(2,1)S(1)}, bf16[64,2176]{1,0:T(8,128)(2,1)S(1)}, u32[]{:S(2)}, u32[]{:S(2)}) collective-permute-start(bf16[64,2176]{1,0:T(8,128)(2,1)S(1)} %ring_add.33), channel_id=1, source_target_pairs={{0,4},{2,6},{8,0},{10,2},{16,8},{18,10},{24,16},{26,18},{28,24},{3... | collective-permute-start | bytes 835592 | tf_op jit(solution)/shard_map/ppermute | solution.py:400
  282.5 8.0 %collective-permute-start.27 = (bf16[64,2176]{1,0:T(8,128)(2,1)S(1)}, bf16[64,2176]{1,0:T(8,128)(2,1)S(1)}, u32[]{:S(2)}, u32[]{:S(2)}) collective-permute-start(bf16[64,2176]{1,0:T(8,128)(2,1)S(1)} %ring_add.31), channel_id=1, source_target_pairs={{0,8},{2,10},{8,16},{10,18},{16,24},{18,26},{24,28},{26,30},{28,20... | collective-permute-start | bytes 835592 | tf_op jit(solution)/shard_map/ppermute | solution.py:400
  282.9 8.3 %collective-permute-start.49 = (bf16[128,2048]{1,0:T(8,128)(2,1)S(1)}, bf16[128,2048]{1,0:T(8,128)(2,1)S(1)}, u32[]{:S(2)}, u32[]{:S(2)}) collective-permute-start(bf16[128,2048]{1,0:T(8,128)(2,1)S(1)} %ring_add.34.refs_4_), channel_id=1, source_target_pairs={{0,2},{2,0},{4,6},{6,4},{8,10},{10,8},{12,14},{14,12},{16,18},{18,... | collective-permute-start | bytes 1572872 | tf_op jit(solution)/shard_map/ppermute | solution.py:403
  282.9 10.0 %collective-permute-start.48 = (bf16[128,2048]{1,0:T(8,128)(2,1)S(1)}, bf16[128,2048]{1,0:T(8,128)(2,1)S(1)}, u32[]{:S(2)}, u32[]{:S(2)}) collective-permute-start(bf16[128,2048]{1,0:T(8,128)(2,1)S(1)} %collective-permute-done.33.refs_3_), channel_id=1, source_target_pairs={{0,2},{2,0},{4,6},{6,4},{8,10},{10,8},{12,14},{14,12},{16,18},{18,... | collective-permute-start | bytes 1572872 | tf_op jit(solution)/shard_map/ppermute | solution.py:403
  283.4 9.9 %collective-permute-start.44 = (bf16[64,2048]{1,0:T(8,128)(2,1)S(1)}, bf16[64,2048]{1,0:T(8,128)(2,1)S(1)}, u32[]{:S(2)}, u32[]{:S(2)}) collective-permute-start(bf16[64,2048]{1,0:T(8,128)(2,1)S(1)} %slice.43), channel_id=1, source_target_pairs={{0,4},{2,6},{8,0},{10,2},{16,8},{18,10},{24,16},{26,18},{28,24},{3... | collective-permute-start | bytes 786440 | tf_op jit(solution)/shard_map/ppermute | solution.py:400
  288.7 6.4 %collective-permute-start.43 = (bf16[64,2048]{1,0:T(8,128)(2,1)S(1)}, bf16[64,2048]{1,0:T(8,128)(2,1)S(1)}, u32[]{:S(2)}, u32[]{:S(2)}) collective-permute-start(bf16[64,2048]{1,0:T(8,128)(2,1)S(1)} %slice.42), channel_id=1, source_target_pairs={{0,8},{2,10},{8,16},{10,18},{16,24},{18,26},{24,28},{26,30},{28,20... | collective-permute-start | bytes 786440 | tf_op jit(solution)/shard_map/ppermute | solution.py:400
  290.5 4.6 %collective-permute-start.50 = (bf16[128,2048]{1,0:T(8,128)(2,1)S(1)}, bf16[128,2048]{1,0:T(8,128)(2,1)S(1)}, u32[]{:S(2)}, u32[]{:S(2)}) collective-permute-start(bf16[128,2048]{1,0:T(8,128)(2,1)S(1)} %collective-permute-done.34.refs_5_), channel_id=1, source_target_pairs={{0,2},{2,0},{4,6},{6,4},{8,10},{10,8},{12,14},{14,12},{16,18},{18,... | collective-permute-start | bytes 1572872 | tf_op jit(solution)/shard_map/ppermute | solution.py:403
  291.2 9.1 %collective-permute-start.40 = (bf16[64,2176]{1,0:T(8,128)(2,1)S(1)}, bf16[64,2176]{1,0:T(8,128)(2,1)S(1)}, u32[]{:S(2)}, u32[]{:S(2)}) collective-permute-start(bf16[64,2176]{1,0:T(8,128)(2,1)S(1)} %ring_add.35.refs_4_), channel_id=1, source_target_pairs={{0,4},{2,6},{8,0},{10,2},{16,8},{18,10},{24,16},{26,18},{28,24},{3... | collective-permute-start | bytes 835592 | tf_op jit(solution)/shard_map/ppermute | solution.py:400
  292.9 8.8 %collective-permute-start.39 = (bf16[64,2176]{1,0:T(8,128)(2,1)S(1)}, bf16[64,2176]{1,0:T(8,128)(2,1)S(1)}, u32[]{:S(2)}, u32[]{:S(2)}) collective-permute-start(bf16[64,2176]{1,0:T(8,128)(2,1)S(1)} %ring_add.35.refs_4_), channel_id=1, source_target_pairs={{0,8},{2,10},{8,16},{10,18},{16,24},{18,26},{24,28},{26,30},{28,20... | collective-permute-start | bytes 835592 | tf_op jit(solution)/shard_map/ppermute | solution.py:400
  293.3 8.3 %collective-permute-start.47 = (bf16[128,2048]{1,0:T(8,128)(2,1)S(1)}, bf16[128,2048]{1,0:T(8,128)(2,1)S(1)}, u32[]{:S(2)}, u32[]{:S(2)}) collective-permute-start(bf16[128,2048]{1,0:T(8,128)(2,1)S(1)} %collective-permute-done.35.refs_2_), channel_id=1, source_target_pairs={{0,2},{2,0},{4,6},{6,4},{8,10},{10,8},{12,14},{14,12},{16,18},{18,... | collective-permute-start | bytes 1572872 | tf_op jit(solution)/shard_map/ppermute | solution.py:403
  295.0 7.1 %collective-permute-start.51 = (bf16[128,2048]{1,0:T(8,128)(2,1)S(1)}, bf16[128,2048]{1,0:T(8,128)(2,1)S(1)}, u32[]{:S(2)}, u32[]{:S(2)}) collective-permute-start(bf16[128,2048]{1,0:T(8,128)(2,1)S(1)} %collective-permute-done.36.refs_6_), channel_id=1, source_target_pairs={{0,2},{2,0},{4,6},{6,4},{8,10},{10,8},{12,14},{14,12},{16,18},{18,... | collective-permute-start | bytes 1572872 | tf_op jit(solution)/shard_map/ppermute | solution.py:403
  295.0 8.6 %collective-permute-start.45 = (bf16[64,2048]{1,0:T(8,128)(2,1)S(1)}, bf16[64,2048]{1,0:T(8,128)(2,1)S(1)}, u32[]{:S(2)}, u32[]{:S(2)}) collective-permute-start(bf16[64,2048]{1,0:T(8,128)(2,1)S(1)} %collective-permute-done.43.refs_0_), channel_id=1, source_target_pairs={{0,2},{2,0},{4,6},{6,4},{8,10},{10,8},{12,14},{14,12},{16,18},{18,... | collective-permute-start | bytes 786440 | tf_op jit(solution)/shard_map/ppermute | solution.py:403
  300.3 4.9 %collective-permute-start.46 = (bf16[128,2048]{1,0:T(8,128)(2,1)S(1)}, bf16[128,2048]{1,0:T(8,128)(2,1)S(1)}, u32[]{:S(2)}, u32[]{:S(2)}) collective-permute-start(bf16[128,2048]{1,0:T(8,128)(2,1)S(1)} %collective-permute-done.37.refs_1_), channel_id=1, source_target_pairs={{0,2},{2,0},{4,6},{6,4},{8,10},{10,8},{12,14},{14,12},{16,18},{18,... | collective-permute-start | bytes 1572872 | tf_op jit(solution)/shard_map/ppermute | solution.py:403
  301.6 3.6 %collective-permute-start.52 = (bf16[128,2048]{1,0:T(8,128)(2,1)S(1)}, bf16[128,2048]{1,0:T(8,128)(2,1)S(1)}, u32[]{:S(2)}, u32[]{:S(2)}) collective-permute-start(bf16[128,2048]{1,0:T(8,128)(2,1)S(1)} %collective-permute-done.38.refs_7_), channel_id=1, source_target_pairs={{0,2},{2,0},{4,6},{6,4},{8,10},{10,8},{12,14},{14,12},{16,18},{18,... | collective-permute-start | bytes 1572872 | tf_op jit(solution)/shard_map/ppermute | solution.py:403
  301.7 9.1 %collective-permute-start.41 = (bf16[64,2176]{1,0:T(8,128)(2,1)S(1)}, bf16[64,2176]{1,0:T(8,128)(2,1)S(1)}, u32[]{:S(2)}, u32[]{:S(2)}) collective-permute-start(bf16[64,2176]{1,0:T(8,128)(2,1)S(1)} %collective-permute-done.39.refs_3_), channel_id=1, source_target_pairs={{0,8},{2,10},{8,16},{10,18},{16,24},{18,26},{24,28},{26,30},{28,20... | collective-permute-start | bytes 835592 | tf_op jit(solution)/shard_map/ppermute | solution.py:400
  302.1 8.8 %collective-permute-start.42 = (bf16[64,2176]{1,0:T(8,128)(2,1)S(1)}, bf16[64,2176]{1,0:T(8,128)(2,1)S(1)}, u32[]{:S(2)}, u32[]{:S(2)}) collective-permute-start(bf16[64,2176]{1,0:T(8,128)(2,1)S(1)} %collective-permute-done.40.refs_5_), channel_id=1, source_target_pairs={{0,4},{2,6},{8,0},{10,2},{16,8},{18,10},{24,16},{26,18},{28,24},{3... | collective-permute-start | bytes 835592 | tf_op jit(solution)/shard_map/ppermute | solution.py:400
  310.9 8.1 %collective-permute-start.54 = (bf16[64,2176]{1,0:T(8,128)(2,1)S(1)}, bf16[64,2176]{1,0:T(8,128)(2,1)S(1)}, u32[]{:S(2)}, u32[]{:S(2)}) collective-permute-start(bf16[64,2176]{1,0:T(8,128)(2,1)S(1)} %collective-permute-done.41.refs_2_), channel_id=1, source_target_pairs={{0,8},{2,10},{8,16},{10,18},{16,24},{18,26},{24,28},{26,30},{28,20... | collective-permute-start | bytes 835592 | tf_op jit(solution)/shard_map/ppermute | solution.py:400
  311.8 7.7 %collective-permute-start.55 = (bf16[64,2176]{1,0:T(8,128)(2,1)S(1)}, bf16[64,2176]{1,0:T(8,128)(2,1)S(1)}, u32[]{:S(2)}, u32[]{:S(2)}) collective-permute-start(bf16[64,2176]{1,0:T(8,128)(2,1)S(1)} %collective-permute-done.42.refs_6_), channel_id=1, source_target_pairs={{0,4},{2,6},{8,0},{10,2},{16,8},{18,10},{24,16},{26,18},{28,24},{3... | collective-permute-start | bytes 835592 | tf_op jit(solution)/shard_map/ppermute | solution.py:400
  312.9 7.9 %collective-permute-start.62 = (bf16[64,2176]{1,0:T(8,128)(2,1)S(1)}, bf16[64,2176]{1,0:T(8,128)(2,1)S(1)}, u32[]{:S(2)}, u32[]{:S(2)}) collective-permute-start(bf16[64,2176]{1,0:T(8,128)(2,1)S(1)} %ring_add.35.refs_4_), channel_id=1, source_target_pairs={{0,2},{2,0},{4,6},{6,4},{8,10},{10,8},{12,14},{14,12},{16,18},{18,... | collective-permute-start | bytes 835592 | tf_op jit(solution)/shard_map/ppermute | solution.py:403
  312.9 8.7 %collective-permute-start.61 = (bf16[64,2176]{1,0:T(8,128)(2,1)S(1)}, bf16[64,2176]{1,0:T(8,128)(2,1)S(1)}, u32[]{:S(2)}, u32[]{:S(2)}) collective-permute-start(bf16[64,2176]{1,0:T(8,128)(2,1)S(1)} %collective-permute-done.39.refs_3_), channel_id=1, source_target_pairs={{0,2},{2,0},{4,6},{6,4},{8,10},{10,8},{12,14},{14,12},{16,18},{18,... | collective-permute-start | bytes 835592 | tf_op jit(solution)/shard_map/ppermute | solution.py:403
  313.4 12.9 %collective-permute-start.63 = (bf16[64,2176]{1,0:T(8,128)(2,1)S(1)}, bf16[64,2176]{1,0:T(8,128)(2,1)S(1)}, u32[]{:S(2)}, u32[]{:S(2)}) collective-permute-start(bf16[64,2176]{1,0:T(8,128)(2,1)S(1)} %collective-permute-done.40.refs_5_), channel_id=1, source_target_pairs={{0,2},{2,0},{4,6},{6,4},{8,10},{10,8},{12,14},{14,12},{16,18},{18,... | collective-permute-start | bytes 835592 | tf_op jit(solution)/shard_map/ppermute | solution.py:403
  319.0 7.8 %collective-permute-start.60 = (bf16[64,2176]{1,0:T(8,128)(2,1)S(1)}, bf16[64,2176]{1,0:T(8,128)(2,1)S(1)}, u32[]{:S(2)}, u32[]{:S(2)}) collective-permute-start(bf16[64,2176]{1,0:T(8,128)(2,1)S(1)} %collective-permute-done.41.refs_2_), channel_id=1, source_target_pairs={{0,2},{2,0},{4,6},{6,4},{8,10},{10,8},{12,14},{14,12},{16,18},{18,... | collective-permute-start | bytes 835592 | tf_op jit(solution)/shard_map/ppermute | solution.py:403
  319.5 5.7 %collective-permute-start.57 = (bf16[32,2176]{1,0:T(8,128)(2,1)S(1)}, bf16[32,2176]{1,0:T(8,128)(2,1)S(1)}, u32[]{:S(2)}, u32[]{:S(2)}) collective-permute-start(bf16[32,2176]{1,0:T(8,128)(2,1)S(1)} %slice.45), channel_id=1, source_target_pairs={{0,4},{2,6},{8,0},{10,2},{16,8},{18,10},{24,16},{26,18},{28,24},{3... | collective-permute-start | bytes 417800 | tf_op jit(solution)/shard_map/ppermute | solution.py:400
  320.9 5.5 %collective-permute-start.56 = (bf16[32,2176]{1,0:T(8,128)(2,1)S(1)}, bf16[32,2176]{1,0:T(8,128)(2,1)S(1)}, u32[]{:S(2)}, u32[]{:S(2)}) collective-permute-start(bf16[32,2176]{1,0:T(8,128)(2,1)S(1)} %slice.44), channel_id=1, source_target_pairs={{0,8},{2,10},{8,16},{10,18},{16,24},{18,26},{24,28},{26,30},{28,20... | collective-permute-start | bytes 417800 | tf_op jit(solution)/shard_map/ppermute | solution.py:400
  321.6 6.4 %collective-permute-start.64 = (bf16[64,2176]{1,0:T(8,128)(2,1)S(1)}, bf16[64,2176]{1,0:T(8,128)(2,1)S(1)}, u32[]{:S(2)}, u32[]{:S(2)}) collective-permute-start(bf16[64,2176]{1,0:T(8,128)(2,1)S(1)} %collective-permute-done.42.refs_6_), channel_id=1, source_target_pairs={{0,2},{2,0},{4,6},{6,4},{8,10},{10,8},{12,14},{14,12},{16,18},{18,... | collective-permute-start | bytes 835592 | tf_op jit(solution)/shard_map/ppermute | solution.py:403
  325.2 3.1 collective-permute-start.59
  326.3 2.0 collective-permute-start.65
  (16 other events, 129.8 us)

commit v5 on v4

--- a/solution.py
+++ b/solution.py
@@ -1238,13 +1238,18 @@
     up_rows = -(-hidden_units // width)
 
     def spread(value):
-        value = value.reshape(dp_size, width)
+        lines = width // 128
+
+        def rows(low, high):
+            return value[low * lines : high * lines].reshape(-1)
+
+        bias = rows(8 + up_rows, 9 + up_rows)
         return (
-            [value[i] for i in range(6)],
-            jnp.sqrt(value[6, :3] / entries),
-            value[8 + up_rows, :channels],
-            value[8 + up_rows, channels : 2 * channels],
-            value[8 : 8 + up_rows].reshape(-1)[:hidden_units],
+            [rows(i, i + 1) for i in range(6)],
+            jnp.sqrt(value[6 * lines, :3] / entries),
+            bias[:channels],
+            bias[channels : 2 * channels],
+            rows(8, 8 + up_rows)[:hidden_units],
         )
 
     while under_way:

time: 339 us -> 338 us (level)
  no operation moved by 1% of the time
where the time goes in v5:
time: 338 us; the launch traced here: 335 us
  Pallas kernels  133 us (39%)
  waiting for transfers between devices  127 us (38%)
  starting transfers between devices  59.6 us (18%)
  local copies, waits for them, and re-layouts  5.61 us (2%)
  other arithmetic  4.12 us (1%)
  matrix products  3.58 us (1%)
    ppermute x32, waiting for transfers between devices, shift(): return lax.ppermute(value, 'dp', pairs)  67.3 us
    ppermute x32, starting transfers between devices, shift(): return lax.ppermute(value, 'dp', pairs)  33.3 us
    ppermute x8, waiting for transfers between devices, fetch(): lax.ppermute(rows, 'tensor', [((k + s) % ranks, k) for k in range(ranks)])  32.9 us
    pallas_call x2, Pallas kernels, attend_back(): pl.pallas_call(functools.partial(attend_back_kernel, plan, 3, len(earlier...  22.4 us
    ppermute x7, waiting for transfers between devices, hand_over(): lax.ppermute(share, 'tensor', [(k, (k + s) % ranks) for k in range(ranks)])  20.4 us
    pallas_call x4, Pallas kernels, ffn_forward(): pl.pallas_call(body, grid=(steps,), in_specs=[whole, pl.BlockSpec((width,...  20.3 us
    pallas_call x3, Pallas kernels, grad_halves(): pl.pallas_call(body, in_specs=[pl.BlockSpec(memory_space=pltpu.SMEM)] + [...  20.1 us
    pallas_call x4, Pallas kernels, ffn_back(): pl.pallas_call(body, grid=(steps,), in_specs=[whole, part, pl.BlockSpec((...  17 us
  transfers between devices with their start and end apart: 67, of which 30 were waited for; matrix products, arithmetic and copies ran while one was open for 3% of the time, Pallas kernels for 36%

profile of v5, /device:TPU:0, one launch (start us, length us, event | category | flops | bytes accessed | tf_op | source)
XLA Modules:
  0.0 335.1 jit_solution(5073313440025882947)
XLA Ops:
  0.7 3.0 collective-permute-start
  8.1 1.8 fusion
  9.9 17.1 %collective-permute-done.refs_2_ = bf16[512,1024]{1,0:T(8,128)(2,1)S(1)} collective-permute-done((bf16[512,1024]{1,0:T(8,128)(2,1)}, bf16[512,1024]{1,0:T(8,128)(2,1)S(1)}, u32[]{:S(2)}, u32[]{:S(2)}) %collective-permute-start) | collective-permute-done | bytes 1048608 | tf_op jit(solution)/shard_map/ppermute | solution.py:361
  27.0 1.8 fusion.1
  29.1 5.8 %attend.2 = (bf16[512,512]{1,0:T(8,128)(2,1)S(1)}, f32[2,8,256]{2,1,0:T(8,128)S(1)}) custom-call(s32[4]{0:T(128)S(1)} %pad_add_fusion.table_ref, s32[8,42]{1,0:T(8,128)S(1)} %copy.40.rb_ref, bf16[1024,1536]{1,0:T(8,128)(2,1)S(1)} %pad_maximum_fusion.q_ref.k_ref.v_ref, bf16[1024,1536]{1,0:T(8,128)(2,1)S(1)} %pad_maximum_fusion.q_ref.k_ref.v_ref, ...), custom_call_target="tpu_custom_call" | custom-call | flops 1024 | bytes 1024 | tf_op jit(solution)/shard_map/attend/pallas_call | solution.py:281
  35.7 1.8 collective-permute-start.1
  37.5 5.6 %attend.3 = (bf16[512,512]{1,0:T(8,128)(2,1)S(1)}, f32[2,8,256]{2,1,0:T(8,128)S(1)}) custom-call(s32[4]{0:T(128)S(1)} %pad_add_fusion.table_ref, s32[8,42]{1,0:T(8,128)S(1)} %copy.40.rb_ref, bf16[1024,1536]{1,0:T(8,128)(2,1)S(1)} %pad_maximum_fusion.q_ref.k_ref.v_ref, bf16[1024,1536]{1,0:T(8,128)(2,1)S(1)} %pad_maximum_fusion.q_ref.k_ref.v_ref, ...), custom_call_target="tpu_custom_call" | custom-call | flops 1024 | bytes 1024 | tf_op jit(solution)/shard_map/attend/pallas_call | solution.py:281
  45.9 4.7 %collective-permute-done.1.refs_1_ = bf16[256,1024]{1,0:T(8,128)(2,1)S(1)} collective-permute-done((bf16[256,1024]{1,0:T(8,128)(2,1)S(1)}, bf16[256,1024]{1,0:T(8,128)(2,1)S(1)}, u32[]{:S(2)}, u32[]{:S(2)}) %collective-permute-start.1) | collective-permute-done | bytes 524320 | tf_op jit(solution)/shard_map/ppermute | solution.py:368
  51.4 1.8 collective-permute-start.2
  53.2 5.0 %ffn_forward.4 = (bf16[256,2048]{1,0:T(8,128)(2,1)S(1)}, bf16[256,2048]{1,0:T(8,128)(2,1)S(1)}, f32[256,1024]{1,0:T(8,128)S(1)}) custom-call(bf16[256,1024]{1,0:T(8,128)(2,1)S(1)} %get-tuple-element.408.x_ref.refs_2_.refs_8_, bf16[1024,2048]{1,0:T(8,128)(2,1)S(1)} %copy-done, bf16[1,2048]{1,0:T(2,128)(2,1)S(1)} %reshape.127.b_ref, ...), custom_call_target="tpu_custom_call" | custom-call | flops 1024 | bytes 1024 | tf_op jit(solution)/shard_map/ffn_forward/pallas_call | solution.py:804
  58.3 3.6 %collective-permute-done.3.refs_1_ = bf16[256,1024]{1,0:T(8,128)(2,1)S(1)} collective-permute-done((bf16[256,1024]{1,0:T(8,128)(2,1)S(1)}, bf16[256,1024]{1,0:T(8,128)(2,1)S(1)}, u32[]{:S(2)}, u32[]{:S(2)}) %collective-permute-start.3) | collective-permute-done | bytes 524320 | tf_op jit(solution)/shard_map/ppermute | solution.py:368
  62.7 1.8 collective-permute-start.5
  64.5 5.1 %ffn_forward.5 = (bf16[256,2048]{1,0:T(8,128)(2,1)S(1)}, bf16[256,2048]{1,0:T(8,128)(2,1)S(1)}, f32[256,1024]{1,0:T(8,128)S(1)}) custom-call(bf16[256,1024]{1,0:T(8,128)(2,1)S(1)} %get-tuple-element.410.x_ref.refs_2_.refs_10_, bf16[1024,2048]{1,0:T(8,128)(2,1)S(1)} %copy-done, bf16[1,2048]{1,0:T(2,128)(2,1)S(1)} %reshape.127.b_ref, ...), custom_call_target="tpu_custom_call" | custom-call | flops 1024 | bytes 1024 | tf_op jit(solution)/shard_map/ffn_forward/pallas_call | solution.py:804
  69.5 3.6 %collective-permute-done.2.x_ref.refs_9_ = bf16[256,1024]{1,0:T(8,128)(2,1)S(1)} collective-permute-done((bf16[256,1024]{1,0:T(8,128)(2,1)S(1)}, bf16[256,1024]{1,0:T(8,128)(2,1)S(1)}, u32[]{:S(2)}, u32[]{:S(2)}) %collective-permute-start.2) | collective-permute-done | bytes 524320 | tf_op jit(solution)/shard_map/ppermute | solution.py:361
  73.1 5.1 %ffn_forward.6 = (bf16[256,2048]{1,0:T(8,128)(2,1)S(1)}, bf16[256,2048]{1,0:T(8,128)(2,1)S(1)}, bf16[256,1024]{1,0:T(8,128)(2,1)S(1)}) custom-call(bf16[256,1024]{1,0:T(8,128)(2,1)S(1)} %collective-permute-done.2.x_ref.refs_9_, bf16[1024,2048]{1,0:T(8,128)(2,1)S(1)} %copy-done, bf16[1,2048]{1,0:T(2,128)(2,1)S(1)} %reshape.127.b_ref, ...), custom_call_target="tpu_custom_call" | custom-call | flops 1024 | bytes 1024 | tf_op jit(solution)/shard_map/ffn_forward/pallas_call | solution.py:804
  78.2 1.8 collective-permute-start.4
  80.0 4.3 %collective-permute-done.5.x_ref.refs_11_ = bf16[256,1024]{1,0:T(8,128)(2,1)S(1)} collective-permute-done((bf16[256,1024]{1,0:T(8,128)(2,1)S(1)}, bf16[256,1024]{1,0:T(8,128)(2,1)S(1)}, u32[]{:S(2)}, u32[]{:S(2)}) %collective-permute-start.5) | collective-permute-done | bytes 524320 | tf_op jit(solution)/shard_map/ppermute | solution.py:361
  84.3 5.1 %ffn_forward.7 = (bf16[256,2048]{1,0:T(8,128)(2,1)S(1)}, bf16[256,2048]{1,0:T(8,128)(2,1)S(1)}, bf16[256,1024]{1,0:T(8,128)(2,1)S(1)}) custom-call(bf16[256,1024]{1,0:T(8,128)(2,1)S(1)} %collective-permute-done.5.x_ref.refs_11_, bf16[1024,2048]{1,0:T(8,128)(2,1)S(1)} %copy-done, bf16[1,2048]{1,0:T(2,128)(2,1)S(1)} %reshape.127.b_ref, ...), custom_call_target="tpu_custom_call" | custom-call | flops 1024 | bytes 1024 | tf_op jit(solution)/shard_map/ffn_forward/pallas_call | solution.py:804
  89.4 1.8 collective-permute-start.6
  91.3 4.3 %collective-permute-done.4.refs_1_ = bf16[256,1024]{1,0:T(8,128)(2,1)S(1)} collective-permute-done((bf16[256,1024]{1,0:T(8,128)(2,1)S(1)}, bf16[256,1024]{1,0:T(8,128)(2,1)S(1)}, u32[]{:S(2)}, u32[]{:S(2)}) %collective-permute-start.4) | collective-permute-done | bytes 524320 | tf_op jit(solution)/shard_map/ppermute | solution.py:368
  95.6 1.6 norm_two.2
  97.2 1.8 collective-permute-start.8
  99.0 7.8 %collective-permute-done.6.refs_1_ = bf16[256,1024]{1,0:T(8,128)(2,1)S(1)} collective-permute-done((bf16[256,1024]{1,0:T(8,128)(2,1)S(1)}, bf16[256,1024]{1,0:T(8,128)(2,1)S(1)}, u32[]{:S(2)}, u32[]{:S(2)}) %collective-permute-start.6) | collective-permute-done | bytes 524320 | tf_op jit(solution)/shard_map/ppermute | solution.py:368
  108.0 1.8 collective-permute-start.7
  109.8 4.3 %ffn_back.4 = (bf16[256,2048]{1,0:T(8,128)(2,1)S(1)}, f32[1,2048]{1,0:T(1,128)S(1)}, f32[256,1024]{1,0:T(8,128)S(1)}) custom-call(bf16[256,1024]{1,0:T(8,128)(2,1)S(1)} %get-tuple-element.419.g_ref.refs_4_.refs_2_, bf16[256,2048]{1,0:T(8,128)(2,1)S(1)} %get-tuple-element.370.slope_ref, bf16[2048,1024]{1,0:T(8,128)(2,1)S(1)} %copy-done.1, ...), custom_call_target="tpu_custom_call" | custom-call | flops 1024 | bytes 1024 | tf_op jit(solution)/shard_map/ffn_back/pallas_call | solution.py:839
  114.1 4.3 %ffn_back.5 = (bf16[256,2048]{1,0:T(8,128)(2,1)S(1)}, f32[1,2048]{1,0:T(1,128)S(1)}, f32[256,1024]{1,0:T(8,128)S(1)}) custom-call(bf16[256,1024]{1,0:T(8,128)(2,1)S(1)} %get-tuple-element.425.g_ref.refs_6_.refs_2_, bf16[256,2048]{1,0:T(8,128)(2,1)S(1)} %get-tuple-element.373.slope_ref, bf16[2048,1024]{1,0:T(8,128)(2,1)S(1)} %copy-done.1, ...), custom_call_target="tpu_custom_call" | custom-call | flops 1024 | bytes 1024 | tf_op jit(solution)/shard_map/ffn_back/pallas_call | solution.py:839
  118.3 4.2 %ffn_back.6 = (bf16[256,2048]{1,0:T(8,128)(2,1)S(1)}, f32[1,2048]{1,0:T(1,128)S(1)}, bf16[256,1024]{1,0:T(8,128)(2,1)S(1)}) custom-call(bf16[256,1024]{1,0:T(8,128)(2,1)S(1)} %collective-permute-done.8.g_ref.refs_5_, bf16[256,2048]{1,0:T(8,128)(2,1)S(1)} %get-tuple-element.381.slope_ref, bf16[2048,1024]{1,0:T(8,128)(2,1)S(1)} %copy-done.1, ...), custom_call_target="tpu_custom_call" | custom-call | flops 1024 | bytes 1024 | tf_op jit(solution)/shard_map/ffn_back/pallas_call | solution.py:839
  124.1 5.2 %collective-permute-done.7.g_ref.refs_7_ = bf16[256,1024]{1,0:T(8,128)(2,1)S(1)} collective-permute-done((bf16[256,1024]{1,0:T(8,128)(2,1)S(1)}, bf16[256,1024]{1,0:T(8,128)(2,1)S(1)}, u32[]{:S(2)}, u32[]{:S(2)}) %collective-permute-start.7) | collective-permute-done | bytes 524320 | tf_op jit(solution)/shard_map/ppermute | solution.py:361
  129.3 4.2 %ffn_back.7 = (bf16[256,2048]{1,0:T(8,128)(2,1)S(1)}, f32[1,2048]{1,0:T(1,128)S(1)}, bf16[256,1024]{1,0:T(8,128)(2,1)S(1)}) custom-call(bf16[256,1024]{1,0:T(8,128)(2,1)S(1)} %collective-permute-done.7.g_ref.refs_7_, bf16[256,2048]{1,0:T(8,128)(2,1)S(1)} %get-tuple-element.384.slope_ref, bf16[2048,1024]{1,0:T(8,128)(2,1)S(1)} %copy-done.1, ...), custom_call_target="tpu_custom_call" | custom-call | flops 1024 | bytes 1024 | tf_op jit(solution)/shard_map/ffn_back/pallas_call | solution.py:839
  133.5 1.8 collective-permute-start.9
  135.3 13.8 %grad_halves.3 = (bf16[8,128,2048]{2,1,0:T(8,128)(2,1)}, bf16[8,128,2048]{2,1,0:T(8,128)(2,1)S(1)}) custom-call(s32[4]{0:T(128)S(1)} %pad_add_fusion.table_ref, bf16[256,2048]{1,0:T(8,128)(2,1)S(1)} %get-tuple-element.400.refs_0_, bf16[256,2048]{1,0:T(8,128)(2,1)S(1)} %get-tuple-element.401.refs_1_, bf16[256,2048]{1,0:T(8,128)(2,1)S(1)} %get-tuple-element.402.refs_2_, ...), custom_call_target="tpu_custom_call" | custom-call | flops 1024 | bytes 1024 | tf_op jit(solution)/shard_map/grad_halves/pallas_call | solution.py:650
  153.5 4.9 %collective-permute-done.13.moved_ref = bf16[8,128,2048]{2,1,0:T(8,128)(2,1)S(1)} collective-permute-done((bf16[8,128,2048]{2,1,0:T(8,128)(2,1)}, bf16[8,128,2048]{2,1,0:T(8,128)(2,1)S(1)}, u32[]{:S(2)}, u32[]{:S(2)}) %collective-permute-start.13) | collective-permute-done | bytes 4194336 | tf_op jit(solution)/shard_map/ppermute | solution.py:403
  159.0 1.6 collective-permute-start.15
  163.1 2.7 collective-permute-done.12.x_ref.refs_7_
  168.2 1.6 collective-permute-start.17
  171.2 10.8 %attend_back.2 = (bf16[512,512]{1,0:T(8,128)(2,1)S(1)}, f32[1024,512]{1,0:T(8,128)S(1)}, f32[1024,512]{1,0:T(8,128)S(1)}) custom-call(s32[4]{0:T(128)S(1)} %pad_add_fusion.table_ref, s32[8,42]{1,0:T(8,128)S(1)} %copy.40.rb_ref, bf16[1024,1536]{1,0:T(8,128)(2,1)S(1)} %pad_maximum_fusion.q_ref.k_ref.v_ref, ...), custom_call_target="tpu_custom_call" | custom-call | flops 1024 | bytes 1024 | tf_op jit(solution)/shard_map/attend_back/pallas_call | solution.py:324
  183.3 1.6 collective-permute-start.20
  187.6 11.6 %attend_back.3 = (bf16[1024,1536]{1,0:T(8,128)(2,1)S(1)}, f32[8,1024]{1,0:T(8,128)S(1)}) custom-call(s32[4]{0:T(128)S(1)} %pad_add_fusion.table_ref, s32[8,42]{1,0:T(8,128)S(1)} %copy.40.rb_ref, bf16[1024,1536]{1,0:T(8,128)(2,1)S(1)} %pad_maximum_fusion.q_ref.k_ref.v_ref, bf16[1024,1536]{1,0:T(8,128)(2,1)S(1)} %pad_maximum_fusion.q_ref.k_ref.v_ref, ...), custom_call_target="tpu_custom_call" | custom-call | flops 1024 | bytes 1024 | tf_op jit(solution)/shard_map/attend_back/pallas_call | solution.py:324
  199.2 3.1 grad_halves.5
  204.1 2.1 product.18
  206.9 1.5 collective-permute-start.32
  208.9 3.1 grad_halves.4.kept_ref
  213.2 2.2 product.19
  215.4 5.5 %collective-permute-done.32.refs_1_ = bf16[128,2048]{1,0:T(8,128)(2,1)S(1)} collective-permute-done((bf16[128,2048]{1,0:T(8,128)(2,1)S(1)}, bf16[128,2048]{1,0:T(8,128)(2,1)S(1)}, u32[]{:S(2)}, u32[]{:S(2)}) %collective-permute-start.32) | collective-permute-done | bytes 524320 | tf_op jit(solution)/shard_map/ppermute | solution.py:400
  223.0 1.6 collective-permute-start.34
  227.1 13.1 %collective-permute-done.24.refs_0_ = bf16[32,2176]{1,0:T(8,128)(2,1)S(1)} collective-permute-done((bf16[32,2176]{1,0:T(8,128)(2,1)S(1)}, bf16[32,2176]{1,0:T(8,128)(2,1)S(1)}, u32[]{:S(2)}, u32[]{:S(2)}) %collective-permute-start.24) | collective-permute-done | bytes 139296 | tf_op jit(solution)/shard_map/ppermute | solution.py:400
  241.7 1.6 add_convert_fusion
  243.7 1.6 collective-permute-start.36
  245.7 1.6 collective-permute-start.28
  247.3 13.6 %collective-permute-done.25.refs_0_ = bf16[64,2176]{1,0:T(8,128)(2,1)S(1)} collective-permute-done((bf16[64,2176]{1,0:T(8,128)(2,1)S(1)}, bf16[64,2176]{1,0:T(8,128)(2,1)S(1)}, u32[]{:S(2)}, u32[]{:S(2)}) %collective-permute-start.25) | collective-permute-done | bytes 278560 | tf_op jit(solution)/shard_map/ppermute | solution.py:400
  264.9 1.6 collective-permute-start.38
  266.5 12.7 %collective-permute-done.26.refs_0_ = bf16[64,2176]{1,0:T(8,128)(2,1)S(1)} collective-permute-done((bf16[64,2176]{1,0:T(8,128)(2,1)S(1)}, bf16[64,2176]{1,0:T(8,128)(2,1)S(1)}, u32[]{:S(2)}, u32[]{:S(2)}) %collective-permute-start.26) | collective-permute-done | bytes 278560 | tf_op jit(solution)/shard_map/ppermute | solution.py:400
  280.6 1.8 collective-permute-start.30
  283.4 1.6 collective-permute-start.44
  285.1 3.6 %collective-permute-done.30.refs_1_ = bf16[64,2176]{1,0:T(8,128)(2,1)S(1)} collective-permute-done((bf16[64,2176]{1,0:T(8,128)(2,1)S(1)}, bf16[64,2176]{1,0:T(8,128)(2,1)S(1)}, u32[]{:S(2)}, u32[]{:S(2)}) %collective-permute-start.30) | collective-permute-done | bytes 278560 | tf_op jit(solution)/shard_map/ppermute | solution.py:400
  291.2 1.6 collective-permute-start.40
  293.3 1.7 collective-permute-done.43.refs_0_
  295.6 4.8 %collective-permute-done.40.refs_5_ = bf16[64,2176]{1,0:T(8,128)(2,1)S(1)} collective-permute-done((bf16[64,2176]{1,0:T(8,128)(2,1)S(1)}, bf16[64,2176]{1,0:T(8,128)(2,1)S(1)}, u32[]{:S(2)}, u32[]{:S(2)}) %collective-permute-start.40) | collective-permute-done | bytes 278560 | tf_op jit(solution)/shard_map/ppermute | solution.py:400
  302.1 1.6 collective-permute-start.42
  303.7 1.5 collective-permute-done.53.refs_17_
  305.2 4.6 %place_pieces.3 = f32[2,8,128,1024]{3,2,1,0:T(8,128)} custom-call(s32[4]{0:T(128)S(1)} %pad_add_fusion.table_ref, bf16[64,2048]{1,0:T(8,128)(2,1)S(1)} %collective-permute-done.43.refs_0_, bf16[128,2048]{1,0:T(8,128)(2,1)S(1)} %collective-permute-done.37.refs_1_, bf16[128,2048]{1,0:T(8,128)(2,1)S(1)} %collective-permute-done.35.refs_2_, ...), custom_call_target="tpu_custom_call" | custom-call | flops 1024 | bytes 1024 | tf_op jit(solution)/shard_map/place_pieces/pallas_call | solution.py:533
  313.4 4.6 %place_pieces.4 = f32[2,8,64,2048]{3,2,1,0:T(8,128)} custom-call(s32[4]{0:T(128)S(1)} %pad_add_fusion.table_ref, bf16[64,2048]{1,0:T(8,128)(2,1)S(1)} %collective-permute-done.43.refs_0_, bf16[128,2048]{1,0:T(8,128)(2,1)S(1)} %collective-permute-done.37.refs_1_, bf16[128,2048]{1,0:T(8,128)(2,1)S(1)} %collective-permute-done.35.refs_2_, ...), custom_call_target="tpu_custom_call" | custom-call | flops 1024 | bytes 1024 | tf_op jit(solution)/shard_map/place_pieces/pallas_call | solution.py:533
  321.6 3.6 %collective-permute-done.57.refs_8_ = bf16[32,2176]{1,0:T(8,128)(2,1)S(1)} collective-permute-done((bf16[32,2176]{1,0:T(8,128)(2,1)S(1)}, bf16[32,2176]{1,0:T(8,128)(2,1)S(1)}, u32[]{:S(2)}, u32[]{:S(2)}) %collective-permute-start.57) | collective-permute-done | bytes 139296 | tf_op jit(solution)/shard_map/ppermute | solution.py:400
  328.3 4.2 %place_pieces.5 = (f32[2,8,64,512]{3,2,1,0:T(8,128)}, f32[2,8,64,512]{3,2,1,0:T(8,128)}, f32[2,8,64,512]{3,2,1,0:T(8,128)}, f32[2,8,8,128]{3,2,1,0:T(8,128)S(1)}, f32[2,8,32,1024]{3,2,1,0:T(8,128)}) custom-call(s32[4]{0:T(128)S(1)} %pad_add_fusion.table_ref, bf16[32,2176]{1,0:T(8,128)(2,1)S(1)} %collective-permute-done.56.refs_0_, ...), custom_call_target="tpu_custom_call" | custom-call | flops 1024 | bytes 1024 | tf_op jit(solution)/shard_map/place_pieces/pallas_call | solution.py:533
  (179 shorter events, 62.6 us)
Async XLA Ops:
  0.7 26.4 %collective-permute-start = (bf16[512,1024]{1,0:T(8,128)(2,1)}, bf16[512,1024]{1,0:T(8,128)(2,1)S(1)}, u32[]{:S(2)}, u32[]{:S(2)}) collective-permute-start(bf16[512,1024]{1,0:T(8,128)(2,1)} %bitcast.42), channel_id=1, source_target_pairs={{1,0},{0,1},{3,2},{2,3},{5,4},{4,5},{7,6},{6,7},{9,8},{8,9},{11,10... | collective-permute-start | bytes 3145736 | tf_op jit(solution)/shard_map/ppermute | solution.py:361
  35.7 14.9 %collective-permute-start.1 = (bf16[256,1024]{1,0:T(8,128)(2,1)S(1)}, bf16[256,1024]{1,0:T(8,128)(2,1)S(1)}, u32[]{:S(2)}, u32[]{:S(2)}) collective-permute-start(bf16[256,1024]{1,0:T(8,128)(2,1)S(1)} %product.10), channel_id=1, source_target_pairs={{0,1},{1,0},{2,3},{3,2},{4,5},{5,4},{6,7},{7,6},{8,9},{9,8},{10,11... | collective-permute-start | bytes 1572872 | tf_op jit(solution)/shard_map/ppermute | solution.py:368
  43.9 18.0 %collective-permute-start.3 = (bf16[256,1024]{1,0:T(8,128)(2,1)S(1)}, bf16[256,1024]{1,0:T(8,128)(2,1)S(1)}, u32[]{:S(2)}, u32[]{:S(2)}) collective-permute-start(bf16[256,1024]{1,0:T(8,128)(2,1)S(1)} %product.11), channel_id=1, source_target_pairs={{0,1},{1,0},{2,3},{3,2},{4,5},{5,4},{6,7},{7,6},{8,9},{9,8},{10,11... | collective-permute-start | bytes 1572872 | tf_op jit(solution)/shard_map/ppermute | solution.py:368
  51.4 21.7 %collective-permute-start.2 = (bf16[256,1024]{1,0:T(8,128)(2,1)S(1)}, bf16[256,1024]{1,0:T(8,128)(2,1)S(1)}, u32[]{:S(2)}, u32[]{:S(2)}) collective-permute-start(bf16[256,1024]{1,0:T(8,128)(2,1)S(1)} %get-tuple-element.408.x_ref.refs_2_.refs_8_), channel_id=1, source_target_pairs={{1,0},{0,1},{3,2},{2,3},{5,4},{4,5},{7,6},{6,7},{9,8},{8,9},{11,10... | collective-permute-start | bytes 1572872 | tf_op jit(solution)/shard_map/ppermute | solution.py:361
  62.7 21.7 %collective-permute-start.5 = (bf16[256,1024]{1,0:T(8,128)(2,1)S(1)}, bf16[256,1024]{1,0:T(8,128)(2,1)S(1)}, u32[]{:S(2)}, u32[]{:S(2)}) collective-permute-start(bf16[256,1024]{1,0:T(8,128)(2,1)S(1)} %get-tuple-element.410.x_ref.refs_2_.refs_10_), channel_id=1, source_target_pairs={{1,0},{0,1},{3,2},{2,3},{5,4},{4,5},{7,6},{6,7},{9,8},{8,9},{11,10... | collective-permute-start | bytes 1572872 | tf_op jit(solution)/shard_map/ppermute | solution.py:361
  78.2 17.3 %collective-permute-start.4 = (bf16[256,1024]{1,0:T(8,128)(2,1)S(1)}, bf16[256,1024]{1,0:T(8,128)(2,1)S(1)}, u32[]{:S(2)}, u32[]{:S(2)}) collective-permute-start(bf16[256,1024]{1,0:T(8,128)(2,1)S(1)} %get-tuple-element.352), channel_id=1, source_target_pairs={{0,1},{1,0},{2,3},{3,2},{4,5},{5,4},{6,7},{7,6},{8,9},{9,8},{10,11... | collective-permute-start | bytes 1572872 | tf_op jit(solution)/shard_map/ppermute | solution.py:368
  89.4 17.4 %collective-permute-start.6 = (bf16[256,1024]{1,0:T(8,128)(2,1)S(1)}, bf16[256,1024]{1,0:T(8,128)(2,1)S(1)}, u32[]{:S(2)}, u32[]{:S(2)}) collective-permute-start(bf16[256,1024]{1,0:T(8,128)(2,1)S(1)} %get-tuple-element.354), channel_id=1, source_target_pairs={{0,1},{1,0},{2,3},{3,2},{4,5},{5,4},{6,7},{7,6},{8,9},{9,8},{10,11... | collective-permute-start | bytes 1572872 | tf_op jit(solution)/shard_map/ppermute | solution.py:368
  97.2 21.1 %collective-permute-start.8 = (bf16[256,1024]{1,0:T(8,128)(2,1)S(1)}, bf16[256,1024]{1,0:T(8,128)(2,1)S(1)}, u32[]{:S(2)}, u32[]{:S(2)}) collective-permute-start(bf16[256,1024]{1,0:T(8,128)(2,1)S(1)} %get-tuple-element.419.g_ref.refs_4_.refs_2_), channel_id=1, source_target_pairs={{1,0},{0,1},{3,2},{2,3},{5,4},{4,5},{7,6},{6,7},{9,8},{8,9},{11,10... | collective-permute-start | bytes 1572872 | tf_op jit(solution)/shard_map/ppermute | solution.py:361
  108.0 21.3 %collective-permute-start.7 = (bf16[256,1024]{1,0:T(8,128)(2,1)S(1)}, bf16[256,1024]{1,0:T(8,128)(2,1)S(1)}, u32[]{:S(2)}, u32[]{:S(2)}) collective-permute-start(bf16[256,1024]{1,0:T(8,128)(2,1)S(1)} %get-tuple-element.425.g_ref.refs_6_.refs_2_), channel_id=1, source_target_pairs={{1,0},{0,1},{3,2},{2,3},{5,4},{4,5},{7,6},{6,7},{9,8},{8,9},{11,10... | collective-permute-start | bytes 1572872 | tf_op jit(solution)/shard_map/ppermute | solution.py:361
  122.6 26.6 %collective-permute-start.10 = (bf16[256,1024]{1,0:T(8,128)(2,1)S(1)}, bf16[256,1024]{1,0:T(8,128)(2,1)S(1)}, u32[]{:S(2)}, u32[]{:S(2)}) collective-permute-start(bf16[256,1024]{1,0:T(8,128)(2,1)S(1)} %get-tuple-element.389), channel_id=1, source_target_pairs={{0,1},{1,0},{2,3},{3,2},{4,5},{5,4},{6,7},{7,6},{8,9},{9,8},{10,11... | collective-permute-start | bytes 1572872 | tf_op jit(solution)/shard_map/ppermute | solution.py:368
  133.5 16.5 %collective-permute-start.9 = (bf16[256,1024]{1,0:T(8,128)(2,1)S(1)}, bf16[256,1024]{1,0:T(8,128)(2,1)S(1)}, u32[]{:S(2)}, u32[]{:S(2)}) collective-permute-start(bf16[256,1024]{1,0:T(8,128)(2,1)S(1)} %get-tuple-element.385), channel_id=1, source_target_pairs={{0,1},{1,0},{2,3},{3,2},{4,5},{5,4},{6,7},{7,6},{8,9},{9,8},{10,11... | collective-permute-start | bytes 1572872 | tf_op jit(solution)/shard_map/ppermute | solution.py:368
  151.0 7.4 %collective-permute-start.13 = (bf16[8,128,2048]{2,1,0:T(8,128)(2,1)}, bf16[8,128,2048]{2,1,0:T(8,128)(2,1)S(1)}, u32[]{:S(2)}, u32[]{:S(2)}) collective-permute-start(bf16[8,128,2048]{2,1,0:T(8,128)(2,1)} %get-tuple-element.433), channel_id=1, source_target_pairs={{0,2},{2,0},{4,6},{6,4},{8,10},{10,8},{12,14},{14,12},{16,18},{18,... | collective-permute-start | bytes 12582920 | tf_op jit(solution)/shard_map/ppermute | solution.py:403
  151.0 14.8 %collective-permute-start.12 = (bf16[256,1024]{1,0:T(8,128)(2,1)S(1)}, bf16[256,1024]{1,0:T(8,128)(2,1)S(1)}, u32[]{:S(2)}, u32[]{:S(2)}) collective-permute-start(bf16[256,1024]{1,0:T(8,128)(2,1)S(1)} %get-tuple-element.537.x_ref.refs_6_), channel_id=1, source_target_pairs={{1,0},{0,1},{3,2},{2,3},{5,4},{4,5},{7,6},{6,7},{9,8},{8,9},{11,10... | collective-permute-start | bytes 1572872 | tf_op jit(solution)/shard_map/ppermute | solution.py:361
  159.0 8.4 %collective-permute-start.15 = (bf16[64,2048]{1,0:T(8,128)(2,1)S(1)}, bf16[64,2048]{1,0:T(8,128)(2,1)S(1)}, u32[]{:S(2)}, u32[]{:S(2)}) collective-permute-start(bf16[64,2048]{1,0:T(8,128)(2,1)S(1)} %ring_add.18), channel_id=1, source_target_pairs={{0,8},{2,10},{8,16},{10,18},{16,24},{18,26},{24,28},{26,30},{28,20... | collective-permute-start | bytes 786440 | tf_op jit(solution)/shard_map/ppermute | solution.py:400
  161.3 8.6 %collective-permute-start.14 = (bf16[64,2048]{1,0:T(8,128)(2,1)S(1)}, bf16[64,2048]{1,0:T(8,128)(2,1)S(1)}, u32[]{:S(2)}, u32[]{:S(2)}) collective-permute-start(bf16[64,2048]{1,0:T(8,128)(2,1)S(1)} %ring_add.19), channel_id=1, source_target_pairs={{0,4},{2,6},{8,0},{10,2},{16,8},{18,10},{24,16},{26,18},{28,24},{3... | collective-permute-start | bytes 786440 | tf_op jit(solution)/shard_map/ppermute | solution.py:400
  161.8 20.3 %collective-permute-start.11 = (bf16[256,1024]{1,0:T(8,128)(2,1)S(1)}, bf16[256,1024]{1,0:T(8,128)(2,1)S(1)}, u32[]{:S(2)}, u32[]{:S(2)}) collective-permute-start(bf16[256,1024]{1,0:T(8,128)(2,1)S(1)} %get-tuple-element.538.x_ref.refs_8_), channel_id=1, source_target_pairs={{1,0},{0,1},{3,2},{2,3},{5,4},{4,5},{7,6},{6,7},{9,8},{8,9},{11,10... | collective-permute-start | bytes 1572872 | tf_op jit(solution)/shard_map/ppermute | solution.py:361
  168.2 14.3 %collective-permute-start.17 = (bf16[128,2048]{1,0:T(8,128)(2,1)S(1)}, bf16[128,2048]{1,0:T(8,128)(2,1)S(1)}, u32[]{:S(2)}, u32[]{:S(2)}) collective-permute-start(bf16[128,2048]{1,0:T(8,128)(2,1)S(1)} %ring_add.20), channel_id=1, source_target_pairs={{0,8},{2,10},{8,16},{10,18},{16,24},{18,26},{24,28},{26,30},{28,20... | collective-permute-start | bytes 1572872 | tf_op jit(solution)/shard_map/ppermute | solution.py:400
  170.7 14.3 %collective-permute-start.16 = (bf16[128,2048]{1,0:T(8,128)(2,1)S(1)}, bf16[128,2048]{1,0:T(8,128)(2,1)S(1)}, u32[]{:S(2)}, u32[]{:S(2)}) collective-permute-start(bf16[128,2048]{1,0:T(8,128)(2,1)S(1)} %ring_add.21), channel_id=1, source_target_pairs={{0,4},{2,6},{8,0},{10,2},{16,8},{18,10},{24,16},{26,18},{28,24},{3... | collective-permute-start | bytes 1572872 | tf_op jit(solution)/shard_map/ppermute | solution.py:400
  183.3 19.1 %collective-permute-start.20 = (bf16[128,2048]{1,0:T(8,128)(2,1)S(1)}, bf16[128,2048]{1,0:T(8,128)(2,1)S(1)}, u32[]{:S(2)}, u32[]{:S(2)}) collective-permute-start(bf16[128,2048]{1,0:T(8,128)(2,1)S(1)} %ring_add.22), channel_id=1, source_target_pairs={{0,8},{2,10},{8,16},{10,18},{16,24},{18,26},{24,28},{26,30},{28,20... | collective-permute-start | bytes 1572872 | tf_op jit(solution)/shard_map/ppermute | solution.py:400
  185.7 17.4 %collective-permute-start.19 = (bf16[128,2048]{1,0:T(8,128)(2,1)S(1)}, bf16[128,2048]{1,0:T(8,128)(2,1)S(1)}, u32[]{:S(2)}, u32[]{:S(2)}) collective-permute-start(bf16[128,2048]{1,0:T(8,128)(2,1)S(1)} %ring_add.23), channel_id=1, source_target_pairs={{0,4},{2,6},{8,0},{10,2},{16,8},{18,10},{24,16},{26,18},{28,24},{3... | collective-permute-start | bytes 1572872 | tf_op jit(solution)/shard_map/ppermute | solution.py:400
  186.2 13.0 %collective-permute-start.18 = (f32[8,1024]{1,0:T(8,128)S(1)}, f32[8,1024]{1,0:T(8,128)S(1)}, u32[]{:S(2)}, u32[]{:S(2)}) collective-permute-start(f32[8,1024]{1,0:T(8,128)S(1)} %sum_kernel.1.refs_0_), channel_id=1, source_target_pairs={{1,0},{0,1},{3,2},{2,3},{5,4},{4,5},{7,6},{6,7},{9,8},{8,9},{11,10... | collective-permute-start | bytes 98312 | tf_op jit(solution)/shard_map/ppermute | solution.py:361
  204.0 8.1 %collective-permute-start.21 = (bf16[8,64,2176]{2,1,0:T(8,128)(2,1)S(1)}, bf16[8,64,2176]{2,1,0:T(8,128)(2,1)S(1)}, u32[]{:S(2)}, u32[]{:S(2)}) collective-permute-start(bf16[8,64,2176]{2,1,0:T(8,128)(2,1)S(1)} %grad_halves.5), channel_id=1, source_target_pairs={{0,2},{2,0},{4,6},{6,4},{8,10},{10,8},{12,14},{14,12},{16,18},{18,... | collective-permute-start | bytes 6684680 | tf_op jit(solution)/shard_map/ppermute | solution.py:403
  206.2 35.5 %collective-permute-start.22 = (bf16[512,1024]{1,0:T(8,128)(2,1)S(1)}, bf16[512,1024]{1,0:T(8,128)(2,1)S(1)}, u32[]{:S(2)}, u32[]{:S(2)}) collective-permute-start(bf16[512,1024]{1,0:T(8,128)(2,1)S(1)} %product.18), channel_id=1, source_target_pairs={{0,1},{1,0},{2,3},{3,2},{4,5},{5,4},{6,7},{7,6},{8,9},{9,8},{10,11... | collective-permute-start | bytes 3145736 | tf_op jit(solution)/shard_map/ppermute | solution.py:368
  206.9 14.0 %collective-permute-start.32 = (bf16[128,2048]{1,0:T(8,128)(2,1)S(1)}, bf16[128,2048]{1,0:T(8,128)(2,1)S(1)}, u32[]{:S(2)}, u32[]{:S(2)}) collective-permute-start(bf16[128,2048]{1,0:T(8,128)(2,1)S(1)} %ring_add.25), channel_id=1, source_target_pairs={{0,4},{2,6},{8,0},{10,2},{16,8},{18,10},{24,16},{26,18},{28,24},{3... | collective-permute-start | bytes 1572872 | tf_op jit(solution)/shard_map/ppermute | solution.py:400
  208.4 13.7 %collective-permute-start.31 = (bf16[128,2048]{1,0:T(8,128)(2,1)S(1)}, bf16[128,2048]{1,0:T(8,128)(2,1)S(1)}, u32[]{:S(2)}, u32[]{:S(2)}) collective-permute-start(bf16[128,2048]{1,0:T(8,128)(2,1)S(1)} %ring_add.24), channel_id=1, source_target_pairs={{0,8},{2,10},{8,16},{10,18},{16,24},{18,26},{24,28},{26,30},{28,20... | collective-permute-start | bytes 1572872 | tf_op jit(solution)/shard_map/ppermute | solution.py:400
  223.0 20.3 %collective-permute-start.34 = (bf16[128,2048]{1,0:T(8,128)(2,1)S(1)}, bf16[128,2048]{1,0:T(8,128)(2,1)S(1)}, u32[]{:S(2)}, u32[]{:S(2)}) collective-permute-start(bf16[128,2048]{1,0:T(8,128)(2,1)S(1)} %ring_add.34.refs_4_), channel_id=1, source_target_pairs={{0,4},{2,6},{8,0},{10,2},{16,8},{18,10},{24,16},{26,18},{28,24},{3... | collective-permute-start | bytes 1572872 | tf_op jit(solution)/shard_map/ppermute | solution.py:400
  224.7 18.6 %collective-permute-start.33 = (bf16[128,2048]{1,0:T(8,128)(2,1)S(1)}, bf16[128,2048]{1,0:T(8,128)(2,1)S(1)}, u32[]{:S(2)}, u32[]{:S(2)}) collective-permute-start(bf16[128,2048]{1,0:T(8,128)(2,1)S(1)} %ring_add.34.refs_4_), channel_id=1, source_target_pairs={{0,8},{2,10},{8,16},{10,18},{16,24},{18,26},{24,28},{26,30},{28,20... | collective-permute-start | bytes 1572872 | tf_op jit(solution)/shard_map/ppermute | solution.py:400
  225.1 15.1 %collective-permute-start.24 = (bf16[32,2176]{1,0:T(8,128)(2,1)S(1)}, bf16[32,2176]{1,0:T(8,128)(2,1)S(1)}, u32[]{:S(2)}, u32[]{:S(2)}) collective-permute-start(bf16[32,2176]{1,0:T(8,128)(2,1)S(1)} %ring_add.26), channel_id=1, source_target_pairs={{0,8},{2,10},{8,16},{10,18},{16,24},{18,26},{24,28},{26,30},{28,20... | collective-permute-start | bytes 417800 | tf_op jit(solution)/shard_map/ppermute | solution.py:400
  225.6 15.4 %collective-permute-start.23 = (bf16[32,2176]{1,0:T(8,128)(2,1)S(1)}, bf16[32,2176]{1,0:T(8,128)(2,1)S(1)}, u32[]{:S(2)}, u32[]{:S(2)}) collective-permute-start(bf16[32,2176]{1,0:T(8,128)(2,1)S(1)} %ring_add.27), channel_id=1, source_target_pairs={{0,4},{2,6},{8,0},{10,2},{16,8},{18,10},{24,16},{26,18},{28,24},{3... | collective-permute-start | bytes 417800 | tf_op jit(solution)/shard_map/ppermute | solution.py:400
  243.3 19.1 %collective-permute-start.35 = (bf16[128,2048]{1,0:T(8,128)(2,1)S(1)}, bf16[128,2048]{1,0:T(8,128)(2,1)S(1)}, u32[]{:S(2)}, u32[]{:S(2)}) collective-permute-start(bf16[128,2048]{1,0:T(8,128)(2,1)S(1)} %collective-permute-done.33.refs_3_), channel_id=1, source_target_pairs={{0,8},{2,10},{8,16},{10,18},{16,24},{18,26},{24,28},{26,30},{28,20... | collective-permute-start | bytes 1572872 | tf_op jit(solution)/shard_map/ppermute | solution.py:400
  243.7 18.7 %collective-permute-start.36 = (bf16[128,2048]{1,0:T(8,128)(2,1)S(1)}, bf16[128,2048]{1,0:T(8,128)(2,1)S(1)}, u32[]{:S(2)}, u32[]{:S(2)}) collective-permute-start(bf16[128,2048]{1,0:T(8,128)(2,1)S(1)} %collective-permute-done.34.refs_5_), channel_id=1, source_target_pairs={{0,4},{2,6},{8,0},{10,2},{16,8},{18,10},{24,16},{26,18},{28,24},{3... | collective-permute-start | bytes 1572872 | tf_op jit(solution)/shard_map/ppermute | solution.py:400
  245.3 15.6 %collective-permute-start.25 = (bf16[64,2176]{1,0:T(8,128)(2,1)S(1)}, bf16[64,2176]{1,0:T(8,128)(2,1)S(1)}, u32[]{:S(2)}, u32[]{:S(2)}) collective-permute-start(bf16[64,2176]{1,0:T(8,128)(2,1)S(1)} %ring_add.28), channel_id=1, source_target_pairs={{0,8},{2,10},{8,16},{10,18},{16,24},{18,26},{24,28},{26,30},{28,20... | collective-permute-start | bytes 835592 | tf_op jit(solution)/shard_map/ppermute | solution.py:400
  245.7 15.9 %collective-permute-start.28 = (bf16[64,2176]{1,0:T(8,128)(2,1)S(1)}, bf16[64,2176]{1,0:T(8,128)(2,1)S(1)}, u32[]{:S(2)}, u32[]{:S(2)}) collective-permute-start(bf16[64,2176]{1,0:T(8,128)(2,1)S(1)} %ring_add.29), channel_id=1, source_target_pairs={{0,4},{2,6},{8,0},{10,2},{16,8},{18,10},{24,16},{26,18},{28,24},{3... | collective-permute-start | bytes 835592 | tf_op jit(solution)/shard_map/ppermute | solution.py:400
  262.4 20.5 %collective-permute-start.37 = (bf16[128,2048]{1,0:T(8,128)(2,1)S(1)}, bf16[128,2048]{1,0:T(8,128)(2,1)S(1)}, u32[]{:S(2)}, u32[]{:S(2)}) collective-permute-start(bf16[128,2048]{1,0:T(8,128)(2,1)S(1)} %collective-permute-done.35.refs_2_), channel_id=1, source_target_pairs={{0,8},{2,10},{8,16},{10,18},{16,24},{18,26},{24,28},{26,30},{28,20... | collective-permute-start | bytes 1572872 | tf_op jit(solution)/shard_map/ppermute | solution.py:400
  262.9 16.3 %collective-permute-start.26 = (bf16[64,2176]{1,0:T(8,128)(2,1)S(1)}, bf16[64,2176]{1,0:T(8,128)(2,1)S(1)}, u32[]{:S(2)}, u32[]{:S(2)}) collective-permute-start(bf16[64,2176]{1,0:T(8,128)(2,1)S(1)} %ring_add.30), channel_id=1, source_target_pairs={{0,8},{2,10},{8,16},{10,18},{16,24},{18,26},{24,28},{26,30},{28,20... | collective-permute-start | bytes 835592 | tf_op jit(solution)/shard_map/ppermute | solution.py:400
  264.3 15.6 %collective-permute-start.29 = (bf16[64,2176]{1,0:T(8,128)(2,1)S(1)}, bf16[64,2176]{1,0:T(8,128)(2,1)S(1)}, u32[]{:S(2)}, u32[]{:S(2)}) collective-permute-start(bf16[64,2176]{1,0:T(8,128)(2,1)S(1)} %ring_add.32), channel_id=1, source_target_pairs={{0,4},{2,6},{8,0},{10,2},{16,8},{18,10},{24,16},{26,18},{28,24},{3... | collective-permute-start | bytes 835592 | tf_op jit(solution)/shard_map/ppermute | solution.py:400
  264.9 18.5 %collective-permute-start.38 = (bf16[128,2048]{1,0:T(8,128)(2,1)S(1)}, bf16[128,2048]{1,0:T(8,128)(2,1)S(1)}, u32[]{:S(2)}, u32[]{:S(2)}) collective-permute-start(bf16[128,2048]{1,0:T(8,128)(2,1)S(1)} %collective-permute-done.36.refs_6_), channel_id=1, source_target_pairs={{0,4},{2,6},{8,0},{10,2},{16,8},{18,10},{24,16},{26,18},{28,24},{3... | collective-permute-start | bytes 1572872 | tf_op jit(solution)/shard_map/ppermute | solution.py:400
  280.6 8.1 %collective-permute-start.30 = (bf16[64,2176]{1,0:T(8,128)(2,1)S(1)}, bf16[64,2176]{1,0:T(8,128)(2,1)S(1)}, u32[]{:S(2)}, u32[]{:S(2)}) collective-permute-start(bf16[64,2176]{1,0:T(8,128)(2,1)S(1)} %ring_add.33), channel_id=1, source_target_pairs={{0,4},{2,6},{8,0},{10,2},{16,8},{18,10},{24,16},{26,18},{28,24},{3... | collective-permute-start | bytes 835592 | tf_op jit(solution)/shard_map/ppermute | solution.py:400
  282.4 8.0 %collective-permute-start.27 = (bf16[64,2176]{1,0:T(8,128)(2,1)S(1)}, bf16[64,2176]{1,0:T(8,128)(2,1)S(1)}, u32[]{:S(2)}, u32[]{:S(2)}) collective-permute-start(bf16[64,2176]{1,0:T(8,128)(2,1)S(1)} %ring_add.31), channel_id=1, source_target_pairs={{0,8},{2,10},{8,16},{10,18},{16,24},{18,26},{24,28},{26,30},{28,20... | collective-permute-start | bytes 835592 | tf_op jit(solution)/shard_map/ppermute | solution.py:400
  282.9 8.3 %collective-permute-start.49 = (bf16[128,2048]{1,0:T(8,128)(2,1)S(1)}, bf16[128,2048]{1,0:T(8,128)(2,1)S(1)}, u32[]{:S(2)}, u32[]{:S(2)}) collective-permute-start(bf16[128,2048]{1,0:T(8,128)(2,1)S(1)} %ring_add.34.refs_4_), channel_id=1, source_target_pairs={{0,2},{2,0},{4,6},{6,4},{8,10},{10,8},{12,14},{14,12},{16,18},{18,... | collective-permute-start | bytes 1572872 | tf_op jit(solution)/shard_map/ppermute | solution.py:403
  282.9 9.9 %collective-permute-start.48 = (bf16[128,2048]{1,0:T(8,128)(2,1)S(1)}, bf16[128,2048]{1,0:T(8,128)(2,1)S(1)}, u32[]{:S(2)}, u32[]{:S(2)}) collective-permute-start(bf16[128,2048]{1,0:T(8,128)(2,1)S(1)} %collective-permute-done.33.refs_3_), channel_id=1, source_target_pairs={{0,2},{2,0},{4,6},{6,4},{8,10},{10,8},{12,14},{14,12},{16,18},{18,... | collective-permute-start | bytes 1572872 | tf_op jit(solution)/shard_map/ppermute | solution.py:403
  283.4 9.9 %collective-permute-start.44 = (bf16[64,2048]{1,0:T(8,128)(2,1)S(1)}, bf16[64,2048]{1,0:T(8,128)(2,1)S(1)}, u32[]{:S(2)}, u32[]{:S(2)}) collective-permute-start(bf16[64,2048]{1,0:T(8,128)(2,1)S(1)} %slice.52), channel_id=1, source_target_pairs={{0,4},{2,6},{8,0},{10,2},{16,8},{18,10},{24,16},{26,18},{28,24},{3... | collective-permute-start | bytes 786440 | tf_op jit(solution)/shard_map/ppermute | solution.py:400
  288.7 6.4 %collective-permute-start.43 = (bf16[64,2048]{1,0:T(8,128)(2,1)S(1)}, bf16[64,2048]{1,0:T(8,128)(2,1)S(1)}, u32[]{:S(2)}, u32[]{:S(2)}) collective-permute-start(bf16[64,2048]{1,0:T(8,128)(2,1)S(1)} %slice.51), channel_id=1, source_target_pairs={{0,8},{2,10},{8,16},{10,18},{16,24},{18,26},{24,28},{26,30},{28,20... | collective-permute-start | bytes 786440 | tf_op jit(solution)/shard_map/ppermute | solution.py:400
  290.5 4.6 %collective-permute-start.50 = (bf16[128,2048]{1,0:T(8,128)(2,1)S(1)}, bf16[128,2048]{1,0:T(8,128)(2,1)S(1)}, u32[]{:S(2)}, u32[]{:S(2)}) collective-permute-start(bf16[128,2048]{1,0:T(8,128)(2,1)S(1)} %collective-permute-done.34.refs_5_), channel_id=1, source_target_pairs={{0,2},{2,0},{4,6},{6,4},{8,10},{10,8},{12,14},{14,12},{16,18},{18,... | collective-permute-start | bytes 1572872 | tf_op jit(solution)/shard_map/ppermute | solution.py:403
  291.2 9.1 %collective-permute-start.40 = (bf16[64,2176]{1,0:T(8,128)(2,1)S(1)}, bf16[64,2176]{1,0:T(8,128)(2,1)S(1)}, u32[]{:S(2)}, u32[]{:S(2)}) collective-permute-start(bf16[64,2176]{1,0:T(8,128)(2,1)S(1)} %ring_add.35.refs_4_), channel_id=1, source_target_pairs={{0,4},{2,6},{8,0},{10,2},{16,8},{18,10},{24,16},{26,18},{28,24},{3... | collective-permute-start | bytes 835592 | tf_op jit(solution)/shard_map/ppermute | solution.py:400
  292.8 8.8 %collective-permute-start.39 = (bf16[64,2176]{1,0:T(8,128)(2,1)S(1)}, bf16[64,2176]{1,0:T(8,128)(2,1)S(1)}, u32[]{:S(2)}, u32[]{:S(2)}) collective-permute-start(bf16[64,2176]{1,0:T(8,128)(2,1)S(1)} %ring_add.35.refs_4_), channel_id=1, source_target_pairs={{0,8},{2,10},{8,16},{10,18},{16,24},{18,26},{24,28},{26,30},{28,20... | collective-permute-start | bytes 835592 | tf_op jit(solution)/shard_map/ppermute | solution.py:400
  293.3 8.3 %collective-permute-start.47 = (bf16[128,2048]{1,0:T(8,128)(2,1)S(1)}, bf16[128,2048]{1,0:T(8,128)(2,1)S(1)}, u32[]{:S(2)}, u32[]{:S(2)}) collective-permute-start(bf16[128,2048]{1,0:T(8,128)(2,1)S(1)} %collective-permute-done.35.refs_2_), channel_id=1, source_target_pairs={{0,2},{2,0},{4,6},{6,4},{8,10},{10,8},{12,14},{14,12},{16,18},{18,... | collective-permute-start | bytes 1572872 | tf_op jit(solution)/shard_map/ppermute | solution.py:403
  295.0 7.1 %collective-permute-start.51 = (bf16[128,2048]{1,0:T(8,128)(2,1)S(1)}, bf16[128,2048]{1,0:T(8,128)(2,1)S(1)}, u32[]{:S(2)}, u32[]{:S(2)}) collective-permute-start(bf16[128,2048]{1,0:T(8,128)(2,1)S(1)} %collective-permute-done.36.refs_6_), channel_id=1, source_target_pairs={{0,2},{2,0},{4,6},{6,4},{8,10},{10,8},{12,14},{14,12},{16,18},{18,... | collective-permute-start | bytes 1572872 | tf_op jit(solution)/shard_map/ppermute | solution.py:403
  295.0 8.6 %collective-permute-start.45 = (bf16[64,2048]{1,0:T(8,128)(2,1)S(1)}, bf16[64,2048]{1,0:T(8,128)(2,1)S(1)}, u32[]{:S(2)}, u32[]{:S(2)}) collective-permute-start(bf16[64,2048]{1,0:T(8,128)(2,1)S(1)} %collective-permute-done.43.refs_0_), channel_id=1, source_target_pairs={{0,2},{2,0},{4,6},{6,4},{8,10},{10,8},{12,14},{14,12},{16,18},{18,... | collective-permute-start | bytes 786440 | tf_op jit(solution)/shard_map/ppermute | solution.py:403
  300.3 4.9 %collective-permute-start.46 = (bf16[128,2048]{1,0:T(8,128)(2,1)S(1)}, bf16[128,2048]{1,0:T(8,128)(2,1)S(1)}, u32[]{:S(2)}, u32[]{:S(2)}) collective-permute-start(bf16[128,2048]{1,0:T(8,128)(2,1)S(1)} %collective-permute-done.37.refs_1_), channel_id=1, source_target_pairs={{0,2},{2,0},{4,6},{6,4},{8,10},{10,8},{12,14},{14,12},{16,18},{18,... | collective-permute-start | bytes 1572872 | tf_op jit(solution)/shard_map/ppermute | solution.py:403
  301.6 3.6 %collective-permute-start.52 = (bf16[128,2048]{1,0:T(8,128)(2,1)S(1)}, bf16[128,2048]{1,0:T(8,128)(2,1)S(1)}, u32[]{:S(2)}, u32[]{:S(2)}) collective-permute-start(bf16[128,2048]{1,0:T(8,128)(2,1)S(1)} %collective-permute-done.38.refs_7_), channel_id=1, source_target_pairs={{0,2},{2,0},{4,6},{6,4},{8,10},{10,8},{12,14},{14,12},{16,18},{18,... | collective-permute-start | bytes 1572872 | tf_op jit(solution)/shard_map/ppermute | solution.py:403
  301.6 9.1 %collective-permute-start.41 = (bf16[64,2176]{1,0:T(8,128)(2,1)S(1)}, bf16[64,2176]{1,0:T(8,128)(2,1)S(1)}, u32[]{:S(2)}, u32[]{:S(2)}) collective-permute-start(bf16[64,2176]{1,0:T(8,128)(2,1)S(1)} %collective-permute-done.39.refs_3_), channel_id=1, source_target_pairs={{0,8},{2,10},{8,16},{10,18},{16,24},{18,26},{24,28},{26,30},{28,20... | collective-permute-start | bytes 835592 | tf_op jit(solution)/shard_map/ppermute | solution.py:400
  302.1 8.8 %collective-permute-start.42 = (bf16[64,2176]{1,0:T(8,128)(2,1)S(1)}, bf16[64,2176]{1,0:T(8,128)(2,1)S(1)}, u32[]{:S(2)}, u32[]{:S(2)}) collective-permute-start(bf16[64,2176]{1,0:T(8,128)(2,1)S(1)} %collective-permute-done.40.refs_5_), channel_id=1, source_target_pairs={{0,4},{2,6},{8,0},{10,2},{16,8},{18,10},{24,16},{26,18},{28,24},{3... | collective-permute-start | bytes 835592 | tf_op jit(solution)/shard_map/ppermute | solution.py:400
  310.9 8.1 %collective-permute-start.54 = (bf16[64,2176]{1,0:T(8,128)(2,1)S(1)}, bf16[64,2176]{1,0:T(8,128)(2,1)S(1)}, u32[]{:S(2)}, u32[]{:S(2)}) collective-permute-start(bf16[64,2176]{1,0:T(8,128)(2,1)S(1)} %collective-permute-done.41.refs_2_), channel_id=1, source_target_pairs={{0,8},{2,10},{8,16},{10,18},{16,24},{18,26},{24,28},{26,30},{28,20... | collective-permute-start | bytes 835592 | tf_op jit(solution)/shard_map/ppermute | solution.py:400
  311.8 7.7 %collective-permute-start.55 = (bf16[64,2176]{1,0:T(8,128)(2,1)S(1)}, bf16[64,2176]{1,0:T(8,128)(2,1)S(1)}, u32[]{:S(2)}, u32[]{:S(2)}) collective-permute-start(bf16[64,2176]{1,0:T(8,128)(2,1)S(1)} %collective-permute-done.42.refs_6_), channel_id=1, source_target_pairs={{0,4},{2,6},{8,0},{10,2},{16,8},{18,10},{24,16},{26,18},{28,24},{3... | collective-permute-start | bytes 835592 | tf_op jit(solution)/shard_map/ppermute | solution.py:400
  312.9 7.9 %collective-permute-start.62 = (bf16[64,2176]{1,0:T(8,128)(2,1)S(1)}, bf16[64,2176]{1,0:T(8,128)(2,1)S(1)}, u32[]{:S(2)}, u32[]{:S(2)}) collective-permute-start(bf16[64,2176]{1,0:T(8,128)(2,1)S(1)} %ring_add.35.refs_4_), channel_id=1, source_target_pairs={{0,2},{2,0},{4,6},{6,4},{8,10},{10,8},{12,14},{14,12},{16,18},{18,... | collective-permute-start | bytes 835592 | tf_op jit(solution)/shard_map/ppermute | solution.py:403
  312.9 8.7 %collective-permute-start.61 = (bf16[64,2176]{1,0:T(8,128)(2,1)S(1)}, bf16[64,2176]{1,0:T(8,128)(2,1)S(1)}, u32[]{:S(2)}, u32[]{:S(2)}) collective-permute-start(bf16[64,2176]{1,0:T(8,128)(2,1)S(1)} %collective-permute-done.39.refs_3_), channel_id=1, source_target_pairs={{0,2},{2,0},{4,6},{6,4},{8,10},{10,8},{12,14},{14,12},{16,18},{18,... | collective-permute-start | bytes 835592 | tf_op jit(solution)/shard_map/ppermute | solution.py:403
  313.4 12.9 %collective-permute-start.63 = (bf16[64,2176]{1,0:T(8,128)(2,1)S(1)}, bf16[64,2176]{1,0:T(8,128)(2,1)S(1)}, u32[]{:S(2)}, u32[]{:S(2)}) collective-permute-start(bf16[64,2176]{1,0:T(8,128)(2,1)S(1)} %collective-permute-done.40.refs_5_), channel_id=1, source_target_pairs={{0,2},{2,0},{4,6},{6,4},{8,10},{10,8},{12,14},{14,12},{16,18},{18,... | collective-permute-start | bytes 835592 | tf_op jit(solution)/shard_map/ppermute | solution.py:403
  319.0 7.8 %collective-permute-start.60 = (bf16[64,2176]{1,0:T(8,128)(2,1)S(1)}, bf16[64,2176]{1,0:T(8,128)(2,1)S(1)}, u32[]{:S(2)}, u32[]{:S(2)}) collective-permute-start(bf16[64,2176]{1,0:T(8,128)(2,1)S(1)} %collective-permute-done.41.refs_2_), channel_id=1, source_target_pairs={{0,2},{2,0},{4,6},{6,4},{8,10},{10,8},{12,14},{14,12},{16,18},{18,... | collective-permute-start | bytes 835592 | tf_op jit(solution)/shard_map/ppermute | solution.py:403
  319.5 5.7 %collective-permute-start.57 = (bf16[32,2176]{1,0:T(8,128)(2,1)S(1)}, bf16[32,2176]{1,0:T(8,128)(2,1)S(1)}, u32[]{:S(2)}, u32[]{:S(2)}) collective-permute-start(bf16[32,2176]{1,0:T(8,128)(2,1)S(1)} %slice.54), channel_id=1, source_target_pairs={{0,4},{2,6},{8,0},{10,2},{16,8},{18,10},{24,16},{26,18},{28,24},{3... | collective-permute-start | bytes 417800 | tf_op jit(solution)/shard_map/ppermute | solution.py:400
  320.8 5.5 %collective-permute-start.56 = (bf16[32,2176]{1,0:T(8,128)(2,1)S(1)}, bf16[32,2176]{1,0:T(8,128)(2,1)S(1)}, u32[]{:S(2)}, u32[]{:S(2)}) collective-permute-start(bf16[32,2176]{1,0:T(8,128)(2,1)S(1)} %slice.53), channel_id=1, source_target_pairs={{0,8},{2,10},{8,16},{10,18},{16,24},{18,26},{24,28},{26,30},{28,20... | collective-permute-start | bytes 417800 | tf_op jit(solution)/shard_map/ppermute | solution.py:400
  321.6 6.4 %collective-permute-start.64 = (bf16[64,2176]{1,0:T(8,128)(2,1)S(1)}, bf16[64,2176]{1,0:T(8,128)(2,1)S(1)}, u32[]{:S(2)}, u32[]{:S(2)}) collective-permute-start(bf16[64,2176]{1,0:T(8,128)(2,1)S(1)} %collective-permute-done.42.refs_6_), channel_id=1, source_target_pairs={{0,2},{2,0},{4,6},{6,4},{8,10},{10,8},{12,14},{14,12},{16,18},{18,... | collective-permute-start | bytes 835592 | tf_op jit(solution)/shard_map/ppermute | solution.py:403
  325.2 3.1 collective-permute-start.59
  326.3 2.0 collective-permute-start.65
  (16 other events, 129.8 us)
